TPU v7x, 256 devices: a whole 4x4x8 slice. The times are simulated.
256 devices in a mesh: dp: 32 (over z, y_hi, core), owner: 8 (over y_lo, x).
Axes of the slice: x: 4, y: 4 (y_hi: 2, y_lo: 2; y = y_hi * 2 + y_lo), z: 8, core: 2. Of those that a mesh axis runs over, the one named last changes fastest.
Arguments:
- hidden: bfloat16 [4096, 4096], P('dp'), may hold values from -6 to 6
- norm_gain: float32 [4096], replicated, may hold values from 0.3 to 3
- cotangent: bfloat16 [4096, 6144], P('dp'), may hold values from -30 to 30
Outputs:
- update: bfloat16 [6144, 4096], P('dp', 'owner')
All inputs are finite; a program needn't handle non-finite values. Where the computation divides by a largest or mean magnitude, that divisor is 1e-20 or more.
Results may differ from a plain program's by a relative error of at most 0.014.
Values may be sent and summed in bfloat16 or wider, within the bound.
No kernel may reach another device: no remote copies, remote signals or barrier semaphores. Data moves between devices by JAX's collectives and lax.ppermute only.
A program may use at most 128 MiB of HBM per device.

v0:
```python
import functools

import jax
import jax.numpy as jnp
from jax import lax
from jax.experimental import pallas as pl
from jax.experimental.pallas import tpu as pltpu
from jax.sharding import Mesh
from jax.sharding import PartitionSpec as P

TILE = 1024
PIECE = 256
HALF = 512
Z, YH, CORE, YL, X = "dp_0", "dp_1", "dp_2", "owner_0", "owner_1"
DP = (Z, YH, CORE)
OWNER = (YL, X)
DAMPING = 0.1
bf16, f32 = jnp.bfloat16, jnp.float32
PARAMS = pltpu.CompilerParams(vmem_limit_bytes=48 * 1024 * 1024)
SMEM = pl.BlockSpec(memory_space=pltpu.SMEM)

AWAY = (4, 3, 3, 2, 2, 1, 1, 0, 0)
SWAP2 = [(0, 1), (1, 0)]
SWAP_X = [(0, 1), (1, 0), (2, 3), (3, 2)]
SWAP_BOTH = [(4 * a + b, 4 * (1 - a) + (b ^ 1)) for a in range(2) for b in range(4)]


def tdot(a, b):
    return lax.dot_general(a, b, (((0,), (0,)), ((), ())), preferred_element_type=f32)


def mdot(a, b):
    return jnp.dot(a, b, preferred_element_type=f32)


def aligned(start, size):
    return pl.ds(pl.multiple_of(start, size), size)


def pick_kernel(out_blocks, at_ref, cot_ref, pick_ref):
    h, k = at_ref[0], at_ref[1]
    for j in range(out_blocks):
        here = slice(j * HALF, (j + 1) * HALF)
        there = slice(out_blocks * HALF + j * PIECE, out_blocks * HALF + (j + 1) * PIECE)
        pick_ref[:, here] = cot_ref[:, aligned(j * TILE + h * HALF, HALF)]
        pick_ref[:, there] = cot_ref[:, aligned(j * TILE + k * PIECE, PIECE)]


def factor_kernel(out_blocks, at_ref, pick_ref, recv_ref, own_ref, got_ref, part_ref):
    i = pl.program_id(0)
    h, plane, block, piece = at_ref[0], at_ref[2 + 3 * i], at_ref[3 + 3 * i], at_ref[4 + 3 * i]
    left = aligned(block * HALF + piece * PIECE, PIECE)
    right = aligned(out_blocks * HALF + block * PIECE, PIECE)
    part_ref[0, :, :PIECE] = (
        tdot(pick_ref[:, left], pick_ref[:, right]) + tdot(recv_ref[:, left], recv_ref[:, right])
    ).astype(bf16)
    rows, here = aligned((2 * h + piece) * PIECE, PIECE), aligned(plane * 128, 128)
    part_ref[0, :, PIECE:] = (
        tdot(own_ref[:, rows], own_ref[:, here]) + tdot(got_ref[:, rows], got_ref[:, here])
    ).astype(bf16)


def cross_kernel(at_ref, pick_ref, recv_ref, own_ref, got_ref, keep_ref, give_ref):
    i = pl.program_id(0)
    yh, block, piece = at_ref[1], at_ref[3 + 3 * i], at_ref[4 + 3 * i]
    for side, ref in ((yh, keep_ref), (1 - yh, give_ref)):
        rows = aligned(block * HALF + piece * PIECE + side * 128, 128)
        ref[0] = (
            tdot(pick_ref[:, rows], own_ref[...]) + tdot(recv_ref[:, rows], got_ref[...])
        ).astype(bf16)


def assemble_out_kernel(at_ref, own_ref, other_ref, *refs):
    yl, x = at_ref[0], at_ref[1]
    out_ref = refs[-1]
    for s in range(4):
        source = (x - s + 4) % 4
        for b in range(2):
            column = 2 * jnp.where(b == 0, yl, 1 - yl) + source // 2
            value = (own_ref, other_ref)[b][...] if s == 0 else refs[s - 1][b]
            out_ref[source % 2, :, aligned(column * PIECE, PIECE)] = value


def scale_of(tokens, sums_ref):
    largest = jnp.zeros((), f32)
    for r in range(4):
        rows = matrix_rows(tokens, sums_ref, r * PIECE)
        largest = jnp.maximum(largest, jnp.max(jnp.sum(jnp.abs(rows), axis=1)))
    return 1.0 / largest


def eye_rows(start, count):
    row = lax.broadcasted_iota(jnp.int32, (count, TILE), 0) + start
    return (row == lax.broadcasted_iota(jnp.int32, (count, TILE), 1)).astype(f32)


def matrix_rows(tokens, sums_ref, start):
    return sums_ref[start : start + PIECE, :].astype(f32) / tokens + DAMPING * eye_rows(start, PIECE)


def in_inverse_kernel(
    tokens, at_ref, shard_ref, one_ref, two_ref, three_ref, far_ref, other_ref,
    out_ref, sums_ref, first_ref, low_ref,
):
    z, core = at_ref[0], at_ref[1]
    back = 1 - 2 * core

    def put(h, away, value):
        here = aligned((z + away + 8) % 8 * 128, 128)
        for piece in range(2):
            rows = aligned((2 * h + piece) * PIECE, PIECE)
            sums_ref[rows, here] = value[:, piece * 128 : (piece + 1) * 128]

    for h in range(2):
        put(h, 0, shard_ref[h])
        for d, ref in ((1, one_ref), (2, two_ref), (3, three_ref)):
            put(h, back * d, ref[h])
            put(h, -back * d, other_ref[2 * (d - 1) + h])
    put(core, 4, far_ref[0])
    put(1 - core, 4, other_ref[6])
    scale = scale_of(tokens, sums_ref)
    for r in range(4):
        here = slice(r * PIECE, (r + 1) * PIECE)
        rows = matrix_rows(tokens, sums_ref, r * PIECE)
        first = 2.0 * scale * eye_rows(r * PIECE, PIECE) - (scale * scale) * rows
        first_ref[here, :] = first
        low_ref[here, :] = first.astype(bf16)
        sums_ref[here, :] = rows.astype(bf16)
    for r in range(4):
        here = slice(r * PIECE, (r + 1) * PIECE)
        product = mdot(low_ref[here, :], sums_ref[...]).astype(bf16)
        out_ref[here, :] = (2.0 * first_ref[here, :] - mdot(product, low_ref[...])).astype(bf16)


def out_inverse_kernel(tokens, count, at_ref, own_ref, other_ref, out_ref, sums_ref, first_ref, low_ref):
    core = at_ref[0]
    for half in range(2):
        sums_ref[aligned((2 * half + core) * PIECE, PIECE), :] = own_ref[half]
        sums_ref[aligned((2 * half + 1 - core) * PIECE, PIECE), :] = other_ref[half]
    scale = scale_of(tokens, sums_ref)
    first_ref[:count, :] = jnp.zeros((count, TILE), f32)
    first_ref[count + TILE :, :] = jnp.zeros((count, TILE), f32)
    for r in range(4):
        here = slice(r * PIECE, (r + 1) * PIECE)
        rows = matrix_rows(tokens, sums_ref, r * PIECE)
        first = 2.0 * scale * eye_rows(r * PIECE, PIECE) - (scale * scale) * rows
        first_ref[count + r * PIECE : count + (r + 1) * PIECE, :] = first
        low_ref[here, :] = first.astype(bf16)
        sums_ref[here, :] = rows.astype(bf16)
    for part in range(2):
        rows = first_ref[pl.ds(pl.multiple_of(at_ref[1 + part], 64), count), :]
        product = mdot(rows.astype(bf16), sums_ref[...]).astype(bf16)
        out_ref[part * count : (part + 1) * count, :] = (
            2.0 * rows - mdot(product, low_ref[...])
        ).astype(bf16)


def call(kernel, outs, *args, scratch=()):
    outs = [jax.ShapeDtypeStruct(shape, dtype) for shape, dtype in outs]

    def whole(a):
        return pl.BlockSpec(a.shape, lambda i: (0,) * len(a.shape))

    result = pl.pallas_call(
        kernel,
        grid=(1,),
        out_shape=outs,
        in_specs=[SMEM] + [whole(a) for a in args[1:]],
        out_specs=[whole(a) for a in outs],
        scratch_shapes=[pltpu.VMEM(shape, dtype) for shape, dtype in scratch],
        compiler_params=PARAMS,
    )(*args)
    return result[0] if len(outs) == 1 else result


def ring_pairs(away=0, skip=False):
    pairs = []
    for plane in range(8):
        for core, way in ((0, -1), (1, 1)):
            if not skip or (plane + way * away) % 4 != 2:
                pairs.append((2 * plane + core, 2 * ((plane + way) % 8) + core))
    return pairs


def phase(*sends):
    values = lax.optimization_barrier(tuple(send[0] for send in sends))
    got = [lax.ppermute(value, *send[1:]) for value, send in zip(values, sends)]
    return lax.optimization_barrier(tuple(got))


def added(*parts):
    return functools.reduce(jnp.add, [p.astype(f32) for p in parts])


def in_order(flag, own, other):
    first = jnp.where(flag == 0, own, other)
    second = jnp.where(flag == 0, other, own)
    return jnp.stack([first, second])


def all_sum(value, axis):
    n = lax.axis_size(axis)
    shares = lax.all_to_all(jnp.full((n, 128), value, f32), axis, 0, 0, tiled=True)
    return jnp.sum(shares[:, 0])


def shards(hidden, norm_gain, cotangent):
    z, yh, core = lax.axis_index(Z), lax.axis_index(YH), lax.axis_index(CORE)
    yl, x = lax.axis_index(YL), lax.axis_index(X)
    k, h = 2 * yl + x // 2, x % 2
    here, width = hidden.shape
    out_width = cotangent.shape[1]
    out_blocks = out_width // TILE
    tokens = here * lax.axis_size(DP)

    def numbers(*values):
        return jnp.stack([jnp.asarray(v, jnp.int32) for v in values])

    pick = call(
        functools.partial(pick_kernel, out_blocks),
        [((here, out_blocks * (HALF + PIECE)), bf16)],
        numbers(h, k),
        cotangent,
    )
    recv = lax.ppermute(pick, CORE, SWAP2)

    states = hidden.astype(f32)
    rms = lax.rsqrt(jnp.mean(states * states, axis=1, keepdims=True) + 1e-05)
    gain = lax.dynamic_slice_in_dim(norm_gain, k * TILE, TILE)
    mine = lax.dynamic_slice_in_dim(hidden, k * TILE, TILE, 1)
    normed = (mine.astype(f32) * rms * gain).astype(bf16)
    normed_recv = lax.ppermute(normed, CORE, SWAP2)

    way = 2 * core - 1
    table = []
    for i, away in enumerate(AWAY):
        plane = (z + way * away + 8) % 8
        piece = core if i in (0, 7) else 1 - core if i == 8 else (i + 1) % 2
        table += [plane, 3 * (plane // 4) + plane % 4 - plane % 4 // 2, piece]
    table = numbers(h, yh, *table)

    def slots(kernel, count, block, n_out):
        tokens_in = (pick, recv, normed, normed_recv)
        return pl.pallas_call(
            kernel,
            grid_spec=pltpu.PrefetchScalarGridSpec(
                num_scalar_prefetch=1,
                grid=(count,),
                in_specs=[pl.BlockSpec(a.shape, lambda i, at: (0, 0)) for a in tokens_in],
                out_specs=[pl.BlockSpec((1, *block), lambda i, at: (i, 0, 0))] * n_out,
            ),
            out_shape=[jax.ShapeDtypeStruct((count, *block), bf16)] * n_out,
            compiler_params=PARAMS,
        )(table, *tokens_in)

    (part,) = slots(functools.partial(factor_kernel, out_blocks), 9, (PIECE, PIECE + 128), 1)
    keep, give = slots(cross_kernel, 8, (128, TILE), 2)

    def y_send(slot):
        return give[slot], YH, SWAP2

    def ring(value, *args):
        return value, (Z, CORE), ring_pairs(*args)

    def widened(got):
        nothing = jnp.zeros_like(got)
        return in_order(core, got, nothing)

    (far,) = phase(ring(part[0]))
    far, y0 = phase(ring(added(part[1:3], widened(far)).astype(bf16)), y_send(0))
    far, y1 = phase(ring(added(part[3:5], far).astype(bf16)), y_send(1))
    far, y2 = phase(ring(added(part[5:7], far).astype(bf16)), y_send(2))
    both_in = jnp.concatenate([far[0, :, PIECE:], far[1, :, PIECE:]], 1)
    out_own = jnp.where(core == 0, far[0, :, :PIECE], far[1, :, :PIECE])
    out_other = jnp.where(core == 0, far[1, :, :PIECE], far[0, :, :PIECE])
    (other,) = phase((jnp.concatenate([out_other, both_in], 1), CORE, SWAP2))
    here_in = in_order(core, part[7, :, PIECE:], part[8, :, PIECE:])
    local = jnp.concatenate([part[7, :, :PIECE], here_in[0], here_in[1]], 1)
    tiles = (added(jnp.concatenate([out_own, both_in], 1), other) + local.astype(f32)).astype(bf16)
    other, far = phase((tiles, YH, SWAP2), ring(added(keep[0], y0).astype(bf16), 4, True))
    tiles = added(tiles, other).astype(bf16)
    out_tile, in_tile = tiles[:, :PIECE], tiles[:, PIECE:]
    near_in, near_out, far, y3 = phase(
        (in_tile, X, SWAP_X),
        (out_tile, YL, SWAP2),
        ring(added(keep[1:3], jnp.stack([y1, y2]), widened(far)).astype(bf16), 3, True),
        y_send(3),
    )
    shard = in_order(h, in_tile, near_in)
    both = jnp.stack([out_tile, near_out])

    def x_send(s):
        return both, X, [(i, (i + s) % 4) for i in range(4)]

    one, x1 = phase(ring(shard), x_send(1))
    two, x2 = phase(ring(one), x_send(2))
    three, x3 = phase(ring(two), x_send(3))
    last, y4 = phase(ring(jnp.where(core == 0, three[:1], three[1:])), y_send(4))
    out_half = call(
        assemble_out_kernel, [((2, PIECE, TILE), bf16)], numbers(yl, x), out_tile, near_out, x1, x2, x3
    )
    cross, in_other, y5, y6 = phase(
        ring(added(keep[3:5], jnp.stack([y3, y4]), far).astype(bf16), 2, True),
        (jnp.concatenate([one, two, three, last], 0), CORE, SWAP2),
        y_send(5),
        y_send(6),
    )
    cross, out_other, y7 = phase(
        ring(added(keep[5:7], jnp.stack([y5, y6]), cross).astype(bf16), 1, True),
        (out_half, CORE, SWAP2),
        y_send(7),
    )
    (other,) = phase((jnp.where(core == 0, cross[1], cross[0]), CORE, SWAP2))
    cross = added(jnp.where(core == 0, cross[0], cross[1]), other, keep[7], y7).astype(bf16)
    square = (TILE, TILE)
    in_inverse = call(
        functools.partial(in_inverse_kernel, tokens),
        [(square, bf16)],
        numbers(z, core),
        shard,
        one,
        two,
        three,
        last,
        in_other,
        scratch=[(square, bf16), (square, f32), (square, bf16)],
    )

    m = z % 4
    row = 2 * yh + core
    slice_rows = out_width // lax.axis_size(DP)
    base = TILE * (m - m // 2)
    near = jnp.where(m == 3, 2, m + 1)
    own_at = jnp.where(m == 2, TILE, slice_rows * (4 * m + row) - base)
    near_at = jnp.where(m == 2, TILE, slice_rows * (4 * near + row) - base)
    own_at, near_at = [jnp.clip(a, -slice_rows, TILE) + slice_rows for a in (own_at, near_at)]
    out_inverse = call(
        functools.partial(out_inverse_kernel, tokens, slice_rows),
        [((2 * slice_rows, TILE), bf16)],
        numbers(core, own_at, near_at),
        out_half,
        out_other,
        scratch=[(square, bf16), ((TILE + 2 * slice_rows, TILE), f32), (square, bf16)],
    )

    middle = mdot(cross, in_inverse).astype(bf16)
    mine = lax.dynamic_slice_in_dim(middle, h * HALF, HALF, 1)
    theirs = lax.dynamic_slice_in_dim(middle, (1 - h) * HALF, HALF, 1)
    near_x, near_y, near_xy = phase(
        (theirs, X, SWAP_X), (mine, YH, SWAP2), (theirs, (YH, X), SWAP_BOTH)
    )
    middle = in_order(h, in_order(yh, mine, near_y), in_order(yh, near_x, near_xy))
    other = lax.ppermute(middle, CORE, SWAP2)
    middle = jnp.moveaxis(in_order(core, middle, other), 0, 1).reshape(TILE, HALF)
    result = mdot(out_inverse, middle)

    near_part = result[slice_rows:].astype(bf16)
    up = lax.ppermute(near_part, Z, [(0, 1), (1, 2), (4, 5), (5, 6)])
    down = lax.ppermute(near_part, Z, [(3, 2), (7, 6)])
    squares = all_sum(all_sum(jnp.sum(result * result), OWNER), DP)
    summed = result[:slice_rows] + up.astype(f32) + down.astype(f32)
    return (summed * lax.rsqrt(squares / (width * out_width) + 1e-06)).astype(bf16)


def solution(mesh):
    split = Mesh(mesh.devices.reshape(8, 2, 2, 2, 4), DP + OWNER)
    return jax.shard_map(
        shards,
        mesh=split,
        in_specs=(P(DP, None), P(), P(DP, None)),
        out_specs=P(DP, OWNER),
        check_vma=False,
    )
```

profile of v0, /device:TPU:16, one launch (start us, length us, event | category | flops | bytes accessed | tf_op | source)
XLA Modules:
  0.0 214.5 jit_solution(2218687671736401129)
XLA Ops:
  6.1 3.3 %shard_map.38 = bf16[9,256,384]{2,1,0:T(8,128)(2,1)S(1)} custom-call(s32[29]{0:T(128)S(1)} %stack.202.at_ref, bf16[128,4608]{1,0:T(8,128)(2,1)S(1)} %shard_map.37.pick_ref, bf16[128,4608]{1,0:T(8,128)(2,1)S(1)} %collective-permute-done.recv_ref, bf16[128,1024]{1,0:T(8,128)(2,1)S(1)} %multiply_convert_fusion.own_ref, ...), custom_call_target="tpu_custom_call" | custom-call | tf_op jit(solution)/shard_map/pallas_call | solution.py:244
  9.4 5.9 %collective-permute-start.2 = (bf16[256,384]{1,0:T(8,128)(2,1)S(1)}, bf16[256,384]{1,0:T(8,128)(2,1)S(1)}, u32[]{:S(2)}, u32[]{:S(2)}) collective-permute-start(bf16[256,384]{1,0:T(8,128)(2,1)S(1)} %slice_bitcast_fusion.8), channel_id=1, source_target_pairs={{0,224},{8,40},{32,0},{40,72},{64,32},{72,104},{96,64},{104,136},{... | collective-permute-start | bytes 589832 | tf_op jit(solution)/shard_map/ppermute | solution.py:187
  15.4 5.7 %shard_map.39 = (bf16[8,128,1024]{2,1,0:T(8,128)(2,1)S(1)}, bf16[8,128,1024]{2,1,0:T(8,128)(2,1)}) custom-call(s32[29]{0:T(128)S(1)} %stack.202.at_ref, bf16[128,4608]{1,0:T(8,128)(2,1)S(1)} %shard_map.37.pick_ref, bf16[128,4608]{1,0:T(8,128)(2,1)S(1)} %collective-permute-done.recv_ref, bf16[128,1024]{1,0:T(8,128)(2,1)S(1)} %multiply_convert_fusion.own_ref, ...), custom_call_target="tpu_custom_call" | custom-call | tf_op jit(solution)/shard_map/pallas_call | solution.py:244
  21.1 3.4 %slice_bitcast_fusion = (bf16[128,1024]{1,0:T(8,128)(2,1)}, bf16[128,1024]{1,0:T(8,128)(2,1)}, bf16[128,1024]{1,0:T(8,128)(2,1)}, bf16[128,1024]{1,0:T(8,128)(2,...) fusion(bf16[8,128,1024]{2,1,0:T(8,128)(2,1)} %get-tuple-element.67), kind=kLoop, calls=%fused_computation.41 | loop fusion | bytes 4194304 | tf_op jit(solution)/shard_map/squeeze | solution.py:260
  26.0 7.5 %collective-permute-done.4 = bf16[128,1024]{1,0:T(8,128)(2,1)S(1)} collective-permute-done((bf16[128,1024]{1,0:T(8,128)(2,1)S(1)}, bf16[128,1024]{1,0:T(8,128)(2,1)S(1)}, u32[]{:S(2)}, u32[]{:S(2)}) %collective-permute-start.4) | collective-permute-done | bytes 262176 | tf_op jit(solution)/shard_map/ppermute | solution.py:187
  35.4 7.5 %collective-permute-done.6 = bf16[128,1024]{1,0:T(8,128)(2,1)S(1)} collective-permute-done((bf16[128,1024]{1,0:T(8,128)(2,1)S(1)}, bf16[128,1024]{1,0:T(8,128)(2,1)S(1)}, u32[]{:S(2)}, u32[]{:S(2)}) %collective-permute-start.6) | collective-permute-done | bytes 262176 | tf_op jit(solution)/shard_map/ppermute | solution.py:187
  45.2 7.5 %collective-permute-done.8 = bf16[128,1024]{1,0:T(8,128)(2,1)S(1)} collective-permute-done((bf16[128,1024]{1,0:T(8,128)(2,1)S(1)}, bf16[128,1024]{1,0:T(8,128)(2,1)S(1)}, u32[]{:S(2)}, u32[]{:S(2)}) %collective-permute-start.8) | collective-permute-done | bytes 262176 | tf_op jit(solution)/shard_map/ppermute | solution.py:187
  55.0 3.5 %collective-permute-start.11 = (bf16[128,1024]{1,0:T(8,128)(2,1)S(1)}, bf16[128,1024]{1,0:T(8,128)(2,1)S(1)}, u32[]{:S(2)}, u32[]{:S(2)}) collective-permute-start(bf16[128,1024]{1,0:T(8,128)(2,1)S(1)} %fusion.2), channel_id=1, source_target_pairs={{0,224},{8,40},{32,0},{40,72},{96,64},{104,136},{128,96},{136,168}... | collective-permute-start | bytes 786440 | tf_op jit(solution)/shard_map/ppermute | solution.py:187
  58.6 6.0 %collective-permute-done.10 = bf16[256,512]{1,0:T(8,128)(2,1)S(1)} collective-permute-done((bf16[256,512]{1,0:T(8,128)(2,1)S(1)}, bf16[256,512]{1,0:T(8,128)(2,1)S(1)}, u32[]{:S(2)}, u32[]{:S(2)}) %collective-permute-start.10) | collective-permute-done | bytes 262176 | tf_op jit(solution)/shard_map/ppermute | solution.py:187
  65.7 3.7 %collective-permute-start.14 = (bf16[2,128,1024]{2,1,0:T(8,128)(2,1)}, bf16[2,128,1024]{2,1,0:T(8,128)(2,1)S(1)}, u32[]{:S(2)}, u32[]{:S(2)}) collective-permute-start(bf16[2,128,1024]{2,1,0:T(8,128)(2,1)} %add_convert_fusion.2), channel_id=1, source_target_pairs={{0,224},{8,40},{40,72},{64,32},{72,104},{96,64},{128,96},{136,168}... | collective-permute-start | bytes 1572872 | tf_op jit(solution)/shard_map/ppermute | solution.py:187
  69.4 3.2 %collective-permute-start.15 = (bf16[128,1024]{1,0:T(8,128)(2,1)S(1)}, bf16[128,1024]{1,0:T(8,128)(2,1)}, u32[]{:S(2)}, u32[]{:S(2)}) collective-permute-start(bf16[128,1024]{1,0:T(8,128)(2,1)S(1)} %get-tuple-element.88), channel_id=1, source_target_pairs={{0,16},{16,0},{1,17},{17,1},{2,18},{18,2},{3,19},{19,3},{4,20},{20... | collective-permute-start | bytes 786440 | tf_op jit(solution)/shard_map/ppermute | solution.py:187
  75.5 2.3 %collective-permute-done.12 = bf16[256,256]{1,0:T(8,128)(2,1)} collective-permute-done((bf16[256,256]{1,0:T(8,128)(2,1)S(1)}, bf16[256,256]{1,0:T(8,128)(2,1)}, u32[]{:S(2)}, u32[]{:S(2)}) %collective-permute-start.12) | collective-permute-done | bytes 131104 | tf_op jit(solution)/shard_map/ppermute | solution.py:187
  84.0 3.6 %collective-permute-done.16.one_ref = bf16[2,256,256]{2,1,0:T(8,128)(2,1)S(1)} collective-permute-done((bf16[2,256,256]{2,1,0:T(8,128)(2,1)S(1)}, bf16[2,256,256]{2,1,0:T(8,128)(2,1)S(1)}, u32[]{:S(2)}, u32[]{:S(2)}) %collective-permute-start.16) | collective-permute-done | bytes 262176 | tf_op jit(solution)/shard_map/ppermute | solution.py:187
  87.5 3.6 %collective-permute-done.17.refs_0_ = bf16[2,256,256]{2,1,0:T(8,128)(2,1)S(1)} collective-permute-done((bf16[2,256,256]{2,1,0:T(8,128)(2,1)S(1)}, bf16[2,256,256]{2,1,0:T(8,128)(2,1)S(1)}, u32[]{:S(2)}, u32[]{:S(2)}) %collective-permute-start.17) | collective-permute-done | bytes 262176 | tf_op jit(solution)/shard_map/ppermute | solution.py:187
  94.1 4.3 %collective-permute-done.18.two_ref = bf16[2,256,256]{2,1,0:T(8,128)(2,1)S(1)} collective-permute-done((bf16[2,256,256]{2,1,0:T(8,128)(2,1)S(1)}, bf16[2,256,256]{2,1,0:T(8,128)(2,1)S(1)}, u32[]{:S(2)}, u32[]{:S(2)}) %collective-permute-start.18) | collective-permute-done | bytes 262176 | tf_op jit(solution)/shard_map/ppermute | solution.py:187
  98.4 4.1 %collective-permute-done.19.refs_1_ = bf16[2,256,256]{2,1,0:T(8,128)(2,1)S(1)} collective-permute-done((bf16[2,256,256]{2,1,0:T(8,128)(2,1)S(1)}, bf16[2,256,256]{2,1,0:T(8,128)(2,1)S(1)}, u32[]{:S(2)}, u32[]{:S(2)}) %collective-permute-start.19) | collective-permute-done | bytes 262176 | tf_op jit(solution)/shard_map/ppermute | solution.py:187
  104.2 4.6 %collective-permute-done.20.three_ref = bf16[2,256,256]{2,1,0:T(8,128)(2,1)S(1)} collective-permute-done((bf16[2,256,256]{2,1,0:T(8,128)(2,1)S(1)}, bf16[2,256,256]{2,1,0:T(8,128)(2,1)S(1)}, u32[]{:S(2)}, u32[]{:S(2)}) %collective-permute-start.20) | collective-permute-done | bytes 262176 | tf_op jit(solution)/shard_map/ppermute | solution.py:187
  108.8 2.3 %collective-permute-done.21.refs_2_ = bf16[2,256,256]{2,1,0:T(8,128)(2,1)S(1)} collective-permute-done((bf16[2,256,256]{2,1,0:T(8,128)(2,1)S(1)}, bf16[2,256,256]{2,1,0:T(8,128)(2,1)S(1)}, u32[]{:S(2)}, u32[]{:S(2)}) %collective-permute-start.21) | collective-permute-done | bytes 262176 | tf_op jit(solution)/shard_map/ppermute | solution.py:187
  112.8 4.8 %collective-permute-done.22.far_ref = bf16[1,256,256]{2,1,0:T(8,128)(2,1)S(1)} collective-permute-done((bf16[1,256,256]{2,1,0:T(8,128)(2,1)S(1)}, bf16[1,256,256]{2,1,0:T(8,128)(2,1)S(1)}, u32[]{:S(2)}, u32[]{:S(2)}) %collective-permute-start.22) | collective-permute-done | bytes 131104 | tf_op jit(solution)/shard_map/ppermute | solution.py:187
  117.6 3.3 %collective-permute-done.23 = bf16[128,1024]{1,0:T(8,128)(2,1)S(1)} collective-permute-done((bf16[128,1024]{1,0:T(8,128)(2,1)}, bf16[128,1024]{1,0:T(8,128)(2,1)S(1)}, u32[]{:S(2)}, u32[]{:S(2)}) %collective-permute-start.23) | collective-permute-done | bytes 262176 | tf_op jit(solution)/shard_map/ppermute | solution.py:187
  124.8 2.6 %collective-permute-start.27 = (bf16[128,1024]{1,0:T(8,128)(2,1)S(1)}, bf16[128,1024]{1,0:T(8,128)(2,1)S(1)}, u32[]{:S(2)}, u32[]{:S(2)}) collective-permute-start(bf16[128,1024]{1,0:T(8,128)(2,1)S(1)} %copy-done.23), channel_id=1, source_target_pairs={{0,16},{16,0},{1,17},{17,1},{2,18},{18,2},{3,19},{19,3},{4,20},{20... | collective-permute-start | bytes 786440 | tf_op jit(solution)/shard_map/ppermute | solution.py:187
  129.0 5.4 %collective-permute-done.26 = bf16[128,1024]{1,0:T(8,128)(2,1)S(1)} collective-permute-done((bf16[128,1024]{1,0:T(8,128)(2,1)S(1)}, bf16[128,1024]{1,0:T(8,128)(2,1)S(1)}, u32[]{:S(2)}, u32[]{:S(2)}) %collective-permute-start.26) | collective-permute-done | bytes 262176 | tf_op jit(solution)/shard_map/ppermute | solution.py:187
  134.4 5.2 %collective-permute-done.27 = bf16[128,1024]{1,0:T(8,128)(2,1)S(1)} collective-permute-done((bf16[128,1024]{1,0:T(8,128)(2,1)S(1)}, bf16[128,1024]{1,0:T(8,128)(2,1)S(1)}, u32[]{:S(2)}, u32[]{:S(2)}) %collective-permute-start.27) | collective-permute-done | bytes 262176 | tf_op jit(solution)/shard_map/ppermute | solution.py:187
  140.0 4.0 %collective-permute-start.28 = (bf16[2,128,1024]{2,1,0:T(8,128)(2,1)S(1)}, bf16[2,128,1024]{2,1,0:T(8,128)(2,1)S(1)}, u32[]{:S(2)}, u32[]{:S(2)}) collective-permute-start(bf16[2,128,1024]{2,1,0:T(8,128)(2,1)S(1)} %add_convert_fusion), channel_id=1, source_target_pairs={{0,224},{8,40},{32,0},{64,32},{72,104},{104,136},{128,96},{136,168... | collective-permute-start | bytes 1572872 | tf_op jit(solution)/shard_map/ppermute | solution.py:187
  144.9 7.3 %collective-permute-done.30 = bf16[128,1024]{1,0:T(8,128)(2,1)S(1)} collective-permute-done((bf16[128,1024]{1,0:T(8,128)(2,1)S(1)}, bf16[128,1024]{1,0:T(8,128)(2,1)S(1)}, u32[]{:S(2)}, u32[]{:S(2)}) %collective-permute-start.30) | collective-permute-done | bytes 262176 | tf_op jit(solution)/shard_map/ppermute | solution.py:187
  158.3 6.8 %shard_map.42 = bf16[1024,1024]{1,0:T(8,128)(2,1)S(1)} custom-call(s32[2]{0:T(128)S(1)} %pad_add_fusion.3.at_ref, bf16[2,256,256]{2,1,0:T(8,128)(2,1)S(1)} %copy-done.10, bf16[2,256,256]{2,1,0:T(8,128)(2,1)S(1)} %copy-done.6, bf16[2,256,256]{2,1,0:T(8,128)(2,1)S(1)} %copy-done.8, bf16[2,256,256]{2,1,0:T(8,128)(2,1)S(1)} %collective-permute-done.20.three_ref, ...), custom_call_target="tpu_custom_call" | custom-call | tf_op jit(solution)/shard_map/pallas_call | solution.py:164
  167.9 3.8 %collective-permute-start.34 = (bf16[128,512]{1,0:T(8,128)(2,1)S(1)}, bf16[128,512]{1,0:T(8,128)(2,1)S(1)}, u32[]{:S(2)}, u32[]{:S(2)}) collective-permute-start(bf16[128,512]{1,0:T(8,128)(2,1)S(1)} %get-tuple-element.125), channel_id=1, source_target_pairs={{0,17},{1,16},{2,19},{3,18},{16,1},{17,0},{18,3},{19,2},{4,21},{5,... | collective-permute-start | bytes 393224 | tf_op jit(solution)/shard_map/ppermute | solution.py:187
  172.6 4.4 %collective-permute-done.33 = bf16[128,512]{1,0:T(8,128)(2,1)S(1)} collective-permute-done((bf16[128,512]{1,0:T(8,128)(2,1)S(1)}, bf16[128,512]{1,0:T(8,128)(2,1)S(1)}, u32[]{:S(2)}, u32[]{:S(2)}) %collective-permute-start.33) | collective-permute-done | bytes 131104 | tf_op jit(solution)/shard_map/ppermute | solution.py:187
  178.1 4.6 %shard_map.41 = bf16[384,1024]{1,0:T(8,128)(2,1)S(1)} custom-call(s32[3]{0:T(128)S(1)} %pad_add_fusion.at_ref, bf16[2,256,1024]{2,1,0:T(8,128)(2,1)S(1)} %shard_map.40.own_ref, bf16[2,256,1024]{2,1,0:T(8,128)(2,1)S(1)} %copy-done.4), custom_call_target="tpu_custom_call" | custom-call | tf_op jit(solution)/shard_map/pallas_call | solution.py:164
  185.5 5.0 %all-to-all-start = ((f32[8,1,128]{2,1,0:T(1,128)}), f32[8,1,128]{2,1,0:T(1,128)S(1)}, u32[]{:S(2)}, u32[]{:S(2)}) async-start(f32[8,1,128]{2,1,0:T(1,128)} %broadcast_in_dim.16), calls=%async_computation | async-start | bytes 8192 | tf_op jit(solution)/shard_map/all_to_all | solution.py:203
  192.8 3.7 %all-to-all-done = f32[8,1,128]{2,1,0:T(1,128)S(1)} async-done(((f32[8,1,128]{2,1,0:T(1,128)}), f32[8,1,128]{2,1,0:T(1,128)S(1)}, u32[]{:S(2)}, u32[]{:S(2)}) %all-to-all-start) | async-done | bytes 4128 | tf_op jit(solution)/shard_map/all_to_all | solution.py:203
  197.8 14.6 %all_to_all.18 = f32[32,1,128]{2,1,0:T(1,128)S(1)} all-to-all(f32[32,1,128]{2,1,0:T(1,128)S(1)} %broadcast_in_dim.17), channel_id=1, replica_groups=mesh['dp_0'=8,'dp_1'=2,'dp_2'=2,'owner_0'=2,'owner_1'=4] {'dp_0','dp_1',..., dimensions={0} | all-to-all | bytes 32768 | tf_op jit(solution)/shard_map/all_to_all | solution.py:203
  (156 shorter events, 55.5 us)
Async XLA Ops:
  9.4 15.0 %collective-permute-start.2 = (bf16[256,384]{1,0:T(8,128)(2,1)S(1)}, bf16[256,384]{1,0:T(8,128)(2,1)S(1)}, u32[]{:S(2)}, u32[]{:S(2)}) collective-permute-start(bf16[256,384]{1,0:T(8,128)(2,1)S(1)} %slice_bitcast_fusion.8), channel_id=1, source_target_pairs={{0,224},{8,40},{32,0},{40,72},{64,32},{72,104},{96,64},{104,136},{... | collective-permute-start | bytes 589832 | tf_op jit(solution)/shard_map/ppermute | solution.py:187
  24.6 9.0 %collective-permute-start.3 = (bf16[2,256,384]{2,1,0:T(8,128)(2,1)S(1)}, bf16[2,256,384]{2,1,0:T(8,128)(2,1)S(1)}, u32[]{:S(2)}, u32[]{:S(2)}) collective-permute-start(bf16[2,256,384]{2,1,0:T(8,128)(2,1)S(1)} %add_convert_fusion.5), channel_id=1, source_target_pairs={{0,224},{8,40},{32,0},{40,72},{64,32},{72,104},{96,64},{104,136},{... | collective-permute-start | bytes 1179656 | tf_op jit(solution)/shard_map/ppermute | solution.py:187
  25.7 7.9 %collective-permute-start.4 = (bf16[128,1024]{1,0:T(8,128)(2,1)S(1)}, bf16[128,1024]{1,0:T(8,128)(2,1)S(1)}, u32[]{:S(2)}, u32[]{:S(2)}) collective-permute-start(bf16[128,1024]{1,0:T(8,128)(2,1)S(1)} %get-tuple-element.69), channel_id=1, source_target_pairs={{0,16},{16,0},{1,17},{17,1},{2,18},{18,2},{3,19},{19,3},{4,20},{20... | collective-permute-start | bytes 786440 | tf_op jit(solution)/shard_map/ppermute | solution.py:187
  33.7 9.3 %collective-permute-start.5 = (bf16[2,256,384]{2,1,0:T(8,128)(2,1)S(1)}, bf16[2,256,384]{2,1,0:T(8,128)(2,1)S(1)}, u32[]{:S(2)}, u32[]{:S(2)}) collective-permute-start(bf16[2,256,384]{2,1,0:T(8,128)(2,1)S(1)} %add_convert_fusion.4), channel_id=1, source_target_pairs={{0,224},{8,40},{32,0},{40,72},{64,32},{72,104},{96,64},{104,136},{... | collective-permute-start | bytes 1179656 | tf_op jit(solution)/shard_map/ppermute | solution.py:187
  35.1 7.9 %collective-permute-start.6 = (bf16[128,1024]{1,0:T(8,128)(2,1)S(1)}, bf16[128,1024]{1,0:T(8,128)(2,1)S(1)}, u32[]{:S(2)}, u32[]{:S(2)}) collective-permute-start(bf16[128,1024]{1,0:T(8,128)(2,1)S(1)} %get-tuple-element.72), channel_id=1, source_target_pairs={{0,16},{16,0},{1,17},{17,1},{2,18},{18,2},{3,19},{19,3},{4,20},{20... | collective-permute-start | bytes 786440 | tf_op jit(solution)/shard_map/ppermute | solution.py:187
  43.1 9.7 %collective-permute-start.7 = (bf16[2,256,384]{2,1,0:T(8,128)(2,1)S(1)}, bf16[2,256,384]{2,1,0:T(8,128)(2,1)S(1)}, u32[]{:S(2)}, u32[]{:S(2)}) collective-permute-start(bf16[2,256,384]{2,1,0:T(8,128)(2,1)S(1)} %add_convert_fusion.3), channel_id=1, source_target_pairs={{0,224},{8,40},{32,0},{40,72},{64,32},{72,104},{96,64},{104,136},{... | collective-permute-start | bytes 1179656 | tf_op jit(solution)/shard_map/ppermute | solution.py:187
  44.9 7.9 %collective-permute-start.8 = (bf16[128,1024]{1,0:T(8,128)(2,1)S(1)}, bf16[128,1024]{1,0:T(8,128)(2,1)S(1)}, u32[]{:S(2)}, u32[]{:S(2)}) collective-permute-start(bf16[128,1024]{1,0:T(8,128)(2,1)S(1)} %get-tuple-element.75), channel_id=1, source_target_pairs={{0,16},{16,0},{1,17},{17,1},{2,18},{18,2},{3,19},{19,3},{4,20},{20... | collective-permute-start | bytes 786440 | tf_op jit(solution)/shard_map/ppermute | solution.py:187
  54.6 9.9 %collective-permute-start.10 = (bf16[256,512]{1,0:T(8,128)(2,1)S(1)}, bf16[256,512]{1,0:T(8,128)(2,1)S(1)}, u32[]{:S(2)}, u32[]{:S(2)}) collective-permute-start(bf16[256,512]{1,0:T(8,128)(2,1)S(1)} %add_convert_fusion.7), channel_id=1, source_target_pairs={{0,16},{16,0},{1,17},{17,1},{2,18},{18,2},{3,19},{19,3},{4,20},{20... | collective-permute-start | bytes 786440 | tf_op jit(solution)/shard_map/ppermute | solution.py:187
  55.0 9.5 %collective-permute-start.11 = (bf16[128,1024]{1,0:T(8,128)(2,1)S(1)}, bf16[128,1024]{1,0:T(8,128)(2,1)S(1)}, u32[]{:S(2)}, u32[]{:S(2)}) collective-permute-start(bf16[128,1024]{1,0:T(8,128)(2,1)S(1)} %fusion.2), channel_id=1, source_target_pairs={{0,224},{8,40},{32,0},{40,72},{96,64},{104,136},{128,96},{136,168}... | collective-permute-start | bytes 786440 | tf_op jit(solution)/shard_map/ppermute | solution.py:187
  65.7 14.0 %collective-permute-start.14 = (bf16[2,128,1024]{2,1,0:T(8,128)(2,1)}, bf16[2,128,1024]{2,1,0:T(8,128)(2,1)S(1)}, u32[]{:S(2)}, u32[]{:S(2)}) collective-permute-start(bf16[2,128,1024]{2,1,0:T(8,128)(2,1)} %add_convert_fusion.2), channel_id=1, source_target_pairs={{0,224},{8,40},{40,72},{64,32},{72,104},{96,64},{128,96},{136,168}... | collective-permute-start | bytes 1572872 | tf_op jit(solution)/shard_map/ppermute | solution.py:187
  69.4 10.3 %collective-permute-start.15 = (bf16[128,1024]{1,0:T(8,128)(2,1)S(1)}, bf16[128,1024]{1,0:T(8,128)(2,1)}, u32[]{:S(2)}, u32[]{:S(2)}) collective-permute-start(bf16[128,1024]{1,0:T(8,128)(2,1)S(1)} %get-tuple-element.88), channel_id=1, source_target_pairs={{0,16},{16,0},{1,17},{17,1},{2,18},{18,2},{3,19},{19,3},{4,20},{20... | collective-permute-start | bytes 786440 | tf_op jit(solution)/shard_map/ppermute | solution.py:187
  80.9 6.6 %collective-permute-start.16 = (bf16[2,256,256]{2,1,0:T(8,128)(2,1)S(1)}, bf16[2,256,256]{2,1,0:T(8,128)(2,1)S(1)}, u32[]{:S(2)}, u32[]{:S(2)}) collective-permute-start(bf16[2,256,256]{2,1,0:T(8,128)(2,1)S(1)} %get-tuple-element.164.shard_ref), channel_id=1, source_target_pairs={{0,224},{8,40},{32,0},{40,72},{64,32},{72,104},{96,64},{104,136},{... | collective-permute-start | bytes 786440 | tf_op jit(solution)/shard_map/ppermute | solution.py:187
  82.5 8.7 %collective-permute-start.17 = (bf16[2,256,256]{2,1,0:T(8,128)(2,1)S(1)}, bf16[2,256,256]{2,1,0:T(8,128)(2,1)S(1)}, u32[]{:S(2)}, u32[]{:S(2)}) collective-permute-start(bf16[2,256,256]{2,1,0:T(8,128)(2,1)S(1)} %get-tuple-element.100), channel_id=1, source_target_pairs={{0,1},{1,2},{2,3},{3,0},{4,5},{5,6},{6,7},{7,4},{8,9},{9,10},{10,1... | collective-permute-start | bytes 786440 | tf_op jit(solution)/shard_map/ppermute | solution.py:187
  91.1 7.3 %collective-permute-start.18 = (bf16[2,256,256]{2,1,0:T(8,128)(2,1)S(1)}, bf16[2,256,256]{2,1,0:T(8,128)(2,1)S(1)}, u32[]{:S(2)}, u32[]{:S(2)}) collective-permute-start(bf16[2,256,256]{2,1,0:T(8,128)(2,1)S(1)} %collective-permute-done.16.one_ref), channel_id=1, source_target_pairs={{0,224},{8,40},{32,0},{40,72},{64,32},{72,104},{96,64},{104,136},{... | collective-permute-start | bytes 786440 | tf_op jit(solution)/shard_map/ppermute | solution.py:187
  92.3 10.1 %collective-permute-start.19 = (bf16[2,256,256]{2,1,0:T(8,128)(2,1)S(1)}, bf16[2,256,256]{2,1,0:T(8,128)(2,1)S(1)}, u32[]{:S(2)}, u32[]{:S(2)}) collective-permute-start(bf16[2,256,256]{2,1,0:T(8,128)(2,1)S(1)} %get-tuple-element.100), channel_id=1, source_target_pairs={{0,2},{1,3},{2,0},{3,1},{4,6},{5,7},{6,4},{7,5},{8,10},{9,11},{10,... | collective-permute-start | bytes 786440 | tf_op jit(solution)/shard_map/ppermute | solution.py:187
  102.5 6.4 %collective-permute-start.20 = (bf16[2,256,256]{2,1,0:T(8,128)(2,1)S(1)}, bf16[2,256,256]{2,1,0:T(8,128)(2,1)S(1)}, u32[]{:S(2)}, u32[]{:S(2)}) collective-permute-start(bf16[2,256,256]{2,1,0:T(8,128)(2,1)S(1)} %collective-permute-done.18.two_ref), channel_id=1, source_target_pairs={{0,224},{8,40},{32,0},{40,72},{64,32},{72,104},{96,64},{104,136},{... | collective-permute-start | bytes 786440 | tf_op jit(solution)/shard_map/ppermute | solution.py:187
  102.5 8.7 %collective-permute-start.21 = (bf16[2,256,256]{2,1,0:T(8,128)(2,1)S(1)}, bf16[2,256,256]{2,1,0:T(8,128)(2,1)S(1)}, u32[]{:S(2)}, u32[]{:S(2)}) collective-permute-start(bf16[2,256,256]{2,1,0:T(8,128)(2,1)S(1)} %get-tuple-element.100), channel_id=1, source_target_pairs={{0,3},{1,0},{2,1},{3,2},{4,7},{5,4},{6,5},{7,6},{8,11},{9,8},{10,9... | collective-permute-start | bytes 786440 | tf_op jit(solution)/shard_map/ppermute | solution.py:187
  111.2 9.7 %collective-permute-start.23 = (bf16[128,1024]{1,0:T(8,128)(2,1)}, bf16[128,1024]{1,0:T(8,128)(2,1)S(1)}, u32[]{:S(2)}, u32[]{:S(2)}) collective-permute-start(bf16[128,1024]{1,0:T(8,128)(2,1)} %get-tuple-element.105), channel_id=1, source_target_pairs={{0,16},{16,0},{1,17},{17,1},{2,18},{18,2},{3,19},{19,3},{4,20},{20... | collective-permute-start | bytes 786440 | tf_op jit(solution)/shard_map/ppermute | solution.py:187
  122.3 17.3 %collective-permute-start.25 = (bf16[7,256,256]{2,1,0:T(8,128)(2,1)S(1)}, bf16[7,256,256]{2,1,0:T(8,128)(2,1)S(1)}, u32[]{:S(2)}, u32[]{:S(2)}) collective-permute-start(bf16[7,256,256]{2,1,0:T(8,128)(2,1)S(1)} %pad_maximum_fusion), channel_id=1, source_target_pairs={{0,8},{8,0},{1,9},{9,1},{2,10},{10,2},{3,11},{11,3},{4,12},{12,4},... | collective-permute-start | bytes 2752520 | tf_op jit(solution)/shard_map/ppermute | solution.py:187
  122.4 17.2 %collective-permute-start.24 = (bf16[2,128,1024]{2,1,0:T(8,128)(2,1)S(1)}, bf16[2,128,1024]{2,1,0:T(8,128)(2,1)S(1)}, u32[]{:S(2)}, u32[]{:S(2)}) collective-permute-start(bf16[2,128,1024]{2,1,0:T(8,128)(2,1)S(1)} %add_convert_fusion.1), channel_id=1, source_target_pairs={{32,0},{40,72},{64,32},{72,104},{96,64},{104,136},{160,128},{168,2... | collective-permute-start | bytes 1572872 | tf_op jit(solution)/shard_map/ppermute | solution.py:187
  123.8 10.7 %collective-permute-start.26 = (bf16[128,1024]{1,0:T(8,128)(2,1)S(1)}, bf16[128,1024]{1,0:T(8,128)(2,1)S(1)}, u32[]{:S(2)}, u32[]{:S(2)}) collective-permute-start(bf16[128,1024]{1,0:T(8,128)(2,1)S(1)} %copy-done.24), channel_id=1, source_target_pairs={{0,16},{16,0},{1,17},{17,1},{2,18},{18,2},{3,19},{19,3},{4,20},{20... | collective-permute-start | bytes 786440 | tf_op jit(solution)/shard_map/ppermute | solution.py:187
  124.8 14.9 %collective-permute-start.27 = (bf16[128,1024]{1,0:T(8,128)(2,1)S(1)}, bf16[128,1024]{1,0:T(8,128)(2,1)S(1)}, u32[]{:S(2)}, u32[]{:S(2)}) collective-permute-start(bf16[128,1024]{1,0:T(8,128)(2,1)S(1)} %copy-done.23), channel_id=1, source_target_pairs={{0,16},{16,0},{1,17},{17,1},{2,18},{18,2},{3,19},{19,3},{4,20},{20... | collective-permute-start | bytes 786440 | tf_op jit(solution)/shard_map/ppermute | solution.py:187
  139.9 12.3 %collective-permute-start.29 = (bf16[2,256,1024]{2,1,0:T(8,128)(2,1)S(1)}, bf16[2,256,1024]{2,1,0:T(8,128)(2,1)S(1)}, u32[]{:S(2)}, u32[]{:S(2)}) collective-permute-start(bf16[2,256,1024]{2,1,0:T(8,128)(2,1)S(1)} %shard_map.40.own_ref), channel_id=1, source_target_pairs={{0,8},{8,0},{1,9},{9,1},{2,10},{10,2},{3,11},{11,3},{4,12},{12,4},... | collective-permute-start | bytes 3145736 | tf_op jit(solution)/shard_map/ppermute | solution.py:187
  140.0 12.2 %collective-permute-start.28 = (bf16[2,128,1024]{2,1,0:T(8,128)(2,1)S(1)}, bf16[2,128,1024]{2,1,0:T(8,128)(2,1)S(1)}, u32[]{:S(2)}, u32[]{:S(2)}) collective-permute-start(bf16[2,128,1024]{2,1,0:T(8,128)(2,1)S(1)} %add_convert_fusion), channel_id=1, source_target_pairs={{0,224},{8,40},{32,0},{64,32},{72,104},{104,136},{128,96},{136,168... | collective-permute-start | bytes 1572872 | tf_op jit(solution)/shard_map/ppermute | solution.py:187
  144.0 8.2 %collective-permute-start.30 = (bf16[128,1024]{1,0:T(8,128)(2,1)S(1)}, bf16[128,1024]{1,0:T(8,128)(2,1)S(1)}, u32[]{:S(2)}, u32[]{:S(2)}) collective-permute-start(bf16[128,1024]{1,0:T(8,128)(2,1)S(1)} %copy-done.22), channel_id=1, source_target_pairs={{0,16},{16,0},{1,17},{17,1},{2,18},{18,2},{3,19},{19,3},{4,20},{20... | collective-permute-start | bytes 786440 | tf_op jit(solution)/shard_map/ppermute | solution.py:187
  154.1 10.9 %collective-permute-start.31 = (bf16[128,1024]{1,0:T(8,128)(2,1)}, bf16[128,1024]{1,0:T(8,128)(2,1)}, u32[]{:S(2)}, u32[]{:S(2)}) collective-permute-start(bf16[128,1024]{1,0:T(8,128)(2,1)} %select_bitcast_fusion.2), channel_id=1, source_target_pairs={{0,8},{8,0},{1,9},{9,1},{2,10},{10,2},{3,11},{11,3},{4,12},{12,4},... | collective-permute-start | bytes 786440 | tf_op jit(solution)/shard_map/ppermute | solution.py:187
  166.6 6.0 %collective-permute-start.32 = (bf16[128,512]{1,0:T(8,128)(2,1)S(1)}, bf16[128,512]{1,0:T(8,128)(2,1)S(1)}, u32[]{:S(2)}, u32[]{:S(2)}) collective-permute-start(bf16[128,512]{1,0:T(8,128)(2,1)S(1)} %get-tuple-element.125), channel_id=1, source_target_pairs={{0,1},{1,0},{2,3},{3,2},{4,5},{5,4},{6,7},{7,6},{8,9},{9,8},{10,11... | collective-permute-start | bytes 393224 | tf_op jit(solution)/shard_map/ppermute | solution.py:187
  167.0 10.0 %collective-permute-start.33 = (bf16[128,512]{1,0:T(8,128)(2,1)S(1)}, bf16[128,512]{1,0:T(8,128)(2,1)S(1)}, u32[]{:S(2)}, u32[]{:S(2)}) collective-permute-start(bf16[128,512]{1,0:T(8,128)(2,1)S(1)} %get-tuple-element.124), channel_id=1, source_target_pairs={{0,16},{16,0},{1,17},{17,1},{2,18},{18,2},{3,19},{19,3},{4,20},{20... | collective-permute-start | bytes 393224 | tf_op jit(solution)/shard_map/ppermute | solution.py:187
  167.9 9.1 %collective-permute-start.34 = (bf16[128,512]{1,0:T(8,128)(2,1)S(1)}, bf16[128,512]{1,0:T(8,128)(2,1)S(1)}, u32[]{:S(2)}, u32[]{:S(2)}) collective-permute-start(bf16[128,512]{1,0:T(8,128)(2,1)S(1)} %get-tuple-element.125), channel_id=1, source_target_pairs={{0,17},{1,16},{2,19},{3,18},{16,1},{17,0},{18,3},{19,2},{4,21},{5,... | collective-permute-start | bytes 393224 | tf_op jit(solution)/shard_map/ppermute | solution.py:187
  185.5 11.1 %all-to-all-start = ((f32[8,1,128]{2,1,0:T(1,128)}), f32[8,1,128]{2,1,0:T(1,128)S(1)}, u32[]{:S(2)}, u32[]{:S(2)}) async-start(f32[8,1,128]{2,1,0:T(1,128)} %broadcast_in_dim.16), calls=%async_computation | async-start | bytes 8192 | tf_op jit(solution)/shard_map/all_to_all | solution.py:203
  190.5 23.2 %collective-permute-start.36 = (bf16[192,512]{1,0:T(8,128)(2,1)S(1)}, bf16[192,512]{1,0:T(8,128)(2,1)S(1)}, u32[]{:S(2)}, u32[]{:S(2)}) collective-permute-start(bf16[192,512]{1,0:T(8,128)(2,1)S(1)} %slice.209), channel_id=1, source_target_pairs={{0,32},{32,64},{128,160},{160,192},{1,33},{33,65},{129,161},{161,1... | collective-permute-start | bytes 589832 | tf_op jit(solution)/shard_map/ppermute | solution.py:358
  192.1 21.6 %collective-permute-start.37 = (bf16[192,512]{1,0:T(8,128)(2,1)S(1)}, bf16[192,512]{1,0:T(8,128)(2,1)S(1)}, u32[]{:S(2)}, u32[]{:S(2)}) collective-permute-start(bf16[192,512]{1,0:T(8,128)(2,1)S(1)} %slice.209), channel_id=1, source_target_pairs={{96,64},{224,192},{97,65},{225,193},{98,66},{226,194},{99,67},{227... | collective-permute-start | bytes 589832 | tf_op jit(solution)/shard_map/ppermute | solution.py:359
  (34 other events, 464.9 us)
where the time goes:
time: 219 us; the launch traced here: 214 us
  waiting for transfers between devices  92.9 us (42%)
  starting transfers between devices  56.7 us (26%)
  Pallas kernels  21.7 us (10%)
  blocking collectives  14.6 us (7%)
  local copies, waits for them, and re-layouts  14.4 us (7%)
  other arithmetic  10 us (5%)
  matrix products  2.81 us (1%)
    ppermute x33, waiting for transfers between devices, phase(): got = [lax.ppermute(value, *send[1:]) for value, send in zip(values, sends)]  88.1 us
    ppermute x33, starting transfers between devices, phase(): got = [lax.ppermute(value, *send[1:]) for value, send in zip(values, sends)]  48.7 us
    all_to_all x1, blocking collectives, all_sum(): lax.all_to_all(jnp.full((n, 128), value, f32), axis, 0, 0, tiled=True)  14.6 us
    pallas_call x4, Pallas kernels, call(): pl.pallas_call(kernel, grid=(1,), out_shape=outs, in_specs=[SMEM] + [whol...  12.7 us
    pallas_call x2, Pallas kernels, slots(): pl.pallas_call(kernel, grid_spec=pltpu.PrefetchScalarGridSpec(num_scalar_...  9.01 us
    unnamed x54, local copies, waits for them, and re-layouts  8.19 us
    all_to_all x1, starting transfers between devices, all_sum(): lax.all_to_all(jnp.full((n, 128), value, f32), axis, 0, 0, tiled=True)  4.98 us
  transfers between devices with their start and end apart: 39, of which 22 were waited for; matrix products, arithmetic and copies ran while one was open for 4% of the time, Pallas kernels for 8%

commit v1 on v0

--- a/solution.py
+++ b/solution.py
@@ -17,9 +17,11 @@
 DAMPING = 0.1
 bf16, f32 = jnp.bfloat16, jnp.float32
 PARAMS = pltpu.CompilerParams(vmem_limit_bytes=48 * 1024 * 1024)
-SMEM = pl.BlockSpec(memory_space=pltpu.SMEM)
 
 AWAY = (4, 3, 3, 2, 2, 1, 1, 0, 0)
+GIVE_SLOT = (0, 1, 2, 3, 4, 4, 5, 5, 6, 7)
+GIVE_START = (0, 0, 0, 0, 0, 64, 0, 64, 0, 0)
+GIVE_ROWS = (128, 128, 128, 128, 64, 64, 64, 64, 128, 128)
 SWAP2 = [(0, 1), (1, 0)]
 SWAP_X = [(0, 1), (1, 0), (2, 3), (3, 2)]
 SWAP_BOTH = [(4 * a + b, 4 * (1 - a) + (b ^ 1)) for a in range(2) for b in range(4)]
@@ -39,11 +41,12 @@
 
 def pick_kernel(out_blocks, at_ref, cot_ref, pick_ref):
     h, k = at_ref[0], at_ref[1]
+    rows = pl.ds(pl.multiple_of(pl.program_id(0) * pick_ref.shape[0], 8), pick_ref.shape[0])
     for j in range(out_blocks):
         here = slice(j * HALF, (j + 1) * HALF)
         there = slice(out_blocks * HALF + j * PIECE, out_blocks * HALF + (j + 1) * PIECE)
-        pick_ref[:, here] = cot_ref[:, aligned(j * TILE + h * HALF, HALF)]
-        pick_ref[:, there] = cot_ref[:, aligned(j * TILE + k * PIECE, PIECE)]
+        pick_ref[:, here] = cot_ref[rows, aligned(j * TILE + h * HALF, HALF)]
+        pick_ref[:, there] = cot_ref[rows, aligned(j * TILE + k * PIECE, PIECE)]
 
 
 def factor_kernel(out_blocks, at_ref, pick_ref, recv_ref, own_ref, got_ref, part_ref):
@@ -60,25 +63,23 @@
     ).astype(bf16)
 
 
-def cross_kernel(at_ref, pick_ref, recv_ref, own_ref, got_ref, keep_ref, give_ref):
+def cross_kernel(at_ref, pick_ref, recv_ref, own_ref, got_ref, keep_ref, *give_refs):
     i = pl.program_id(0)
     yh, block, piece = at_ref[1], at_ref[3 + 3 * i], at_ref[4 + 3 * i]
-    for side, ref in ((yh, keep_ref), (1 - yh, give_ref)):
+
+    def rows_of(side):
         rows = aligned(block * HALF + piece * PIECE + side * 128, 128)
-        ref[0] = (
+        return (
             tdot(pick_ref[:, rows], own_ref[...]) + tdot(recv_ref[:, rows], got_ref[...])
         ).astype(bf16)
 
-
-def assemble_out_kernel(at_ref, own_ref, other_ref, *refs):
-    yl, x = at_ref[0], at_ref[1]
-    out_ref = refs[-1]
-    for s in range(4):
-        source = (x - s + 4) % 4
-        for b in range(2):
-            column = 2 * jnp.where(b == 0, yl, 1 - yl) + source // 2
-            value = (own_ref, other_ref)[b][...] if s == 0 else refs[s - 1][b]
-            out_ref[source % 2, :, aligned(column * PIECE, PIECE)] = value
+    keep_ref[0] = rows_of(yh)
+    give = rows_of(1 - yh)
+    for slot, start, ref in zip(GIVE_SLOT, GIVE_START, give_refs):
+
+        @pl.when(i == slot)
+        def _():
+            ref[...] = give[start : start + ref.shape[0]]
 
 
 def scale_of(tokens, sums_ref):
@@ -98,79 +99,85 @@
     return sums_ref[start : start + PIECE, :].astype(f32) / tokens + DAMPING * eye_rows(start, PIECE)
 
 
-def in_inverse_kernel(
-    tokens, at_ref, shard_ref, one_ref, two_ref, three_ref, far_ref, other_ref,
-    out_ref, sums_ref, first_ref, low_ref,
-):
-    z, core = at_ref[0], at_ref[1]
-    back = 1 - 2 * core
-
-    def put(h, away, value):
-        here = aligned((z + away + 8) % 8 * 128, 128)
-        for piece in range(2):
-            rows = aligned((2 * h + piece) * PIECE, PIECE)
-            sums_ref[rows, here] = value[:, piece * 128 : (piece + 1) * 128]
-
-    for h in range(2):
-        put(h, 0, shard_ref[h])
-        for d, ref in ((1, one_ref), (2, two_ref), (3, three_ref)):
-            put(h, back * d, ref[h])
-            put(h, -back * d, other_ref[2 * (d - 1) + h])
-    put(core, 4, far_ref[0])
-    put(1 - core, 4, other_ref[6])
+def split_factor(tokens, sums_ref, first_ref, low_ref, offset):
     scale = scale_of(tokens, sums_ref)
     for r in range(4):
         here = slice(r * PIECE, (r + 1) * PIECE)
         rows = matrix_rows(tokens, sums_ref, r * PIECE)
         first = 2.0 * scale * eye_rows(r * PIECE, PIECE) - (scale * scale) * rows
-        first_ref[here, :] = first
+        first_ref[offset + r * PIECE : offset + (r + 1) * PIECE, :] = first
         low_ref[here, :] = first.astype(bf16)
         sums_ref[here, :] = rows.astype(bf16)
-    for r in range(4):
-        here = slice(r * PIECE, (r + 1) * PIECE)
-        product = mdot(low_ref[here, :], sums_ref[...]).astype(bf16)
-        out_ref[here, :] = (2.0 * first_ref[here, :] - mdot(product, low_ref[...])).astype(bf16)
+
+
+def inverse_rows(rows, sums_ref, low_ref):
+    product = mdot(rows.astype(bf16), sums_ref[...]).astype(bf16)
+    return (2.0 * rows - mdot(product, low_ref[...])).astype(bf16)
+
+
+def in_inverse_kernel(
+    tokens, at_ref, shard_ref, one_ref, two_ref, three_ref, far_ref, other_ref,
+    out_ref, sums_ref, first_ref, low_ref,
+):
+    i = pl.program_id(0)
+
+    @pl.when(i == 0)
+    def _():
+        z, core = at_ref[0], at_ref[1]
+        back = 1 - 2 * core
+
+        def put(h, away, value):
+            here = aligned((z + away + 8) % 8 * 128, 128)
+            for piece in range(2):
+                rows = aligned((2 * h + piece) * PIECE, PIECE)
+                sums_ref[rows, here] = value[:, piece * 128 : (piece + 1) * 128]
+
+        for h in range(2):
+            put(h, 0, shard_ref[h])
+            for d, ref in ((1, one_ref), (2, two_ref), (3, three_ref)):
+                put(h, back * d, ref[h])
+                put(h, -back * d, other_ref[2 * (d - 1) + h])
+        put(core, 4, far_ref[0])
+        put(1 - core, 4, other_ref[6])
+        split_factor(tokens, sums_ref, first_ref, low_ref, 0)
+
+    out_ref[...] = inverse_rows(first_ref[aligned(i * PIECE, PIECE), :], sums_ref, low_ref)
 
 
 def out_inverse_kernel(tokens, count, at_ref, own_ref, other_ref, out_ref, sums_ref, first_ref, low_ref):
-    core = at_ref[0]
-    for half in range(2):
-        sums_ref[aligned((2 * half + core) * PIECE, PIECE), :] = own_ref[half]
-        sums_ref[aligned((2 * half + 1 - core) * PIECE, PIECE), :] = other_ref[half]
-    scale = scale_of(tokens, sums_ref)
-    first_ref[:count, :] = jnp.zeros((count, TILE), f32)
-    first_ref[count + TILE :, :] = jnp.zeros((count, TILE), f32)
-    for r in range(4):
-        here = slice(r * PIECE, (r + 1) * PIECE)
-        rows = matrix_rows(tokens, sums_ref, r * PIECE)
-        first = 2.0 * scale * eye_rows(r * PIECE, PIECE) - (scale * scale) * rows
-        first_ref[count + r * PIECE : count + (r + 1) * PIECE, :] = first
-        low_ref[here, :] = first.astype(bf16)
-        sums_ref[here, :] = rows.astype(bf16)
-    for part in range(2):
-        rows = first_ref[pl.ds(pl.multiple_of(at_ref[1 + part], 64), count), :]
-        product = mdot(rows.astype(bf16), sums_ref[...]).astype(bf16)
-        out_ref[part * count : (part + 1) * count, :] = (
-            2.0 * rows - mdot(product, low_ref[...])
-        ).astype(bf16)
-
-
-def call(kernel, outs, *args, scratch=()):
-    outs = [jax.ShapeDtypeStruct(shape, dtype) for shape, dtype in outs]
-
+    i = pl.program_id(0)
+
+    @pl.when(i == 0)
+    def _():
+        core = at_ref[0]
+        for owner in range(8):
+            here = slice(owner // 2 * PIECE, (owner // 2 + 1) * PIECE)
+            for piece, ref in ((core, own_ref), (1 - core, other_ref)):
+                sums_ref[aligned((2 * (owner % 2) + piece) * PIECE, PIECE), here] = ref[owner]
+        first_ref[:count, :] = jnp.zeros((count, TILE), f32)
+        first_ref[count + TILE :, :] = jnp.zeros((count, TILE), f32)
+        split_factor(tokens, sums_ref, first_ref, low_ref, count)
+
+    rows = first_ref[pl.ds(pl.multiple_of(at_ref[1 + i], 64), count), :]
+    out_ref[...] = inverse_rows(rows, sums_ref, low_ref)
+
+
+def call(kernel, steps, block, out_shape, at, *args, scratch=()):
     def whole(a):
-        return pl.BlockSpec(a.shape, lambda i: (0,) * len(a.shape))
-
-    result = pl.pallas_call(
+        return pl.BlockSpec(a.shape, lambda i, at: (0,) * len(a.shape))
+
+    return pl.pallas_call(
         kernel,
-        grid=(1,),
-        out_shape=outs,
-        in_specs=[SMEM] + [whole(a) for a in args[1:]],
-        out_specs=[whole(a) for a in outs],
-        scratch_shapes=[pltpu.VMEM(shape, dtype) for shape, dtype in scratch],
+        grid_spec=pltpu.PrefetchScalarGridSpec(
+            num_scalar_prefetch=1,
+            grid=(steps,),
+            in_specs=[whole(a) for a in args],
+            out_specs=pl.BlockSpec(block, lambda i, at: (i, 0)),
+            scratch_shapes=[pltpu.VMEM(shape, dtype) for shape, dtype in scratch],
+        ),
+        out_shape=jax.ShapeDtypeStruct(out_shape, bf16),
         compiler_params=PARAMS,
-    )(*args)
-    return result[0] if len(outs) == 1 else result
+    )(at, *args)
 
 
 def ring_pairs(away=0, skip=False):
@@ -218,7 +225,9 @@
 
     pick = call(
         functools.partial(pick_kernel, out_blocks),
-        [((here, out_blocks * (HALF + PIECE)), bf16)],
+        4,
+        (here // 4, out_blocks * (HALF + PIECE)),
+        (here, out_blocks * (HALF + PIECE)),
         numbers(h, k),
         cotangent,
     )
@@ -239,25 +248,27 @@
         table += [plane, 3 * (plane // 4) + plane % 4 - plane % 4 // 2, piece]
     table = numbers(h, yh, *table)
 
-    def slots(kernel, count, block, n_out):
+    def slots(kernel, count, block, gives=()):
         tokens_in = (pick, recv, normed, normed_recv)
+        rows = [(n, TILE) for n in gives]
         return pl.pallas_call(
             kernel,
             grid_spec=pltpu.PrefetchScalarGridSpec(
                 num_scalar_prefetch=1,
                 grid=(count,),
                 in_specs=[pl.BlockSpec(a.shape, lambda i, at: (0, 0)) for a in tokens_in],
-                out_specs=[pl.BlockSpec((1, *block), lambda i, at: (i, 0, 0))] * n_out,
+                out_specs=[pl.BlockSpec((1, *block), lambda i, at: (i, 0, 0))]
+                + [pl.BlockSpec(r, lambda i, at: (0, 0)) for r in rows],
             ),
-            out_shape=[jax.ShapeDtypeStruct((count, *block), bf16)] * n_out,
+            out_shape=[jax.ShapeDtypeStruct(r, bf16) for r in [(count, *block)] + rows],
             compiler_params=PARAMS,
         )(table, *tokens_in)
 
-    (part,) = slots(functools.partial(factor_kernel, out_blocks), 9, (PIECE, PIECE + 128), 1)
-    keep, give = slots(cross_kernel, 8, (128, TILE), 2)
-
-    def y_send(slot):
-        return give[slot], YH, SWAP2
+    (part,) = slots(functools.partial(factor_kernel, out_blocks), 9, (PIECE, PIECE + 128))
+    keep, *give = slots(cross_kernel, 8, (128, TILE), GIVE_ROWS)
+
+    def y_send(i):
+        return give[i], YH, SWAP2
 
     def ring(value, *args):
         return value, (Z, CORE), ring_pairs(*args)
@@ -280,42 +291,29 @@
     other, far = phase((tiles, YH, SWAP2), ring(added(keep[0], y0).astype(bf16), 4, True))
     tiles = added(tiles, other).astype(bf16)
     out_tile, in_tile = tiles[:, :PIECE], tiles[:, PIECE:]
-    near_in, near_out, far, y3 = phase(
+    out_tiles = lax.all_gather(out_tile, OWNER)
+    near_in, far, y3 = phase(
         (in_tile, X, SWAP_X),
-        (out_tile, YL, SWAP2),
         ring(added(keep[1:3], jnp.stack([y1, y2]), widened(far)).astype(bf16), 3, True),
         y_send(3),
     )
     shard = in_order(h, in_tile, near_in)
-    both = jnp.stack([out_tile, near_out])
-
-    def x_send(s):
-        return both, X, [(i, (i + s) % 4) for i in range(4)]
-
-    one, x1 = phase(ring(shard), x_send(1))
-    two, x2 = phase(ring(one), x_send(2))
-    three, x3 = phase(ring(two), x_send(3))
-    last, y4 = phase(ring(jnp.where(core == 0, three[:1], three[1:])), y_send(4))
-    out_half = call(
-        assemble_out_kernel, [((2, PIECE, TILE), bf16)], numbers(yl, x), out_tile, near_out, x1, x2, x3
-    )
-    cross, in_other, y5, y6 = phase(
+    one, y4 = phase(ring(shard), y_send(4))
+    two, y5 = phase(ring(one), y_send(5))
+    three, y6 = phase(ring(two), y_send(6))
+    last, y7 = phase(ring(jnp.where(core == 0, three[:1], three[1:])), y_send(7))
+    y4, y5 = jnp.concatenate([y4, y5]), jnp.concatenate([y6, y7])
+    cross, in_other, y6 = phase(
         ring(added(keep[3:5], jnp.stack([y3, y4]), far).astype(bf16), 2, True),
         (jnp.concatenate([one, two, three, last], 0), CORE, SWAP2),
-        y_send(5),
-        y_send(6),
-    )
-    cross, out_other, y7 = phase(
-        ring(added(keep[5:7], jnp.stack([y5, y6]), cross).astype(bf16), 1, True),
-        (out_half, CORE, SWAP2),
-        y_send(7),
-    )
-    (other,) = phase((jnp.where(core == 0, cross[1], cross[0]), CORE, SWAP2))
-    cross = added(jnp.where(core == 0, cross[0], cross[1]), other, keep[7], y7).astype(bf16)
+        y_send(8),
+    )
     square = (TILE, TILE)
     in_inverse = call(
         functools.partial(in_inverse_kernel, tokens),
-        [(square, bf16)],
+        4,
+        (PIECE, TILE),
+        square,
         numbers(z, core),
         shard,
         one,
@@ -325,7 +323,14 @@
         in_other,
         scratch=[(square, bf16), (square, f32), (square, bf16)],
     )
-
+    cross, out_other, y7 = phase(
+        ring(added(keep[5:7], jnp.stack([y5, y6]), cross).astype(bf16), 1, True),
+        (out_tiles, CORE, SWAP2),
+        y_send(9),
+    )
+    cross, in_inverse = lax.optimization_barrier((cross, in_inverse))
+    (other,) = phase((jnp.where(core == 0, cross[1], cross[0]), CORE, SWAP2))
+    cross = added(jnp.where(core == 0, cross[0], cross[1]), other, keep[7], y7).astype(bf16)
     m = z % 4
     row = 2 * yh + core
     slice_rows = out_width // lax.axis_size(DP)
@@ -336,9 +341,11 @@
     own_at, near_at = [jnp.clip(a, -slice_rows, TILE) + slice_rows for a in (own_at, near_at)]
     out_inverse = call(
         functools.partial(out_inverse_kernel, tokens, slice_rows),
-        [((2 * slice_rows, TILE), bf16)],
+        2,
+        (slice_rows, TILE),
+        (2 * slice_rows, TILE),
         numbers(core, own_at, near_at),
-        out_half,
+        out_tiles,
         out_other,
         scratch=[(square, bf16), ((TILE + 2 * slice_rows, TILE), f32), (square, bf16)],
     )

time: 219 us -> 236 us (1.078)
  waiting for transfers between devices: 92.9 us -> 78.5 us
  between operations: 1.29 us -> 14.7 us
  starting transfers between devices: 56.7 us -> 64.8 us
  other arithmetic: 10 us -> 17.2 us
    ppermute x33 -> x31, waiting for transfers between devices: 88.1 us -> 62.9 us  [phase(): got = [lax.ppermute(value, *send[1:]) for value, send in zip(values, sends)]]
    all_gather x0 -> x1, waiting for transfers between devices: none -> 10.5 us  [shards(): out_tiles = lax.all_gather(out_tile, OWNER)]
    ppermute x33 -> x31, starting transfers between devices: 48.7 us -> 58.6 us  [phase(): got = [lax.ppermute(value, *send[1:]) for value, send in zip(values, sends)]]
    unnamed x54 -> x64, local copies, waits for them, and re-layouts: 8.19 us -> 12 us
    squeeze x1 -> x0, local copies, waits for them, and re-layouts: 3.37 us -> none  [y_send(): return (give[slot], YH, SWAP2)]
    another operation x8 -> x7, other arithmetic: 2.19 us -> 5.02 us  [in_order(): return jnp.stack([first, second])]
    pallas_call x4 -> x3, Pallas kernels: 12.7 us -> 14.1 us  [call(): pl.pallas_call(kernel, grid_spec=pltpu.PrefetchScalarGridSpec(num_scalar_...]
  transfers between devices with their start and end apart: 39 -> 38, of which waited for: 22 -> 18; matrix products, arithmetic and copies ran while one was open for 4% -> 4% of each run, Pallas kernels for 8% -> 8%
where the time goes in v1:
time: 236 us; the launch traced here: 232 us
  waiting for transfers between devices  78.5 us (33%)
  starting transfers between devices  64.8 us (27%)
  Pallas kernels  23.6 us (10%)
  other arithmetic  17.2 us (7%)
  local copies, waits for them, and re-layouts  15.5 us (7%)
  between operations  14.7 us (6%)
  blocking collectives  14.3 us (6%)
  matrix products  3.08 us (1%)
    ppermute x31, waiting for transfers between devices, phase(): got = [lax.ppermute(value, *send[1:]) for value, send in zip(values, sends)]  62.9 us
    ppermute x31, starting transfers between devices, phase(): got = [lax.ppermute(value, *send[1:]) for value, send in zip(values, sends)]  58.6 us
    all_to_all x1, blocking collectives, all_sum(): lax.all_to_all(jnp.full((n, 128), value, f32), axis, 0, 0, tiled=True)  14.3 us
    pallas_call x3, Pallas kernels, call(): pl.pallas_call(kernel, grid_spec=pltpu.PrefetchScalarGridSpec(num_scalar_...  14.1 us
    unnamed x64, local copies, waits for them, and re-layouts  12 us
    all_gather x1, waiting for transfers between devices, shards(): out_tiles = lax.all_gather(out_tile, OWNER)  10.5 us
    pallas_call x2, Pallas kernels, slots(): pl.pallas_call(kernel, grid_spec=pltpu.PrefetchScalarGridSpec(num_scalar_...  9.51 us
    another operation x7, other arithmetic, in_order(): return jnp.stack([first, second])  5.02 us
  transfers between devices with their start and end apart: 38, of which 18 were waited for; matrix products, arithmetic and copies ran while one was open for 4% of the time, Pallas kernels for 8%

profile of v1, /device:TPU:16, one launch (start us, length us, event | category | flops | bytes accessed | tf_op | source)
XLA Modules:
  0.0 231.7 jit_solution(4918518269705509150)
XLA Ops:
  15.0 3.3 %shard_map.38 = bf16[9,256,384]{2,1,0:T(8,128)(2,1)S(1)} custom-call(s32[29]{0:T(128)S(1)} %stack.181.at_ref, bf16[128,4608]{1,0:T(8,128)(2,1)S(1)} %shard_map.37.pick_ref, bf16[128,4608]{1,0:T(8,128)(2,1)S(1)} %copy-done.1, bf16[128,1024]{1,0:T(8,128)(2,1)S(1)} %multiply_convert_fusion.own_ref, bf16[128,1024]{1,0:T(8,128)(2,1)S(1)} %collective-permute-done.1.got_ref), custom_call_target="tpu_custom_call" | custom-call | tf_op jit(solution)/shard_map/pallas_call | solution.py:254
  19.0 5.9 %collective-permute-start.2 = (bf16[256,384]{1,0:T(8,128)(2,1)}, bf16[256,384]{1,0:T(8,128)(2,1)}, u32[]{:S(2)}, u32[]{:S(2)}) collective-permute-start(bf16[256,384]{1,0:T(8,128)(2,1)} %slice_bitcast_fusion), channel_id=1, source_target_pairs={{0,224},{8,40},{32,0},{40,72},{64,32},{72,104},{96,64},{104,136},{... | collective-permute-start | bytes 589832 | tf_op jit(solution)/shard_map/ppermute | solution.py:194
  26.1 6.2 %shard_map.39 = (bf16[8,128,1024]{2,1,0:T(8,128)(2,1)}, bf16[128,1024]{1,0:T(8,128)(2,1)S(1)}, bf16[128,1024]{1,0:T(8,128)(2,1)S(1)}, bf16[128,1024]{1,0:T(8,128...) custom-call(s32[29]{0:T(128)S(1)} %stack.181.at_ref, ...), custom_call_target="tpu_custom_call" | custom-call | tf_op jit(solution)/shard_map/pallas_call | solution.py:254
  35.1 7.5 %collective-permute-done.4 = bf16[128,1024]{1,0:T(8,128)(2,1)S(1)} collective-permute-done((bf16[128,1024]{1,0:T(8,128)(2,1)S(1)}, bf16[128,1024]{1,0:T(8,128)(2,1)S(1)}, u32[]{:S(2)}, u32[]{:S(2)}) %collective-permute-start.4) | collective-permute-done | bytes 262176 | tf_op jit(solution)/shard_map/ppermute | solution.py:194
  44.5 7.5 %collective-permute-done.6 = bf16[128,1024]{1,0:T(8,128)(2,1)S(1)} collective-permute-done((bf16[128,1024]{1,0:T(8,128)(2,1)S(1)}, bf16[128,1024]{1,0:T(8,128)(2,1)S(1)}, u32[]{:S(2)}, u32[]{:S(2)}) %collective-permute-start.6) | collective-permute-done | bytes 262176 | tf_op jit(solution)/shard_map/ppermute | solution.py:194
  54.4 7.5 %collective-permute-done.8 = bf16[128,1024]{1,0:T(8,128)(2,1)S(1)} collective-permute-done((bf16[128,1024]{1,0:T(8,128)(2,1)S(1)}, bf16[128,1024]{1,0:T(8,128)(2,1)S(1)}, u32[]{:S(2)}, u32[]{:S(2)}) %collective-permute-start.8) | collective-permute-done | bytes 262176 | tf_op jit(solution)/shard_map/ppermute | solution.py:194
  64.1 3.5 %collective-permute-start.11 = (bf16[128,1024]{1,0:T(8,128)(2,1)S(1)}, bf16[128,1024]{1,0:T(8,128)(2,1)S(1)}, u32[]{:S(2)}, u32[]{:S(2)}) collective-permute-start(bf16[128,1024]{1,0:T(8,128)(2,1)S(1)} %fusion.2), channel_id=1, source_target_pairs={{0,224},{8,40},{32,0},{40,72},{96,64},{104,136},{128,96},{136,168}... | collective-permute-start | bytes 786440 | tf_op jit(solution)/shard_map/ppermute | solution.py:194
  67.7 6.0 %collective-permute-done.10 = bf16[256,512]{1,0:T(8,128)(2,1)S(1)} collective-permute-done((bf16[256,512]{1,0:T(8,128)(2,1)S(1)}, bf16[256,512]{1,0:T(8,128)(2,1)S(1)}, u32[]{:S(2)}, u32[]{:S(2)}) %collective-permute-start.10) | collective-permute-done | bytes 262176 | tf_op jit(solution)/shard_map/ppermute | solution.py:194
  73.8 2.3 add_convert_fusion.2
  76.1 3.6 %collective-permute-start.13 = (bf16[2,128,1024]{2,1,0:T(8,128)(2,1)}, bf16[2,128,1024]{2,1,0:T(8,128)(2,1)S(1)}, u32[]{:S(2)}, u32[]{:S(2)}) collective-permute-start(bf16[2,128,1024]{2,1,0:T(8,128)(2,1)} %add_convert_fusion.2), channel_id=1, source_target_pairs={{0,224},{8,40},{40,72},{64,32},{72,104},{96,64},{128,96},{136,168}... | collective-permute-start | bytes 1572872 | tf_op jit(solution)/shard_map/ppermute | solution.py:194
  79.6 3.2 %collective-permute-start.14 = (bf16[128,1024]{1,0:T(8,128)(2,1)}, bf16[128,1024]{1,0:T(8,128)(2,1)}, u32[]{:S(2)}, u32[]{:S(2)}) collective-permute-start(bf16[128,1024]{1,0:T(8,128)(2,1)} %get-tuple-element.97), channel_id=1, source_target_pairs={{0,16},{16,0},{1,17},{17,1},{2,18},{18,2},{3,19},{19,3},{4,20},{20... | collective-permute-start | bytes 786440 | tf_op jit(solution)/shard_map/ppermute | solution.py:194
  84.4 3.6 %collective-permute-done.12 = bf16[256,256]{1,0:T(8,128)(2,1)} collective-permute-done((bf16[256,256]{1,0:T(8,128)(2,1)S(1)}, bf16[256,256]{1,0:T(8,128)(2,1)}, u32[]{:S(2)}, u32[]{:S(2)}) %collective-permute-start.12) | collective-permute-done | bytes 131104 | tf_op jit(solution)/shard_map/ppermute | solution.py:194
  89.7 2.3 collective-permute-start.15
  92.7 3.1 %collective-permute-start.16 = (bf16[64,1024]{1,0:T(8,128)(2,1)S(1)}, bf16[64,1024]{1,0:T(8,128)(2,1)S(1)}, u32[]{:S(2)}, u32[]{:S(2)}) collective-permute-start(bf16[64,1024]{1,0:T(8,128)(2,1)S(1)} %copy-done.22), channel_id=1, source_target_pairs={{0,16},{16,0},{1,17},{17,1},{2,18},{18,2},{3,19},{19,3},{4,20},{20... | collective-permute-start | bytes 393224 | tf_op jit(solution)/shard_map/ppermute | solution.py:194
  95.9 3.3 %collective-permute-done.16 = bf16[64,1024]{1,0:T(8,128)(2,1)S(1)} collective-permute-done((bf16[64,1024]{1,0:T(8,128)(2,1)S(1)}, bf16[64,1024]{1,0:T(8,128)(2,1)S(1)}, u32[]{:S(2)}, u32[]{:S(2)}) %collective-permute-start.16) | collective-permute-done | bytes 131104 | tf_op jit(solution)/shard_map/ppermute | solution.py:194
  100.0 2.8 %collective-permute-start.18 = (bf16[64,1024]{1,0:T(8,128)(2,1)S(1)}, bf16[64,1024]{1,0:T(8,128)(2,1)S(1)}, u32[]{:S(2)}, u32[]{:S(2)}) collective-permute-start(bf16[64,1024]{1,0:T(8,128)(2,1)S(1)} %copy-done.20), channel_id=1, source_target_pairs={{0,16},{16,0},{1,17},{17,1},{2,18},{18,2},{3,19},{19,3},{4,20},{20... | collective-permute-start | bytes 393224 | tf_op jit(solution)/shard_map/ppermute | solution.py:194
  102.7 4.4 %collective-permute-done.18 = bf16[64,1024]{1,0:T(8,128)(2,1)S(1)} collective-permute-done((bf16[64,1024]{1,0:T(8,128)(2,1)S(1)}, bf16[64,1024]{1,0:T(8,128)(2,1)S(1)}, u32[]{:S(2)}, u32[]{:S(2)}) %collective-permute-start.18) | collective-permute-done | bytes 131104 | tf_op jit(solution)/shard_map/ppermute | solution.py:194
  111.3 3.4 %collective-permute-done.20 = bf16[64,1024]{1,0:T(8,128)(2,1)S(1)} collective-permute-done((bf16[64,1024]{1,0:T(8,128)(2,1)S(1)}, bf16[64,1024]{1,0:T(8,128)(2,1)S(1)}, u32[]{:S(2)}, u32[]{:S(2)}) %collective-permute-start.20) | collective-permute-done | bytes 131104 | tf_op jit(solution)/shard_map/ppermute | solution.py:194
  115.3 2.6 %collective-permute-start.21 = (bf16[1,256,256]{2,1,0:T(8,128)(2,1)S(1)}, bf16[1,256,256]{2,1,0:T(8,128)(2,1)S(1)}, u32[]{:S(2)}, u32[]{:S(2)}) collective-permute-start(bf16[1,256,256]{2,1,0:T(8,128)(2,1)S(1)} %slice_select_fusion), channel_id=1, source_target_pairs={{0,224},{8,40},{32,0},{40,72},{64,32},{72,104},{96,64},{104,136},{... | collective-permute-start | bytes 393224 | tf_op jit(solution)/shard_map/ppermute | solution.py:194
  117.9 3.8 %collective-permute-start.22 = (bf16[64,1024]{1,0:T(8,128)(2,1)S(1)}, bf16[64,1024]{1,0:T(8,128)(2,1)S(1)}, u32[]{:S(2)}, u32[]{:S(2)}) collective-permute-start(bf16[64,1024]{1,0:T(8,128)(2,1)S(1)} %copy-done.16), channel_id=1, source_target_pairs={{0,16},{16,0},{1,17},{17,1},{2,18},{18,2},{3,19},{19,3},{4,20},{20... | collective-permute-start | bytes 393224 | tf_op jit(solution)/shard_map/ppermute | solution.py:194
  126.2 3.6 %collective-permute-start.25 = (bf16[128,1024]{1,0:T(8,128)(2,1)S(1)}, bf16[128,1024]{1,0:T(8,128)(2,1)S(1)}, u32[]{:S(2)}, u32[]{:S(2)}) collective-permute-start(bf16[128,1024]{1,0:T(8,128)(2,1)S(1)} %copy-done.14), channel_id=1, source_target_pairs={{0,16},{16,0},{1,17},{17,1},{2,18},{18,2},{3,19},{19,3},{4,20},{20... | collective-permute-start | bytes 786440 | tf_op jit(solution)/shard_map/ppermute | solution.py:194
  129.9 10.4 %collective-permute-done.25 = bf16[128,1024]{1,0:T(8,128)(2,1)S(1)} collective-permute-done((bf16[128,1024]{1,0:T(8,128)(2,1)S(1)}, bf16[128,1024]{1,0:T(8,128)(2,1)S(1)}, u32[]{:S(2)}, u32[]{:S(2)}) %collective-permute-start.25) | collective-permute-done | bytes 262176 | tf_op jit(solution)/shard_map/ppermute | solution.py:194
  142.3 10.5 %all-gather.3.cloned.1.call-done = bf16[2048,256]{1,0:T(8,128)(2,1)} async-done(((bf16[256,256]{1,0:T(8,128)(2,1)}), bf16[2048,256]{1,0:T(8,128)(2,1)}) %all-gather.3.cloned.1.call-update) | async-done | bytes 1048592 | tf_op jit(solution)/shard_map/all_gather | solution.py:294
  152.8 5.3 %collective-permute-start.26 = (bf16[2,128,1024]{2,1,0:T(8,128)(2,1)}, bf16[2,128,1024]{2,1,0:T(8,128)(2,1)}, u32[]{:S(2)}, u32[]{:S(2)}) collective-permute-start(bf16[2,128,1024]{2,1,0:T(8,128)(2,1)} %add_convert_fusion), channel_id=1, source_target_pairs={{0,224},{8,40},{32,0},{64,32},{72,104},{104,136},{128,96},{136,168... | collective-permute-start | bytes 1572872 | tf_op jit(solution)/shard_map/ppermute | solution.py:194
  163.1 8.5 %shard_map.41 = bf16[1024,1024]{1,0:T(8,128)(2,1)S(1)} custom-call(s32[2]{0:T(128)S(1)} %pad_add_fusion.2.at_ref, bf16[2,256,256]{2,1,0:T(8,128)(2,1)S(1)} %copy-done.10, bf16[2,256,256]{2,1,0:T(8,128)(2,1)S(1)} %copy-done.6, bf16[2,256,256]{2,1,0:T(8,128)(2,1)S(1)} %copy-done.8, bf16[2,256,256]{2,1,0:T(8,128)(2,1)S(1)} %collective-permute-done.19.three_ref, ...), custom_call_target="tpu_custom_call" | custom-call | tf_op jit(solution)/shard_map/pallas_call | solution.py:169
  177.3 2.8 %collective-permute-start.31 = (bf16[128,512]{1,0:T(8,128)(2,1)S(1)}, bf16[128,512]{1,0:T(8,128)(2,1)S(1)}, u32[]{:S(2)}, u32[]{:S(2)}) collective-permute-start(bf16[128,512]{1,0:T(8,128)(2,1)S(1)} %get-tuple-element.138), channel_id=1, source_target_pairs={{0,16},{16,0},{1,17},{17,1},{2,18},{18,2},{3,19},{19,3},{4,20},{20... | collective-permute-start | bytes 393224 | tf_op jit(solution)/shard_map/ppermute | solution.py:194
  180.1 2.2 collective-permute-start.32
  182.8 3.1 %collective-permute-done.31 = bf16[128,512]{1,0:T(8,128)(2,1)S(1)} collective-permute-done((bf16[128,512]{1,0:T(8,128)(2,1)S(1)}, bf16[128,512]{1,0:T(8,128)(2,1)S(1)}, u32[]{:S(2)}, u32[]{:S(2)}) %collective-permute-start.31) | collective-permute-done | bytes 131104 | tf_op jit(solution)/shard_map/ppermute | solution.py:194
  188.8 4.9 %shard_map.40 = bf16[384,1024]{1,0:T(8,128)(2,1)S(1)} custom-call(s32[3]{0:T(128)S(1)} %pad_add_fusion.at_ref, bf16[8,256,256]{2,1,0:T(8,128)(2,1)S(1)} %bitcast.93, bf16[8,256,256]{2,1,0:T(8,128)(2,1)S(1)} %collective-permute-done.27.other_ref), custom_call_target="tpu_custom_call" | custom-call | tf_op jit(solution)/shard_map/pallas_call | solution.py:169
  197.6 3.6 %all-to-all-start = ((f32[8,1,128]{2,1,0:T(1,128)}), f32[8,1,128]{2,1,0:T(1,128)S(1)}, u32[]{:S(2)}, u32[]{:S(2)}) async-start(f32[8,1,128]{2,1,0:T(1,128)} %broadcast_in_dim.16), calls=%async_computation | async-start | bytes 8192 | tf_op jit(solution)/shard_map/all_to_all | solution.py:210
  203.2 4.1 %all-to-all-done = f32[8,1,128]{2,1,0:T(1,128)S(1)} async-done(((f32[8,1,128]{2,1,0:T(1,128)}), f32[8,1,128]{2,1,0:T(1,128)S(1)}, u32[]{:S(2)}, u32[]{:S(2)}) %all-to-all-start) | async-done | bytes 4128 | tf_op jit(solution)/shard_map/all_to_all | solution.py:210
  208.5 14.3 %all_to_all.18 = f32[32,1,128]{2,1,0:T(1,128)S(1)} all-to-all(f32[32,1,128]{2,1,0:T(1,128)S(1)} %broadcast_in_dim.17), channel_id=1, replica_groups=mesh['dp_0'=8,'dp_1'=2,'dp_2'=2,'owner_0'=2,'owner_1'=4] {'dp_0','dp_1',..., dimensions={0} | all-to-all | bytes 32768 | tf_op jit(solution)/shard_map/all_to_all | solution.py:210
  (163 shorter events, 58.0 us)
Async XLA Ops:
  6.5 146.3 %all-gather.3.cloned.1.call-start = ((), (), s32[]{:S(2)}) async-start(), calls=%async_computation.2 | async-start | bytes 1179648 | tf_op jit(solution)/shard_map/all_gather | solution.py:294
  19.0 13.4 %collective-permute-start.2 = (bf16[256,384]{1,0:T(8,128)(2,1)}, bf16[256,384]{1,0:T(8,128)(2,1)}, u32[]{:S(2)}, u32[]{:S(2)}) collective-permute-start(bf16[256,384]{1,0:T(8,128)(2,1)} %slice_bitcast_fusion), channel_id=1, source_target_pairs={{0,224},{8,40},{32,0},{40,72},{64,32},{72,104},{96,64},{104,136},{... | collective-permute-start | bytes 589832 | tf_op jit(solution)/shard_map/ppermute | solution.py:194
  33.7 9.0 %collective-permute-start.3 = (bf16[2,256,384]{2,1,0:T(8,128)(2,1)S(1)}, bf16[2,256,384]{2,1,0:T(8,128)(2,1)S(1)}, u32[]{:S(2)}, u32[]{:S(2)}) collective-permute-start(bf16[2,256,384]{2,1,0:T(8,128)(2,1)S(1)} %add_convert_fusion.5), channel_id=1, source_target_pairs={{0,224},{8,40},{32,0},{40,72},{64,32},{72,104},{96,64},{104,136},{... | collective-permute-start | bytes 1179656 | tf_op jit(solution)/shard_map/ppermute | solution.py:194
  34.8 7.9 %collective-permute-start.4 = (bf16[128,1024]{1,0:T(8,128)(2,1)S(1)}, bf16[128,1024]{1,0:T(8,128)(2,1)S(1)}, u32[]{:S(2)}, u32[]{:S(2)}) collective-permute-start(bf16[128,1024]{1,0:T(8,128)(2,1)S(1)} %get-tuple-element.76), channel_id=1, source_target_pairs={{0,16},{16,0},{1,17},{17,1},{2,18},{18,2},{3,19},{19,3},{4,20},{20... | collective-permute-start | bytes 786440 | tf_op jit(solution)/shard_map/ppermute | solution.py:194
  42.8 9.3 %collective-permute-start.5 = (bf16[2,256,384]{2,1,0:T(8,128)(2,1)S(1)}, bf16[2,256,384]{2,1,0:T(8,128)(2,1)S(1)}, u32[]{:S(2)}, u32[]{:S(2)}) collective-permute-start(bf16[2,256,384]{2,1,0:T(8,128)(2,1)S(1)} %add_convert_fusion.4), channel_id=1, source_target_pairs={{0,224},{8,40},{32,0},{40,72},{64,32},{72,104},{96,64},{104,136},{... | collective-permute-start | bytes 1179656 | tf_op jit(solution)/shard_map/ppermute | solution.py:194
  44.2 7.9 %collective-permute-start.6 = (bf16[128,1024]{1,0:T(8,128)(2,1)S(1)}, bf16[128,1024]{1,0:T(8,128)(2,1)S(1)}, u32[]{:S(2)}, u32[]{:S(2)}) collective-permute-start(bf16[128,1024]{1,0:T(8,128)(2,1)S(1)} %get-tuple-element.80), channel_id=1, source_target_pairs={{0,16},{16,0},{1,17},{17,1},{2,18},{18,2},{3,19},{19,3},{4,20},{20... | collective-permute-start | bytes 786440 | tf_op jit(solution)/shard_map/ppermute | solution.py:194
  52.2 9.7 %collective-permute-start.7 = (bf16[2,256,384]{2,1,0:T(8,128)(2,1)S(1)}, bf16[2,256,384]{2,1,0:T(8,128)(2,1)S(1)}, u32[]{:S(2)}, u32[]{:S(2)}) collective-permute-start(bf16[2,256,384]{2,1,0:T(8,128)(2,1)S(1)} %add_convert_fusion.3), channel_id=1, source_target_pairs={{0,224},{8,40},{32,0},{40,72},{64,32},{72,104},{96,64},{104,136},{... | collective-permute-start | bytes 1179656 | tf_op jit(solution)/shard_map/ppermute | solution.py:194
  54.0 7.9 %collective-permute-start.8 = (bf16[128,1024]{1,0:T(8,128)(2,1)S(1)}, bf16[128,1024]{1,0:T(8,128)(2,1)S(1)}, u32[]{:S(2)}, u32[]{:S(2)}) collective-permute-start(bf16[128,1024]{1,0:T(8,128)(2,1)S(1)} %get-tuple-element.84), channel_id=1, source_target_pairs={{0,16},{16,0},{1,17},{17,1},{2,18},{18,2},{3,19},{19,3},{4,20},{20... | collective-permute-start | bytes 786440 | tf_op jit(solution)/shard_map/ppermute | solution.py:194
  63.7 9.9 %collective-permute-start.10 = (bf16[256,512]{1,0:T(8,128)(2,1)S(1)}, bf16[256,512]{1,0:T(8,128)(2,1)S(1)}, u32[]{:S(2)}, u32[]{:S(2)}) collective-permute-start(bf16[256,512]{1,0:T(8,128)(2,1)S(1)} %add_convert_fusion.7), channel_id=1, source_target_pairs={{0,16},{16,0},{1,17},{17,1},{2,18},{18,2},{3,19},{19,3},{4,20},{20... | collective-permute-start | bytes 786440 | tf_op jit(solution)/shard_map/ppermute | solution.py:194
  64.1 9.5 %collective-permute-start.11 = (bf16[128,1024]{1,0:T(8,128)(2,1)S(1)}, bf16[128,1024]{1,0:T(8,128)(2,1)S(1)}, u32[]{:S(2)}, u32[]{:S(2)}) collective-permute-start(bf16[128,1024]{1,0:T(8,128)(2,1)S(1)} %fusion.2), channel_id=1, source_target_pairs={{0,224},{8,40},{32,0},{40,72},{96,64},{104,136},{128,96},{136,168}... | collective-permute-start | bytes 786440 | tf_op jit(solution)/shard_map/ppermute | solution.py:194
  76.1 11.9 %collective-permute-start.13 = (bf16[2,128,1024]{2,1,0:T(8,128)(2,1)}, bf16[2,128,1024]{2,1,0:T(8,128)(2,1)S(1)}, u32[]{:S(2)}, u32[]{:S(2)}) collective-permute-start(bf16[2,128,1024]{2,1,0:T(8,128)(2,1)} %add_convert_fusion.2), channel_id=1, source_target_pairs={{0,224},{8,40},{40,72},{64,32},{72,104},{96,64},{128,96},{136,168}... | collective-permute-start | bytes 1572872 | tf_op jit(solution)/shard_map/ppermute | solution.py:194
  79.6 8.3 %collective-permute-start.14 = (bf16[128,1024]{1,0:T(8,128)(2,1)}, bf16[128,1024]{1,0:T(8,128)(2,1)}, u32[]{:S(2)}, u32[]{:S(2)}) collective-permute-start(bf16[128,1024]{1,0:T(8,128)(2,1)} %get-tuple-element.97), channel_id=1, source_target_pairs={{0,16},{16,0},{1,17},{17,1},{2,18},{18,2},{3,19},{19,3},{4,20},{20... | collective-permute-start | bytes 786440 | tf_op jit(solution)/shard_map/ppermute | solution.py:194
  89.7 9.5 %collective-permute-start.15 = (bf16[2,256,256]{2,1,0:T(8,128)(2,1)S(1)}, bf16[2,256,256]{2,1,0:T(8,128)(2,1)S(1)}, u32[]{:S(2)}, u32[]{:S(2)}) collective-permute-start(bf16[2,256,256]{2,1,0:T(8,128)(2,1)S(1)} %pad_maximum_fusion.6.shard_ref), channel_id=1, source_target_pairs={{0,224},{8,40},{32,0},{40,72},{64,32},{72,104},{96,64},{104,136},{... | collective-permute-start | bytes 786440 | tf_op jit(solution)/shard_map/ppermute | solution.py:194
  92.7 6.5 %collective-permute-start.16 = (bf16[64,1024]{1,0:T(8,128)(2,1)S(1)}, bf16[64,1024]{1,0:T(8,128)(2,1)S(1)}, u32[]{:S(2)}, u32[]{:S(2)}) collective-permute-start(bf16[64,1024]{1,0:T(8,128)(2,1)S(1)} %copy-done.22), channel_id=1, source_target_pairs={{0,16},{16,0},{1,17},{17,1},{2,18},{18,2},{3,19},{19,3},{4,20},{20... | collective-permute-start | bytes 393224 | tf_op jit(solution)/shard_map/ppermute | solution.py:194
  99.2 7.9 %collective-permute-start.17 = (bf16[2,256,256]{2,1,0:T(8,128)(2,1)S(1)}, bf16[2,256,256]{2,1,0:T(8,128)(2,1)S(1)}, u32[]{:S(2)}, u32[]{:S(2)}) collective-permute-start(bf16[2,256,256]{2,1,0:T(8,128)(2,1)S(1)} %collective-permute-done.15.one_ref), channel_id=1, source_target_pairs={{0,224},{8,40},{32,0},{40,72},{64,32},{72,104},{96,64},{104,136},{... | collective-permute-start | bytes 786440 | tf_op jit(solution)/shard_map/ppermute | solution.py:194
  100.0 7.2 %collective-permute-start.18 = (bf16[64,1024]{1,0:T(8,128)(2,1)S(1)}, bf16[64,1024]{1,0:T(8,128)(2,1)S(1)}, u32[]{:S(2)}, u32[]{:S(2)}) collective-permute-start(bf16[64,1024]{1,0:T(8,128)(2,1)S(1)} %copy-done.20), channel_id=1, source_target_pairs={{0,16},{16,0},{1,17},{17,1},{2,18},{18,2},{3,19},{19,3},{4,20},{20... | collective-permute-start | bytes 393224 | tf_op jit(solution)/shard_map/ppermute | solution.py:194
  107.1 7.5 %collective-permute-start.19 = (bf16[2,256,256]{2,1,0:T(8,128)(2,1)S(1)}, bf16[2,256,256]{2,1,0:T(8,128)(2,1)S(1)}, u32[]{:S(2)}, u32[]{:S(2)}) collective-permute-start(bf16[2,256,256]{2,1,0:T(8,128)(2,1)S(1)} %collective-permute-done.17.two_ref), channel_id=1, source_target_pairs={{0,224},{8,40},{32,0},{40,72},{64,32},{72,104},{96,64},{104,136},{... | collective-permute-start | bytes 786440 | tf_op jit(solution)/shard_map/ppermute | solution.py:194
  108.2 6.5 %collective-permute-start.20 = (bf16[64,1024]{1,0:T(8,128)(2,1)S(1)}, bf16[64,1024]{1,0:T(8,128)(2,1)S(1)}, u32[]{:S(2)}, u32[]{:S(2)}) collective-permute-start(bf16[64,1024]{1,0:T(8,128)(2,1)S(1)} %copy-done.18), channel_id=1, source_target_pairs={{0,16},{16,0},{1,17},{17,1},{2,18},{18,2},{3,19},{19,3},{4,20},{20... | collective-permute-start | bytes 393224 | tf_op jit(solution)/shard_map/ppermute | solution.py:194
  115.3 7.8 %collective-permute-start.21 = (bf16[1,256,256]{2,1,0:T(8,128)(2,1)S(1)}, bf16[1,256,256]{2,1,0:T(8,128)(2,1)S(1)}, u32[]{:S(2)}, u32[]{:S(2)}) collective-permute-start(bf16[1,256,256]{2,1,0:T(8,128)(2,1)S(1)} %slice_select_fusion), channel_id=1, source_target_pairs={{0,224},{8,40},{32,0},{40,72},{64,32},{72,104},{96,64},{104,136},{... | collective-permute-start | bytes 393224 | tf_op jit(solution)/shard_map/ppermute | solution.py:194
  117.9 6.8 %collective-permute-start.22 = (bf16[64,1024]{1,0:T(8,128)(2,1)S(1)}, bf16[64,1024]{1,0:T(8,128)(2,1)S(1)}, u32[]{:S(2)}, u32[]{:S(2)}) collective-permute-start(bf16[64,1024]{1,0:T(8,128)(2,1)S(1)} %copy-done.16), channel_id=1, source_target_pairs={{0,16},{16,0},{1,17},{17,1},{2,18},{18,2},{3,19},{19,3},{4,20},{20... | collective-permute-start | bytes 393224 | tf_op jit(solution)/shard_map/ppermute | solution.py:194
  124.8 15.5 %collective-permute-start.24 = (bf16[7,256,256]{2,1,0:T(8,128)(2,1)S(1)}, bf16[7,256,256]{2,1,0:T(8,128)(2,1)S(1)}, u32[]{:S(2)}, u32[]{:S(2)}) collective-permute-start(bf16[7,256,256]{2,1,0:T(8,128)(2,1)S(1)} %pad_maximum_fusion), channel_id=1, source_target_pairs={{0,8},{8,0},{1,9},{9,1},{2,10},{10,2},{3,11},{11,3},{4,12},{12,4},... | collective-permute-start | bytes 2752520 | tf_op jit(solution)/shard_map/ppermute | solution.py:194
  124.9 15.4 %collective-permute-start.23 = (bf16[2,128,1024]{2,1,0:T(8,128)(2,1)S(1)}, bf16[2,128,1024]{2,1,0:T(8,128)(2,1)S(1)}, u32[]{:S(2)}, u32[]{:S(2)}) collective-permute-start(bf16[2,128,1024]{2,1,0:T(8,128)(2,1)S(1)} %add_convert_fusion.1), channel_id=1, source_target_pairs={{32,0},{40,72},{64,32},{72,104},{96,64},{104,136},{160,128},{168,2... | collective-permute-start | bytes 1572872 | tf_op jit(solution)/shard_map/ppermute | solution.py:194
  126.2 14.1 %collective-permute-start.25 = (bf16[128,1024]{1,0:T(8,128)(2,1)S(1)}, bf16[128,1024]{1,0:T(8,128)(2,1)S(1)}, u32[]{:S(2)}, u32[]{:S(2)}) collective-permute-start(bf16[128,1024]{1,0:T(8,128)(2,1)S(1)} %copy-done.14), channel_id=1, source_target_pairs={{0,16},{16,0},{1,17},{17,1},{2,18},{18,2},{3,19},{19,3},{4,20},{20... | collective-permute-start | bytes 786440 | tf_op jit(solution)/shard_map/ppermute | solution.py:194
  152.8 18.8 %collective-permute-start.27 = (bf16[8,256,256]{2,1,0:T(8,128)(2,1)}, bf16[8,256,256]{2,1,0:T(8,128)(2,1)S(1)}, u32[]{:S(2)}, u32[]{:S(2)}) collective-permute-start(bf16[8,256,256]{2,1,0:T(8,128)(2,1)} %bitcast.92), channel_id=1, source_target_pairs={{0,8},{8,0},{1,9},{9,1},{2,10},{10,2},{3,11},{11,3},{4,12},{12,4},... | collective-permute-start | bytes 3145736 | tf_op jit(solution)/shard_map/ppermute | solution.py:194
  152.8 18.8 %collective-permute-start.26 = (bf16[2,128,1024]{2,1,0:T(8,128)(2,1)}, bf16[2,128,1024]{2,1,0:T(8,128)(2,1)}, u32[]{:S(2)}, u32[]{:S(2)}) collective-permute-start(bf16[2,128,1024]{2,1,0:T(8,128)(2,1)} %add_convert_fusion), channel_id=1, source_target_pairs={{0,224},{8,40},{32,0},{64,32},{72,104},{104,136},{128,96},{136,168... | collective-permute-start | bytes 1572872 | tf_op jit(solution)/shard_map/ppermute | solution.py:194
  158.1 13.5 %collective-permute-start.28 = (bf16[128,1024]{1,0:T(8,128)(2,1)}, bf16[128,1024]{1,0:T(8,128)(2,1)S(1)}, u32[]{:S(2)}, u32[]{:S(2)}) collective-permute-start(bf16[128,1024]{1,0:T(8,128)(2,1)} %get-tuple-element.130), channel_id=1, source_target_pairs={{0,16},{16,0},{1,17},{17,1},{2,18},{18,2},{3,19},{19,3},{4,20},{20... | collective-permute-start | bytes 786440 | tf_op jit(solution)/shard_map/ppermute | solution.py:194
  177.0 5.8 %collective-permute-start.30 = (bf16[128,512]{1,0:T(8,128)(2,1)S(1)}, bf16[128,512]{1,0:T(8,128)(2,1)S(1)}, u32[]{:S(2)}, u32[]{:S(2)}) collective-permute-start(bf16[128,512]{1,0:T(8,128)(2,1)S(1)} %get-tuple-element.139), channel_id=1, source_target_pairs={{0,1},{1,0},{2,3},{3,2},{4,5},{5,4},{6,7},{7,6},{8,9},{9,8},{10,11... | collective-permute-start | bytes 393224 | tf_op jit(solution)/shard_map/ppermute | solution.py:194
  177.3 8.7 %collective-permute-start.31 = (bf16[128,512]{1,0:T(8,128)(2,1)S(1)}, bf16[128,512]{1,0:T(8,128)(2,1)S(1)}, u32[]{:S(2)}, u32[]{:S(2)}) collective-permute-start(bf16[128,512]{1,0:T(8,128)(2,1)S(1)} %get-tuple-element.138), channel_id=1, source_target_pairs={{0,16},{16,0},{1,17},{17,1},{2,18},{18,2},{3,19},{19,3},{4,20},{20... | collective-permute-start | bytes 393224 | tf_op jit(solution)/shard_map/ppermute | solution.py:194
  180.1 7.7 %collective-permute-start.32 = (bf16[128,512]{1,0:T(8,128)(2,1)S(1)}, bf16[128,512]{1,0:T(8,128)(2,1)S(1)}, u32[]{:S(2)}, u32[]{:S(2)}) collective-permute-start(bf16[128,512]{1,0:T(8,128)(2,1)S(1)} %get-tuple-element.139), channel_id=1, source_target_pairs={{0,17},{1,16},{2,19},{3,18},{16,1},{17,0},{18,3},{19,2},{4,21},{5,... | collective-permute-start | bytes 393224 | tf_op jit(solution)/shard_map/ppermute | solution.py:194
  197.6 9.7 %all-to-all-start = ((f32[8,1,128]{2,1,0:T(1,128)}), f32[8,1,128]{2,1,0:T(1,128)S(1)}, u32[]{:S(2)}, u32[]{:S(2)}) async-start(f32[8,1,128]{2,1,0:T(1,128)} %broadcast_in_dim.16), calls=%async_computation | async-start | bytes 8192 | tf_op jit(solution)/shard_map/all_to_all | solution.py:210
  201.2 22.9 %collective-permute-start.34 = (bf16[192,512]{1,0:T(8,128)(2,1)S(1)}, bf16[192,512]{1,0:T(8,128)(2,1)S(1)}, u32[]{:S(2)}, u32[]{:S(2)}) collective-permute-start(bf16[192,512]{1,0:T(8,128)(2,1)S(1)} %slice.168), channel_id=1, source_target_pairs={{0,32},{32,64},{128,160},{160,192},{1,33},{33,65},{129,161},{161,1... | collective-permute-start | bytes 589832 | tf_op jit(solution)/shard_map/ppermute | solution.py:365
  202.5 21.6 %collective-permute-start.35 = (bf16[192,512]{1,0:T(8,128)(2,1)S(1)}, bf16[192,512]{1,0:T(8,128)(2,1)S(1)}, u32[]{:S(2)}, u32[]{:S(2)}) collective-permute-start(bf16[192,512]{1,0:T(8,128)(2,1)S(1)} %slice.168), channel_id=1, source_target_pairs={{96,64},{224,192},{97,65},{225,193},{98,66},{226,194},{99,67},{227... | collective-permute-start | bytes 589832 | tf_op jit(solution)/shard_map/ppermute | solution.py:366
  (38 other events, 427.5 us)
Sparse Core Ops, SparseCore 0:
  110.5 42.3 all-gather.2

commit v2 on v1

--- a/solution.py
+++ b/solution.py
@@ -19,9 +19,7 @@
 PARAMS = pltpu.CompilerParams(vmem_limit_bytes=48 * 1024 * 1024)
 
 AWAY = (4, 3, 3, 2, 2, 1, 1, 0, 0)
-GIVE_SLOT = (0, 1, 2, 3, 4, 4, 5, 5, 6, 7)
-GIVE_START = (0, 0, 0, 0, 0, 64, 0, 64, 0, 0)
-GIVE_ROWS = (128, 128, 128, 128, 64, 64, 64, 64, 128, 128)
+GIVE_SLOTS = ((0,), (1,), (2,), (3, 4), (5, 6), (7,))
 SWAP2 = [(0, 1), (1, 0)]
 SWAP_X = [(0, 1), (1, 0), (2, 3), (3, 2)]
 SWAP_BOTH = [(4 * a + b, 4 * (1 - a) + (b ^ 1)) for a in range(2) for b in range(4)]
@@ -49,37 +47,62 @@
         pick_ref[:, there] = cot_ref[rows, aligned(j * TILE + k * PIECE, PIECE)]
 
 
-def factor_kernel(out_blocks, at_ref, pick_ref, recv_ref, own_ref, got_ref, part_ref):
+def load_tokens(pick_ref, recv_ref, own_ref, got_ref, out_ref, in_ref, sems):
+    count = pick_ref.shape[0]
+    copies = [
+        pltpu.make_async_copy(src, dst.at[pl.ds(start, count)], sems.at[n])
+        for n, (src, dst, start) in enumerate(
+            (
+                (pick_ref, out_ref, 0),
+                (recv_ref, out_ref, count),
+                (own_ref, in_ref, 0),
+                (got_ref, in_ref, count),
+            )
+        )
+    ]
+    for copy in copies:
+        copy.start()
+    for copy in copies:
+        copy.wait()
+
+
+def factor_kernel(out_blocks, at_ref, pick_ref, recv_ref, own_ref, got_ref, part_ref, out_ref, in_ref, sems):
     i = pl.program_id(0)
+
+    @pl.when(i == 0)
+    def _():
+        load_tokens(pick_ref, recv_ref, own_ref, got_ref, out_ref, in_ref, sems)
+
     h, plane, block, piece = at_ref[0], at_ref[2 + 3 * i], at_ref[3 + 3 * i], at_ref[4 + 3 * i]
-    left = aligned(block * HALF + piece * PIECE, PIECE)
-    right = aligned(out_blocks * HALF + block * PIECE, PIECE)
-    part_ref[0, :, :PIECE] = (
-        tdot(pick_ref[:, left], pick_ref[:, right]) + tdot(recv_ref[:, left], recv_ref[:, right])
-    ).astype(bf16)
-    rows, here = aligned((2 * h + piece) * PIECE, PIECE), aligned(plane * 128, 128)
-    part_ref[0, :, PIECE:] = (
-        tdot(own_ref[:, rows], own_ref[:, here]) + tdot(got_ref[:, rows], got_ref[:, here])
-    ).astype(bf16)
-
-
-def cross_kernel(at_ref, pick_ref, recv_ref, own_ref, got_ref, keep_ref, *give_refs):
+    left = out_ref[:, aligned(block * HALF + piece * PIECE, PIECE)]
+    right = out_ref[:, aligned(out_blocks * HALF + block * PIECE, PIECE)]
+    part_ref[0, :, :PIECE] = tdot(left, right).astype(bf16)
+    rows = in_ref[:, aligned((2 * h + piece) * PIECE, PIECE)]
+    part_ref[0, :, PIECE:] = tdot(rows, in_ref[:, aligned(plane * 128, 128)]).astype(bf16)
+
+
+def cross_kernel(at_ref, pick_ref, recv_ref, own_ref, got_ref, keep_ref, *refs):
+    give_refs, (out_ref, in_ref, sems) = refs[:-3], refs[-3:]
     i = pl.program_id(0)
+
+    @pl.when(i == 0)
+    def _():
+        load_tokens(pick_ref, recv_ref, own_ref, got_ref, out_ref, in_ref, sems)
+
     yh, block, piece = at_ref[1], at_ref[3 + 3 * i], at_ref[4 + 3 * i]
 
     def rows_of(side):
-        rows = aligned(block * HALF + piece * PIECE + side * 128, 128)
-        return (
-            tdot(pick_ref[:, rows], own_ref[...]) + tdot(recv_ref[:, rows], got_ref[...])
-        ).astype(bf16)
+        rows = out_ref[:, aligned(block * HALF + piece * PIECE + side * 128, 128)]
+        return tdot(rows, in_ref[...]).astype(bf16)
 
     keep_ref[0] = rows_of(yh)
     give = rows_of(1 - yh)
-    for slot, start, ref in zip(GIVE_SLOT, GIVE_START, give_refs):
-
-        @pl.when(i == slot)
-        def _():
-            ref[...] = give[start : start + ref.shape[0]]
+    for slots, ref in zip(GIVE_SLOTS, give_refs):
+        for n, slot in enumerate(slots):
+
+            @pl.when(i == slot)
+            def _():
+                ref[n] = give
 
 
 def scale_of(tokens, sums_ref):
@@ -116,7 +139,7 @@
 
 
 def in_inverse_kernel(
-    tokens, at_ref, shard_ref, one_ref, two_ref, three_ref, far_ref, other_ref,
+    tokens, at_ref, shard_ref, own_ref, other_ref,
     out_ref, sums_ref, first_ref, low_ref,
 ):
     i = pl.program_id(0)
@@ -134,10 +157,10 @@
 
         for h in range(2):
             put(h, 0, shard_ref[h])
-            for d, ref in ((1, one_ref), (2, two_ref), (3, three_ref)):
-                put(h, back * d, ref[h])
+            for d in (1, 2, 3):
+                put(h, back * d, own_ref[2 * (d - 1) + h])
                 put(h, -back * d, other_ref[2 * (d - 1) + h])
-        put(core, 4, far_ref[0])
+        put(core, 4, own_ref[6])
         put(1 - core, 4, other_ref[6])
         split_factor(tokens, sums_ref, first_ref, low_ref, 0)
 
@@ -250,22 +273,27 @@
 
     def slots(kernel, count, block, gives=()):
         tokens_in = (pick, recv, normed, normed_recv)
-        rows = [(n, TILE) for n in gives]
+        more = [(len(slots), *block) for slots in gives]
         return pl.pallas_call(
             kernel,
             grid_spec=pltpu.PrefetchScalarGridSpec(
                 num_scalar_prefetch=1,
                 grid=(count,),
-                in_specs=[pl.BlockSpec(a.shape, lambda i, at: (0, 0)) for a in tokens_in],
+                in_specs=[pl.BlockSpec(memory_space=pl.ANY) for _ in tokens_in],
                 out_specs=[pl.BlockSpec((1, *block), lambda i, at: (i, 0, 0))]
-                + [pl.BlockSpec(r, lambda i, at: (0, 0)) for r in rows],
+                + [pl.BlockSpec(m, lambda i, at: (0, 0, 0)) for m in more],
+                scratch_shapes=[
+                    pltpu.VMEM((2 * here, pick.shape[1]), bf16),
+                    pltpu.VMEM((2 * here, TILE), bf16),
+                    pltpu.SemaphoreType.DMA((4,)),
+                ],
             ),
-            out_shape=[jax.ShapeDtypeStruct(r, bf16) for r in [(count, *block)] + rows],
+            out_shape=[jax.ShapeDtypeStruct(m, bf16) for m in [(count, *block)] + more],
             compiler_params=PARAMS,
         )(table, *tokens_in)
 
     (part,) = slots(functools.partial(factor_kernel, out_blocks), 9, (PIECE, PIECE + 128))
-    keep, *give = slots(cross_kernel, 8, (128, TILE), GIVE_ROWS)
+    keep, *give = slots(cross_kernel, 8, (128, TILE), GIVE_SLOTS)
 
     def y_send(i):
         return give[i], YH, SWAP2
@@ -288,25 +316,26 @@
     here_in = in_order(core, part[7, :, PIECE:], part[8, :, PIECE:])
     local = jnp.concatenate([part[7, :, :PIECE], here_in[0], here_in[1]], 1)
     tiles = (added(jnp.concatenate([out_own, both_in], 1), other) + local.astype(f32)).astype(bf16)
-    other, far = phase((tiles, YH, SWAP2), ring(added(keep[0], y0).astype(bf16), 4, True))
+    other, far = phase((tiles, YH, SWAP2), ring(added(keep[0], y0[0]).astype(bf16), 4, True))
     tiles = added(tiles, other).astype(bf16)
     out_tile, in_tile = tiles[:, :PIECE], tiles[:, PIECE:]
-    out_tiles = lax.all_gather(out_tile, OWNER)
-    near_in, far, y3 = phase(
+    copies = jnp.broadcast_to(out_tile[None], (8, PIECE, PIECE))
+    out_tiles = lax.all_to_all(copies, OWNER, 0, 0, tiled=True)
+    near_in, far, y34 = phase(
         (in_tile, X, SWAP_X),
-        ring(added(keep[1:3], jnp.stack([y1, y2]), widened(far)).astype(bf16), 3, True),
+        ring(added(keep[1:3], jnp.concatenate([y1, y2]), widened(far)).astype(bf16), 3, True),
         y_send(3),
     )
     shard = in_order(h, in_tile, near_in)
-    one, y4 = phase(ring(shard), y_send(4))
-    two, y5 = phase(ring(one), y_send(5))
-    three, y6 = phase(ring(two), y_send(6))
-    last, y7 = phase(ring(jnp.where(core == 0, three[:1], three[1:])), y_send(7))
-    y4, y5 = jnp.concatenate([y4, y5]), jnp.concatenate([y6, y7])
-    cross, in_other, y6 = phase(
-        ring(added(keep[3:5], jnp.stack([y3, y4]), far).astype(bf16), 2, True),
-        (jnp.concatenate([one, two, three, last], 0), CORE, SWAP2),
-        y_send(8),
+    (one,) = phase(ring(shard))
+    (two,) = phase(ring(one))
+    (three,) = phase(ring(two))
+    (last,) = phase(ring(jnp.where(core == 0, three[:1], three[1:])))
+    in_own = jnp.concatenate([one, two, three, last], 0)
+    cross, in_other, y56 = phase(
+        ring(added(keep[3:5], y34, far).astype(bf16), 2, True),
+        (in_own, CORE, SWAP2),
+        y_send(4),
     )
     square = (TILE, TILE)
     in_inverse = call(
@@ -316,21 +345,18 @@
         square,
         numbers(z, core),
         shard,
-        one,
-        two,
-        three,
-        last,
+        in_own,
         in_other,
         scratch=[(square, bf16), (square, f32), (square, bf16)],
     )
     cross, out_other, y7 = phase(
-        ring(added(keep[5:7], jnp.stack([y5, y6]), cross).astype(bf16), 1, True),
+        ring(added(keep[5:7], y56, cross).astype(bf16), 1, True),
         (out_tiles, CORE, SWAP2),
-        y_send(9),
+        y_send(5),
     )
     cross, in_inverse = lax.optimization_barrier((cross, in_inverse))
     (other,) = phase((jnp.where(core == 0, cross[1], cross[0]), CORE, SWAP2))
-    cross = added(jnp.where(core == 0, cross[0], cross[1]), other, keep[7], y7).astype(bf16)
+    cross = added(jnp.where(core == 0, cross[0], cross[1]), other, keep[7], y7[0]).astype(bf16)
     m = z % 4
     row = 2 * yh + core
     slice_rows = out_width // lax.axis_size(DP)

time: 236 us -> 226 us (0.958)
  between operations: 14.7 us -> 1.15 us
  waiting for transfers between devices: 78.5 us -> 87.6 us
  starting transfers between devices: 64.8 us -> 61.6 us
  other arithmetic: 17.2 us -> 14.6 us
  local copies, waits for them, and re-layouts: 15.5 us -> 12.9 us
    ppermute x31 -> x27, waiting for transfers between devices: 62.9 us -> 82.5 us  [phase(): got = [lax.ppermute(value, *send[1:]) for value, send in zip(values, sends)]]
    all_gather x1 -> x0, waiting for transfers between devices: 10.5 us -> none  [shards(): out_tiles = lax.all_gather(out_tile, OWNER)]
    ppermute x31 -> x27, starting transfers between devices: 58.6 us -> 49 us  [phase(): got = [lax.ppermute(value, *send[1:]) for value, send in zip(values, sends)]]
    all_to_all x0 -> x1, starting transfers between devices: none -> 5.15 us  [shards(): out_tiles = lax.all_to_all(copies, OWNER, 0, 0, tiled=True)]
    unnamed x64 -> x26, local copies, waits for them, and re-layouts: 12 us -> 8.37 us
  transfers between devices with their start and end apart: 38 -> 34, of which waited for: 18 -> 18; matrix products, arithmetic and copies ran while one was open for 4% -> 5% of each run, Pallas kernels for 8% -> 9%
where the time goes in v2:
time: 226 us; the launch traced here: 222 us
  waiting for transfers between devices  87.6 us (39%)
  starting transfers between devices  61.6 us (27%)
  Pallas kernels  23.9 us (11%)
  blocking collectives  16.2 us (7%)
  other arithmetic  14.6 us (6%)
  local copies, waits for them, and re-layouts  12.9 us (6%)
  matrix products  3.74 us (2%)
    ppermute x27, waiting for transfers between devices, phase(): got = [lax.ppermute(value, *send[1:]) for value, send in zip(values, sends)]  82.5 us
    ppermute x27, starting transfers between devices, phase(): got = [lax.ppermute(value, *send[1:]) for value, send in zip(values, sends)]  49 us
    all_to_all x1, blocking collectives, all_sum(): lax.all_to_all(jnp.full((n, 128), value, f32), axis, 0, 0, tiled=True)  16.2 us
    pallas_call x3, Pallas kernels, call(): pl.pallas_call(kernel, grid_spec=pltpu.PrefetchScalarGridSpec(num_scalar_...  14.1 us
    pallas_call x2, Pallas kernels, slots(): pl.pallas_call(kernel, grid_spec=pltpu.PrefetchScalarGridSpec(num_scalar_...  9.79 us
    unnamed x26, local copies, waits for them, and re-layouts  8.37 us
    all_to_all x1, starting transfers between devices, shards(): out_tiles = lax.all_to_all(copies, OWNER, 0, 0, tiled=True)  5.15 us
    all_to_all x1, starting transfers between devices, all_sum(): lax.all_to_all(jnp.full((n, 128), value, f32), axis, 0, 0, tiled=True)  4.87 us
  transfers between devices with their start and end apart: 34, of which 18 were waited for; matrix products, arithmetic and copies ran while one was open for 5% of the time, Pallas kernels for 9%

profile of v2, /device:TPU:16, one launch (start us, length us, event | category | flops | bytes accessed | tf_op | source)
XLA Modules:
  0.0 221.8 jit_solution(16011862607283830952)
XLA Ops:
  8.5 3.7 %shard_map.38 = bf16[9,256,384]{2,1,0:T(8,128)(2,1)S(1)} custom-call(s32[29]{0:T(128)S(1)} %stack.154.at_ref, bf16[128,4608]{1,0:T(8,128)(2,1)S(1)} %shard_map.37.pick_ref, bf16[128,4608]{1,0:T(8,128)(2,1)S(1)} %copy-done.1, bf16[128,1024]{1,0:T(8,128)(2,1)S(1)} %multiply_convert_fusion.own_ref, bf16[128,1024]{1,0:T(8,128)(2,1)S(1)} %collective-permute-done.1.got_ref), custom_call_target="tpu_custom_call" | custom-call | tf_op jit(solution)/shard_map/pallas_call | solution.py:277
  12.8 5.9 %collective-permute-start.2 = (bf16[256,384]{1,0:T(8,128)(2,1)}, bf16[256,384]{1,0:T(8,128)(2,1)}, u32[]{:S(2)}, u32[]{:S(2)}) collective-permute-start(bf16[256,384]{1,0:T(8,128)(2,1)} %slice_bitcast_fusion), channel_id=1, source_target_pairs={{0,224},{8,40},{32,0},{40,72},{64,32},{72,104},{96,64},{104,136},{... | collective-permute-start | bytes 589832 | tf_op jit(solution)/shard_map/ppermute | solution.py:217
  20.0 6.1 %shard_map.39 = (bf16[8,128,1024]{2,1,0:T(8,128)(2,1)}, bf16[1,128,1024]{2,1,0:T(8,128)(2,1)S(1)}, bf16[1,128,1024]{2,1,0:T(8,128)(2,1)S(1)}, bf16[1,128,1024]{2...) custom-call(s32[29]{0:T(128)S(1)} %stack.154.at_ref, ...), custom_call_target="tpu_custom_call" | custom-call | tf_op jit(solution)/shard_map/pallas_call | solution.py:277
  28.9 7.5 %collective-permute-done.4 = bf16[1,128,1024]{2,1,0:T(8,128)(2,1)S(1)} collective-permute-done((bf16[1,128,1024]{2,1,0:T(8,128)(2,1)S(1)}, bf16[1,128,1024]{2,1,0:T(8,128)(2,1)S(1)}, u32[]{:S(2)}, u32[]{:S(2)}) %collective-permute-start.4) | collective-permute-done | bytes 262176 | tf_op jit(solution)/shard_map/ppermute | solution.py:217
  38.2 7.5 %collective-permute-done.6 = bf16[1,128,1024]{2,1,0:T(8,128)(2,1)S(1)} collective-permute-done((bf16[1,128,1024]{2,1,0:T(8,128)(2,1)S(1)}, bf16[1,128,1024]{2,1,0:T(8,128)(2,1)S(1)}, u32[]{:S(2)}, u32[]{:S(2)}) %collective-permute-start.6) | collective-permute-done | bytes 262176 | tf_op jit(solution)/shard_map/ppermute | solution.py:217
  48.1 7.5 %collective-permute-done.8 = bf16[1,128,1024]{2,1,0:T(8,128)(2,1)S(1)} collective-permute-done((bf16[1,128,1024]{2,1,0:T(8,128)(2,1)S(1)}, bf16[1,128,1024]{2,1,0:T(8,128)(2,1)S(1)}, u32[]{:S(2)}, u32[]{:S(2)}) %collective-permute-start.8) | collective-permute-done | bytes 262176 | tf_op jit(solution)/shard_map/ppermute | solution.py:217
  57.8 3.5 %collective-permute-start.11 = (bf16[128,1024]{1,0:T(8,128)(2,1)S(1)}, bf16[128,1024]{1,0:T(8,128)(2,1)S(1)}, u32[]{:S(2)}, u32[]{:S(2)}) collective-permute-start(bf16[128,1024]{1,0:T(8,128)(2,1)S(1)} %fusion.4), channel_id=1, source_target_pairs={{0,224},{8,40},{32,0},{40,72},{96,64},{104,136},{128,96},{136,168}... | collective-permute-start | bytes 786440 | tf_op jit(solution)/shard_map/ppermute | solution.py:217
  61.4 6.0 %collective-permute-done.10 = bf16[256,512]{1,0:T(8,128)(2,1)S(1)} collective-permute-done((bf16[256,512]{1,0:T(8,128)(2,1)S(1)}, bf16[256,512]{1,0:T(8,128)(2,1)S(1)}, u32[]{:S(2)}, u32[]{:S(2)}) %collective-permute-start.10) | collective-permute-done | bytes 262176 | tf_op jit(solution)/shard_map/ppermute | solution.py:217
  68.8 3.6 %collective-permute-start.13 = (bf16[2,128,1024]{2,1,0:T(8,128)(2,1)S(1)}, bf16[2,128,1024]{2,1,0:T(8,128)(2,1)S(1)}, u32[]{:S(2)}, u32[]{:S(2)}) collective-permute-start(bf16[2,128,1024]{2,1,0:T(8,128)(2,1)S(1)} %add_convert_fusion.2), channel_id=1, source_target_pairs={{0,224},{8,40},{40,72},{64,32},{72,104},{96,64},{128,96},{136,168}... | collective-permute-start | bytes 1572872 | tf_op jit(solution)/shard_map/ppermute | solution.py:217
  72.4 3.2 %collective-permute-start.14 = (bf16[2,128,1024]{2,1,0:T(8,128)(2,1)}, bf16[2,128,1024]{2,1,0:T(8,128)(2,1)S(1)}, u32[]{:S(2)}, u32[]{:S(2)}) collective-permute-start(bf16[2,128,1024]{2,1,0:T(8,128)(2,1)} %get-tuple-element.77), channel_id=1, source_target_pairs={{0,16},{16,0},{1,17},{17,1},{2,18},{18,2},{3,19},{19,3},{4,20},{20... | collective-permute-start | bytes 1572872 | tf_op jit(solution)/shard_map/ppermute | solution.py:217
  77.1 3.5 %collective-permute-done.12 = bf16[256,256]{1,0:T(8,128)(2,1)S(1)} collective-permute-done((bf16[256,256]{1,0:T(8,128)(2,1)S(1)}, bf16[256,256]{1,0:T(8,128)(2,1)S(1)}, u32[]{:S(2)}, u32[]{:S(2)}) %collective-permute-start.12) | collective-permute-done | bytes 131104 | tf_op jit(solution)/shard_map/ppermute | solution.py:217
  80.6 5.1 %collective-permute-done.14 = bf16[2,128,1024]{2,1,0:T(8,128)(2,1)S(1)} collective-permute-done((bf16[2,128,1024]{2,1,0:T(8,128)(2,1)}, bf16[2,128,1024]{2,1,0:T(8,128)(2,1)S(1)}, u32[]{:S(2)}, u32[]{:S(2)}) %collective-permute-start.14) | collective-permute-done | bytes 524320 | tf_op jit(solution)/shard_map/ppermute | solution.py:217
  86.8 5.4 %collective-permute-done.15 = bf16[2,256,256]{2,1,0:T(8,128)(2,1)S(1)} collective-permute-done((bf16[2,256,256]{2,1,0:T(8,128)(2,1)S(1)}, bf16[2,256,256]{2,1,0:T(8,128)(2,1)S(1)}, u32[]{:S(2)}, u32[]{:S(2)}) %collective-permute-start.15) | collective-permute-done | bytes 262176 | tf_op jit(solution)/shard_map/ppermute | solution.py:217
  92.2 2.2 collective-permute-start.16
  94.4 4.2 %collective-permute-done.16 = bf16[2,256,256]{2,1,0:T(8,128)(2,1)S(1)} collective-permute-done((bf16[2,256,256]{2,1,0:T(8,128)(2,1)S(1)}, bf16[2,256,256]{2,1,0:T(8,128)(2,1)S(1)}, u32[]{:S(2)}, u32[]{:S(2)}) %collective-permute-start.16) | collective-permute-done | bytes 262176 | tf_op jit(solution)/shard_map/ppermute | solution.py:217
  98.6 3.4 %collective-permute-start.17 = (bf16[2,256,256]{2,1,0:T(8,128)(2,1)S(1)}, bf16[2,256,256]{2,1,0:T(8,128)(2,1)S(1)}, u32[]{:S(2)}, u32[]{:S(2)}) collective-permute-start(bf16[2,256,256]{2,1,0:T(8,128)(2,1)S(1)} %collective-permute-done.16), channel_id=1, source_target_pairs={{0,224},{8,40},{32,0},{40,72},{64,32},{72,104},{96,64},{104,136},{... | collective-permute-start | bytes 786440 | tf_op jit(solution)/shard_map/ppermute | solution.py:217
  102.0 3.9 %collective-permute-done.17 = bf16[2,256,256]{2,1,0:T(8,128)(2,1)S(1)} collective-permute-done((bf16[2,256,256]{2,1,0:T(8,128)(2,1)S(1)}, bf16[2,256,256]{2,1,0:T(8,128)(2,1)S(1)}, u32[]{:S(2)}, u32[]{:S(2)}) %collective-permute-start.17) | collective-permute-done | bytes 262176 | tf_op jit(solution)/shard_map/ppermute | solution.py:217
  105.9 3.8 %collective-permute-start.18 = (bf16[1,256,256]{2,1,0:T(8,128)(2,1)S(1)}, bf16[1,256,256]{2,1,0:T(8,128)(2,1)S(1)}, u32[]{:S(2)}, u32[]{:S(2)}) collective-permute-start(bf16[1,256,256]{2,1,0:T(8,128)(2,1)S(1)} %slice_select_fusion), channel_id=1, source_target_pairs={{0,224},{8,40},{32,0},{40,72},{64,32},{72,104},{96,64},{104,136},{... | collective-permute-start | bytes 393224 | tf_op jit(solution)/shard_map/ppermute | solution.py:217
  109.7 2.1 add_convert_fusion.1
  113.5 5.2 %all-to-all-start = ((bf16[8,256,256]{2,1,0:T(8,128)(2,1)}), bf16[8,256,256]{2,1,0:T(8,128)(2,1)S(1)}, u32[]{:S(2)}, u32[]{:S(2)}) async-start(bf16[8,256,256]{2,1,0:T(8,128)(2,1)} %broadcast_in_dim.21), calls=%async_computation | async-start | bytes 2097152 | tf_op jit(solution)/shard_map/all_to_all | solution.py:323
  120.6 9.3 %collective-permute-done.19 = bf16[2,128,1024]{2,1,0:T(8,128)(2,1)S(1)} collective-permute-done((bf16[2,128,1024]{2,1,0:T(8,128)(2,1)}, bf16[2,128,1024]{2,1,0:T(8,128)(2,1)S(1)}, u32[]{:S(2)}, u32[]{:S(2)}) %collective-permute-start.19) | collective-permute-done | bytes 524320 | tf_op jit(solution)/shard_map/ppermute | solution.py:217
  129.9 13.9 %collective-permute-done.21 = bf16[2,128,1024]{2,1,0:T(8,128)(2,1)S(1)} collective-permute-done((bf16[2,128,1024]{2,1,0:T(8,128)(2,1)}, bf16[2,128,1024]{2,1,0:T(8,128)(2,1)S(1)}, u32[]{:S(2)}, u32[]{:S(2)}) %collective-permute-start.21) | collective-permute-done | bytes 524320 | tf_op jit(solution)/shard_map/ppermute | solution.py:217
  143.8 2.5 %add_convert_fusion = bf16[2,128,1024]{2,1,0:T(8,128)(2,1)} fusion(bf16[2,128,1024]{2,1,0:T(8,128)(2,1)S(1)} %collective-permute-done.19, bf16[2,128,1024]{2,1,0:T(8,128)(2,1)S(1)} %collective-permute-done.21, bf16[8,128,1024]{2,1,0:T(8,128)(2,1)} %get-tuple-element.66), kind=kLoop, calls=%fused_computation.3 | loop fusion | flops 1572864 | bytes 2097152 | tf_op jit(solution)/shard_map/convert_element_type | solution.py:353
  146.3 5.9 %collective-permute-start.22 = (bf16[2,128,1024]{2,1,0:T(8,128)(2,1)}, bf16[2,128,1024]{2,1,0:T(8,128)(2,1)S(1)}, u32[]{:S(2)}, u32[]{:S(2)}) collective-permute-start(bf16[2,128,1024]{2,1,0:T(8,128)(2,1)} %add_convert_fusion), channel_id=1, source_target_pairs={{0,224},{8,40},{32,0},{64,32},{72,104},{104,136},{128,96},{136,168... | collective-permute-start | bytes 1572872 | tf_op jit(solution)/shard_map/ppermute | solution.py:217
  152.2 1.9 collective-permute-start.24
  155.3 8.5 %shard_map.41 = bf16[1024,1024]{1,0:T(8,128)(2,1)S(1)} custom-call(s32[2]{0:T(128)S(1)} %pad_add_fusion.2.at_ref, bf16[2,256,256]{2,1,0:T(8,128)(2,1)S(1)} %pad_maximum_fusion.6.shard_ref, bf16[7,256,256]{2,1,0:T(8,128)(2,1)S(1)} %pad_maximum_fusion.own_ref, bf16[7,256,256]{2,1,0:T(8,128)(2,1)S(1)} %copy-done.6), custom_call_target="tpu_custom_call" | custom-call | tf_op jit(solution)/shard_map/pallas_call | solution.py:192
  167.6 2.4 %convolution_convert_fusion = bf16[128,1024]{1,0:T(8,128)(2,1)S(1)} fusion(bf16[1024,1024]{1,0:T(8,128)(2,1)} %copy-done.3, bf16[128,1024]{1,0:T(8,128)(2,1)S(1)} %collective-permute-done.25, bf16[1,128,1024]{2,1,0:T(8,128)(2,1)} %copy-done.12, bf16[8,128,1024]{2,1,0:T(8,128)(2,1)} %get-tuple-element.66, pred[]{:T(512)S(6)} %eq.66, ...), kind=kOutput, calls=%fused_computation.1 | convolution fusion | flops 269746176 | bytes 3670017 | tf_op jit(solution)/shard_map/dot_general | solution.py:33
  175.7 5.8 %collective-permute-done.27 = bf16[128,512]{1,0:T(8,128)(2,1)S(1)} collective-permute-done((bf16[128,512]{1,0:T(8,128)(2,1)S(1)}, bf16[128,512]{1,0:T(8,128)(2,1)S(1)}, u32[]{:S(2)}, u32[]{:S(2)}) %collective-permute-start.27) | collective-permute-done | bytes 131104 | tf_op jit(solution)/shard_map/ppermute | solution.py:217
  182.5 4.9 %shard_map.40 = bf16[384,1024]{1,0:T(8,128)(2,1)S(1)} custom-call(s32[3]{0:T(128)S(1)} %pad_add_fusion.at_ref, bf16[8,256,256]{2,1,0:T(8,128)(2,1)S(1)} %all-to-all-done.own_ref, bf16[8,256,256]{2,1,0:T(8,128)(2,1)S(1)} %collective-permute-done.23.other_ref), custom_call_target="tpu_custom_call" | custom-call | tf_op jit(solution)/shard_map/pallas_call | solution.py:192
  191.3 4.9 %all-to-all-start.1 = ((f32[8,1,128]{2,1,0:T(1,128)}), f32[8,1,128]{2,1,0:T(1,128)S(1)}, u32[]{:S(2)}, u32[]{:S(2)}) async-start(f32[8,1,128]{2,1,0:T(1,128)} %broadcast_in_dim.23), calls=%async_computation.1 | async-start | bytes 8192 | tf_op jit(solution)/shard_map/all_to_all | solution.py:233
  198.2 4.1 %all-to-all-done.1 = f32[8,1,128]{2,1,0:T(1,128)S(1)} async-done(((f32[8,1,128]{2,1,0:T(1,128)}), f32[8,1,128]{2,1,0:T(1,128)S(1)}, u32[]{:S(2)}, u32[]{:S(2)}) %all-to-all-start.1) | async-done | bytes 4128 | tf_op jit(solution)/shard_map/all_to_all | solution.py:233
  203.5 16.2 %all_to_all.23 = f32[32,1,128]{2,1,0:T(1,128)S(1)} all-to-all(f32[32,1,128]{2,1,0:T(1,128)S(1)} %broadcast_in_dim.24), channel_id=1, replica_groups=mesh['dp_0'=8,'dp_1'=2,'dp_2'=2,'owner_0'=2,'owner_1'=4] {'dp_0','dp_1',..., dimensions={0} | all-to-all | bytes 32768 | tf_op jit(solution)/shard_map/all_to_all | solution.py:233
  (115 shorter events, 47.3 us)
Async XLA Ops:
  2.2 3.9 %collective-permute-start = (bf16[128,4608]{1,0:T(8,128)(2,1)S(1)}, bf16[128,4608]{1,0:T(8,128)(2,1)S(1)}, u32[]{:S(2)}, u32[]{:S(2)}) collective-permute-start(bf16[128,4608]{1,0:T(8,128)(2,1)S(1)} %shard_map.37.pick_ref), channel_id=1, source_target_pairs={{0,8},{8,0},{1,9},{9,1},{2,10},{10,2},{3,11},{11,3},{4,12},{12,4},... | collective-permute-start | bytes 3538952 | tf_op jit(solution)/shard_map/ppermute | solution.py:257
  4.4 1.7 collective-permute-start.1
  12.8 13.3 %collective-permute-start.2 = (bf16[256,384]{1,0:T(8,128)(2,1)}, bf16[256,384]{1,0:T(8,128)(2,1)}, u32[]{:S(2)}, u32[]{:S(2)}) collective-permute-start(bf16[256,384]{1,0:T(8,128)(2,1)} %slice_bitcast_fusion), channel_id=1, source_target_pairs={{0,224},{8,40},{32,0},{40,72},{64,32},{72,104},{96,64},{104,136},{... | collective-permute-start | bytes 589832 | tf_op jit(solution)/shard_map/ppermute | solution.py:217
  27.4 9.0 %collective-permute-start.3 = (bf16[2,256,384]{2,1,0:T(8,128)(2,1)S(1)}, bf16[2,256,384]{2,1,0:T(8,128)(2,1)S(1)}, u32[]{:S(2)}, u32[]{:S(2)}) collective-permute-start(bf16[2,256,384]{2,1,0:T(8,128)(2,1)S(1)} %add_convert_fusion.5), channel_id=1, source_target_pairs={{0,224},{8,40},{32,0},{40,72},{64,32},{72,104},{96,64},{104,136},{... | collective-permute-start | bytes 1179656 | tf_op jit(solution)/shard_map/ppermute | solution.py:217
  28.5 7.9 %collective-permute-start.4 = (bf16[1,128,1024]{2,1,0:T(8,128)(2,1)S(1)}, bf16[1,128,1024]{2,1,0:T(8,128)(2,1)S(1)}, u32[]{:S(2)}, u32[]{:S(2)}) collective-permute-start(bf16[1,128,1024]{2,1,0:T(8,128)(2,1)S(1)} %get-tuple-element.56), channel_id=1, source_target_pairs={{0,16},{16,0},{1,17},{17,1},{2,18},{18,2},{3,19},{19,3},{4,20},{20... | collective-permute-start | bytes 786440 | tf_op jit(solution)/shard_map/ppermute | solution.py:217
  36.5 9.3 %collective-permute-start.5 = (bf16[2,256,384]{2,1,0:T(8,128)(2,1)S(1)}, bf16[2,256,384]{2,1,0:T(8,128)(2,1)S(1)}, u32[]{:S(2)}, u32[]{:S(2)}) collective-permute-start(bf16[2,256,384]{2,1,0:T(8,128)(2,1)S(1)} %add_convert_fusion.4), channel_id=1, source_target_pairs={{0,224},{8,40},{32,0},{40,72},{64,32},{72,104},{96,64},{104,136},{... | collective-permute-start | bytes 1179656 | tf_op jit(solution)/shard_map/ppermute | solution.py:217
  37.9 7.9 %collective-permute-start.6 = (bf16[1,128,1024]{2,1,0:T(8,128)(2,1)S(1)}, bf16[1,128,1024]{2,1,0:T(8,128)(2,1)S(1)}, u32[]{:S(2)}, u32[]{:S(2)}) collective-permute-start(bf16[1,128,1024]{2,1,0:T(8,128)(2,1)S(1)} %get-tuple-element.60), channel_id=1, source_target_pairs={{0,16},{16,0},{1,17},{17,1},{2,18},{18,2},{3,19},{19,3},{4,20},{20... | collective-permute-start | bytes 786440 | tf_op jit(solution)/shard_map/ppermute | solution.py:217
  45.9 9.7 %collective-permute-start.7 = (bf16[2,256,384]{2,1,0:T(8,128)(2,1)S(1)}, bf16[2,256,384]{2,1,0:T(8,128)(2,1)S(1)}, u32[]{:S(2)}, u32[]{:S(2)}) collective-permute-start(bf16[2,256,384]{2,1,0:T(8,128)(2,1)S(1)} %add_convert_fusion.3), channel_id=1, source_target_pairs={{0,224},{8,40},{32,0},{40,72},{64,32},{72,104},{96,64},{104,136},{... | collective-permute-start | bytes 1179656 | tf_op jit(solution)/shard_map/ppermute | solution.py:217
  47.7 7.9 %collective-permute-start.8 = (bf16[1,128,1024]{2,1,0:T(8,128)(2,1)S(1)}, bf16[1,128,1024]{2,1,0:T(8,128)(2,1)S(1)}, u32[]{:S(2)}, u32[]{:S(2)}) collective-permute-start(bf16[1,128,1024]{2,1,0:T(8,128)(2,1)S(1)} %get-tuple-element.64), channel_id=1, source_target_pairs={{0,16},{16,0},{1,17},{17,1},{2,18},{18,2},{3,19},{19,3},{4,20},{20... | collective-permute-start | bytes 786440 | tf_op jit(solution)/shard_map/ppermute | solution.py:217
  57.4 9.9 %collective-permute-start.10 = (bf16[256,512]{1,0:T(8,128)(2,1)S(1)}, bf16[256,512]{1,0:T(8,128)(2,1)S(1)}, u32[]{:S(2)}, u32[]{:S(2)}) collective-permute-start(bf16[256,512]{1,0:T(8,128)(2,1)S(1)} %add_convert_fusion.8), channel_id=1, source_target_pairs={{0,16},{16,0},{1,17},{17,1},{2,18},{18,2},{3,19},{19,3},{4,20},{20... | collective-permute-start | bytes 786440 | tf_op jit(solution)/shard_map/ppermute | solution.py:217
  57.8 9.5 %collective-permute-start.11 = (bf16[128,1024]{1,0:T(8,128)(2,1)S(1)}, bf16[128,1024]{1,0:T(8,128)(2,1)S(1)}, u32[]{:S(2)}, u32[]{:S(2)}) collective-permute-start(bf16[128,1024]{1,0:T(8,128)(2,1)S(1)} %fusion.4), channel_id=1, source_target_pairs={{0,224},{8,40},{32,0},{40,72},{96,64},{104,136},{128,96},{136,168}... | collective-permute-start | bytes 786440 | tf_op jit(solution)/shard_map/ppermute | solution.py:217
  68.8 11.8 %collective-permute-start.13 = (bf16[2,128,1024]{2,1,0:T(8,128)(2,1)S(1)}, bf16[2,128,1024]{2,1,0:T(8,128)(2,1)S(1)}, u32[]{:S(2)}, u32[]{:S(2)}) collective-permute-start(bf16[2,128,1024]{2,1,0:T(8,128)(2,1)S(1)} %add_convert_fusion.2), channel_id=1, source_target_pairs={{0,224},{8,40},{40,72},{64,32},{72,104},{96,64},{128,96},{136,168}... | collective-permute-start | bytes 1572872 | tf_op jit(solution)/shard_map/ppermute | solution.py:217
  72.4 13.3 %collective-permute-start.14 = (bf16[2,128,1024]{2,1,0:T(8,128)(2,1)}, bf16[2,128,1024]{2,1,0:T(8,128)(2,1)S(1)}, u32[]{:S(2)}, u32[]{:S(2)}) collective-permute-start(bf16[2,128,1024]{2,1,0:T(8,128)(2,1)} %get-tuple-element.77), channel_id=1, source_target_pairs={{0,16},{16,0},{1,17},{17,1},{2,18},{18,2},{3,19},{19,3},{4,20},{20... | collective-permute-start | bytes 1572872 | tf_op jit(solution)/shard_map/ppermute | solution.py:217
  75.6 5.0 %collective-permute-start.12 = (bf16[256,256]{1,0:T(8,128)(2,1)S(1)}, bf16[256,256]{1,0:T(8,128)(2,1)S(1)}, u32[]{:S(2)}, u32[]{:S(2)}) collective-permute-start(bf16[256,256]{1,0:T(8,128)(2,1)S(1)} %slice.117), channel_id=1, source_target_pairs={{0,1},{1,0},{2,3},{3,2},{4,5},{5,4},{6,7},{7,6},{8,9},{9,8},{10,11... | collective-permute-start | bytes 393224 | tf_op jit(solution)/shard_map/ppermute | solution.py:217
  85.8 6.4 %collective-permute-start.15 = (bf16[2,256,256]{2,1,0:T(8,128)(2,1)S(1)}, bf16[2,256,256]{2,1,0:T(8,128)(2,1)S(1)}, u32[]{:S(2)}, u32[]{:S(2)}) collective-permute-start(bf16[2,256,256]{2,1,0:T(8,128)(2,1)S(1)} %pad_maximum_fusion.6.shard_ref), channel_id=1, source_target_pairs={{0,224},{8,40},{32,0},{40,72},{64,32},{72,104},{96,64},{104,136},{... | collective-permute-start | bytes 786440 | tf_op jit(solution)/shard_map/ppermute | solution.py:217
  92.2 6.4 %collective-permute-start.16 = (bf16[2,256,256]{2,1,0:T(8,128)(2,1)S(1)}, bf16[2,256,256]{2,1,0:T(8,128)(2,1)S(1)}, u32[]{:S(2)}, u32[]{:S(2)}) collective-permute-start(bf16[2,256,256]{2,1,0:T(8,128)(2,1)S(1)} %collective-permute-done.15), channel_id=1, source_target_pairs={{0,224},{8,40},{32,0},{40,72},{64,32},{72,104},{96,64},{104,136},{... | collective-permute-start | bytes 786440 | tf_op jit(solution)/shard_map/ppermute | solution.py:217
  98.6 7.3 %collective-permute-start.17 = (bf16[2,256,256]{2,1,0:T(8,128)(2,1)S(1)}, bf16[2,256,256]{2,1,0:T(8,128)(2,1)S(1)}, u32[]{:S(2)}, u32[]{:S(2)}) collective-permute-start(bf16[2,256,256]{2,1,0:T(8,128)(2,1)S(1)} %collective-permute-done.16), channel_id=1, source_target_pairs={{0,224},{8,40},{32,0},{40,72},{64,32},{72,104},{96,64},{104,136},{... | collective-permute-start | bytes 786440 | tf_op jit(solution)/shard_map/ppermute | solution.py:217
  105.9 6.3 %collective-permute-start.18 = (bf16[1,256,256]{2,1,0:T(8,128)(2,1)S(1)}, bf16[1,256,256]{2,1,0:T(8,128)(2,1)S(1)}, u32[]{:S(2)}, u32[]{:S(2)}) collective-permute-start(bf16[1,256,256]{2,1,0:T(8,128)(2,1)S(1)} %slice_select_fusion), channel_id=1, source_target_pairs={{0,224},{8,40},{32,0},{40,72},{64,32},{72,104},{96,64},{104,136},{... | collective-permute-start | bytes 393224 | tf_op jit(solution)/shard_map/ppermute | solution.py:217
  112.3 31.5 %collective-permute-start.20 = (bf16[7,256,256]{2,1,0:T(8,128)(2,1)S(1)}, bf16[7,256,256]{2,1,0:T(8,128)(2,1)S(1)}, u32[]{:S(2)}, u32[]{:S(2)}) collective-permute-start(bf16[7,256,256]{2,1,0:T(8,128)(2,1)S(1)} %pad_maximum_fusion.own_ref), channel_id=1, source_target_pairs={{0,8},{8,0},{1,9},{9,1},{2,10},{10,2},{3,11},{11,3},{4,12},{12,4},... | collective-permute-start | bytes 2752520 | tf_op jit(solution)/shard_map/ppermute | solution.py:217
  113.5 32.8 %all-to-all-start = ((bf16[8,256,256]{2,1,0:T(8,128)(2,1)}), bf16[8,256,256]{2,1,0:T(8,128)(2,1)S(1)}, u32[]{:S(2)}, u32[]{:S(2)}) async-start(bf16[8,256,256]{2,1,0:T(8,128)(2,1)} %broadcast_in_dim.21), calls=%async_computation | async-start | bytes 2097152 | tf_op jit(solution)/shard_map/all_to_all | solution.py:323
  118.6 11.3 %collective-permute-start.19 = (bf16[2,128,1024]{2,1,0:T(8,128)(2,1)}, bf16[2,128,1024]{2,1,0:T(8,128)(2,1)S(1)}, u32[]{:S(2)}, u32[]{:S(2)}) collective-permute-start(bf16[2,128,1024]{2,1,0:T(8,128)(2,1)} %add_convert_fusion.1), channel_id=1, source_target_pairs={{32,0},{40,72},{64,32},{72,104},{96,64},{104,136},{160,128},{168,2... | collective-permute-start | bytes 1572872 | tf_op jit(solution)/shard_map/ppermute | solution.py:217
  119.9 23.9 %collective-permute-start.21 = (bf16[2,128,1024]{2,1,0:T(8,128)(2,1)}, bf16[2,128,1024]{2,1,0:T(8,128)(2,1)S(1)}, u32[]{:S(2)}, u32[]{:S(2)}) collective-permute-start(bf16[2,128,1024]{2,1,0:T(8,128)(2,1)} %copy-done.7), channel_id=1, source_target_pairs={{0,16},{16,0},{1,17},{17,1},{2,18},{18,2},{3,19},{19,3},{4,20},{20... | collective-permute-start | bytes 1572872 | tf_op jit(solution)/shard_map/ppermute | solution.py:217
  146.3 18.8 %collective-permute-start.23 = (bf16[8,256,256]{2,1,0:T(8,128)(2,1)S(1)}, bf16[8,256,256]{2,1,0:T(8,128)(2,1)S(1)}, u32[]{:S(2)}, u32[]{:S(2)}) collective-permute-start(bf16[8,256,256]{2,1,0:T(8,128)(2,1)S(1)} %all-to-all-done.own_ref), channel_id=1, source_target_pairs={{0,8},{8,0},{1,9},{9,1},{2,10},{10,2},{3,11},{11,3},{4,12},{12,4},... | collective-permute-start | bytes 3145736 | tf_op jit(solution)/shard_map/ppermute | solution.py:217
  146.3 18.8 %collective-permute-start.22 = (bf16[2,128,1024]{2,1,0:T(8,128)(2,1)}, bf16[2,128,1024]{2,1,0:T(8,128)(2,1)S(1)}, u32[]{:S(2)}, u32[]{:S(2)}) collective-permute-start(bf16[2,128,1024]{2,1,0:T(8,128)(2,1)} %add_convert_fusion), channel_id=1, source_target_pairs={{0,224},{8,40},{32,0},{64,32},{72,104},{104,136},{128,96},{136,168... | collective-permute-start | bytes 1572872 | tf_op jit(solution)/shard_map/ppermute | solution.py:217
  152.2 12.9 %collective-permute-start.24 = (bf16[1,128,1024]{2,1,0:T(8,128)(2,1)S(1)}, bf16[1,128,1024]{2,1,0:T(8,128)(2,1)S(1)}, u32[]{:S(2)}, u32[]{:S(2)}) collective-permute-start(bf16[1,128,1024]{2,1,0:T(8,128)(2,1)S(1)} %copy-done.9), channel_id=1, source_target_pairs={{0,16},{16,0},{1,17},{17,1},{2,18},{18,2},{3,19},{19,3},{4,20},{20... | collective-permute-start | bytes 786440 | tf_op jit(solution)/shard_map/ppermute | solution.py:217
  170.1 5.6 %collective-permute-start.26 = (bf16[128,512]{1,0:T(8,128)(2,1)S(1)}, bf16[128,512]{1,0:T(8,128)(2,1)S(1)}, u32[]{:S(2)}, u32[]{:S(2)}) collective-permute-start(bf16[128,512]{1,0:T(8,128)(2,1)S(1)} %get-tuple-element.99), channel_id=1, source_target_pairs={{0,1},{1,0},{2,3},{3,2},{4,5},{5,4},{6,7},{7,6},{8,9},{9,8},{10,11... | collective-permute-start | bytes 393224 | tf_op jit(solution)/shard_map/ppermute | solution.py:217
  171.9 9.6 %collective-permute-start.27 = (bf16[128,512]{1,0:T(8,128)(2,1)S(1)}, bf16[128,512]{1,0:T(8,128)(2,1)S(1)}, u32[]{:S(2)}, u32[]{:S(2)}) collective-permute-start(bf16[128,512]{1,0:T(8,128)(2,1)S(1)} %get-tuple-element.98), channel_id=1, source_target_pairs={{0,16},{16,0},{1,17},{17,1},{2,18},{18,2},{3,19},{19,3},{4,20},{20... | collective-permute-start | bytes 393224 | tf_op jit(solution)/shard_map/ppermute | solution.py:217
  173.5 8.0 %collective-permute-start.28 = (bf16[128,512]{1,0:T(8,128)(2,1)S(1)}, bf16[128,512]{1,0:T(8,128)(2,1)S(1)}, u32[]{:S(2)}, u32[]{:S(2)}) collective-permute-start(bf16[128,512]{1,0:T(8,128)(2,1)S(1)} %get-tuple-element.99), channel_id=1, source_target_pairs={{0,17},{1,16},{2,19},{3,18},{16,1},{17,0},{18,3},{19,2},{4,21},{5,... | collective-permute-start | bytes 393224 | tf_op jit(solution)/shard_map/ppermute | solution.py:217
  182.5 5.0 %collective-permute-start.29 = (bf16[2,2,128,512]{3,2,1,0:T(8,128)(2,1)}, bf16[2,2,128,512]{3,2,1,0:T(8,128)(2,1)}, u32[]{:S(2)}, u32[]{:S(2)}) collective-permute-start(bf16[2,2,128,512]{3,2,1,0:T(8,128)(2,1)} %pad_maximum_fusion.1), channel_id=1, source_target_pairs={{0,8},{8,0},{1,9},{9,1},{2,10},{10,2},{3,11},{11,3},{4,12},{12,4},... | collective-permute-start | bytes 1572872 | tf_op jit(solution)/shard_map/ppermute | solution.py:386
  191.3 11.0 %all-to-all-start.1 = ((f32[8,1,128]{2,1,0:T(1,128)}), f32[8,1,128]{2,1,0:T(1,128)S(1)}, u32[]{:S(2)}, u32[]{:S(2)}) async-start(f32[8,1,128]{2,1,0:T(1,128)} %broadcast_in_dim.23), calls=%async_computation.1 | async-start | bytes 8192 | tf_op jit(solution)/shard_map/all_to_all | solution.py:233
  196.2 24.8 %collective-permute-start.30 = (bf16[192,512]{1,0:T(8,128)(2,1)S(1)}, bf16[192,512]{1,0:T(8,128)(2,1)S(1)}, u32[]{:S(2)}, u32[]{:S(2)}) collective-permute-start(bf16[192,512]{1,0:T(8,128)(2,1)S(1)} %slice.170), channel_id=1, source_target_pairs={{0,32},{32,64},{128,160},{160,192},{1,33},{33,65},{129,161},{161,1... | collective-permute-start | bytes 589832 | tf_op jit(solution)/shard_map/ppermute | solution.py:391
  197.5 23.5 %collective-permute-start.31 = (bf16[192,512]{1,0:T(8,128)(2,1)S(1)}, bf16[192,512]{1,0:T(8,128)(2,1)S(1)}, u32[]{:S(2)}, u32[]{:S(2)}) collective-permute-start(bf16[192,512]{1,0:T(8,128)(2,1)S(1)} %slice.170), channel_id=1, source_target_pairs={{96,64},{224,192},{97,65},{225,193},{98,66},{226,194},{99,67},{227... | collective-permute-start | bytes 589832 | tf_op jit(solution)/shard_map/ppermute | solution.py:392
  (15 other events, 106.8 us)

commit v3 on v2

--- a/solution.py
+++ b/solution.py
@@ -19,7 +19,6 @@
 PARAMS = pltpu.CompilerParams(vmem_limit_bytes=48 * 1024 * 1024)
 
 AWAY = (4, 3, 3, 2, 2, 1, 1, 0, 0)
-GIVE_SLOTS = ((0,), (1,), (2,), (3, 4), (5, 6), (7,))
 SWAP2 = [(0, 1), (1, 0)]
 SWAP_X = [(0, 1), (1, 0), (2, 3), (3, 2)]
 SWAP_BOTH = [(4 * a + b, 4 * (1 - a) + (b ^ 1)) for a in range(2) for b in range(4)]
@@ -73,7 +72,7 @@
     def _():
         load_tokens(pick_ref, recv_ref, own_ref, got_ref, out_ref, in_ref, sems)
 
-    h, plane, block, piece = at_ref[0], at_ref[2 + 3 * i], at_ref[3 + 3 * i], at_ref[4 + 3 * i]
+    h, plane, block, piece = at_ref[0], at_ref[1 + 3 * i], at_ref[2 + 3 * i], at_ref[3 + 3 * i]
     left = out_ref[:, aligned(block * HALF + piece * PIECE, PIECE)]
     right = out_ref[:, aligned(out_blocks * HALF + block * PIECE, PIECE)]
     part_ref[0, :, :PIECE] = tdot(left, right).astype(bf16)
@@ -81,28 +80,16 @@
     part_ref[0, :, PIECE:] = tdot(rows, in_ref[:, aligned(plane * 128, 128)]).astype(bf16)
 
 
-def cross_kernel(at_ref, pick_ref, recv_ref, own_ref, got_ref, keep_ref, *refs):
-    give_refs, (out_ref, in_ref, sems) = refs[:-3], refs[-3:]
+def cross_kernel(at_ref, pick_ref, recv_ref, own_ref, got_ref, cross_ref, out_ref, in_ref, sems):
     i = pl.program_id(0)
 
     @pl.when(i == 0)
     def _():
         load_tokens(pick_ref, recv_ref, own_ref, got_ref, out_ref, in_ref, sems)
 
-    yh, block, piece = at_ref[1], at_ref[3 + 3 * i], at_ref[4 + 3 * i]
-
-    def rows_of(side):
-        rows = out_ref[:, aligned(block * HALF + piece * PIECE + side * 128, 128)]
-        return tdot(rows, in_ref[...]).astype(bf16)
-
-    keep_ref[0] = rows_of(yh)
-    give = rows_of(1 - yh)
-    for slots, ref in zip(GIVE_SLOTS, give_refs):
-        for n, slot in enumerate(slots):
-
-            @pl.when(i == slot)
-            def _():
-                ref[n] = give
+    block, piece = at_ref[2 + 3 * i], at_ref[3 + 3 * i]
+    rows = out_ref[:, aligned(block * HALF + piece * PIECE, PIECE)]
+    cross_ref[0] = tdot(rows, in_ref[...]).astype(bf16)
 
 
 def scale_of(tokens, sums_ref):
@@ -269,34 +256,29 @@
         plane = (z + way * away + 8) % 8
         piece = core if i in (0, 7) else 1 - core if i == 8 else (i + 1) % 2
         table += [plane, 3 * (plane // 4) + plane % 4 - plane % 4 // 2, piece]
-    table = numbers(h, yh, *table)
-
-    def slots(kernel, count, block, gives=()):
+    table = numbers(h, *table)
+
+    def slots(kernel, count, block):
         tokens_in = (pick, recv, normed, normed_recv)
-        more = [(len(slots), *block) for slots in gives]
         return pl.pallas_call(
             kernel,
             grid_spec=pltpu.PrefetchScalarGridSpec(
                 num_scalar_prefetch=1,
                 grid=(count,),
                 in_specs=[pl.BlockSpec(memory_space=pl.ANY) for _ in tokens_in],
-                out_specs=[pl.BlockSpec((1, *block), lambda i, at: (i, 0, 0))]
-                + [pl.BlockSpec(m, lambda i, at: (0, 0, 0)) for m in more],
+                out_specs=pl.BlockSpec((1, *block), lambda i, at: (i, 0, 0)),
                 scratch_shapes=[
                     pltpu.VMEM((2 * here, pick.shape[1]), bf16),
                     pltpu.VMEM((2 * here, TILE), bf16),
                     pltpu.SemaphoreType.DMA((4,)),
                 ],
             ),
-            out_shape=[jax.ShapeDtypeStruct(m, bf16) for m in [(count, *block)] + more],
+            out_shape=jax.ShapeDtypeStruct((count, *block), bf16),
             compiler_params=PARAMS,
         )(table, *tokens_in)
 
-    (part,) = slots(functools.partial(factor_kernel, out_blocks), 9, (PIECE, PIECE + 128))
-    keep, *give = slots(cross_kernel, 8, (128, TILE), GIVE_SLOTS)
-
-    def y_send(i):
-        return give[i], YH, SWAP2
+    part = slots(functools.partial(factor_kernel, out_blocks), 9, (PIECE, PIECE + 128))
+    keep = slots(cross_kernel, 8, (PIECE, TILE))
 
     def ring(value, *args):
         return value, (Z, CORE), ring_pairs(*args)
@@ -306,9 +288,9 @@
         return in_order(core, got, nothing)
 
     (far,) = phase(ring(part[0]))
-    far, y0 = phase(ring(added(part[1:3], widened(far)).astype(bf16)), y_send(0))
-    far, y1 = phase(ring(added(part[3:5], far).astype(bf16)), y_send(1))
-    far, y2 = phase(ring(added(part[5:7], far).astype(bf16)), y_send(2))
+    (far,) = phase(ring(added(part[1:3], widened(far)).astype(bf16)))
+    (far,) = phase(ring(added(part[3:5], far).astype(bf16)))
+    (far,) = phase(ring(added(part[5:7], far).astype(bf16)))
     both_in = jnp.concatenate([far[0, :, PIECE:], far[1, :, PIECE:]], 1)
     out_own = jnp.where(core == 0, far[0, :, :PIECE], far[1, :, :PIECE])
     out_other = jnp.where(core == 0, far[1, :, :PIECE], far[0, :, :PIECE])
@@ -316,26 +298,25 @@
     here_in = in_order(core, part[7, :, PIECE:], part[8, :, PIECE:])
     local = jnp.concatenate([part[7, :, :PIECE], here_in[0], here_in[1]], 1)
     tiles = (added(jnp.concatenate([out_own, both_in], 1), other) + local.astype(f32)).astype(bf16)
-    other, far = phase((tiles, YH, SWAP2), ring(added(keep[0], y0[0]).astype(bf16), 4, True))
+    other, far = phase((tiles, YH, SWAP2), ring(keep[0], 4, True))
     tiles = added(tiles, other).astype(bf16)
     out_tile, in_tile = tiles[:, :PIECE], tiles[:, PIECE:]
     copies = jnp.broadcast_to(out_tile[None], (8, PIECE, PIECE))
+    in_tile, copies = lax.optimization_barrier((in_tile, copies))
+    near_in, far = phase(
+        (in_tile, X, SWAP_X),
+        ring(added(keep[1:3], widened(far)).astype(bf16), 3, True),
+    )
     out_tiles = lax.all_to_all(copies, OWNER, 0, 0, tiled=True)
-    near_in, far, y34 = phase(
-        (in_tile, X, SWAP_X),
-        ring(added(keep[1:3], jnp.concatenate([y1, y2]), widened(far)).astype(bf16), 3, True),
-        y_send(3),
-    )
+    near_in, far, out_tiles = lax.optimization_barrier((near_in, far, out_tiles))
     shard = in_order(h, in_tile, near_in)
     (one,) = phase(ring(shard))
     (two,) = phase(ring(one))
     (three,) = phase(ring(two))
     (last,) = phase(ring(jnp.where(core == 0, three[:1], three[1:])))
     in_own = jnp.concatenate([one, two, three, last], 0)
-    cross, in_other, y56 = phase(
-        ring(added(keep[3:5], y34, far).astype(bf16), 2, True),
-        (in_own, CORE, SWAP2),
-        y_send(4),
+    cross, in_other = phase(
+        ring(added(keep[3:5], far).astype(bf16), 2, True), (in_own, CORE, SWAP2)
     )
     square = (TILE, TILE)
     in_inverse = call(
@@ -349,14 +330,15 @@
         in_other,
         scratch=[(square, bf16), (square, f32), (square, bf16)],
     )
-    cross, out_other, y7 = phase(
-        ring(added(keep[5:7], y56, cross).astype(bf16), 1, True),
-        (out_tiles, CORE, SWAP2),
-        y_send(5),
+    cross, out_other = phase(
+        ring(added(keep[5:7], cross).astype(bf16), 1, True), (out_tiles, CORE, SWAP2)
     )
     cross, in_inverse = lax.optimization_barrier((cross, in_inverse))
     (other,) = phase((jnp.where(core == 0, cross[1], cross[0]), CORE, SWAP2))
-    cross = added(jnp.where(core == 0, cross[0], cross[1]), other, keep[7], y7[0]).astype(bf16)
+    cross = added(jnp.where(core == 0, cross[0], cross[1]), other, keep[7])
+    give = lax.dynamic_slice_in_dim(cross, (1 - yh) * 128, 128, 0).astype(bf16)
+    (other,) = phase((give, YH, SWAP2))
+    cross = added(lax.dynamic_slice_in_dim(cross, yh * 128, 128, 0), other).astype(bf16)
     m = z % 4
     row = 2 * yh + core
     slice_rows = out_width // lax.axis_size(DP)

time: 226 us -> 232 us (1.027)
  waiting for transfers between devices: 87.6 us -> 92.5 us
  starting transfers between devices: 61.6 us -> 65.3 us
  blocking collectives: 16.2 us -> 13.4 us
  other arithmetic: 14.6 us -> 17.3 us
    ppermute x27 -> x22, waiting for transfers between devices: 82.5 us -> 87.6 us  [phase(): got = [lax.ppermute(value, *send[1:]) for value, send in zip(values, sends)]]
    ppermute x27 -> x22, starting transfers between devices: 49 us -> 52.9 us  [phase(): got = [lax.ppermute(value, *send[1:]) for value, send in zip(values, sends)]]
    unnamed x26 -> x18, local copies, waits for them, and re-layouts: 8.37 us -> 4.75 us
    all_to_all x1, blocking collectives: 16.2 us -> 13.4 us  [all_sum(): lax.all_to_all(jnp.full((n, 128), value, f32), axis, 0, 0, tiled=True)]
    add x0 -> x1, other arithmetic: none -> 2.83 us  [added(): return functools.reduce(jnp.add, [p.astype(f32) for p in parts])]
    convert_element_type x7 -> x6, other arithmetic: 7.2 us -> 5.16 us  [the longest x1 1.62 us: shards(): added(keep[1:3], widened(far)).astype(bf16)]
  transfers between devices with their start and end apart: 34 -> 29, of which waited for: 18 -> 18; matrix products, arithmetic and copies ran while one was open for 5% -> 3% of each run, Pallas kernels for 9% -> 9%
where the time goes in v3:
time: 232 us; the launch traced here: 228 us
  waiting for transfers between devices  92.5 us (40%)
  starting transfers between devices  65.3 us (28%)
  Pallas kernels  23.7 us (10%)
  other arithmetic  17.3 us (7%)
  blocking collectives  13.4 us (6%)
  local copies, waits for them, and re-layouts  11.5 us (5%)
  matrix products  2.9 us (1%)
    ppermute x22, waiting for transfers between devices, phase(): got = [lax.ppermute(value, *send[1:]) for value, send in zip(values, sends)]  87.6 us
    ppermute x22, starting transfers between devices, phase(): got = [lax.ppermute(value, *send[1:]) for value, send in zip(values, sends)]  52.9 us
    pallas_call x3, Pallas kernels, call(): pl.pallas_call(kernel, grid_spec=pltpu.PrefetchScalarGridSpec(num_scalar_...  14.1 us
    all_to_all x1, blocking collectives, all_sum(): lax.all_to_all(jnp.full((n, 128), value, f32), axis, 0, 0, tiled=True)  13.4 us
    pallas_call x2, Pallas kernels, slots(): pl.pallas_call(kernel, grid_spec=pltpu.PrefetchScalarGridSpec(num_scalar_...  9.65 us
    all_to_all x1, starting transfers between devices, shards(): out_tiles = lax.all_to_all(copies, OWNER, 0, 0, tiled=True)  5.03 us
    unnamed x18, local copies, waits for them, and re-layouts  4.75 us
    all_to_all x1, starting transfers between devices, all_sum(): lax.all_to_all(jnp.full((n, 128), value, f32), axis, 0, 0, tiled=True)  4.65 us
  transfers between devices with their start and end apart: 29, of which 18 were waited for; matrix products, arithmetic and copies ran while one was open for 3% of the time, Pallas kernels for 9%

profile of v3, /device:TPU:16, one launch (start us, length us, event | category | flops | bytes accessed | tf_op | source)
XLA Modules:
  0.0 227.8 jit_solution(7342508372411413619)
XLA Ops:
  8.5 3.7 %shard_map.38 = bf16[9,256,384]{2,1,0:T(8,128)(2,1)S(1)} custom-call(s32[28]{0:T(128)S(1)} %stack.150.at_ref, bf16[128,4608]{1,0:T(8,128)(2,1)S(1)} %shard_map.37.pick_ref, bf16[128,4608]{1,0:T(8,128)(2,1)S(1)} %copy-done.1, bf16[128,1024]{1,0:T(8,128)(2,1)S(1)} %multiply_convert_fusion.own_ref, bf16[128,1024]{1,0:T(8,128)(2,1)S(1)} %collective-permute-done.1.got_ref), custom_call_target="tpu_custom_call" | custom-call | tf_op jit(solution)/shard_map/pallas_call | solution.py:263
  12.8 5.9 %collective-permute-start.2 = (bf16[256,384]{1,0:T(8,128)(2,1)}, bf16[256,384]{1,0:T(8,128)(2,1)}, u32[]{:S(2)}, u32[]{:S(2)}) collective-permute-start(bf16[256,384]{1,0:T(8,128)(2,1)} %slice_bitcast_fusion.2), channel_id=1, source_target_pairs={{0,224},{8,40},{32,0},{40,72},{64,32},{72,104},{96,64},{104,136},{... | collective-permute-start | bytes 589832 | tf_op jit(solution)/shard_map/ppermute | solution.py:204
  18.7 3.5 %collective-permute-done.2 = bf16[256,384]{1,0:T(8,128)(2,1)} collective-permute-done((bf16[256,384]{1,0:T(8,128)(2,1)}, bf16[256,384]{1,0:T(8,128)(2,1)}, u32[]{:S(2)}, u32[]{:S(2)}) %collective-permute-start.2) | collective-permute-done | bytes 196640 | tf_op jit(solution)/shard_map/ppermute | solution.py:204
  23.3 3.8 %collective-permute-start.3 = (bf16[2,256,384]{2,1,0:T(8,128)(2,1)S(1)}, bf16[2,256,384]{2,1,0:T(8,128)(2,1)S(1)}, u32[]{:S(2)}, u32[]{:S(2)}) collective-permute-start(bf16[2,256,384]{2,1,0:T(8,128)(2,1)S(1)} %add_convert_fusion.5), channel_id=1, source_target_pairs={{0,224},{8,40},{32,0},{40,72},{64,32},{72,104},{96,64},{104,136},{... | collective-permute-start | bytes 1179656 | tf_op jit(solution)/shard_map/ppermute | solution.py:204
  27.0 5.3 %collective-permute-done.3 = bf16[2,256,384]{2,1,0:T(8,128)(2,1)S(1)} collective-permute-done((bf16[2,256,384]{2,1,0:T(8,128)(2,1)S(1)}, bf16[2,256,384]{2,1,0:T(8,128)(2,1)S(1)}, u32[]{:S(2)}, u32[]{:S(2)}) %collective-permute-start.3) | collective-permute-done | bytes 393248 | tf_op jit(solution)/shard_map/ppermute | solution.py:204
  32.4 3.8 %collective-permute-start.4 = (bf16[2,256,384]{2,1,0:T(8,128)(2,1)S(1)}, bf16[2,256,384]{2,1,0:T(8,128)(2,1)S(1)}, u32[]{:S(2)}, u32[]{:S(2)}) collective-permute-start(bf16[2,256,384]{2,1,0:T(8,128)(2,1)S(1)} %add_convert_fusion.4), channel_id=1, source_target_pairs={{0,224},{8,40},{32,0},{40,72},{64,32},{72,104},{96,64},{104,136},{... | collective-permute-start | bytes 1179656 | tf_op jit(solution)/shard_map/ppermute | solution.py:204
  36.2 5.3 %collective-permute-done.4 = bf16[2,256,384]{2,1,0:T(8,128)(2,1)S(1)} collective-permute-done((bf16[2,256,384]{2,1,0:T(8,128)(2,1)S(1)}, bf16[2,256,384]{2,1,0:T(8,128)(2,1)S(1)}, u32[]{:S(2)}, u32[]{:S(2)}) %collective-permute-start.4) | collective-permute-done | bytes 393248 | tf_op jit(solution)/shard_map/ppermute | solution.py:204
  41.6 3.8 %collective-permute-start.5 = (bf16[2,256,384]{2,1,0:T(8,128)(2,1)S(1)}, bf16[2,256,384]{2,1,0:T(8,128)(2,1)S(1)}, u32[]{:S(2)}, u32[]{:S(2)}) collective-permute-start(bf16[2,256,384]{2,1,0:T(8,128)(2,1)S(1)} %add_convert_fusion.3), channel_id=1, source_target_pairs={{0,224},{8,40},{32,0},{40,72},{64,32},{72,104},{96,64},{104,136},{... | collective-permute-start | bytes 1179656 | tf_op jit(solution)/shard_map/ppermute | solution.py:204
  45.4 5.3 %collective-permute-done.5 = bf16[2,256,384]{2,1,0:T(8,128)(2,1)S(1)} collective-permute-done((bf16[2,256,384]{2,1,0:T(8,128)(2,1)S(1)}, bf16[2,256,384]{2,1,0:T(8,128)(2,1)S(1)}, u32[]{:S(2)}, u32[]{:S(2)}) %collective-permute-start.5) | collective-permute-done | bytes 393248 | tf_op jit(solution)/shard_map/ppermute | solution.py:204
  50.9 6.0 %shard_map.39 = bf16[8,256,1024]{2,1,0:T(8,128)(2,1)} custom-call(s32[28]{0:T(128)S(1)} %stack.150.at_ref, bf16[128,4608]{1,0:T(8,128)(2,1)S(1)} %shard_map.37.pick_ref, bf16[128,4608]{1,0:T(8,128)(2,1)S(1)} %copy-done.2, bf16[128,1024]{1,0:T(8,128)(2,1)S(1)} %multiply_convert_fusion.own_ref, bf16[128,1024]{1,0:T(8,128)(2,1)S(1)} %collective-permute-done.1.got_ref), custom_call_target="tpu_custom_call" | custom-call | tf_op jit(solution)/shard_map/pallas_call | solution.py:263
  58.1 5.6 %collective-permute-start.8 = (bf16[256,1024]{1,0:T(8,128)(2,1)S(1)}, bf16[256,1024]{1,0:T(8,128)(2,1)S(1)}, u32[]{:S(2)}, u32[]{:S(2)}) collective-permute-start(bf16[256,1024]{1,0:T(8,128)(2,1)S(1)} %slice_bitcast_fusion.1), channel_id=1, source_target_pairs={{0,224},{8,40},{32,0},{40,72},{96,64},{104,136},{128,96},{136,168}... | collective-permute-start | bytes 1572872 | tf_op jit(solution)/shard_map/ppermute | solution.py:204
  64.1 7.5 %collective-permute-done.7 = bf16[256,512]{1,0:T(8,128)(2,1)S(1)} collective-permute-done((bf16[256,512]{1,0:T(8,128)(2,1)S(1)}, bf16[256,512]{1,0:T(8,128)(2,1)S(1)}, u32[]{:S(2)}, u32[]{:S(2)}) %collective-permute-start.7) | collective-permute-done | bytes 262176 | tf_op jit(solution)/shard_map/ppermute | solution.py:204
  74.5 4.4 %collective-permute-start.10 = (bf16[2,256,1024]{2,1,0:T(8,128)(2,1)S(1)}, bf16[2,256,1024]{2,1,0:T(8,128)(2,1)S(1)}, u32[]{:S(2)}, u32[]{:S(2)}) collective-permute-start(bf16[2,256,1024]{2,1,0:T(8,128)(2,1)S(1)} %add_convert_fusion.2), channel_id=1, source_target_pairs={{0,224},{8,40},{40,72},{64,32},{72,104},{96,64},{128,96},{136,168}... | collective-permute-start | bytes 3145736 | tf_op jit(solution)/shard_map/ppermute | solution.py:204
  78.9 5.0 %all-to-all-start = ((bf16[8,256,256]{2,1,0:T(8,128)(2,1)}), bf16[8,256,256]{2,1,0:T(8,128)(2,1)S(1)}, u32[]{:S(2)}, u32[]{:S(2)}) async-start(bf16[8,256,256]{2,1,0:T(8,128)(2,1)} %broadcast_in_dim.21), calls=%async_computation | async-start | bytes 2097152 | tf_op jit(solution)/shard_map/all_to_all | solution.py:310
  86.0 10.0 %collective-permute-done.9 = bf16[256,256]{1,0:T(8,128)(2,1)S(1)} collective-permute-done((bf16[256,256]{1,0:T(8,128)(2,1)S(1)}, bf16[256,256]{1,0:T(8,128)(2,1)S(1)}, u32[]{:S(2)}, u32[]{:S(2)}) %collective-permute-start.9) | collective-permute-done | bytes 131104 | tf_op jit(solution)/shard_map/ppermute | solution.py:204
  98.4 4.1 %collective-permute-done.11 = bf16[2,256,256]{2,1,0:T(8,128)(2,1)S(1)} collective-permute-done((bf16[2,256,256]{2,1,0:T(8,128)(2,1)S(1)}, bf16[2,256,256]{2,1,0:T(8,128)(2,1)S(1)}, u32[]{:S(2)}, u32[]{:S(2)}) %collective-permute-start.11) | collective-permute-done | bytes 262176 | tf_op jit(solution)/shard_map/ppermute | solution.py:204
  102.5 3.5 %collective-permute-start.12 = (bf16[2,256,256]{2,1,0:T(8,128)(2,1)S(1)}, bf16[2,256,256]{2,1,0:T(8,128)(2,1)S(1)}, u32[]{:S(2)}, u32[]{:S(2)}) collective-permute-start(bf16[2,256,256]{2,1,0:T(8,128)(2,1)S(1)} %collective-permute-done.11), channel_id=1, source_target_pairs={{0,224},{8,40},{32,0},{40,72},{64,32},{72,104},{96,64},{104,136},{... | collective-permute-start | bytes 786440 | tf_op jit(solution)/shard_map/ppermute | solution.py:204
  106.0 3.9 %collective-permute-done.12 = bf16[2,256,256]{2,1,0:T(8,128)(2,1)S(1)} collective-permute-done((bf16[2,256,256]{2,1,0:T(8,128)(2,1)S(1)}, bf16[2,256,256]{2,1,0:T(8,128)(2,1)S(1)}, u32[]{:S(2)}, u32[]{:S(2)}) %collective-permute-start.12) | collective-permute-done | bytes 262176 | tf_op jit(solution)/shard_map/ppermute | solution.py:204
  109.9 3.7 %collective-permute-start.13 = (bf16[2,256,256]{2,1,0:T(8,128)(2,1)S(1)}, bf16[2,256,256]{2,1,0:T(8,128)(2,1)S(1)}, u32[]{:S(2)}, u32[]{:S(2)}) collective-permute-start(bf16[2,256,256]{2,1,0:T(8,128)(2,1)S(1)} %collective-permute-done.12), channel_id=1, source_target_pairs={{0,224},{8,40},{32,0},{40,72},{64,32},{72,104},{96,64},{104,136},{... | collective-permute-start | bytes 786440 | tf_op jit(solution)/shard_map/ppermute | solution.py:204
  113.6 3.9 %collective-permute-done.13 = bf16[2,256,256]{2,1,0:T(8,128)(2,1)S(1)} collective-permute-done((bf16[2,256,256]{2,1,0:T(8,128)(2,1)S(1)}, bf16[2,256,256]{2,1,0:T(8,128)(2,1)S(1)}, u32[]{:S(2)}, u32[]{:S(2)}) %collective-permute-start.13) | collective-permute-done | bytes 262176 | tf_op jit(solution)/shard_map/ppermute | solution.py:204
  117.5 3.9 %collective-permute-start.14 = (bf16[1,256,256]{2,1,0:T(8,128)(2,1)S(1)}, bf16[1,256,256]{2,1,0:T(8,128)(2,1)S(1)}, u32[]{:S(2)}, u32[]{:S(2)}) collective-permute-start(bf16[1,256,256]{2,1,0:T(8,128)(2,1)S(1)} %slice_select_fusion), channel_id=1, source_target_pairs={{0,224},{8,40},{32,0},{40,72},{64,32},{72,104},{96,64},{104,136},{... | collective-permute-start | bytes 393224 | tf_op jit(solution)/shard_map/ppermute | solution.py:204
  127.9 12.8 %collective-permute-done.15 = bf16[2,256,1024]{2,1,0:T(8,128)(2,1)S(1)} collective-permute-done((bf16[2,256,1024]{2,1,0:T(8,128)(2,1)S(1)}, bf16[2,256,1024]{2,1,0:T(8,128)(2,1)S(1)}, u32[]{:S(2)}, u32[]{:S(2)}) %collective-permute-start.15) | collective-permute-done | bytes 1048608 | tf_op jit(solution)/shard_map/ppermute | solution.py:204
  145.0 8.5 %shard_map.41 = bf16[1024,1024]{1,0:T(8,128)(2,1)S(1)} custom-call(s32[2]{0:T(128)S(1)} %pad_add_fusion.2.at_ref, bf16[2,256,256]{2,1,0:T(8,128)(2,1)S(1)} %pad_maximum_fusion.6.shard_ref, bf16[7,256,256]{2,1,0:T(8,128)(2,1)S(1)} %pad_maximum_fusion.own_ref, bf16[7,256,256]{2,1,0:T(8,128)(2,1)S(1)} %collective-permute-done.16.other_ref), custom_call_target="tpu_custom_call" | custom-call | tf_op jit(solution)/shard_map/pallas_call | solution.py:179
  153.5 5.7 %collective-permute-done.17 = bf16[2,256,1024]{2,1,0:T(8,128)(2,1)} collective-permute-done((bf16[2,256,1024]{2,1,0:T(8,128)(2,1)S(1)}, bf16[2,256,1024]{2,1,0:T(8,128)(2,1)}, u32[]{:S(2)}, u32[]{:S(2)}) %collective-permute-start.17) | collective-permute-done | bytes 1048608 | tf_op jit(solution)/shard_map/ppermute | solution.py:204
  164.5 2.8 %convert_add_fusion = f32[256,1024]{1,0:T(8,128)} fusion(bf16[256,1024]{1,0:T(8,128)(2,1)} %collective-permute-done.19, bf16[8,256,1024]{2,1,0:T(8,128)(2,1)} %shard_map.39, pred[]{:T(512)S(6)} %eq.66, bf16[2,256,1024]{2,1,0:T(8,128)(2,1)} %collective-permute-done.17), kind=kLoop, calls=%fused_computation.6 | loop fusion | flops 1572864 | bytes 3145729 | tf_op jit(solution)/shard_map/add | solution.py:209
  169.1 9.3 %collective-permute-done.20 = bf16[128,1024]{1,0:T(8,128)(2,1)} collective-permute-done((bf16[128,1024]{1,0:T(8,128)(2,1)S(1)}, bf16[128,1024]{1,0:T(8,128)(2,1)}, u32[]{:S(2)}, u32[]{:S(2)}) %collective-permute-start.20) | collective-permute-done | bytes 262176 | tf_op jit(solution)/shard_map/ppermute | solution.py:204
  182.4 2.8 %collective-permute-start.23 = (bf16[128,512]{1,0:T(8,128)(2,1)S(1)}, bf16[128,512]{1,0:T(8,128)(2,1)S(1)}, u32[]{:S(2)}, u32[]{:S(2)}) collective-permute-start(bf16[128,512]{1,0:T(8,128)(2,1)S(1)} %get-tuple-element.59), channel_id=1, source_target_pairs={{0,17},{1,16},{2,19},{3,18},{16,1},{17,0},{18,3},{19,2},{4,21},{5,... | collective-permute-start | bytes 393224 | tf_op jit(solution)/shard_map/ppermute | solution.py:204
  185.2 5.3 %collective-permute-done.22 = bf16[128,512]{1,0:T(8,128)(2,1)S(1)} collective-permute-done((bf16[128,512]{1,0:T(8,128)(2,1)S(1)}, bf16[128,512]{1,0:T(8,128)(2,1)S(1)}, u32[]{:S(2)}, u32[]{:S(2)}) %collective-permute-start.22) | collective-permute-done | bytes 131104 | tf_op jit(solution)/shard_map/ppermute | solution.py:204
  191.6 4.9 %shard_map.40 = bf16[384,1024]{1,0:T(8,128)(2,1)S(1)} custom-call(s32[3]{0:T(128)S(1)} %pad_add_fusion.at_ref, bf16[8,256,256]{2,1,0:T(8,128)(2,1)S(1)} %all-to-all-done.own_ref, bf16[8,256,256]{2,1,0:T(8,128)(2,1)S(1)} %copy-done.5), custom_call_target="tpu_custom_call" | custom-call | tf_op jit(solution)/shard_map/pallas_call | solution.py:179
  200.4 4.6 %all-to-all-start.1 = ((f32[8,1,128]{2,1,0:T(1,128)}), f32[8,1,128]{2,1,0:T(1,128)S(1)}, u32[]{:S(2)}, u32[]{:S(2)}) async-start(f32[8,1,128]{2,1,0:T(1,128)} %broadcast_in_dim.23), calls=%async_computation.1 | async-start | bytes 8192 | tf_op jit(solution)/shard_map/all_to_all | solution.py:220
  207.2 3.9 %all-to-all-done.1 = f32[8,1,128]{2,1,0:T(1,128)S(1)} async-done(((f32[8,1,128]{2,1,0:T(1,128)}), f32[8,1,128]{2,1,0:T(1,128)S(1)}, u32[]{:S(2)}, u32[]{:S(2)}) %all-to-all-start.1) | async-done | bytes 4128 | tf_op jit(solution)/shard_map/all_to_all | solution.py:220
  212.3 13.4 %all_to_all.23 = f32[32,1,128]{2,1,0:T(1,128)S(1)} all-to-all(f32[32,1,128]{2,1,0:T(1,128)S(1)} %broadcast_in_dim.24), channel_id=1, replica_groups=mesh['dp_0'=8,'dp_1'=2,'dp_2'=2,'owner_0'=2,'owner_1'=4] {'dp_0','dp_1',..., dimensions={0} | all-to-all | bytes 32768 | tf_op jit(solution)/shard_map/all_to_all | solution.py:220
  (99 shorter events, 50.9 us)
Async XLA Ops:
  2.2 3.9 %collective-permute-start = (bf16[128,4608]{1,0:T(8,128)(2,1)S(1)}, bf16[128,4608]{1,0:T(8,128)(2,1)S(1)}, u32[]{:S(2)}, u32[]{:S(2)}) collective-permute-start(bf16[128,4608]{1,0:T(8,128)(2,1)S(1)} %shard_map.37.pick_ref), channel_id=1, source_target_pairs={{0,8},{8,0},{1,9},{9,1},{2,10},{10,2},{3,11},{11,3},{4,12},{12,4},... | collective-permute-start | bytes 3538952 | tf_op jit(solution)/shard_map/ppermute | solution.py:244
  4.4 1.7 collective-permute-start.1
  12.8 9.4 %collective-permute-start.2 = (bf16[256,384]{1,0:T(8,128)(2,1)}, bf16[256,384]{1,0:T(8,128)(2,1)}, u32[]{:S(2)}, u32[]{:S(2)}) collective-permute-start(bf16[256,384]{1,0:T(8,128)(2,1)} %slice_bitcast_fusion.2), channel_id=1, source_target_pairs={{0,224},{8,40},{32,0},{40,72},{64,32},{72,104},{96,64},{104,136},{... | collective-permute-start | bytes 589832 | tf_op jit(solution)/shard_map/ppermute | solution.py:204
  23.3 27.6 %copy-start.2 = (bf16[128,4608]{1,0:T(8,128)(2,1)S(1)}, bf16[128,4608]{1,0:T(8,128)(2,1)}, u32[]{:S(2)}) copy-start(bf16[128,4608]{1,0:T(8,128)(2,1)} %copy-done) | copy-start | bytes 3538948
  23.3 9.1 %collective-permute-start.3 = (bf16[2,256,384]{2,1,0:T(8,128)(2,1)S(1)}, bf16[2,256,384]{2,1,0:T(8,128)(2,1)S(1)}, u32[]{:S(2)}, u32[]{:S(2)}) collective-permute-start(bf16[2,256,384]{2,1,0:T(8,128)(2,1)S(1)} %add_convert_fusion.5), channel_id=1, source_target_pairs={{0,224},{8,40},{32,0},{40,72},{64,32},{72,104},{96,64},{104,136},{... | collective-permute-start | bytes 1179656 | tf_op jit(solution)/shard_map/ppermute | solution.py:204
  32.4 9.1 %collective-permute-start.4 = (bf16[2,256,384]{2,1,0:T(8,128)(2,1)S(1)}, bf16[2,256,384]{2,1,0:T(8,128)(2,1)S(1)}, u32[]{:S(2)}, u32[]{:S(2)}) collective-permute-start(bf16[2,256,384]{2,1,0:T(8,128)(2,1)S(1)} %add_convert_fusion.4), channel_id=1, source_target_pairs={{0,224},{8,40},{32,0},{40,72},{64,32},{72,104},{96,64},{104,136},{... | collective-permute-start | bytes 1179656 | tf_op jit(solution)/shard_map/ppermute | solution.py:204
  41.6 9.1 %collective-permute-start.5 = (bf16[2,256,384]{2,1,0:T(8,128)(2,1)S(1)}, bf16[2,256,384]{2,1,0:T(8,128)(2,1)S(1)}, u32[]{:S(2)}, u32[]{:S(2)}) collective-permute-start(bf16[2,256,384]{2,1,0:T(8,128)(2,1)S(1)} %add_convert_fusion.3), channel_id=1, source_target_pairs={{0,224},{8,40},{32,0},{40,72},{64,32},{72,104},{96,64},{104,136},{... | collective-permute-start | bytes 1179656 | tf_op jit(solution)/shard_map/ppermute | solution.py:204
  50.7 7.2 %collective-permute-start.6 = (bf16[256,512]{1,0:T(8,128)(2,1)S(1)}, bf16[256,512]{1,0:T(8,128)(2,1)S(1)}, u32[]{:S(2)}, u32[]{:S(2)}) collective-permute-start(bf16[256,512]{1,0:T(8,128)(2,1)S(1)} %pad_maximum_fusion.2), channel_id=1, source_target_pairs={{0,8},{8,0},{1,9},{9,1},{2,10},{10,2},{3,11},{11,3},{4,12},{12,4},... | collective-permute-start | bytes 786440 | tf_op jit(solution)/shard_map/ppermute | solution.py:204
  58.1 13.6 %collective-permute-start.8 = (bf16[256,1024]{1,0:T(8,128)(2,1)S(1)}, bf16[256,1024]{1,0:T(8,128)(2,1)S(1)}, u32[]{:S(2)}, u32[]{:S(2)}) collective-permute-start(bf16[256,1024]{1,0:T(8,128)(2,1)S(1)} %slice_bitcast_fusion.1), channel_id=1, source_target_pairs={{0,224},{8,40},{32,0},{40,72},{96,64},{104,136},{128,96},{136,168}... | collective-permute-start | bytes 1572872 | tf_op jit(solution)/shard_map/ppermute | solution.py:204
  63.7 8.0 %collective-permute-start.7 = (bf16[256,512]{1,0:T(8,128)(2,1)S(1)}, bf16[256,512]{1,0:T(8,128)(2,1)S(1)}, u32[]{:S(2)}, u32[]{:S(2)}) collective-permute-start(bf16[256,512]{1,0:T(8,128)(2,1)S(1)} %add_convert_fusion.8), channel_id=1, source_target_pairs={{0,16},{16,0},{1,17},{17,1},{2,18},{18,2},{3,19},{19,3},{4,20},{20... | collective-permute-start | bytes 786440 | tf_op jit(solution)/shard_map/ppermute | solution.py:204
  74.5 21.4 %collective-permute-start.10 = (bf16[2,256,1024]{2,1,0:T(8,128)(2,1)S(1)}, bf16[2,256,1024]{2,1,0:T(8,128)(2,1)S(1)}, u32[]{:S(2)}, u32[]{:S(2)}) collective-permute-start(bf16[2,256,1024]{2,1,0:T(8,128)(2,1)S(1)} %add_convert_fusion.2), channel_id=1, source_target_pairs={{0,224},{8,40},{40,72},{64,32},{72,104},{96,64},{128,96},{136,168}... | collective-permute-start | bytes 3145736 | tf_op jit(solution)/shard_map/ppermute | solution.py:204
  78.9 17.1 %all-to-all-start = ((bf16[8,256,256]{2,1,0:T(8,128)(2,1)}), bf16[8,256,256]{2,1,0:T(8,128)(2,1)S(1)}, u32[]{:S(2)}, u32[]{:S(2)}) async-start(bf16[8,256,256]{2,1,0:T(8,128)(2,1)} %broadcast_in_dim.21), calls=%async_computation | async-start | bytes 2097152 | tf_op jit(solution)/shard_map/all_to_all | solution.py:310
  84.0 12.0 %collective-permute-start.9 = (bf16[256,256]{1,0:T(8,128)(2,1)S(1)}, bf16[256,256]{1,0:T(8,128)(2,1)S(1)}, u32[]{:S(2)}, u32[]{:S(2)}) collective-permute-start(bf16[256,256]{1,0:T(8,128)(2,1)S(1)} %get-tuple-element.39), channel_id=1, source_target_pairs={{0,1},{1,0},{2,3},{3,2},{4,5},{5,4},{6,7},{7,6},{8,9},{9,8},{10,11... | collective-permute-start | bytes 393224 | tf_op jit(solution)/shard_map/ppermute | solution.py:204
  96.1 6.4 %collective-permute-start.11 = (bf16[2,256,256]{2,1,0:T(8,128)(2,1)S(1)}, bf16[2,256,256]{2,1,0:T(8,128)(2,1)S(1)}, u32[]{:S(2)}, u32[]{:S(2)}) collective-permute-start(bf16[2,256,256]{2,1,0:T(8,128)(2,1)S(1)} %pad_maximum_fusion.6.shard_ref), channel_id=1, source_target_pairs={{0,224},{8,40},{32,0},{40,72},{64,32},{72,104},{96,64},{104,136},{... | collective-permute-start | bytes 786440 | tf_op jit(solution)/shard_map/ppermute | solution.py:204
  102.5 7.4 %collective-permute-start.12 = (bf16[2,256,256]{2,1,0:T(8,128)(2,1)S(1)}, bf16[2,256,256]{2,1,0:T(8,128)(2,1)S(1)}, u32[]{:S(2)}, u32[]{:S(2)}) collective-permute-start(bf16[2,256,256]{2,1,0:T(8,128)(2,1)S(1)} %collective-permute-done.11), channel_id=1, source_target_pairs={{0,224},{8,40},{32,0},{40,72},{64,32},{72,104},{96,64},{104,136},{... | collective-permute-start | bytes 786440 | tf_op jit(solution)/shard_map/ppermute | solution.py:204
  109.9 7.6 %collective-permute-start.13 = (bf16[2,256,256]{2,1,0:T(8,128)(2,1)S(1)}, bf16[2,256,256]{2,1,0:T(8,128)(2,1)S(1)}, u32[]{:S(2)}, u32[]{:S(2)}) collective-permute-start(bf16[2,256,256]{2,1,0:T(8,128)(2,1)S(1)} %collective-permute-done.12), channel_id=1, source_target_pairs={{0,224},{8,40},{32,0},{40,72},{64,32},{72,104},{96,64},{104,136},{... | collective-permute-start | bytes 786440 | tf_op jit(solution)/shard_map/ppermute | solution.py:204
  117.5 6.5 %collective-permute-start.14 = (bf16[1,256,256]{2,1,0:T(8,128)(2,1)S(1)}, bf16[1,256,256]{2,1,0:T(8,128)(2,1)S(1)}, u32[]{:S(2)}, u32[]{:S(2)}) collective-permute-start(bf16[1,256,256]{2,1,0:T(8,128)(2,1)S(1)} %slice_select_fusion), channel_id=1, source_target_pairs={{0,224},{8,40},{32,0},{40,72},{64,32},{72,104},{96,64},{104,136},{... | collective-permute-start | bytes 393224 | tf_op jit(solution)/shard_map/ppermute | solution.py:204
  124.1 16.7 %collective-permute-start.15 = (bf16[2,256,1024]{2,1,0:T(8,128)(2,1)S(1)}, bf16[2,256,1024]{2,1,0:T(8,128)(2,1)S(1)}, u32[]{:S(2)}, u32[]{:S(2)}) collective-permute-start(bf16[2,256,1024]{2,1,0:T(8,128)(2,1)S(1)} %add_convert_fusion.1), channel_id=1, source_target_pairs={{32,0},{40,72},{64,32},{72,104},{96,64},{104,136},{160,128},{168,2... | collective-permute-start | bytes 3145736 | tf_op jit(solution)/shard_map/ppermute | solution.py:204
  125.4 2.6 %collective-permute-start.16 = (bf16[7,256,256]{2,1,0:T(8,128)(2,1)S(1)}, bf16[7,256,256]{2,1,0:T(8,128)(2,1)S(1)}, u32[]{:S(2)}, u32[]{:S(2)}) collective-permute-start(bf16[7,256,256]{2,1,0:T(8,128)(2,1)S(1)} %pad_maximum_fusion.own_ref), channel_id=1, source_target_pairs={{0,8},{8,0},{1,9},{9,1},{2,10},{10,2},{3,11},{11,3},{4,12},{12,4},... | collective-permute-start | bytes 2752520 | tf_op jit(solution)/shard_map/ppermute | solution.py:204
  142.4 16.8 %collective-permute-start.17 = (bf16[2,256,1024]{2,1,0:T(8,128)(2,1)S(1)}, bf16[2,256,1024]{2,1,0:T(8,128)(2,1)}, u32[]{:S(2)}, u32[]{:S(2)}) collective-permute-start(bf16[2,256,1024]{2,1,0:T(8,128)(2,1)S(1)} %add_convert_fusion), channel_id=1, source_target_pairs={{0,224},{8,40},{32,0},{64,32},{72,104},{104,136},{128,96},{136,168... | collective-permute-start | bytes 3145736 | tf_op jit(solution)/shard_map/ppermute | solution.py:204
  144.9 14.3 %collective-permute-start.18 = (bf16[8,256,256]{2,1,0:T(8,128)(2,1)S(1)}, bf16[8,256,256]{2,1,0:T(8,128)(2,1)S(1)}, u32[]{:S(2)}, u32[]{:S(2)}) collective-permute-start(bf16[8,256,256]{2,1,0:T(8,128)(2,1)S(1)} %all-to-all-done.own_ref), channel_id=1, source_target_pairs={{0,8},{8,0},{1,9},{9,1},{2,10},{10,2},{3,11},{11,3},{4,12},{12,4},... | collective-permute-start | bytes 3145736 | tf_op jit(solution)/shard_map/ppermute | solution.py:204
  162.3 2.3 collective-permute-start.19
  168.4 10.0 %collective-permute-start.20 = (bf16[128,1024]{1,0:T(8,128)(2,1)S(1)}, bf16[128,1024]{1,0:T(8,128)(2,1)}, u32[]{:S(2)}, u32[]{:S(2)}) collective-permute-start(bf16[128,1024]{1,0:T(8,128)(2,1)S(1)} %dynamic-slice_convert_fusion), channel_id=1, source_target_pairs={{0,16},{16,0},{1,17},{17,1},{2,18},{18,2},{3,19},{19,3},{4,20},{20... | collective-permute-start | bytes 786440 | tf_op jit(solution)/shard_map/ppermute | solution.py:204
  180.0 11.5 %copy-start.5 = (bf16[8,256,256]{2,1,0:T(8,128)(2,1)S(1)}, bf16[8,256,256]{2,1,0:T(8,128)(2,1)}, u32[]{:S(2)}) copy-start(bf16[8,256,256]{2,1,0:T(8,128)(2,1)} %copy-done.4) | copy-start | bytes 3145732
  180.1 5.1 %collective-permute-start.21 = (bf16[128,512]{1,0:T(8,128)(2,1)S(1)}, bf16[128,512]{1,0:T(8,128)(2,1)S(1)}, u32[]{:S(2)}, u32[]{:S(2)}) collective-permute-start(bf16[128,512]{1,0:T(8,128)(2,1)S(1)} %get-tuple-element.59), channel_id=1, source_target_pairs={{0,1},{1,0},{2,3},{3,2},{4,5},{5,4},{6,7},{7,6},{8,9},{9,8},{10,11... | collective-permute-start | bytes 393224 | tf_op jit(solution)/shard_map/ppermute | solution.py:204
  181.7 8.7 %collective-permute-start.22 = (bf16[128,512]{1,0:T(8,128)(2,1)S(1)}, bf16[128,512]{1,0:T(8,128)(2,1)S(1)}, u32[]{:S(2)}, u32[]{:S(2)}) collective-permute-start(bf16[128,512]{1,0:T(8,128)(2,1)S(1)} %get-tuple-element.58), channel_id=1, source_target_pairs={{0,16},{16,0},{1,17},{17,1},{2,18},{18,2},{3,19},{19,3},{4,20},{20... | collective-permute-start | bytes 393224 | tf_op jit(solution)/shard_map/ppermute | solution.py:204
  182.4 8.1 %collective-permute-start.23 = (bf16[128,512]{1,0:T(8,128)(2,1)S(1)}, bf16[128,512]{1,0:T(8,128)(2,1)S(1)}, u32[]{:S(2)}, u32[]{:S(2)}) collective-permute-start(bf16[128,512]{1,0:T(8,128)(2,1)S(1)} %get-tuple-element.59), channel_id=1, source_target_pairs={{0,17},{1,16},{2,19},{3,18},{16,1},{17,0},{18,3},{19,2},{4,21},{5,... | collective-permute-start | bytes 393224 | tf_op jit(solution)/shard_map/ppermute | solution.py:204
  191.5 5.0 %collective-permute-start.24 = (bf16[2,2,128,512]{3,2,1,0:T(8,128)(2,1)}, bf16[2,2,128,512]{3,2,1,0:T(8,128)(2,1)}, u32[]{:S(2)}, u32[]{:S(2)}) collective-permute-start(bf16[2,2,128,512]{3,2,1,0:T(8,128)(2,1)} %pad_maximum_fusion.1), channel_id=1, source_target_pairs={{0,8},{8,0},{1,9},{9,1},{2,10},{10,2},{3,11},{11,3},{4,12},{12,4},... | collective-permute-start | bytes 1572872 | tf_op jit(solution)/shard_map/ppermute | solution.py:368
  191.6 4.9 %copy-start.7 = (bf16[1,2,128,512]{3,2,1,0:T(8,128)(2,1)S(1)}, bf16[1,2,128,512]{3,2,1,0:T(8,128)(2,1)}, u32[]{:S(2)}) copy-start(bf16[1,2,128,512]{3,2,1,0:T(8,128)(2,1)} %copy-done.6) | copy-start | bytes 786436
  200.4 10.7 %all-to-all-start.1 = ((f32[8,1,128]{2,1,0:T(1,128)}), f32[8,1,128]{2,1,0:T(1,128)S(1)}, u32[]{:S(2)}, u32[]{:S(2)}) async-start(f32[8,1,128]{2,1,0:T(1,128)} %broadcast_in_dim.23), calls=%async_computation.1 | async-start | bytes 8192 | tf_op jit(solution)/shard_map/all_to_all | solution.py:220
  205.0 22.0 %collective-permute-start.26 = (bf16[192,512]{1,0:T(8,128)(2,1)S(1)}, bf16[192,512]{1,0:T(8,128)(2,1)S(1)}, u32[]{:S(2)}, u32[]{:S(2)}) collective-permute-start(bf16[192,512]{1,0:T(8,128)(2,1)S(1)} %slice.170), channel_id=1, source_target_pairs={{96,64},{224,192},{97,65},{225,193},{98,66},{226,194},{99,67},{227... | collective-permute-start | bytes 589832 | tf_op jit(solution)/shard_map/ppermute | solution.py:374
  205.7 21.3 %collective-permute-start.25 = (bf16[192,512]{1,0:T(8,128)(2,1)S(1)}, bf16[192,512]{1,0:T(8,128)(2,1)S(1)}, u32[]{:S(2)}, u32[]{:S(2)}) collective-permute-start(bf16[192,512]{1,0:T(8,128)(2,1)S(1)} %slice.170), channel_id=1, source_target_pairs={{0,32},{32,64},{128,160},{160,192},{1,33},{33,65},{129,161},{161,1... | collective-permute-start | bytes 589832 | tf_op jit(solution)/shard_map/ppermute | solution.py:373
  (6 other events, 7.2 us)

commit v4 on v3

--- a/solution.py
+++ b/solution.py
@@ -80,14 +80,14 @@
     part_ref[0, :, PIECE:] = tdot(rows, in_ref[:, aligned(plane * 128, 128)]).astype(bf16)
 
 
-def cross_kernel(at_ref, pick_ref, recv_ref, own_ref, got_ref, cross_ref, out_ref, in_ref, sems):
+def cross_kernel(base, at_ref, pick_ref, recv_ref, own_ref, got_ref, cross_ref, out_ref, in_ref, sems):
     i = pl.program_id(0)
 
     @pl.when(i == 0)
     def _():
         load_tokens(pick_ref, recv_ref, own_ref, got_ref, out_ref, in_ref, sems)
 
-    block, piece = at_ref[2 + 3 * i], at_ref[3 + 3 * i]
+    block, piece = at_ref[2 + 3 * (base + i)], at_ref[3 + 3 * (base + i)]
     rows = out_ref[:, aligned(block * HALF + piece * PIECE, PIECE)]
     cross_ref[0] = tdot(rows, in_ref[...]).astype(bf16)
 
@@ -154,7 +154,7 @@
     out_ref[...] = inverse_rows(first_ref[aligned(i * PIECE, PIECE), :], sums_ref, low_ref)
 
 
-def out_inverse_kernel(tokens, count, at_ref, own_ref, other_ref, out_ref, sums_ref, first_ref, low_ref):
+def out_inverse_kernel(tokens, at_ref, own_ref, other_ref, out_ref, sums_ref, first_ref, low_ref):
     i = pl.program_id(0)
 
     @pl.when(i == 0)
@@ -164,12 +164,17 @@
             here = slice(owner // 2 * PIECE, (owner // 2 + 1) * PIECE)
             for piece, ref in ((core, own_ref), (1 - core, other_ref)):
                 sums_ref[aligned((2 * (owner % 2) + piece) * PIECE, PIECE), here] = ref[owner]
-        first_ref[:count, :] = jnp.zeros((count, TILE), f32)
-        first_ref[count + TILE :, :] = jnp.zeros((count, TILE), f32)
-        split_factor(tokens, sums_ref, first_ref, low_ref, count)
-
-    rows = first_ref[pl.ds(pl.multiple_of(at_ref[1 + i], 64), count), :]
-    out_ref[...] = inverse_rows(rows, sums_ref, low_ref)
+        split_factor(tokens, sums_ref, first_ref, low_ref, 0)
+
+    outside = jnp.logical_or(i == 0, i == 5)
+
+    @pl.when(outside)
+    def _():
+        out_ref[...] = jnp.zeros_like(out_ref)
+
+    @pl.when(jnp.logical_not(outside))
+    def _():
+        out_ref[...] = inverse_rows(first_ref[aligned((i - 1) * PIECE, PIECE), :], sums_ref, low_ref)
 
 
 def call(kernel, steps, block, out_shape, at, *args, scratch=()):
@@ -188,6 +193,36 @@
         out_shape=jax.ShapeDtypeStruct(out_shape, bf16),
         compiler_params=PARAMS,
     )(at, *args)
+
+
+def join_kernel(at_ref, own_ref, other_ref, here_ref, give_ref, keep_ref):
+    total = added(own_ref[0], other_ref[0], here_ref[0]).astype(bf16)
+
+    @pl.when(pl.program_id(0) == 0)
+    def _():
+        give_ref[...] = total
+
+    @pl.when(pl.program_id(0) == 1)
+    def _():
+        keep_ref[...] = total
+
+
+def join(at, own, other, here):
+    block = (1, 128, TILE)
+    rows = (128, TILE)
+    piece = pl.BlockSpec(block, lambda i, at: (at[0], (1 - at[1]) ^ i, 0))
+    last = pl.BlockSpec(block, lambda i, at: (here.shape[0] - 1, (1 - at[1]) ^ i, 0))
+    return pl.pallas_call(
+        join_kernel,
+        grid_spec=pltpu.PrefetchScalarGridSpec(
+            num_scalar_prefetch=1,
+            grid=(2,),
+            in_specs=[piece, piece, last],
+            out_specs=[pl.BlockSpec(rows, lambda i, at: (0, 0))] * 2,
+        ),
+        out_shape=[jax.ShapeDtypeStruct(rows, bf16)] * 2,
+        compiler_params=PARAMS,
+    )(at, own, other, here)
 
 
 def ring_pairs(away=0, skip=False):
@@ -278,7 +313,8 @@
         )(table, *tokens_in)
 
     part = slots(functools.partial(factor_kernel, out_blocks), 9, (PIECE, PIECE + 128))
-    keep = slots(cross_kernel, 8, (PIECE, TILE))
+    first_cross = slots(functools.partial(cross_kernel, 0), 3, (PIECE, TILE))
+    last_cross = slots(functools.partial(cross_kernel, 3), 5, (PIECE, TILE))
 
     def ring(value, *args):
         return value, (Z, CORE), ring_pairs(*args)
@@ -289,8 +325,10 @@
 
     (far,) = phase(ring(part[0]))
     (far,) = phase(ring(added(part[1:3], widened(far)).astype(bf16)))
+    far, first_cross = lax.optimization_barrier((far, first_cross))
     (far,) = phase(ring(added(part[3:5], far).astype(bf16)))
     (far,) = phase(ring(added(part[5:7], far).astype(bf16)))
+    far, last_cross = lax.optimization_barrier((far, last_cross))
     both_in = jnp.concatenate([far[0, :, PIECE:], far[1, :, PIECE:]], 1)
     out_own = jnp.where(core == 0, far[0, :, :PIECE], far[1, :, :PIECE])
     out_other = jnp.where(core == 0, far[1, :, :PIECE], far[0, :, :PIECE])
@@ -298,25 +336,24 @@
     here_in = in_order(core, part[7, :, PIECE:], part[8, :, PIECE:])
     local = jnp.concatenate([part[7, :, :PIECE], here_in[0], here_in[1]], 1)
     tiles = (added(jnp.concatenate([out_own, both_in], 1), other) + local.astype(f32)).astype(bf16)
-    other, far = phase((tiles, YH, SWAP2), ring(keep[0], 4, True))
+    other, far = phase((tiles, YH, SWAP2), ring(first_cross[0], 4, True))
     tiles = added(tiles, other).astype(bf16)
     out_tile, in_tile = tiles[:, :PIECE], tiles[:, PIECE:]
     copies = jnp.broadcast_to(out_tile[None], (8, PIECE, PIECE))
-    in_tile, copies = lax.optimization_barrier((in_tile, copies))
-    near_in, far = phase(
-        (in_tile, X, SWAP_X),
-        ring(added(keep[1:3], widened(far)).astype(bf16), 3, True),
+    (near_in,) = phase((in_tile, X, SWAP_X))
+    shard = in_order(h, in_tile, near_in)
+    shard, copies = lax.optimization_barrier((shard, copies))
+    one, far = phase(
+        ring(shard), ring(added(first_cross[1:3], widened(far)).astype(bf16), 3, True)
     )
     out_tiles = lax.all_to_all(copies, OWNER, 0, 0, tiled=True)
-    near_in, far, out_tiles = lax.optimization_barrier((near_in, far, out_tiles))
-    shard = in_order(h, in_tile, near_in)
-    (one,) = phase(ring(shard))
+    one, far, out_tiles = lax.optimization_barrier((one, far, out_tiles))
     (two,) = phase(ring(one))
     (three,) = phase(ring(two))
     (last,) = phase(ring(jnp.where(core == 0, three[:1], three[1:])))
     in_own = jnp.concatenate([one, two, three, last], 0)
     cross, in_other = phase(
-        ring(added(keep[3:5], far).astype(bf16), 2, True), (in_own, CORE, SWAP2)
+        ring(added(last_cross[0:2], far).astype(bf16), 2, True), (in_own, CORE, SWAP2)
     )
     square = (TILE, TILE)
     in_inverse = call(
@@ -330,15 +367,12 @@
         in_other,
         scratch=[(square, bf16), (square, f32), (square, bf16)],
     )
-    cross, out_other = phase(
-        ring(added(keep[5:7], cross).astype(bf16), 1, True), (out_tiles, CORE, SWAP2)
-    )
+    (cross,) = phase(ring(added(last_cross[2:4], cross).astype(bf16), 1, True))
     cross, in_inverse = lax.optimization_barrier((cross, in_inverse))
-    (other,) = phase((jnp.where(core == 0, cross[1], cross[0]), CORE, SWAP2))
-    cross = added(jnp.where(core == 0, cross[0], cross[1]), other, keep[7])
-    give = lax.dynamic_slice_in_dim(cross, (1 - yh) * 128, 128, 0).astype(bf16)
-    (other,) = phase((give, YH, SWAP2))
-    cross = added(lax.dynamic_slice_in_dim(cross, yh * 128, 128, 0), other).astype(bf16)
+    (other,) = phase((cross, CORE, SWAP2))
+    give, keep = join(numbers(core, yh), cross, other, last_cross)
+    (other, out_other) = phase((give, YH, SWAP2), (out_tiles, CORE, SWAP2))
+    cross = added(keep, other).astype(bf16)
     m = z % 4
     row = 2 * yh + core
     slice_rows = out_width // lax.axis_size(DP)
@@ -346,18 +380,17 @@
     near = jnp.where(m == 3, 2, m + 1)
     own_at = jnp.where(m == 2, TILE, slice_rows * (4 * m + row) - base)
     near_at = jnp.where(m == 2, TILE, slice_rows * (4 * near + row) - base)
-    own_at, near_at = [jnp.clip(a, -slice_rows, TILE) + slice_rows for a in (own_at, near_at)]
-    out_inverse = call(
-        functools.partial(out_inverse_kernel, tokens, slice_rows),
-        2,
-        (slice_rows, TILE),
-        (2 * slice_rows, TILE),
-        numbers(core, own_at, near_at),
+    own_at, near_at = [jnp.clip(a, -slice_rows, TILE) + PIECE for a in (own_at, near_at)]
+    padded = call(
+        functools.partial(out_inverse_kernel, tokens),
+        6,
+        (PIECE, TILE),
+        (6 * PIECE, TILE),
+        numbers(core),
         out_tiles,
         out_other,
-        scratch=[(square, bf16), ((TILE + 2 * slice_rows, TILE), f32), (square, bf16)],
-    )
-
+        scratch=[(square, bf16), (square, f32), (square, bf16)],
+    )
     middle = mdot(cross, in_inverse).astype(bf16)
     mine = lax.dynamic_slice_in_dim(middle, h * HALF, HALF, 1)
     theirs = lax.dynamic_slice_in_dim(middle, (1 - h) * HALF, HALF, 1)
@@ -365,14 +398,20 @@
         (theirs, X, SWAP_X), (mine, YH, SWAP2), (theirs, (YH, X), SWAP_BOTH)
     )
     middle = in_order(h, in_order(yh, mine, near_y), in_order(yh, near_x, near_xy))
+    middle, padded = lax.optimization_barrier((middle, padded))
     other = lax.ppermute(middle, CORE, SWAP2)
     middle = jnp.moveaxis(in_order(core, middle, other), 0, 1).reshape(TILE, HALF)
+    out_inverse = jnp.concatenate(
+        [lax.dynamic_slice_in_dim(padded, at, slice_rows, 0) for at in (own_at, near_at)], 0
+    )
     result = mdot(out_inverse, middle)
 
     near_part = result[slice_rows:].astype(bf16)
     up = lax.ppermute(near_part, Z, [(0, 1), (1, 2), (4, 5), (5, 6)])
     down = lax.ppermute(near_part, Z, [(3, 2), (7, 6)])
-    squares = all_sum(all_sum(jnp.sum(result * result), OWNER), DP)
+    whole = mdot(padded[PIECE : PIECE + TILE], middle)
+    squares = jnp.where(m == 2, 0.0, jnp.sum(whole * whole))
+    squares = all_sum(all_sum(squares, OWNER), Z)
     summed = result[:slice_rows] + up.astype(f32) + down.astype(f32)
     return (summed * lax.rsqrt(squares / (width * out_width) + 1e-06)).astype(bf16)
 

time: 232 us -> 220 us (0.948); the launches traced: 228 us -> 218 us
  waiting for transfers between devices: 92.5 us -> 80.4 us
  Pallas kernels: 23.7 us -> 30.6 us
  starting transfers between devices: 65.3 us -> 60.5 us
  matrix products: 2.9 us -> 6.44 us
  blocking collectives: 13.4 us -> 10.5 us
    ppermute x22, waiting for transfers between devices: 87.6 us -> 73.8 us  [phase(): got = [lax.ppermute(value, *send[1:]) for value, send in zip(values, sends)]]
    ppermute x22, starting transfers between devices: 52.9 us -> 47.7 us  [phase(): got = [lax.ppermute(value, *send[1:]) for value, send in zip(values, sends)]]
    pallas_call x3, Pallas kernels: 14.1 us -> 17.8 us  [call(): pl.pallas_call(kernel, grid_spec=pltpu.PrefetchScalarGridSpec(num_scalar_...]
    dot_general x2 -> x3, matrix products: 2.9 us -> 6.44 us  [mdot(): return jnp.dot(a, b, preferred_element_type=f32)]
    all_to_all x1, blocking collectives: 13.4 us -> 10.5 us  [all_sum(): lax.all_to_all(jnp.full((n, 128), value, f32), axis, 0, 0, tiled=True)]
    add x1 -> x0, other arithmetic: 2.83 us -> none  [added(): return functools.reduce(jnp.add, [p.astype(f32) for p in parts])]
    pallas_call x2 -> x3, Pallas kernels: 9.65 us -> 10.7 us  [slots(): pl.pallas_call(kernel, grid_spec=pltpu.PrefetchScalarGridSpec(num_scalar_...]
    unnamed x18 -> x24, local copies, waits for them, and re-layouts: 4.75 us -> 5 us
  transfers between devices with their start and end apart: 29 -> 29, of which waited for: 18 -> 20; matrix products, arithmetic and copies ran while one was open for 3% -> 6% of each run, Pallas kernels for 9% -> 10%
where the time goes in v4:
time: 220 us; the launch traced here: 218 us
  waiting for transfers between devices  80.4 us (37%)
  starting transfers between devices  60.5 us (28%)
  Pallas kernels  30.6 us (14%)
  other arithmetic  16.9 us (8%)
  local copies, waits for them, and re-layouts  11.1 us (5%)
  blocking collectives  10.5 us (5%)
  matrix products  6.44 us (3%)
    ppermute x22, waiting for transfers between devices, phase(): got = [lax.ppermute(value, *send[1:]) for value, send in zip(values, sends)]  73.8 us
    ppermute x22, starting transfers between devices, phase(): got = [lax.ppermute(value, *send[1:]) for value, send in zip(values, sends)]  47.7 us
    pallas_call x3, Pallas kernels, call(): pl.pallas_call(kernel, grid_spec=pltpu.PrefetchScalarGridSpec(num_scalar_...  17.8 us
    pallas_call x3, Pallas kernels, slots(): pl.pallas_call(kernel, grid_spec=pltpu.PrefetchScalarGridSpec(num_scalar_...  10.7 us
    all_to_all x1, blocking collectives, all_sum(): lax.all_to_all(jnp.full((n, 128), value, f32), axis, 0, 0, tiled=True)  10.5 us
    dot_general x3, matrix products, mdot(): return jnp.dot(a, b, preferred_element_type=f32)  6.44 us
    all_to_all x1, starting transfers between devices, shards(): out_tiles = lax.all_to_all(copies, OWNER, 0, 0, tiled=True)  5.02 us
    all_to_all x1, starting transfers between devices, all_sum(): lax.all_to_all(jnp.full((n, 128), value, f32), axis, 0, 0, tiled=True)  5.02 us
  transfers between devices with their start and end apart: 29, of which 20 were waited for; matrix products, arithmetic and copies ran while one was open for 6% of the time, Pallas kernels for 10%

profile of v4, /device:TPU:16, one launch (start us, length us, event | category | flops | bytes accessed | tf_op | source)
XLA Modules:
  0.0 218.3 jit_solution(14101809586789074375)
XLA Ops:
  6.2 5.8 %shard_map.38 = bf16[9,256,384]{2,1,0:T(8,128)(2,1)} custom-call(s32[28]{0:T(128)S(1)} %stack.147.at_ref, bf16[128,4608]{1,0:T(8,128)(2,1)S(1)} %shard_map.37.pick_ref, bf16[128,4608]{1,0:T(8,128)(2,1)S(1)} %collective-permute-done.recv_ref, bf16[128,1024]{1,0:T(8,128)(2,1)S(1)} %multiply_convert_fusion.own_ref, ...), custom_call_target="tpu_custom_call" | custom-call | tf_op jit(solution)/shard_map/pallas_call | solution.py:298
  12.9 5.9 %collective-permute-start.2 = (bf16[256,384]{1,0:T(8,128)(2,1)S(1)}, bf16[256,384]{1,0:T(8,128)(2,1)S(1)}, u32[]{:S(2)}, u32[]{:S(2)}) collective-permute-start(bf16[256,384]{1,0:T(8,128)(2,1)S(1)} %slice_bitcast_fusion.1), channel_id=1, source_target_pairs={{0,224},{8,40},{32,0},{40,72},{64,32},{72,104},{96,64},{104,136},{... | collective-permute-start | bytes 589832 | tf_op jit(solution)/shard_map/ppermute | solution.py:239
  18.9 3.2 %collective-permute-done.2 = bf16[256,384]{1,0:T(8,128)(2,1)S(1)} collective-permute-done((bf16[256,384]{1,0:T(8,128)(2,1)S(1)}, bf16[256,384]{1,0:T(8,128)(2,1)S(1)}, u32[]{:S(2)}, u32[]{:S(2)}) %collective-permute-start.2) | collective-permute-done | bytes 196640 | tf_op jit(solution)/shard_map/ppermute | solution.py:239
  23.2 3.8 %collective-permute-start.3 = (bf16[2,256,384]{2,1,0:T(8,128)(2,1)S(1)}, bf16[2,256,384]{2,1,0:T(8,128)(2,1)S(1)}, u32[]{:S(2)}, u32[]{:S(2)}) collective-permute-start(bf16[2,256,384]{2,1,0:T(8,128)(2,1)S(1)} %add_convert_fusion.5), channel_id=1, source_target_pairs={{0,224},{8,40},{32,0},{40,72},{64,32},{72,104},{96,64},{104,136},{... | collective-permute-start | bytes 1179656 | tf_op jit(solution)/shard_map/ppermute | solution.py:239
  27.0 2.1 shard_map.39
  29.1 3.1 %collective-permute-done.3 = bf16[2,256,384]{2,1,0:T(8,128)(2,1)S(1)} collective-permute-done((bf16[2,256,384]{2,1,0:T(8,128)(2,1)S(1)}, bf16[2,256,384]{2,1,0:T(8,128)(2,1)S(1)}, u32[]{:S(2)}, u32[]{:S(2)}) %collective-permute-start.3) | collective-permute-done | bytes 393248 | tf_op jit(solution)/shard_map/ppermute | solution.py:239
  33.4 3.8 %collective-permute-start.4 = (bf16[2,256,384]{2,1,0:T(8,128)(2,1)S(1)}, bf16[2,256,384]{2,1,0:T(8,128)(2,1)S(1)}, u32[]{:S(2)}, u32[]{:S(2)}) collective-permute-start(bf16[2,256,384]{2,1,0:T(8,128)(2,1)S(1)} %add_convert_fusion.4), channel_id=1, source_target_pairs={{0,224},{8,40},{32,0},{40,72},{64,32},{72,104},{96,64},{104,136},{... | collective-permute-start | bytes 1179656 | tf_op jit(solution)/shard_map/ppermute | solution.py:239
  37.1 5.3 %collective-permute-done.4 = bf16[2,256,384]{2,1,0:T(8,128)(2,1)S(1)} collective-permute-done((bf16[2,256,384]{2,1,0:T(8,128)(2,1)S(1)}, bf16[2,256,384]{2,1,0:T(8,128)(2,1)S(1)}, u32[]{:S(2)}, u32[]{:S(2)}) %collective-permute-start.4) | collective-permute-done | bytes 393248 | tf_op jit(solution)/shard_map/ppermute | solution.py:239
  43.5 3.8 %collective-permute-start.5 = (bf16[2,256,384]{2,1,0:T(8,128)(2,1)S(1)}, bf16[2,256,384]{2,1,0:T(8,128)(2,1)S(1)}, u32[]{:S(2)}, u32[]{:S(2)}) collective-permute-start(bf16[2,256,384]{2,1,0:T(8,128)(2,1)S(1)} %add_convert_fusion.3), channel_id=1, source_target_pairs={{0,224},{8,40},{32,0},{40,72},{64,32},{72,104},{96,64},{104,136},{... | collective-permute-start | bytes 1179656 | tf_op jit(solution)/shard_map/ppermute | solution.py:239
  47.3 2.8 %shard_map.40.here_ref = bf16[5,256,1024]{2,1,0:T(8,128)(2,1)S(1)} custom-call(s32[28]{0:T(128)S(1)} %stack.147.at_ref, bf16[128,4608]{1,0:T(8,128)(2,1)S(1)} %copy-done.1, bf16[128,4608]{1,0:T(8,128)(2,1)S(1)} %copy-done.3, bf16[128,1024]{1,0:T(8,128)(2,1)S(1)} %multiply_convert_fusion.own_ref, bf16[128,1024]{1,0:T(8,128)(2,1)S(1)} %collective-permute-done.1.got_ref), custom_call_target="tpu_custom_call" | custom-call | tf_op jit(solution)/shard_map/pallas_call | solution.py:298
  54.4 5.6 %collective-permute-start.8 = (bf16[256,1024]{1,0:T(8,128)(2,1)S(1)}, bf16[256,1024]{1,0:T(8,128)(2,1)}, u32[]{:S(2)}, u32[]{:S(2)}) collective-permute-start(bf16[256,1024]{1,0:T(8,128)(2,1)S(1)} %slice_bitcast_fusion), channel_id=1, source_target_pairs={{0,224},{8,40},{32,0},{40,72},{96,64},{104,136},{128,96},{136,168}... | collective-permute-start | bytes 1572872 | tf_op jit(solution)/shard_map/ppermute | solution.py:239
  60.5 7.6 %collective-permute-done.7 = bf16[256,512]{1,0:T(8,128)(2,1)} collective-permute-done((bf16[256,512]{1,0:T(8,128)(2,1)S(1)}, bf16[256,512]{1,0:T(8,128)(2,1)}, u32[]{:S(2)}, u32[]{:S(2)}) %collective-permute-start.7) | collective-permute-done | bytes 262176 | tf_op jit(solution)/shard_map/ppermute | solution.py:239
  75.3 5.3 %collective-permute-start.11 = (bf16[2,256,1024]{2,1,0:T(8,128)(2,1)}, bf16[2,256,1024]{2,1,0:T(8,128)(2,1)}, u32[]{:S(2)}, u32[]{:S(2)}) collective-permute-start(bf16[2,256,1024]{2,1,0:T(8,128)(2,1)} %add_convert_fusion.2), channel_id=1, source_target_pairs={{0,224},{8,40},{40,72},{64,32},{72,104},{96,64},{128,96},{136,168}... | collective-permute-start | bytes 3145736 | tf_op jit(solution)/shard_map/ppermute | solution.py:239
  80.6 5.0 %all-to-all-start = ((bf16[8,256,256]{2,1,0:T(8,128)(2,1)}), bf16[8,256,256]{2,1,0:T(8,128)(2,1)}, u32[]{:S(2)}, u32[]{:S(2)}) async-start(bf16[8,256,256]{2,1,0:T(8,128)(2,1)} %broadcast_in_dim.21), calls=%async_computation | async-start | bytes 2097152 | tf_op jit(solution)/shard_map/all_to_all | solution.py:349
  85.6 9.3 %collective-permute-done.10 = bf16[2,256,256]{2,1,0:T(8,128)(2,1)S(1)} collective-permute-done((bf16[2,256,256]{2,1,0:T(8,128)(2,1)S(1)}, bf16[2,256,256]{2,1,0:T(8,128)(2,1)S(1)}, u32[]{:S(2)}, u32[]{:S(2)}) %collective-permute-start.10) | collective-permute-done | bytes 262176 | tf_op jit(solution)/shard_map/ppermute | solution.py:239
  94.9 2.3 %all-to-all-done.own_ref = bf16[8,256,256]{2,1,0:T(8,128)(2,1)} async-done(((bf16[8,256,256]{2,1,0:T(8,128)(2,1)}), bf16[8,256,256]{2,1,0:T(8,128)(2,1)}, u32[]{:S(2)}, u32[]{:S(2)}) %all-to-all-start) | async-done | bytes 1048608 | tf_op jit(solution)/shard_map/all_to_all | solution.py:349
  98.6 4.9 %collective-permute-done.12 = bf16[2,256,256]{2,1,0:T(8,128)(2,1)S(1)} collective-permute-done((bf16[2,256,256]{2,1,0:T(8,128)(2,1)S(1)}, bf16[2,256,256]{2,1,0:T(8,128)(2,1)S(1)}, u32[]{:S(2)}, u32[]{:S(2)}) %collective-permute-start.12) | collective-permute-done | bytes 262176 | tf_op jit(solution)/shard_map/ppermute | solution.py:239
  103.6 2.6 %collective-permute-start.13 = (bf16[2,256,256]{2,1,0:T(8,128)(2,1)S(1)}, bf16[2,256,256]{2,1,0:T(8,128)(2,1)S(1)}, u32[]{:S(2)}, u32[]{:S(2)}) collective-permute-start(bf16[2,256,256]{2,1,0:T(8,128)(2,1)S(1)} %collective-permute-done.12), channel_id=1, source_target_pairs={{0,224},{8,40},{32,0},{40,72},{64,32},{72,104},{96,64},{104,136},{... | collective-permute-start | bytes 786440 | tf_op jit(solution)/shard_map/ppermute | solution.py:239
  106.2 3.9 %collective-permute-done.13 = bf16[2,256,256]{2,1,0:T(8,128)(2,1)S(1)} collective-permute-done((bf16[2,256,256]{2,1,0:T(8,128)(2,1)S(1)}, bf16[2,256,256]{2,1,0:T(8,128)(2,1)S(1)}, u32[]{:S(2)}, u32[]{:S(2)}) %collective-permute-start.13) | collective-permute-done | bytes 262176 | tf_op jit(solution)/shard_map/ppermute | solution.py:239
  110.1 3.9 %collective-permute-start.14 = (bf16[1,256,256]{2,1,0:T(8,128)(2,1)S(1)}, bf16[1,256,256]{2,1,0:T(8,128)(2,1)S(1)}, u32[]{:S(2)}, u32[]{:S(2)}) collective-permute-start(bf16[1,256,256]{2,1,0:T(8,128)(2,1)S(1)} %slice_select_fusion), channel_id=1, source_target_pairs={{0,224},{8,40},{32,0},{40,72},{64,32},{72,104},{96,64},{104,136},{... | collective-permute-start | bytes 393224 | tf_op jit(solution)/shard_map/ppermute | solution.py:239
  118.1 2.5 %collective-permute-done.16.other_ref = bf16[7,256,256]{2,1,0:T(8,128)(2,1)S(1)} collective-permute-done((bf16[7,256,256]{2,1,0:T(8,128)(2,1)S(1)}, bf16[7,256,256]{2,1,0:T(8,128)(2,1)S(1)}, u32[]{:S(2)}, u32[]{:S(2)}) %collective-permute-start.16) | collective-permute-done | bytes 917536 | tf_op jit(solution)/shard_map/ppermute | solution.py:239
  120.6 12.8 %collective-permute-done.15 = bf16[2,256,1024]{2,1,0:T(8,128)(2,1)S(1)} collective-permute-done((bf16[2,256,1024]{2,1,0:T(8,128)(2,1)S(1)}, bf16[2,256,1024]{2,1,0:T(8,128)(2,1)S(1)}, u32[]{:S(2)}, u32[]{:S(2)}) %collective-permute-start.15) | collective-permute-done | bytes 1048608 | tf_op jit(solution)/shard_map/ppermute | solution.py:239
  133.8 2.5 %collective-permute-start.17 = (bf16[2,256,1024]{2,1,0:T(8,128)(2,1)S(1)}, bf16[2,256,1024]{2,1,0:T(8,128)(2,1)}, u32[]{:S(2)}, u32[]{:S(2)}) collective-permute-start(bf16[2,256,1024]{2,1,0:T(8,128)(2,1)S(1)} %add_convert_fusion), channel_id=1, source_target_pairs={{0,224},{8,40},{32,0},{64,32},{72,104},{104,136},{128,96},{136,168... | collective-permute-start | bytes 3145736 | tf_op jit(solution)/shard_map/ppermute | solution.py:239
  136.4 8.5 %shard_map.41 = bf16[1024,1024]{1,0:T(8,128)(2,1)S(1)} custom-call(s32[2]{0:T(128)S(1)} %pad_add_fusion.2.at_ref, bf16[2,256,256]{2,1,0:T(8,128)(2,1)S(1)} %pad_maximum_fusion.6.shard_ref, bf16[7,256,256]{2,1,0:T(8,128)(2,1)S(1)} %pad_maximum_fusion.own_ref, bf16[7,256,256]{2,1,0:T(8,128)(2,1)S(1)} %collective-permute-done.16.other_ref), custom_call_target="tpu_custom_call" | custom-call | tf_op jit(solution)/shard_map/pallas_call | solution.py:184
  146.2 4.4 %collective-permute-done.17.own_ref = bf16[2,256,1024]{2,1,0:T(8,128)(2,1)} collective-permute-done((bf16[2,256,1024]{2,1,0:T(8,128)(2,1)S(1)}, bf16[2,256,1024]{2,1,0:T(8,128)(2,1)}, u32[]{:S(2)}, u32[]{:S(2)}) %collective-permute-start.17) | collective-permute-done | bytes 1048608 | tf_op jit(solution)/shard_map/ppermute | solution.py:239
  150.7 2.9 %collective-permute-done.18.other_ref = bf16[2,256,1024]{2,1,0:T(8,128)(2,1)} collective-permute-done((bf16[2,256,1024]{2,1,0:T(8,128)(2,1)}, bf16[2,256,1024]{2,1,0:T(8,128)(2,1)}, u32[]{:S(2)}, u32[]{:S(2)}) %collective-permute-start.18) | collective-permute-done | bytes 1048608 | tf_op jit(solution)/shard_map/ppermute | solution.py:239
  156.2 9.7 %collective-permute-done.19 = bf16[128,1024]{1,0:T(8,128)(2,1)S(1)} collective-permute-done((bf16[128,1024]{1,0:T(8,128)(2,1)S(1)}, bf16[128,1024]{1,0:T(8,128)(2,1)S(1)}, u32[]{:S(2)}, u32[]{:S(2)}) %collective-permute-start.19) | collective-permute-done | bytes 262176 | tf_op jit(solution)/shard_map/ppermute | solution.py:239
  166.0 2.4 %convolution_convert_fusion = bf16[128,1024]{1,0:T(8,128)(2,1)S(1)} fusion(bf16[1024,1024]{1,0:T(8,128)(2,1)} %copy-done.4, bf16[128,1024]{1,0:T(8,128)(2,1)S(1)} %collective-permute-done.19, bf16[128,1024]{1,0:T(8,128)(2,1)S(1)} %get-tuple-element.63), kind=kOutput, calls=%fused_computation.7 | convolution fusion | flops 269090816 | bytes 2883584 | tf_op jit(solution)/shard_map/dot_general | solution.py:32
  170.3 3.2 %collective-permute-start.23 = (bf16[128,512]{1,0:T(8,128)(2,1)S(1)}, bf16[128,512]{1,0:T(8,128)(2,1)}, u32[]{:S(2)}, u32[]{:S(2)}) collective-permute-start(bf16[128,512]{1,0:T(8,128)(2,1)S(1)} %get-tuple-element.72), channel_id=1, source_target_pairs={{0,17},{1,16},{2,19},{3,18},{16,1},{17,0},{18,3},{19,2},{4,21},{5,... | collective-permute-start | bytes 393224 | tf_op jit(solution)/shard_map/ppermute | solution.py:239
  174.7 8.6 %shard_map.43 = bf16[1536,1024]{1,0:T(8,128)(2,1)S(1)} custom-call(s32[1]{0:T(128)} %bitcast.at_ref, bf16[8,256,256]{2,1,0:T(8,128)(2,1)} %all-to-all-done.own_ref, bf16[8,256,256]{2,1,0:T(8,128)(2,1)S(1)} %copy-done.9), custom_call_target="tpu_custom_call" | custom-call | tf_op jit(solution)/shard_map/pallas_call | solution.py:184
  193.4 5.0 %all-to-all-start.1 = ((f32[8,1,128]{2,1,0:T(1,128)}), f32[8,1,128]{2,1,0:T(1,128)S(1)}, u32[]{:S(2)}, u32[]{:S(2)}) async-start(f32[8,1,128]{2,1,0:T(1,128)} %broadcast_in_dim.23), calls=%async_computation.1 | async-start | bytes 8192 | tf_op jit(solution)/shard_map/all_to_all | solution.py:255
  205.7 10.5 %all_to_all.23 = f32[8,1,128]{2,1,0:T(1,128)S(1)} all-to-all(f32[8,1,128]{2,1,0:T(1,128)S(1)} %broadcast_in_dim.24), channel_id=1, replica_groups=mesh['dp_0'=8,'dp_1'=2,'dp_2'=2,'owner_0'=2,'owner_1'=4] {'dp_0'}, dimensions={0} | all-to-all | bytes 8192 | tf_op jit(solution)/shard_map/all_to_all | solution.py:255
  (106 shorter events, 53.3 us)
Async XLA Ops:
  2.2 24.8 %copy-start = (bf16[128,4608]{1,0:T(8,128)(2,1)}, bf16[128,4608]{1,0:T(8,128)(2,1)S(1)}, u32[]{:S(2)}) copy-start(bf16[128,4608]{1,0:T(8,128)(2,1)S(1)} %shard_map.37.pick_ref) | copy-start | bytes 3538948
  2.2 3.9 %collective-permute-start = (bf16[128,4608]{1,0:T(8,128)(2,1)S(1)}, bf16[128,4608]{1,0:T(8,128)(2,1)S(1)}, u32[]{:S(2)}, u32[]{:S(2)}) collective-permute-start(bf16[128,4608]{1,0:T(8,128)(2,1)S(1)} %shard_map.37.pick_ref), channel_id=1, source_target_pairs={{0,8},{8,0},{1,9},{9,1},{2,10},{10,2},{3,11},{11,3},{4,12},{12,4},... | collective-permute-start | bytes 3538952 | tf_op jit(solution)/shard_map/ppermute | solution.py:279
  4.5 1.7 collective-permute-start.1
  6.2 20.8 %copy-start.2 = (bf16[128,4608]{1,0:T(8,128)(2,1)}, bf16[128,4608]{1,0:T(8,128)(2,1)S(1)}, u32[]{:S(2)}) copy-start(bf16[128,4608]{1,0:T(8,128)(2,1)S(1)} %collective-permute-done.recv_ref) | copy-start | bytes 3538948
  12.9 9.1 %collective-permute-start.2 = (bf16[256,384]{1,0:T(8,128)(2,1)S(1)}, bf16[256,384]{1,0:T(8,128)(2,1)S(1)}, u32[]{:S(2)}, u32[]{:S(2)}) collective-permute-start(bf16[256,384]{1,0:T(8,128)(2,1)S(1)} %slice_bitcast_fusion.1), channel_id=1, source_target_pairs={{0,224},{8,40},{32,0},{40,72},{64,32},{72,104},{96,64},{104,136},{... | collective-permute-start | bytes 589832 | tf_op jit(solution)/shard_map/ppermute | solution.py:239
  23.2 9.1 %collective-permute-start.3 = (bf16[2,256,384]{2,1,0:T(8,128)(2,1)S(1)}, bf16[2,256,384]{2,1,0:T(8,128)(2,1)S(1)}, u32[]{:S(2)}, u32[]{:S(2)}) collective-permute-start(bf16[2,256,384]{2,1,0:T(8,128)(2,1)S(1)} %add_convert_fusion.5), channel_id=1, source_target_pairs={{0,224},{8,40},{32,0},{40,72},{64,32},{72,104},{96,64},{104,136},{... | collective-permute-start | bytes 1179656 | tf_op jit(solution)/shard_map/ppermute | solution.py:239
  29.1 24.6 %copy-start.5 = (bf16[3,256,1024]{2,1,0:T(8,128)(2,1)}, bf16[3,256,1024]{2,1,0:T(8,128)(2,1)S(1)}, u32[]{:S(2)}) copy-start(bf16[3,256,1024]{2,1,0:T(8,128)(2,1)S(1)} %shard_map.39) | copy-start | bytes 4718596
  33.4 9.1 %collective-permute-start.4 = (bf16[2,256,384]{2,1,0:T(8,128)(2,1)S(1)}, bf16[2,256,384]{2,1,0:T(8,128)(2,1)S(1)}, u32[]{:S(2)}, u32[]{:S(2)}) collective-permute-start(bf16[2,256,384]{2,1,0:T(8,128)(2,1)S(1)} %add_convert_fusion.4), channel_id=1, source_target_pairs={{0,224},{8,40},{32,0},{40,72},{64,32},{72,104},{96,64},{104,136},{... | collective-permute-start | bytes 1179656 | tf_op jit(solution)/shard_map/ppermute | solution.py:239
  43.5 9.1 %collective-permute-start.5 = (bf16[2,256,384]{2,1,0:T(8,128)(2,1)S(1)}, bf16[2,256,384]{2,1,0:T(8,128)(2,1)S(1)}, u32[]{:S(2)}, u32[]{:S(2)}) collective-permute-start(bf16[2,256,384]{2,1,0:T(8,128)(2,1)S(1)} %add_convert_fusion.3), channel_id=1, source_target_pairs={{0,224},{8,40},{32,0},{40,72},{64,32},{72,104},{96,64},{104,136},{... | collective-permute-start | bytes 1179656 | tf_op jit(solution)/shard_map/ppermute | solution.py:239
  52.7 1.6 collective-permute-start.6
  54.4 13.7 %collective-permute-start.8 = (bf16[256,1024]{1,0:T(8,128)(2,1)S(1)}, bf16[256,1024]{1,0:T(8,128)(2,1)}, u32[]{:S(2)}, u32[]{:S(2)}) collective-permute-start(bf16[256,1024]{1,0:T(8,128)(2,1)S(1)} %slice_bitcast_fusion), channel_id=1, source_target_pairs={{0,224},{8,40},{32,0},{40,72},{96,64},{104,136},{128,96},{136,168}... | collective-permute-start | bytes 1572872 | tf_op jit(solution)/shard_map/ppermute | solution.py:239
  60.0 8.1 %collective-permute-start.7 = (bf16[256,512]{1,0:T(8,128)(2,1)S(1)}, bf16[256,512]{1,0:T(8,128)(2,1)}, u32[]{:S(2)}, u32[]{:S(2)}) collective-permute-start(bf16[256,512]{1,0:T(8,128)(2,1)S(1)} %add_convert_fusion.8), channel_id=1, source_target_pairs={{0,16},{16,0},{1,17},{17,1},{2,18},{18,2},{3,19},{19,3},{4,20},{20... | collective-permute-start | bytes 786440 | tf_op jit(solution)/shard_map/ppermute | solution.py:239
  69.1 5.1 %collective-permute-start.9 = (bf16[256,256]{1,0:T(8,128)(2,1)S(1)}, bf16[256,256]{1,0:T(8,128)(2,1)S(1)}, u32[]{:S(2)}, u32[]{:S(2)}) collective-permute-start(bf16[256,256]{1,0:T(8,128)(2,1)S(1)} %slice.106), channel_id=1, source_target_pairs={{0,1},{1,0},{2,3},{3,2},{4,5},{5,4},{6,7},{7,6},{8,9},{9,8},{10,11... | collective-permute-start | bytes 393224 | tf_op jit(solution)/shard_map/ppermute | solution.py:239
  75.3 19.6 %collective-permute-start.11 = (bf16[2,256,1024]{2,1,0:T(8,128)(2,1)}, bf16[2,256,1024]{2,1,0:T(8,128)(2,1)}, u32[]{:S(2)}, u32[]{:S(2)}) collective-permute-start(bf16[2,256,1024]{2,1,0:T(8,128)(2,1)} %add_convert_fusion.2), channel_id=1, source_target_pairs={{0,224},{8,40},{40,72},{64,32},{72,104},{96,64},{128,96},{136,168}... | collective-permute-start | bytes 3145736 | tf_op jit(solution)/shard_map/ppermute | solution.py:239
  80.6 16.6 %all-to-all-start = ((bf16[8,256,256]{2,1,0:T(8,128)(2,1)}), bf16[8,256,256]{2,1,0:T(8,128)(2,1)}, u32[]{:S(2)}, u32[]{:S(2)}) async-start(bf16[8,256,256]{2,1,0:T(8,128)(2,1)} %broadcast_in_dim.21), calls=%async_computation | async-start | bytes 2097152 | tf_op jit(solution)/shard_map/all_to_all | solution.py:349
  85.6 9.3 %collective-permute-start.10 = (bf16[2,256,256]{2,1,0:T(8,128)(2,1)S(1)}, bf16[2,256,256]{2,1,0:T(8,128)(2,1)S(1)}, u32[]{:S(2)}, u32[]{:S(2)}) collective-permute-start(bf16[2,256,256]{2,1,0:T(8,128)(2,1)S(1)} %pad_maximum_fusion.6.shard_ref), channel_id=1, source_target_pairs={{0,224},{8,40},{32,0},{40,72},{64,32},{72,104},{96,64},{104,136},{... | collective-permute-start | bytes 786440 | tf_op jit(solution)/shard_map/ppermute | solution.py:239
  97.2 6.4 %collective-permute-start.12 = (bf16[2,256,256]{2,1,0:T(8,128)(2,1)S(1)}, bf16[2,256,256]{2,1,0:T(8,128)(2,1)S(1)}, u32[]{:S(2)}, u32[]{:S(2)}) collective-permute-start(bf16[2,256,256]{2,1,0:T(8,128)(2,1)S(1)} %collective-permute-done.10), channel_id=1, source_target_pairs={{0,224},{8,40},{32,0},{40,72},{64,32},{72,104},{96,64},{104,136},{... | collective-permute-start | bytes 786440 | tf_op jit(solution)/shard_map/ppermute | solution.py:239
  103.6 6.5 %collective-permute-start.13 = (bf16[2,256,256]{2,1,0:T(8,128)(2,1)S(1)}, bf16[2,256,256]{2,1,0:T(8,128)(2,1)S(1)}, u32[]{:S(2)}, u32[]{:S(2)}) collective-permute-start(bf16[2,256,256]{2,1,0:T(8,128)(2,1)S(1)} %collective-permute-done.12), channel_id=1, source_target_pairs={{0,224},{8,40},{32,0},{40,72},{64,32},{72,104},{96,64},{104,136},{... | collective-permute-start | bytes 786440 | tf_op jit(solution)/shard_map/ppermute | solution.py:239
  110.1 6.5 %collective-permute-start.14 = (bf16[1,256,256]{2,1,0:T(8,128)(2,1)S(1)}, bf16[1,256,256]{2,1,0:T(8,128)(2,1)S(1)}, u32[]{:S(2)}, u32[]{:S(2)}) collective-permute-start(bf16[1,256,256]{2,1,0:T(8,128)(2,1)S(1)} %slice_select_fusion), channel_id=1, source_target_pairs={{0,224},{8,40},{32,0},{40,72},{64,32},{72,104},{96,64},{104,136},{... | collective-permute-start | bytes 393224 | tf_op jit(solution)/shard_map/ppermute | solution.py:239
  116.7 16.7 %collective-permute-start.15 = (bf16[2,256,1024]{2,1,0:T(8,128)(2,1)S(1)}, bf16[2,256,1024]{2,1,0:T(8,128)(2,1)S(1)}, u32[]{:S(2)}, u32[]{:S(2)}) collective-permute-start(bf16[2,256,1024]{2,1,0:T(8,128)(2,1)S(1)} %add_convert_fusion.1), channel_id=1, source_target_pairs={{32,0},{40,72},{64,32},{72,104},{96,64},{104,136},{160,128},{168,2... | collective-permute-start | bytes 3145736 | tf_op jit(solution)/shard_map/ppermute | solution.py:239
  118.0 2.6 %collective-permute-start.16 = (bf16[7,256,256]{2,1,0:T(8,128)(2,1)S(1)}, bf16[7,256,256]{2,1,0:T(8,128)(2,1)S(1)}, u32[]{:S(2)}, u32[]{:S(2)}) collective-permute-start(bf16[7,256,256]{2,1,0:T(8,128)(2,1)S(1)} %pad_maximum_fusion.own_ref), channel_id=1, source_target_pairs={{0,8},{8,0},{1,9},{9,1},{2,10},{10,2},{3,11},{11,3},{4,12},{12,4},... | collective-permute-start | bytes 2752520 | tf_op jit(solution)/shard_map/ppermute | solution.py:239
  133.8 16.8 %collective-permute-start.17 = (bf16[2,256,1024]{2,1,0:T(8,128)(2,1)S(1)}, bf16[2,256,1024]{2,1,0:T(8,128)(2,1)}, u32[]{:S(2)}, u32[]{:S(2)}) collective-permute-start(bf16[2,256,1024]{2,1,0:T(8,128)(2,1)S(1)} %add_convert_fusion), channel_id=1, source_target_pairs={{0,224},{8,40},{32,0},{64,32},{72,104},{104,136},{128,96},{136,168... | collective-permute-start | bytes 3145736 | tf_op jit(solution)/shard_map/ppermute | solution.py:239
  150.6 3.0 %collective-permute-start.18 = (bf16[2,256,1024]{2,1,0:T(8,128)(2,1)}, bf16[2,256,1024]{2,1,0:T(8,128)(2,1)}, u32[]{:S(2)}, u32[]{:S(2)}) collective-permute-start(bf16[2,256,1024]{2,1,0:T(8,128)(2,1)} %collective-permute-done.17.own_ref), channel_id=1, source_target_pairs={{0,8},{8,0},{1,9},{9,1},{2,10},{10,2},{3,11},{11,3},{4,12},{12,4},... | collective-permute-start | bytes 3145736 | tf_op jit(solution)/shard_map/ppermute | solution.py:239
  155.6 10.3 %collective-permute-start.20 = (bf16[8,256,256]{2,1,0:T(8,128)(2,1)}, bf16[8,256,256]{2,1,0:T(8,128)(2,1)S(1)}, u32[]{:S(2)}, u32[]{:S(2)}) collective-permute-start(bf16[8,256,256]{2,1,0:T(8,128)(2,1)} %all-to-all-done.own_ref), channel_id=1, source_target_pairs={{0,8},{8,0},{1,9},{9,1},{2,10},{10,2},{3,11},{11,3},{4,12},{12,4},... | collective-permute-start | bytes 3145736 | tf_op jit(solution)/shard_map/ppermute | solution.py:239
  155.9 10.1 %collective-permute-start.19 = (bf16[128,1024]{1,0:T(8,128)(2,1)S(1)}, bf16[128,1024]{1,0:T(8,128)(2,1)S(1)}, u32[]{:S(2)}, u32[]{:S(2)}) collective-permute-start(bf16[128,1024]{1,0:T(8,128)(2,1)S(1)} %get-tuple-element.66), channel_id=1, source_target_pairs={{0,16},{16,0},{1,17},{17,1},{2,18},{18,2},{3,19},{19,3},{4,20},{20... | collective-permute-start | bytes 786440 | tf_op jit(solution)/shard_map/ppermute | solution.py:239
  168.4 15.0 %collective-permute-start.21 = (bf16[128,512]{1,0:T(8,128)(2,1)S(1)}, bf16[128,512]{1,0:T(8,128)(2,1)S(1)}, u32[]{:S(2)}, u32[]{:S(2)}) collective-permute-start(bf16[128,512]{1,0:T(8,128)(2,1)S(1)} %get-tuple-element.72), channel_id=1, source_target_pairs={{0,1},{1,0},{2,3},{3,2},{4,5},{5,4},{6,7},{7,6},{8,9},{9,8},{10,11... | collective-permute-start | bytes 393224 | tf_op jit(solution)/shard_map/ppermute | solution.py:239
  170.0 13.4 %collective-permute-start.22 = (bf16[128,512]{1,0:T(8,128)(2,1)S(1)}, bf16[128,512]{1,0:T(8,128)(2,1)}, u32[]{:S(2)}, u32[]{:S(2)}) collective-permute-start(bf16[128,512]{1,0:T(8,128)(2,1)S(1)} %get-tuple-element.71), channel_id=1, source_target_pairs={{0,16},{16,0},{1,17},{17,1},{2,18},{18,2},{3,19},{19,3},{4,20},{20... | collective-permute-start | bytes 393224 | tf_op jit(solution)/shard_map/ppermute | solution.py:239
  170.3 13.1 %collective-permute-start.23 = (bf16[128,512]{1,0:T(8,128)(2,1)S(1)}, bf16[128,512]{1,0:T(8,128)(2,1)}, u32[]{:S(2)}, u32[]{:S(2)}) collective-permute-start(bf16[128,512]{1,0:T(8,128)(2,1)S(1)} %get-tuple-element.72), channel_id=1, source_target_pairs={{0,17},{1,16},{2,19},{3,18},{16,1},{17,0},{18,3},{19,2},{4,21},{5,... | collective-permute-start | bytes 393224 | tf_op jit(solution)/shard_map/ppermute | solution.py:239
  185.3 2.3 %collective-permute-start.24 = (bf16[2,2,128,512]{3,2,1,0:T(8,128)(2,1)}, bf16[2,2,128,512]{3,2,1,0:T(8,128)(2,1)}, u32[]{:S(2)}, u32[]{:S(2)}) collective-permute-start(bf16[2,2,128,512]{3,2,1,0:T(8,128)(2,1)} %pad_maximum_fusion.1), channel_id=1, source_target_pairs={{0,8},{8,0},{1,9},{9,1},{2,10},{10,2},{3,11},{11,3},{4,12},{12,4},... | collective-permute-start | bytes 1572872 | tf_op jit(solution)/shard_map/ppermute | solution.py:402
  193.4 11.1 %all-to-all-start.1 = ((f32[8,1,128]{2,1,0:T(1,128)}), f32[8,1,128]{2,1,0:T(1,128)S(1)}, u32[]{:S(2)}, u32[]{:S(2)}) async-start(f32[8,1,128]{2,1,0:T(1,128)} %broadcast_in_dim.23), calls=%async_computation.1 | async-start | bytes 8192 | tf_op jit(solution)/shard_map/all_to_all | solution.py:255
  200.3 17.2 %collective-permute-start.25 = (bf16[192,512]{1,0:T(8,128)(2,1)S(1)}, bf16[192,512]{1,0:T(8,128)(2,1)S(1)}, u32[]{:S(2)}, u32[]{:S(2)}) collective-permute-start(bf16[192,512]{1,0:T(8,128)(2,1)S(1)} %slice.149), channel_id=1, source_target_pairs={{0,32},{32,64},{128,160},{160,192},{1,33},{33,65},{129,161},{161,1... | collective-permute-start | bytes 589832 | tf_op jit(solution)/shard_map/ppermute | solution.py:410
  201.8 15.7 %collective-permute-start.26 = (bf16[192,512]{1,0:T(8,128)(2,1)S(1)}, bf16[192,512]{1,0:T(8,128)(2,1)S(1)}, u32[]{:S(2)}, u32[]{:S(2)}) collective-permute-start(bf16[192,512]{1,0:T(8,128)(2,1)S(1)} %slice.149), channel_id=1, source_target_pairs={{96,64},{224,192},{97,65},{225,193},{98,66},{226,194},{99,67},{227... | collective-permute-start | bytes 589832 | tf_op jit(solution)/shard_map/ppermute | solution.py:411
  (9 other events, 61.9 us)

commit v5 on v4

--- a/solution.py
+++ b/solution.py
@@ -72,7 +72,7 @@
     def _():
         load_tokens(pick_ref, recv_ref, own_ref, got_ref, out_ref, in_ref, sems)
 
-    h, plane, block, piece = at_ref[0], at_ref[1 + 3 * i], at_ref[2 + 3 * i], at_ref[3 + 3 * i]
+    h, plane, block, piece = at_ref[0], at_ref[2 + 3 * i], at_ref[3 + 3 * i], at_ref[4 + 3 * i]
     left = out_ref[:, aligned(block * HALF + piece * PIECE, PIECE)]
     right = out_ref[:, aligned(out_blocks * HALF + block * PIECE, PIECE)]
     part_ref[0, :, :PIECE] = tdot(left, right).astype(bf16)
@@ -80,16 +80,28 @@
     part_ref[0, :, PIECE:] = tdot(rows, in_ref[:, aligned(plane * 128, 128)]).astype(bf16)
 
 
-def cross_kernel(base, at_ref, pick_ref, recv_ref, own_ref, got_ref, cross_ref, out_ref, in_ref, sems):
+def cross_kernel(base, gives, at_ref, pick_ref, recv_ref, own_ref, got_ref, keep_ref, *refs):
+    give_refs, (out_ref, in_ref, sems) = refs[:-3], refs[-3:]
     i = pl.program_id(0)
 
     @pl.when(i == 0)
     def _():
         load_tokens(pick_ref, recv_ref, own_ref, got_ref, out_ref, in_ref, sems)
 
-    block, piece = at_ref[2 + 3 * (base + i)], at_ref[3 + 3 * (base + i)]
-    rows = out_ref[:, aligned(block * HALF + piece * PIECE, PIECE)]
-    cross_ref[0] = tdot(rows, in_ref[...]).astype(bf16)
+    yh, block, piece = at_ref[1], at_ref[3 + 3 * (base + i)], at_ref[4 + 3 * (base + i)]
+
+    def rows_of(side):
+        rows = out_ref[:, aligned(block * HALF + piece * PIECE + side * 128, 128)]
+        return tdot(rows, in_ref[...]).astype(bf16)
+
+    keep_ref[0] = rows_of(yh)
+    give = rows_of(1 - yh)
+    for slots, ref in zip(gives, give_refs):
+        for n, slot in enumerate(slots):
+
+            @pl.when(i + base == slot)
+            def _():
+                ref[n] = give
 
 
 def scale_of(tokens, sums_ref):
@@ -195,36 +207,6 @@
     )(at, *args)
 
 
-def join_kernel(at_ref, own_ref, other_ref, here_ref, give_ref, keep_ref):
-    total = added(own_ref[0], other_ref[0], here_ref[0]).astype(bf16)
-
-    @pl.when(pl.program_id(0) == 0)
-    def _():
-        give_ref[...] = total
-
-    @pl.when(pl.program_id(0) == 1)
-    def _():
-        keep_ref[...] = total
-
-
-def join(at, own, other, here):
-    block = (1, 128, TILE)
-    rows = (128, TILE)
-    piece = pl.BlockSpec(block, lambda i, at: (at[0], (1 - at[1]) ^ i, 0))
-    last = pl.BlockSpec(block, lambda i, at: (here.shape[0] - 1, (1 - at[1]) ^ i, 0))
-    return pl.pallas_call(
-        join_kernel,
-        grid_spec=pltpu.PrefetchScalarGridSpec(
-            num_scalar_prefetch=1,
-            grid=(2,),
-            in_specs=[piece, piece, last],
-            out_specs=[pl.BlockSpec(rows, lambda i, at: (0, 0))] * 2,
-        ),
-        out_shape=[jax.ShapeDtypeStruct(rows, bf16)] * 2,
-        compiler_params=PARAMS,
-    )(at, own, other, here)
-
-
 def ring_pairs(away=0, skip=False):
     pairs = []
     for plane in range(8):
@@ -291,30 +273,38 @@
         plane = (z + way * away + 8) % 8
         piece = core if i in (0, 7) else 1 - core if i == 8 else (i + 1) % 2
         table += [plane, 3 * (plane // 4) + plane % 4 - plane % 4 // 2, piece]
-    table = numbers(h, *table)
-
-    def slots(kernel, count, block):
+    table = numbers(h, yh, *table)
+
+    def slots(kernel, count, block, gives=()):
         tokens_in = (pick, recv, normed, normed_recv)
+        more = [(len(slots), *block) for slots in gives]
         return pl.pallas_call(
             kernel,
             grid_spec=pltpu.PrefetchScalarGridSpec(
                 num_scalar_prefetch=1,
                 grid=(count,),
                 in_specs=[pl.BlockSpec(memory_space=pl.ANY) for _ in tokens_in],
-                out_specs=pl.BlockSpec((1, *block), lambda i, at: (i, 0, 0)),
+                out_specs=[pl.BlockSpec((1, *block), lambda i, at: (i, 0, 0))]
+                + [pl.BlockSpec(m, lambda i, at: (0, 0, 0)) for m in more],
                 scratch_shapes=[
                     pltpu.VMEM((2 * here, pick.shape[1]), bf16),
                     pltpu.VMEM((2 * here, TILE), bf16),
                     pltpu.SemaphoreType.DMA((4,)),
                 ],
             ),
-            out_shape=jax.ShapeDtypeStruct((count, *block), bf16),
+            out_shape=[jax.ShapeDtypeStruct(m, bf16) for m in [(count, *block)] + more],
             compiler_params=PARAMS,
         )(table, *tokens_in)
 
-    part = slots(functools.partial(factor_kernel, out_blocks), 9, (PIECE, PIECE + 128))
-    first_cross = slots(functools.partial(cross_kernel, 0), 3, (PIECE, TILE))
-    last_cross = slots(functools.partial(cross_kernel, 3), 5, (PIECE, TILE))
+    def cross_part(base, count, gives):
+        return slots(functools.partial(cross_kernel, base, gives), count, (128, TILE), gives)
+
+    (part,) = slots(functools.partial(factor_kernel, out_blocks), 9, (PIECE, PIECE + 128))
+    keep_a, give_0, give_1, give_2 = cross_part(0, 3, ((0,), (1,), (2,)))
+    keep_b, give_34, give_5, give_6, give_7 = cross_part(3, 5, ((3, 4), (5,), (6,), (7,)))
+
+    def to_other_y(value):
+        return value, YH, SWAP2
 
     def ring(value, *args):
         return value, (Z, CORE), ring_pairs(*args)
@@ -324,11 +314,10 @@
         return in_order(core, got, nothing)
 
     (far,) = phase(ring(part[0]))
-    (far,) = phase(ring(added(part[1:3], widened(far)).astype(bf16)))
-    far, first_cross = lax.optimization_barrier((far, first_cross))
-    (far,) = phase(ring(added(part[3:5], far).astype(bf16)))
-    (far,) = phase(ring(added(part[5:7], far).astype(bf16)))
-    far, last_cross = lax.optimization_barrier((far, last_cross))
+    far, y0 = phase(ring(added(part[1:3], widened(far)).astype(bf16)), to_other_y(give_0))
+    far, y1 = phase(ring(added(part[3:5], far).astype(bf16)), to_other_y(give_1))
+    far, y2 = phase(ring(added(part[5:7], far).astype(bf16)), to_other_y(give_2))
+    far, keep_b = lax.optimization_barrier((far, keep_b))
     both_in = jnp.concatenate([far[0, :, PIECE:], far[1, :, PIECE:]], 1)
     out_own = jnp.where(core == 0, far[0, :, :PIECE], far[1, :, :PIECE])
     out_other = jnp.where(core == 0, far[1, :, :PIECE], far[0, :, :PIECE])
@@ -336,24 +325,27 @@
     here_in = in_order(core, part[7, :, PIECE:], part[8, :, PIECE:])
     local = jnp.concatenate([part[7, :, :PIECE], here_in[0], here_in[1]], 1)
     tiles = (added(jnp.concatenate([out_own, both_in], 1), other) + local.astype(f32)).astype(bf16)
-    other, far = phase((tiles, YH, SWAP2), ring(first_cross[0], 4, True))
+    other, far = phase((tiles, YH, SWAP2), ring(added(keep_a[0], y0[0]).astype(bf16), 4, True))
     tiles = added(tiles, other).astype(bf16)
     out_tile, in_tile = tiles[:, :PIECE], tiles[:, PIECE:]
     copies = jnp.broadcast_to(out_tile[None], (8, PIECE, PIECE))
     (near_in,) = phase((in_tile, X, SWAP_X))
     shard = in_order(h, in_tile, near_in)
     shard, copies = lax.optimization_barrier((shard, copies))
-    one, far = phase(
-        ring(shard), ring(added(first_cross[1:3], widened(far)).astype(bf16), 3, True)
+    both_y = jnp.concatenate([y1, y2])
+    one, far, y34 = phase(
+        ring(shard),
+        ring(added(keep_a[1:3], both_y, widened(far)).astype(bf16), 3, True),
+        to_other_y(give_34),
     )
     out_tiles = lax.all_to_all(copies, OWNER, 0, 0, tiled=True)
-    one, far, out_tiles = lax.optimization_barrier((one, far, out_tiles))
-    (two,) = phase(ring(one))
-    (three,) = phase(ring(two))
-    (last,) = phase(ring(jnp.where(core == 0, three[:1], three[1:])))
+    one, far, y34, out_tiles = lax.optimization_barrier((one, far, y34, out_tiles))
+    two, y5 = phase(ring(one), to_other_y(give_5))
+    three, y6 = phase(ring(two), to_other_y(give_6))
+    last, y7 = phase(ring(jnp.where(core == 0, three[:1], three[1:])), to_other_y(give_7))
     in_own = jnp.concatenate([one, two, three, last], 0)
     cross, in_other = phase(
-        ring(added(last_cross[0:2], far).astype(bf16), 2, True), (in_own, CORE, SWAP2)
+        ring(added(keep_b[0:2], y34, far).astype(bf16), 2, True), (in_own, CORE, SWAP2)
     )
     square = (TILE, TILE)
     in_inverse = call(
@@ -367,12 +359,12 @@
         in_other,
         scratch=[(square, bf16), (square, f32), (square, bf16)],
     )
-    (cross,) = phase(ring(added(last_cross[2:4], cross).astype(bf16), 1, True))
+    both_y = jnp.concatenate([y5, y6])
+    (cross,) = phase(ring(added(keep_b[2:4], both_y, cross).astype(bf16), 1, True))
     cross, in_inverse = lax.optimization_barrier((cross, in_inverse))
-    (other,) = phase((cross, CORE, SWAP2))
-    give, keep = join(numbers(core, yh), cross, other, last_cross)
-    (other, out_other) = phase((give, YH, SWAP2), (out_tiles, CORE, SWAP2))
-    cross = added(keep, other).astype(bf16)
+    other, out_other = phase((cross, CORE, SWAP2), (out_tiles, CORE, SWAP2))
+    own, other = [jnp.where(core == 0, a[0], a[1]) for a in (cross, other)]
+    cross = added(own, other, keep_b[4], y7[0]).astype(bf16)
     m = z % 4
     row = 2 * yh + core
     slice_rows = out_width // lax.axis_size(DP)
@@ -411,7 +403,7 @@
     down = lax.ppermute(near_part, Z, [(3, 2), (7, 6)])
     whole = mdot(padded[PIECE : PIECE + TILE], middle)
     squares = jnp.where(m == 2, 0.0, jnp.sum(whole * whole))
-    squares = all_sum(all_sum(squares, OWNER), Z)
+    squares = all_sum(all_sum(squares, Z), OWNER)
     summed = result[:slice_rows] + up.astype(f32) + down.astype(f32)
     return (summed * lax.rsqrt(squares / (width * out_width) + 1e-06)).astype(bf16)
 

time: 220 us -> 211 us (0.959)
  other arithmetic: 16.9 us -> 11.6 us
  Pallas kernels: 30.6 us -> 26.8 us
  waiting for transfers between devices: 80.4 us -> 83.5 us
  starting transfers between devices: 60.5 us -> 57.7 us
    ppermute x22 -> x28, waiting for transfers between devices: 73.8 us -> 80.2 us  [phase(): got = [lax.ppermute(value, *send[1:]) for value, send in zip(values, sends)]]
    ppermute x22 -> x28, starting transfers between devices: 47.7 us -> 43.2 us  [phase(): got = [lax.ppermute(value, *send[1:]) for value, send in zip(values, sends)]]
    convert_element_type x6 -> x7, other arithmetic: 6.71 us -> 3.4 us  [the longest x1 1.47 us: shards(): added(keep_b[0:2], y34, far).astype(bf16)]
    ppermute x1, starting transfers between devices: 1.46 us -> 3.94 us  [shards(): up = lax.ppermute(near_part, Z, [(0, 1), (1, 2), (4, 5), (5, 6)])]
    all_to_all x1, waiting for transfers between devices: 2.27 us -> 0.01 us  [shards(): out_tiles = lax.all_to_all(copies, OWNER, 0, 0, tiled=True)]
    unnamed x24 -> x51, local copies, waits for them, and re-layouts: 5 us -> 6.38 us
  transfers between devices with their start and end apart: 29 -> 35, of which waited for: 20 -> 20; matrix products, arithmetic and copies ran while one was open for 6% -> 5% of each run, Pallas kernels for 10% -> 11%
where the time goes in v5:
time: 211 us; the launch traced here: 210 us
  waiting for transfers between devices  83.5 us (40%)
  starting transfers between devices  57.7 us (27%)
  Pallas kernels  26.8 us (13%)
  blocking collectives  11.8 us (6%)
  other arithmetic  11.6 us (5%)
  local copies, waits for them, and re-layouts  10.6 us (5%)
  matrix products  5.95 us (3%)
    ppermute x28, waiting for transfers between devices, phase(): got = [lax.ppermute(value, *send[1:]) for value, send in zip(values, sends)]  80.2 us
    ppermute x28, starting transfers between devices, phase(): got = [lax.ppermute(value, *send[1:]) for value, send in zip(values, sends)]  43.2 us
    pallas_call x3, Pallas kernels, call(): pl.pallas_call(kernel, grid_spec=pltpu.PrefetchScalarGridSpec(num_scalar_...  17.8 us
    all_to_all x1, blocking collectives, all_sum(): lax.all_to_all(jnp.full((n, 128), value, f32), axis, 0, 0, tiled=True)  11.8 us
    pallas_call x3, Pallas kernels, slots(): pl.pallas_call(kernel, grid_spec=pltpu.PrefetchScalarGridSpec(num_scalar_...  8.93 us
    unnamed x51, local copies, waits for them, and re-layouts  6.38 us
    dot_general x3, matrix products, mdot(): return jnp.dot(a, b, preferred_element_type=f32)  5.95 us
    all_to_all x1, starting transfers between devices, shards(): out_tiles = lax.all_to_all(copies, OWNER, 0, 0, tiled=True)  5.3 us
  transfers between devices with their start and end apart: 35, of which 20 were waited for; matrix products, arithmetic and copies ran while one was open for 5% of the time, Pallas kernels for 11%

profile of v5, /device:TPU:16, one launch (start us, length us, event | category | flops | bytes accessed | tf_op | source)
XLA Modules:
  0.0 210.0 jit_solution(6436361393948294083)
XLA Ops:
  6.1 3.7 %shard_map.38 = bf16[9,256,384]{2,1,0:T(8,128)(2,1)S(1)} custom-call(s32[29]{0:T(128)S(1)} %stack.142.at_ref, bf16[128,4608]{1,0:T(8,128)(2,1)S(1)} %shard_map.37.pick_ref, bf16[128,4608]{1,0:T(8,128)(2,1)S(1)} %collective-permute-done.recv_ref, bf16[128,1024]{1,0:T(8,128)(2,1)S(1)} %multiply_convert_fusion.own_ref, ...), custom_call_target="tpu_custom_call" | custom-call | tf_op jit(solution)/shard_map/pallas_call | solution.py:281
  11.1 5.9 %collective-permute-start.2 = (bf16[256,384]{1,0:T(8,128)(2,1)S(1)}, bf16[256,384]{1,0:T(8,128)(2,1)S(1)}, u32[]{:S(2)}, u32[]{:S(2)}) collective-permute-start(bf16[256,384]{1,0:T(8,128)(2,1)S(1)} %slice_bitcast_fusion), channel_id=1, source_target_pairs={{0,224},{8,40},{32,0},{40,72},{64,32},{72,104},{96,64},{104,136},{... | collective-permute-start | bytes 589832 | tf_op jit(solution)/shard_map/ppermute | solution.py:221
  17.0 2.2 %shard_map.39 = (bf16[3,128,1024]{2,1,0:T(8,128)(2,1)S(1)}, bf16[1,128,1024]{2,1,0:T(8,128)(2,1)S(1)}, bf16[1,128,1024]{2,1,0:T(8,128)(2,1)S(1)}, bf16[1,128,1024]{2,1,0:T(8,128)(2,1)S(1)}) custom-call(s32[29]{0:T(128)S(1)} %stack.142.at_ref, bf16[128,4608]{1,0:T(8,128)(2,1)S(1)} %shard_map.37.pick_ref, bf16[128,4608]{1,0:T(8,128)(2,1)S(1)} %collective-permute-done.recv_ref, ...), custom_call_target="tpu_custom_call" | custom-call | tf_op jit(solution)/shard_map/pallas_call | solution.py:281
  20.4 3.8 %collective-permute-start.3 = (bf16[2,256,384]{2,1,0:T(8,128)(2,1)S(1)}, bf16[2,256,384]{2,1,0:T(8,128)(2,1)S(1)}, u32[]{:S(2)}, u32[]{:S(2)}) collective-permute-start(bf16[2,256,384]{2,1,0:T(8,128)(2,1)S(1)} %add_convert_fusion.5), channel_id=1, source_target_pairs={{0,224},{8,40},{32,0},{40,72},{64,32},{72,104},{96,64},{104,136},{... | collective-permute-start | bytes 1179656 | tf_op jit(solution)/shard_map/ppermute | solution.py:221
  24.5 7.5 %collective-permute-done.4 = bf16[1,128,1024]{2,1,0:T(8,128)(2,1)S(1)} collective-permute-done((bf16[1,128,1024]{2,1,0:T(8,128)(2,1)S(1)}, bf16[1,128,1024]{2,1,0:T(8,128)(2,1)S(1)}, u32[]{:S(2)}, u32[]{:S(2)}) %collective-permute-start.4) | collective-permute-done | bytes 262176 | tf_op jit(solution)/shard_map/ppermute | solution.py:221
  33.7 7.5 %collective-permute-done.6 = bf16[1,128,1024]{2,1,0:T(8,128)(2,1)S(1)} collective-permute-done((bf16[1,128,1024]{2,1,0:T(8,128)(2,1)S(1)}, bf16[1,128,1024]{2,1,0:T(8,128)(2,1)S(1)}, u32[]{:S(2)}, u32[]{:S(2)}) %collective-permute-start.6) | collective-permute-done | bytes 262176 | tf_op jit(solution)/shard_map/ppermute | solution.py:221
  42.8 3.0 %shard_map.40 = (bf16[5,128,1024]{2,1,0:T(8,128)(2,1)S(1)}, bf16[2,128,1024]{2,1,0:T(8,128)(2,1)S(1)}, bf16[1,128,1024]{2,1,0:T(8,128)(2,1)S(1)}, bf16[1,128,102...) custom-call(s32[29]{0:T(128)S(1)} %stack.142.at_ref, bf16[128,4608]{1,0:T(8,128)(2,1)S(1)} %shard_map.37.pick_ref, ...), custom_call_target="tpu_custom_call" | custom-call | tf_op jit(solution)/shard_map/pallas_call | solution.py:281
  45.9 4.4 %collective-permute-done.8 = bf16[1,128,1024]{2,1,0:T(8,128)(2,1)S(1)} collective-permute-done((bf16[1,128,1024]{2,1,0:T(8,128)(2,1)S(1)}, bf16[1,128,1024]{2,1,0:T(8,128)(2,1)S(1)}, u32[]{:S(2)}, u32[]{:S(2)}) %collective-permute-start.8) | collective-permute-done | bytes 262176 | tf_op jit(solution)/shard_map/ppermute | solution.py:221
  52.6 3.0 %collective-permute-start.11 = (bf16[128,1024]{1,0:T(8,128)(2,1)S(1)}, bf16[128,1024]{1,0:T(8,128)(2,1)S(1)}, u32[]{:S(2)}, u32[]{:S(2)}) collective-permute-start(bf16[128,1024]{1,0:T(8,128)(2,1)S(1)} %fusion.11), channel_id=1, source_target_pairs={{0,224},{8,40},{32,0},{40,72},{96,64},{104,136},{128,96},{136,168}... | collective-permute-start | bytes 786440 | tf_op jit(solution)/shard_map/ppermute | solution.py:221
  55.6 6.5 %collective-permute-done.10 = bf16[256,512]{1,0:T(8,128)(2,1)S(1)} collective-permute-done((bf16[256,512]{1,0:T(8,128)(2,1)S(1)}, bf16[256,512]{1,0:T(8,128)(2,1)S(1)}, u32[]{:S(2)}, u32[]{:S(2)}) %collective-permute-start.10) | collective-permute-done | bytes 262176 | tf_op jit(solution)/shard_map/ppermute | solution.py:221
  64.4 3.5 %collective-permute-done.12 = bf16[256,256]{1,0:T(8,128)(2,1)S(1)} collective-permute-done((bf16[256,256]{1,0:T(8,128)(2,1)S(1)}, bf16[256,256]{1,0:T(8,128)(2,1)S(1)}, u32[]{:S(2)}, u32[]{:S(2)}) %collective-permute-start.12) | collective-permute-done | bytes 131104 | tf_op jit(solution)/shard_map/ppermute | solution.py:221
  69.0 5.3 %all-to-all-start = ((bf16[8,256,256]{2,1,0:T(8,128)(2,1)}), bf16[8,256,256]{2,1,0:T(8,128)(2,1)S(1)}, u32[]{:S(2)}, u32[]{:S(2)}) async-start(bf16[8,256,256]{2,1,0:T(8,128)(2,1)} %broadcast_in_dim.21), calls=%async_computation | async-start | bytes 2097152 | tf_op jit(solution)/shard_map/all_to_all | solution.py:341
  76.8 3.7 %collective-permute-start.14 = (bf16[2,128,1024]{2,1,0:T(8,128)(2,1)S(1)}, bf16[2,128,1024]{2,1,0:T(8,128)(2,1)S(1)}, u32[]{:S(2)}, u32[]{:S(2)}) collective-permute-start(bf16[2,128,1024]{2,1,0:T(8,128)(2,1)S(1)} %add_convert_fusion.2), channel_id=1, source_target_pairs={{0,224},{8,40},{40,72},{64,32},{72,104},{96,64},{128,96},{136,168}... | collective-permute-start | bytes 1572872 | tf_op jit(solution)/shard_map/ppermute | solution.py:221
  82.3 7.7 %collective-permute-done.13 = bf16[2,256,256]{2,1,0:T(8,128)(2,1)S(1)} collective-permute-done((bf16[2,256,256]{2,1,0:T(8,128)(2,1)S(1)}, bf16[2,256,256]{2,1,0:T(8,128)(2,1)S(1)}, u32[]{:S(2)}, u32[]{:S(2)}) %collective-permute-start.13) | collective-permute-done | bytes 262176 | tf_op jit(solution)/shard_map/ppermute | solution.py:221
  90.7 8.5 %collective-permute-done.15 = bf16[2,128,1024]{2,1,0:T(8,128)(2,1)} collective-permute-done((bf16[2,128,1024]{2,1,0:T(8,128)(2,1)S(1)}, bf16[2,128,1024]{2,1,0:T(8,128)(2,1)}, u32[]{:S(2)}, u32[]{:S(2)}) %collective-permute-start.15) | collective-permute-done | bytes 524320 | tf_op jit(solution)/shard_map/ppermute | solution.py:221
  99.3 2.1 %collective-permute-start.17 = (bf16[1,128,1024]{2,1,0:T(8,128)(2,1)}, bf16[1,128,1024]{2,1,0:T(8,128)(2,1)S(1)}, u32[]{:S(2)}, u32[]{:S(2)}) collective-permute-start(bf16[1,128,1024]{2,1,0:T(8,128)(2,1)} %copy-done.14), channel_id=1, source_target_pairs={{0,16},{16,0},{1,17},{17,1},{2,18},{18,2},{3,19},{19,3},{4,20},{20... | collective-permute-start | bytes 786440 | tf_op jit(solution)/shard_map/ppermute | solution.py:221
  101.5 4.4 %collective-permute-done.16 = bf16[2,256,256]{2,1,0:T(8,128)(2,1)S(1)} collective-permute-done((bf16[2,256,256]{2,1,0:T(8,128)(2,1)}, bf16[2,256,256]{2,1,0:T(8,128)(2,1)S(1)}, u32[]{:S(2)}, u32[]{:S(2)}) %collective-permute-start.16) | collective-permute-done | bytes 262176 | tf_op jit(solution)/shard_map/ppermute | solution.py:221
  105.9 4.4 %collective-permute-done.17 = bf16[1,128,1024]{2,1,0:T(8,128)(2,1)S(1)} collective-permute-done((bf16[1,128,1024]{2,1,0:T(8,128)(2,1)}, bf16[1,128,1024]{2,1,0:T(8,128)(2,1)S(1)}, u32[]{:S(2)}, u32[]{:S(2)}) %collective-permute-start.17) | collective-permute-done | bytes 262176 | tf_op jit(solution)/shard_map/ppermute | solution.py:221
  114.6 2.1 collective-permute-done.18
  116.7 3.6 %collective-permute-done.19 = bf16[1,128,1024]{2,1,0:T(8,128)(2,1)S(1)} collective-permute-done((bf16[1,128,1024]{2,1,0:T(8,128)(2,1)}, bf16[1,128,1024]{2,1,0:T(8,128)(2,1)S(1)}, u32[]{:S(2)}, u32[]{:S(2)}) %collective-permute-start.19) | collective-permute-done | bytes 262176 | tf_op jit(solution)/shard_map/ppermute | solution.py:221
  123.7 3.2 %collective-permute-done.20 = bf16[1,256,256]{2,1,0:T(8,128)(2,1)S(1)} collective-permute-done((bf16[1,256,256]{2,1,0:T(8,128)(2,1)S(1)}, bf16[1,256,256]{2,1,0:T(8,128)(2,1)S(1)}, u32[]{:S(2)}, u32[]{:S(2)}) %collective-permute-start.20) | collective-permute-done | bytes 131104 | tf_op jit(solution)/shard_map/ppermute | solution.py:221
  129.7 9.8 %collective-permute-done.22 = bf16[2,128,1024]{2,1,0:T(8,128)(2,1)S(1)} collective-permute-done((bf16[2,128,1024]{2,1,0:T(8,128)(2,1)S(1)}, bf16[2,128,1024]{2,1,0:T(8,128)(2,1)S(1)}, u32[]{:S(2)}, u32[]{:S(2)}) %collective-permute-start.22) | collective-permute-done | bytes 524320 | tf_op jit(solution)/shard_map/ppermute | solution.py:221
  139.8 4.1 %collective-permute-start.24 = (bf16[2,128,1024]{2,1,0:T(8,128)(2,1)S(1)}, bf16[2,128,1024]{2,1,0:T(8,128)(2,1)}, u32[]{:S(2)}, u32[]{:S(2)}) collective-permute-start(bf16[2,128,1024]{2,1,0:T(8,128)(2,1)S(1)} %add_convert_fusion), channel_id=1, source_target_pairs={{0,224},{8,40},{32,0},{64,32},{72,104},{104,136},{128,96},{136,168... | collective-permute-start | bytes 1572872 | tf_op jit(solution)/shard_map/ppermute | solution.py:221
  144.0 8.5 %shard_map.41 = bf16[1024,1024]{1,0:T(8,128)(2,1)S(1)} custom-call(s32[2]{0:T(128)S(1)} %pad_add_fusion.1.at_ref, bf16[2,256,256]{2,1,0:T(8,128)(2,1)S(1)} %pad_maximum_fusion.5.shard_ref, bf16[7,256,256]{2,1,0:T(8,128)(2,1)S(1)} %constant_dynamic-update-slice_fusion.own_ref, bf16[7,256,256]{2,1,0:T(8,128)(2,1)S(1)} %collective-permute-done.23.other_ref), custom_call_target="tpu_custom_call" | custom-call | tf_op jit(solution)/shard_map/pallas_call | solution.py:196
  153.1 3.2 %collective-permute-done.25 = bf16[2,128,1024]{2,1,0:T(8,128)(2,1)} collective-permute-done((bf16[2,128,1024]{2,1,0:T(8,128)(2,1)}, bf16[2,128,1024]{2,1,0:T(8,128)(2,1)}, u32[]{:S(2)}, u32[]{:S(2)}) %collective-permute-start.25) | collective-permute-done | bytes 524320 | tf_op jit(solution)/shard_map/ppermute | solution.py:221
  156.3 1.9 convolution_convert_fusion
  160.2 3.1 %collective-permute-start.29 = (bf16[128,512]{1,0:T(8,128)(2,1)S(1)}, bf16[128,512]{1,0:T(8,128)(2,1)}, u32[]{:S(2)}, u32[]{:S(2)}) collective-permute-start(bf16[128,512]{1,0:T(8,128)(2,1)S(1)} %get-tuple-element.136), channel_id=1, source_target_pairs={{0,17},{1,16},{2,19},{3,18},{16,1},{17,0},{18,3},{19,2},{4,21},{5,... | collective-permute-start | bytes 393224 | tf_op jit(solution)/shard_map/ppermute | solution.py:221
  164.6 8.6 %shard_map.42 = bf16[1536,1024]{1,0:T(8,128)(2,1)S(1)} custom-call(s32[1]{0:T(128)} %bitcast.4.at_ref, bf16[8,256,256]{2,1,0:T(8,128)(2,1)S(1)} %copy-done.3, bf16[8,256,256]{2,1,0:T(8,128)(2,1)} %collective-permute-done.26.other_ref), custom_call_target="tpu_custom_call" | custom-call | tf_op jit(solution)/shard_map/pallas_call | solution.py:196
  180.0 2.1 %multiply_reduce_fusion = f32[]{:T(128)} fusion(bf16[1024,512]{1,0:T(8,128)(2,1)S(1)} %bitcast.69, bf16[1536,1024]{1,0:T(8,128)(2,1)S(1)} %shard_map.42), kind=kOutput, calls=%fused_computation | convolution fusion | flops 1074790400 | bytes 3145732 | tf_op jit(solution)/shard_map/dot_general | solution.py:32
  183.3 4.0 %all-to-all-start.1 = ((f32[8,1,128]{2,1,0:T(1,128)}), f32[8,1,128]{2,1,0:T(1,128)S(1)}, u32[]{:S(2)}, u32[]{:S(2)}) async-start(f32[8,1,128]{2,1,0:T(1,128)} %broadcast_in_dim.23), calls=%async_computation.1 | async-start | bytes 8192 | tf_op jit(solution)/shard_map/all_to_all | solution.py:237
  189.3 3.9 %collective-permute-start.31 = (bf16[192,512]{1,0:T(8,128)(2,1)S(1)}, bf16[192,512]{1,0:T(8,128)(2,1)S(1)}, u32[]{:S(2)}, u32[]{:S(2)}) collective-permute-start(bf16[192,512]{1,0:T(8,128)(2,1)S(1)} %slice.187), channel_id=1, source_target_pairs={{0,32},{32,64},{128,160},{160,192},{1,33},{33,65},{129,161},{161,1... | collective-permute-start | bytes 589832 | tf_op jit(solution)/shard_map/ppermute | solution.py:402
  196.2 11.8 %all_to_all.23 = f32[8,1,128]{2,1,0:T(1,128)S(1)} all-to-all(f32[8,1,128]{2,1,0:T(1,128)S(1)} %broadcast_in_dim.24), channel_id=1, replica_groups=mesh['dp_0'=8,'dp_1'=2,'dp_2'=2,'owner_0'=2,'owner_1'=4] {'owner_0','own..., dimensions={0} | all-to-all | bytes 8192 | tf_op jit(solution)/shard_map/all_to_all | solution.py:237
  (143 shorter events, 50.7 us)
Async XLA Ops:
  2.2 3.9 %collective-permute-start = (bf16[128,4608]{1,0:T(8,128)(2,1)S(1)}, bf16[128,4608]{1,0:T(8,128)(2,1)S(1)}, u32[]{:S(2)}, u32[]{:S(2)}) collective-permute-start(bf16[128,4608]{1,0:T(8,128)(2,1)S(1)} %shard_map.37.pick_ref), channel_id=1, source_target_pairs={{0,8},{8,0},{1,9},{9,1},{2,10},{10,2},{3,11},{11,3},{4,12},{12,4},... | collective-permute-start | bytes 3538952 | tf_op jit(solution)/shard_map/ppermute | solution.py:261
  11.1 9.1 %collective-permute-start.2 = (bf16[256,384]{1,0:T(8,128)(2,1)S(1)}, bf16[256,384]{1,0:T(8,128)(2,1)S(1)}, u32[]{:S(2)}, u32[]{:S(2)}) collective-permute-start(bf16[256,384]{1,0:T(8,128)(2,1)S(1)} %slice_bitcast_fusion), channel_id=1, source_target_pairs={{0,224},{8,40},{32,0},{40,72},{64,32},{72,104},{96,64},{104,136},{... | collective-permute-start | bytes 589832 | tf_op jit(solution)/shard_map/ppermute | solution.py:221
  20.4 11.6 %collective-permute-start.3 = (bf16[2,256,384]{2,1,0:T(8,128)(2,1)S(1)}, bf16[2,256,384]{2,1,0:T(8,128)(2,1)S(1)}, u32[]{:S(2)}, u32[]{:S(2)}) collective-permute-start(bf16[2,256,384]{2,1,0:T(8,128)(2,1)S(1)} %add_convert_fusion.5), channel_id=1, source_target_pairs={{0,224},{8,40},{32,0},{40,72},{64,32},{72,104},{96,64},{104,136},{... | collective-permute-start | bytes 1179656 | tf_op jit(solution)/shard_map/ppermute | solution.py:221
  24.1 7.9 %collective-permute-start.4 = (bf16[1,128,1024]{2,1,0:T(8,128)(2,1)S(1)}, bf16[1,128,1024]{2,1,0:T(8,128)(2,1)S(1)}, u32[]{:S(2)}, u32[]{:S(2)}) collective-permute-start(bf16[1,128,1024]{2,1,0:T(8,128)(2,1)S(1)} %get-tuple-element.76), channel_id=1, source_target_pairs={{0,16},{16,0},{1,17},{17,1},{2,18},{18,2},{3,19},{19,3},{4,20},{20... | collective-permute-start | bytes 786440 | tf_op jit(solution)/shard_map/ppermute | solution.py:221
  32.1 9.1 %collective-permute-start.5 = (bf16[2,256,384]{2,1,0:T(8,128)(2,1)S(1)}, bf16[2,256,384]{2,1,0:T(8,128)(2,1)S(1)}, u32[]{:S(2)}, u32[]{:S(2)}) collective-permute-start(bf16[2,256,384]{2,1,0:T(8,128)(2,1)S(1)} %add_convert_fusion.4), channel_id=1, source_target_pairs={{0,224},{8,40},{32,0},{40,72},{64,32},{72,104},{96,64},{104,136},{... | collective-permute-start | bytes 1179656 | tf_op jit(solution)/shard_map/ppermute | solution.py:221
  33.3 7.9 %collective-permute-start.6 = (bf16[1,128,1024]{2,1,0:T(8,128)(2,1)S(1)}, bf16[1,128,1024]{2,1,0:T(8,128)(2,1)S(1)}, u32[]{:S(2)}, u32[]{:S(2)}) collective-permute-start(bf16[1,128,1024]{2,1,0:T(8,128)(2,1)S(1)} %get-tuple-element.80), channel_id=1, source_target_pairs={{0,16},{16,0},{1,17},{17,1},{2,18},{18,2},{3,19},{19,3},{4,20},{20... | collective-permute-start | bytes 786440 | tf_op jit(solution)/shard_map/ppermute | solution.py:221
  41.3 9.1 %collective-permute-start.7 = (bf16[2,256,384]{2,1,0:T(8,128)(2,1)S(1)}, bf16[2,256,384]{2,1,0:T(8,128)(2,1)S(1)}, u32[]{:S(2)}, u32[]{:S(2)}) collective-permute-start(bf16[2,256,384]{2,1,0:T(8,128)(2,1)S(1)} %add_convert_fusion.3), channel_id=1, source_target_pairs={{0,224},{8,40},{32,0},{40,72},{64,32},{72,104},{96,64},{104,136},{... | collective-permute-start | bytes 1179656 | tf_op jit(solution)/shard_map/ppermute | solution.py:221
  42.5 7.9 %collective-permute-start.8 = (bf16[1,128,1024]{2,1,0:T(8,128)(2,1)S(1)}, bf16[1,128,1024]{2,1,0:T(8,128)(2,1)S(1)}, u32[]{:S(2)}, u32[]{:S(2)}) collective-permute-start(bf16[1,128,1024]{2,1,0:T(8,128)(2,1)S(1)} %get-tuple-element.84), channel_id=1, source_target_pairs={{0,16},{16,0},{1,17},{17,1},{2,18},{18,2},{3,19},{19,3},{4,20},{20... | collective-permute-start | bytes 786440 | tf_op jit(solution)/shard_map/ppermute | solution.py:221
  52.2 9.9 %collective-permute-start.10 = (bf16[256,512]{1,0:T(8,128)(2,1)S(1)}, bf16[256,512]{1,0:T(8,128)(2,1)S(1)}, u32[]{:S(2)}, u32[]{:S(2)}) collective-permute-start(bf16[256,512]{1,0:T(8,128)(2,1)S(1)} %add_convert_fusion.9), channel_id=1, source_target_pairs={{0,16},{16,0},{1,17},{17,1},{2,18},{18,2},{3,19},{19,3},{4,20},{20... | collective-permute-start | bytes 786440 | tf_op jit(solution)/shard_map/ppermute | solution.py:221
  52.6 9.5 %collective-permute-start.11 = (bf16[128,1024]{1,0:T(8,128)(2,1)S(1)}, bf16[128,1024]{1,0:T(8,128)(2,1)S(1)}, u32[]{:S(2)}, u32[]{:S(2)}) collective-permute-start(bf16[128,1024]{1,0:T(8,128)(2,1)S(1)} %fusion.11), channel_id=1, source_target_pairs={{0,224},{8,40},{32,0},{40,72},{96,64},{104,136},{128,96},{136,168}... | collective-permute-start | bytes 786440 | tf_op jit(solution)/shard_map/ppermute | solution.py:221
  62.9 5.1 %collective-permute-start.12 = (bf16[256,256]{1,0:T(8,128)(2,1)S(1)}, bf16[256,256]{1,0:T(8,128)(2,1)S(1)}, u32[]{:S(2)}, u32[]{:S(2)}) collective-permute-start(bf16[256,256]{1,0:T(8,128)(2,1)S(1)} %slice.126), channel_id=1, source_target_pairs={{0,1},{1,0},{2,3},{3,2},{4,5},{5,4},{6,7},{7,6},{8,9},{9,8},{10,11... | collective-permute-start | bytes 393224 | tf_op jit(solution)/shard_map/ppermute | solution.py:221
  69.0 30.2 %all-to-all-start = ((bf16[8,256,256]{2,1,0:T(8,128)(2,1)}), bf16[8,256,256]{2,1,0:T(8,128)(2,1)S(1)}, u32[]{:S(2)}, u32[]{:S(2)}) async-start(bf16[8,256,256]{2,1,0:T(8,128)(2,1)} %broadcast_in_dim.21), calls=%async_computation | async-start | bytes 2097152 | tf_op jit(solution)/shard_map/all_to_all | solution.py:341
  76.8 13.2 %collective-permute-start.14 = (bf16[2,128,1024]{2,1,0:T(8,128)(2,1)S(1)}, bf16[2,128,1024]{2,1,0:T(8,128)(2,1)S(1)}, u32[]{:S(2)}, u32[]{:S(2)}) collective-permute-start(bf16[2,128,1024]{2,1,0:T(8,128)(2,1)S(1)} %add_convert_fusion.2), channel_id=1, source_target_pairs={{0,224},{8,40},{40,72},{64,32},{72,104},{96,64},{128,96},{136,168}... | collective-permute-start | bytes 1572872 | tf_op jit(solution)/shard_map/ppermute | solution.py:221
  80.6 18.7 %collective-permute-start.15 = (bf16[2,128,1024]{2,1,0:T(8,128)(2,1)S(1)}, bf16[2,128,1024]{2,1,0:T(8,128)(2,1)}, u32[]{:S(2)}, u32[]{:S(2)}) collective-permute-start(bf16[2,128,1024]{2,1,0:T(8,128)(2,1)S(1)} %copy-done.10), channel_id=1, source_target_pairs={{0,16},{16,0},{1,17},{17,1},{2,18},{18,2},{3,19},{19,3},{4,20},{20... | collective-permute-start | bytes 1572872 | tf_op jit(solution)/shard_map/ppermute | solution.py:221
  82.3 7.7 %collective-permute-start.13 = (bf16[2,256,256]{2,1,0:T(8,128)(2,1)S(1)}, bf16[2,256,256]{2,1,0:T(8,128)(2,1)S(1)}, u32[]{:S(2)}, u32[]{:S(2)}) collective-permute-start(bf16[2,256,256]{2,1,0:T(8,128)(2,1)S(1)} %pad_maximum_fusion.5.shard_ref), channel_id=1, source_target_pairs={{0,224},{8,40},{32,0},{40,72},{64,32},{72,104},{96,64},{104,136},{... | collective-permute-start | bytes 786440 | tf_op jit(solution)/shard_map/ppermute | solution.py:221
  99.2 6.7 %collective-permute-start.16 = (bf16[2,256,256]{2,1,0:T(8,128)(2,1)}, bf16[2,256,256]{2,1,0:T(8,128)(2,1)S(1)}, u32[]{:S(2)}, u32[]{:S(2)}) collective-permute-start(bf16[2,256,256]{2,1,0:T(8,128)(2,1)} %copy-done.18), channel_id=1, source_target_pairs={{0,224},{8,40},{32,0},{40,72},{64,32},{72,104},{96,64},{104,136},{... | collective-permute-start | bytes 786440 | tf_op jit(solution)/shard_map/ppermute | solution.py:221
  99.3 11.0 %collective-permute-start.17 = (bf16[1,128,1024]{2,1,0:T(8,128)(2,1)}, bf16[1,128,1024]{2,1,0:T(8,128)(2,1)S(1)}, u32[]{:S(2)}, u32[]{:S(2)}) collective-permute-start(bf16[1,128,1024]{2,1,0:T(8,128)(2,1)} %copy-done.14), channel_id=1, source_target_pairs={{0,16},{16,0},{1,17},{17,1},{2,18},{18,2},{3,19},{19,3},{4,20},{20... | collective-permute-start | bytes 786440 | tf_op jit(solution)/shard_map/ppermute | solution.py:221
  110.3 6.4 %collective-permute-start.18 = (bf16[2,256,256]{2,1,0:T(8,128)(2,1)S(1)}, bf16[2,256,256]{2,1,0:T(8,128)(2,1)S(1)}, u32[]{:S(2)}, u32[]{:S(2)}) collective-permute-start(bf16[2,256,256]{2,1,0:T(8,128)(2,1)S(1)} %collective-permute-done.16), channel_id=1, source_target_pairs={{0,224},{8,40},{32,0},{40,72},{64,32},{72,104},{96,64},{104,136},{... | collective-permute-start | bytes 786440 | tf_op jit(solution)/shard_map/ppermute | solution.py:221
  111.4 8.9 %collective-permute-start.19 = (bf16[1,128,1024]{2,1,0:T(8,128)(2,1)}, bf16[1,128,1024]{2,1,0:T(8,128)(2,1)S(1)}, u32[]{:S(2)}, u32[]{:S(2)}) collective-permute-start(bf16[1,128,1024]{2,1,0:T(8,128)(2,1)} %copy-done.13), channel_id=1, source_target_pairs={{0,16},{16,0},{1,17},{17,1},{2,18},{18,2},{3,19},{19,3},{4,20},{20... | collective-permute-start | bytes 786440 | tf_op jit(solution)/shard_map/ppermute | solution.py:221
  120.3 8.0 %collective-permute-start.21 = (bf16[1,128,1024]{2,1,0:T(8,128)(2,1)S(1)}, bf16[1,128,1024]{2,1,0:T(8,128)(2,1)S(1)}, u32[]{:S(2)}, u32[]{:S(2)}) collective-permute-start(bf16[1,128,1024]{2,1,0:T(8,128)(2,1)S(1)} %copy-done.12), channel_id=1, source_target_pairs={{0,16},{16,0},{1,17},{17,1},{2,18},{18,2},{3,19},{19,3},{4,20},{20... | collective-permute-start | bytes 786440 | tf_op jit(solution)/shard_map/ppermute | solution.py:221
  121.9 5.0 %collective-permute-start.20 = (bf16[1,256,256]{2,1,0:T(8,128)(2,1)S(1)}, bf16[1,256,256]{2,1,0:T(8,128)(2,1)S(1)}, u32[]{:S(2)}, u32[]{:S(2)}) collective-permute-start(bf16[1,256,256]{2,1,0:T(8,128)(2,1)S(1)} %slice_select_fusion), channel_id=1, source_target_pairs={{0,224},{8,40},{32,0},{40,72},{64,32},{72,104},{96,64},{104,136},{... | collective-permute-start | bytes 393224 | tf_op jit(solution)/shard_map/ppermute | solution.py:221
  128.3 11.2 %collective-permute-start.23 = (bf16[7,256,256]{2,1,0:T(8,128)(2,1)S(1)}, bf16[7,256,256]{2,1,0:T(8,128)(2,1)S(1)}, u32[]{:S(2)}, u32[]{:S(2)}) collective-permute-start(bf16[7,256,256]{2,1,0:T(8,128)(2,1)S(1)} %constant_dynamic-update-slice_fusion.own_ref), channel_id=1, source_target_pairs={{0,8},{8,0},{1,9},{9,1},{2,10},{10,2},{3,11},{11,3},{4,12},{12,4},... | collective-permute-start | bytes 2752520 | tf_op jit(solution)/shard_map/ppermute | solution.py:221
  128.4 11.1 %collective-permute-start.22 = (bf16[2,128,1024]{2,1,0:T(8,128)(2,1)S(1)}, bf16[2,128,1024]{2,1,0:T(8,128)(2,1)S(1)}, u32[]{:S(2)}, u32[]{:S(2)}) collective-permute-start(bf16[2,128,1024]{2,1,0:T(8,128)(2,1)S(1)} %add_convert_fusion.1), channel_id=1, source_target_pairs={{32,0},{40,72},{64,32},{72,104},{96,64},{104,136},{160,128},{168,2... | collective-permute-start | bytes 1572872 | tf_op jit(solution)/shard_map/ppermute | solution.py:221
  139.8 12.7 %collective-permute-start.24 = (bf16[2,128,1024]{2,1,0:T(8,128)(2,1)S(1)}, bf16[2,128,1024]{2,1,0:T(8,128)(2,1)}, u32[]{:S(2)}, u32[]{:S(2)}) collective-permute-start(bf16[2,128,1024]{2,1,0:T(8,128)(2,1)S(1)} %add_convert_fusion), channel_id=1, source_target_pairs={{0,224},{8,40},{32,0},{64,32},{72,104},{104,136},{128,96},{136,168... | collective-permute-start | bytes 1572872 | tf_op jit(solution)/shard_map/ppermute | solution.py:221
  152.5 3.8 %collective-permute-start.26 = (bf16[8,256,256]{2,1,0:T(8,128)(2,1)S(1)}, bf16[8,256,256]{2,1,0:T(8,128)(2,1)}, u32[]{:S(2)}, u32[]{:S(2)}) collective-permute-start(bf16[8,256,256]{2,1,0:T(8,128)(2,1)S(1)} %all-to-all-done.own_ref), channel_id=1, source_target_pairs={{0,8},{8,0},{1,9},{9,1},{2,10},{10,2},{3,11},{11,3},{4,12},{12,4},... | collective-permute-start | bytes 3145736 | tf_op jit(solution)/shard_map/ppermute | solution.py:221
  152.6 3.7 %collective-permute-start.25 = (bf16[2,128,1024]{2,1,0:T(8,128)(2,1)}, bf16[2,128,1024]{2,1,0:T(8,128)(2,1)}, u32[]{:S(2)}, u32[]{:S(2)}) collective-permute-start(bf16[2,128,1024]{2,1,0:T(8,128)(2,1)} %collective-permute-done.24), channel_id=1, source_target_pairs={{0,8},{8,0},{1,9},{9,1},{2,10},{10,2},{3,11},{11,3},{4,12},{12,4},... | collective-permute-start | bytes 1572872 | tf_op jit(solution)/shard_map/ppermute | solution.py:221
  158.3 15.0 %collective-permute-start.27 = (bf16[128,512]{1,0:T(8,128)(2,1)S(1)}, bf16[128,512]{1,0:T(8,128)(2,1)S(1)}, u32[]{:S(2)}, u32[]{:S(2)}) collective-permute-start(bf16[128,512]{1,0:T(8,128)(2,1)S(1)} %get-tuple-element.136), channel_id=1, source_target_pairs={{0,1},{1,0},{2,3},{3,2},{4,5},{5,4},{6,7},{7,6},{8,9},{9,8},{10,11... | collective-permute-start | bytes 393224 | tf_op jit(solution)/shard_map/ppermute | solution.py:221
  160.0 13.3 %collective-permute-start.28 = (bf16[128,512]{1,0:T(8,128)(2,1)S(1)}, bf16[128,512]{1,0:T(8,128)(2,1)}, u32[]{:S(2)}, u32[]{:S(2)}) collective-permute-start(bf16[128,512]{1,0:T(8,128)(2,1)S(1)} %get-tuple-element.135), channel_id=1, source_target_pairs={{0,16},{16,0},{1,17},{17,1},{2,18},{18,2},{3,19},{19,3},{4,20},{20... | collective-permute-start | bytes 393224 | tf_op jit(solution)/shard_map/ppermute | solution.py:221
  160.2 13.0 %collective-permute-start.29 = (bf16[128,512]{1,0:T(8,128)(2,1)S(1)}, bf16[128,512]{1,0:T(8,128)(2,1)}, u32[]{:S(2)}, u32[]{:S(2)}) collective-permute-start(bf16[128,512]{1,0:T(8,128)(2,1)S(1)} %get-tuple-element.136), channel_id=1, source_target_pairs={{0,17},{1,16},{2,19},{3,18},{16,1},{17,0},{18,3},{19,2},{4,21},{5,... | collective-permute-start | bytes 393224 | tf_op jit(solution)/shard_map/ppermute | solution.py:221
  183.3 11.6 %all-to-all-start.1 = ((f32[8,1,128]{2,1,0:T(1,128)}), f32[8,1,128]{2,1,0:T(1,128)S(1)}, u32[]{:S(2)}, u32[]{:S(2)}) async-start(f32[8,1,128]{2,1,0:T(1,128)} %broadcast_in_dim.23), calls=%async_computation.1 | async-start | bytes 8192 | tf_op jit(solution)/shard_map/all_to_all | solution.py:237
  189.3 20.0 %collective-permute-start.31 = (bf16[192,512]{1,0:T(8,128)(2,1)S(1)}, bf16[192,512]{1,0:T(8,128)(2,1)S(1)}, u32[]{:S(2)}, u32[]{:S(2)}) collective-permute-start(bf16[192,512]{1,0:T(8,128)(2,1)S(1)} %slice.187), channel_id=1, source_target_pairs={{0,32},{32,64},{128,160},{160,192},{1,33},{33,65},{129,161},{161,1... | collective-permute-start | bytes 589832 | tf_op jit(solution)/shard_map/ppermute | solution.py:402
  193.2 16.0 %collective-permute-start.32 = (bf16[192,512]{1,0:T(8,128)(2,1)S(1)}, bf16[192,512]{1,0:T(8,128)(2,1)S(1)}, u32[]{:S(2)}, u32[]{:S(2)}) collective-permute-start(bf16[192,512]{1,0:T(8,128)(2,1)S(1)} %slice.187), channel_id=1, source_target_pairs={{96,64},{224,192},{97,65},{225,193},{98,66},{226,194},{99,67},{227... | collective-permute-start | bytes 589832 | tf_op jit(solution)/shard_map/ppermute | solution.py:403
  (27 other events, 310.6 us)

commit v6 on v5

--- a/solution.py
+++ b/solution.py
@@ -65,7 +65,10 @@
         copy.wait()
 
 
-def factor_kernel(out_blocks, at_ref, pick_ref, recv_ref, own_ref, got_ref, part_ref, out_ref, in_ref, sems):
+def factor_kernel(
+    out_blocks, at_ref, pick_ref, recv_ref, own_ref, got_ref,
+    part_ref, first_ref, out_ref, in_ref, sems,
+):
     i = pl.program_id(0)
 
     @pl.when(i == 0)
@@ -75,9 +78,16 @@
     h, plane, block, piece = at_ref[0], at_ref[2 + 3 * i], at_ref[3 + 3 * i], at_ref[4 + 3 * i]
     left = out_ref[:, aligned(block * HALF + piece * PIECE, PIECE)]
     right = out_ref[:, aligned(out_blocks * HALF + block * PIECE, PIECE)]
-    part_ref[0, :, :PIECE] = tdot(left, right).astype(bf16)
     rows = in_ref[:, aligned((2 * h + piece) * PIECE, PIECE)]
-    part_ref[0, :, PIECE:] = tdot(rows, in_ref[:, aligned(plane * 128, 128)]).astype(bf16)
+    tiles = (
+        tdot(left, right).astype(bf16),
+        tdot(rows, in_ref[:, aligned(plane * 128, 128)]).astype(bf16),
+    )
+    for here, ref in ((i == 0, first_ref), (i > 0, part_ref)):
+
+        @pl.when(here)
+        def _():
+            ref[0, :, :PIECE], ref[0, :, PIECE:] = tiles
 
 
 def cross_kernel(base, gives, at_ref, pick_ref, recv_ref, own_ref, got_ref, keep_ref, *refs):
@@ -275,7 +285,7 @@
         table += [plane, 3 * (plane // 4) + plane % 4 - plane % 4 // 2, piece]
     table = numbers(h, yh, *table)
 
-    def slots(kernel, count, block, gives=()):
+    def slots(kernel, count, block, gives, skip=0):
         tokens_in = (pick, recv, normed, normed_recv)
         more = [(len(slots), *block) for slots in gives]
         return pl.pallas_call(
@@ -284,7 +294,7 @@
                 num_scalar_prefetch=1,
                 grid=(count,),
                 in_specs=[pl.BlockSpec(memory_space=pl.ANY) for _ in tokens_in],
-                out_specs=[pl.BlockSpec((1, *block), lambda i, at: (i, 0, 0))]
+                out_specs=[pl.BlockSpec((1, *block), lambda i, at: (jnp.maximum(i - skip, 0), 0, 0))]
                 + [pl.BlockSpec(m, lambda i, at: (0, 0, 0)) for m in more],
                 scratch_shapes=[
                     pltpu.VMEM((2 * here, pick.shape[1]), bf16),
@@ -292,16 +302,17 @@
                     pltpu.SemaphoreType.DMA((4,)),
                 ],
             ),
-            out_shape=[jax.ShapeDtypeStruct(m, bf16) for m in [(count, *block)] + more],
+            out_shape=[jax.ShapeDtypeStruct(m, bf16) for m in [(count - skip, *block)] + more],
             compiler_params=PARAMS,
         )(table, *tokens_in)
 
     def cross_part(base, count, gives):
         return slots(functools.partial(cross_kernel, base, gives), count, (128, TILE), gives)
 
-    (part,) = slots(functools.partial(factor_kernel, out_blocks), 9, (PIECE, PIECE + 128))
+    block = (PIECE, PIECE + 128)
+    part, part_0 = slots(functools.partial(factor_kernel, out_blocks), 9, block, ((0,),), 1)
     keep_a, give_0, give_1, give_2 = cross_part(0, 3, ((0,), (1,), (2,)))
-    keep_b, give_34, give_5, give_6, give_7 = cross_part(3, 5, ((3, 4), (5,), (6,), (7,)))
+    keep_b, *give_b = cross_part(3, 5, ((3,), (4,), (5,), (6,), (7,)))
 
     def to_other_y(value):
         return value, YH, SWAP2
@@ -313,17 +324,17 @@
         nothing = jnp.zeros_like(got)
         return in_order(core, got, nothing)
 
-    (far,) = phase(ring(part[0]))
-    far, y0 = phase(ring(added(part[1:3], widened(far)).astype(bf16)), to_other_y(give_0))
-    far, y1 = phase(ring(added(part[3:5], far).astype(bf16)), to_other_y(give_1))
-    far, y2 = phase(ring(added(part[5:7], far).astype(bf16)), to_other_y(give_2))
+    (far,) = phase(ring(part_0[0]))
+    far, y0 = phase(ring(added(part[0:2], widened(far)).astype(bf16)), to_other_y(give_0))
+    far, y1 = phase(ring(added(part[2:4], far).astype(bf16)), to_other_y(give_1))
+    far, y2 = phase(ring(added(part[4:6], far).astype(bf16)), to_other_y(give_2))
     far, keep_b = lax.optimization_barrier((far, keep_b))
     both_in = jnp.concatenate([far[0, :, PIECE:], far[1, :, PIECE:]], 1)
     out_own = jnp.where(core == 0, far[0, :, :PIECE], far[1, :, :PIECE])
     out_other = jnp.where(core == 0, far[1, :, :PIECE], far[0, :, :PIECE])
     (other,) = phase((jnp.concatenate([out_other, both_in], 1), CORE, SWAP2))
-    here_in = in_order(core, part[7, :, PIECE:], part[8, :, PIECE:])
-    local = jnp.concatenate([part[7, :, :PIECE], here_in[0], here_in[1]], 1)
+    here_in = in_order(core, part[6, :, PIECE:], part[7, :, PIECE:])
+    local = jnp.concatenate([part[6, :, :PIECE], here_in[0], here_in[1]], 1)
     tiles = (added(jnp.concatenate([out_own, both_in], 1), other) + local.astype(f32)).astype(bf16)
     other, far = phase((tiles, YH, SWAP2), ring(added(keep_a[0], y0[0]).astype(bf16), 4, True))
     tiles = added(tiles, other).astype(bf16)
@@ -331,21 +342,21 @@
     copies = jnp.broadcast_to(out_tile[None], (8, PIECE, PIECE))
     (near_in,) = phase((in_tile, X, SWAP_X))
     shard = in_order(h, in_tile, near_in)
-    shard, copies = lax.optimization_barrier((shard, copies))
     both_y = jnp.concatenate([y1, y2])
-    one, far, y34 = phase(
+    one, far, y3 = phase(
         ring(shard),
         ring(added(keep_a[1:3], both_y, widened(far)).astype(bf16), 3, True),
-        to_other_y(give_34),
-    )
+        to_other_y(give_b[0]),
+    )
+    two, y4 = phase(ring(one), to_other_y(give_b[1]))
+    three, y5 = phase(ring(two), to_other_y(give_b[2]))
+    last, y6 = phase(ring(jnp.where(core == 0, three[:1], three[1:])), to_other_y(give_b[3]))
+    in_own = jnp.concatenate([one, two, three, last], 0)
+    in_own, copies = lax.optimization_barrier((in_own, copies))
     out_tiles = lax.all_to_all(copies, OWNER, 0, 0, tiled=True)
-    one, far, y34, out_tiles = lax.optimization_barrier((one, far, y34, out_tiles))
-    two, y5 = phase(ring(one), to_other_y(give_5))
-    three, y6 = phase(ring(two), to_other_y(give_6))
-    last, y7 = phase(ring(jnp.where(core == 0, three[:1], three[1:])), to_other_y(give_7))
-    in_own = jnp.concatenate([one, two, three, last], 0)
+    both_y = jnp.concatenate([y3, y4])
     cross, in_other = phase(
-        ring(added(keep_b[0:2], y34, far).astype(bf16), 2, True), (in_own, CORE, SWAP2)
+        ring(added(keep_b[0:2], both_y, far).astype(bf16), 2, True), (in_own, CORE, SWAP2)
     )
     square = (TILE, TILE)
     in_inverse = call(
@@ -360,7 +371,9 @@
         scratch=[(square, bf16), (square, f32), (square, bf16)],
     )
     both_y = jnp.concatenate([y5, y6])
-    (cross,) = phase(ring(added(keep_b[2:4], both_y, cross).astype(bf16), 1, True))
+    cross, y7 = phase(
+        ring(added(keep_b[2:4], both_y, cross).astype(bf16), 1, True), to_other_y(give_b[4])
+    )
     cross, in_inverse = lax.optimization_barrier((cross, in_inverse))
     other, out_other = phase((cross, CORE, SWAP2), (out_tiles, CORE, SWAP2))
     own, other = [jnp.where(core == 0, a[0], a[1]) for a in (cross, other)]

time: 211 us -> 207 us (0.981)
  waiting for transfers between devices: 83.5 us -> 62.2 us
  starting transfers between devices: 57.7 us -> 70.5 us
  local copies, waits for them, and re-layouts: 10.6 us -> 13.7 us
  matrix products: 5.95 us -> 8.11 us
    ppermute x28 -> x29, waiting for transfers between devices: 80.2 us -> 58.8 us  [phase(): got = [lax.ppermute(value, *send[1:]) for value, send in zip(values, sends)]]
    ppermute x28 -> x29, starting transfers between devices: 43.2 us -> 54.4 us  [phase(): got = [lax.ppermute(value, *send[1:]) for value, send in zip(values, sends)]]
    dot_general x3, matrix products: 5.95 us -> 8.11 us  [mdot(): return jnp.dot(a, b, preferred_element_type=f32)]
    unnamed x51 -> x52, local copies, waits for them, and re-layouts: 6.38 us -> 8.44 us
  transfers between devices with their start and end apart: 35 -> 36, of which waited for: 20 -> 19; matrix products, arithmetic and copies ran while one was open for 5% -> 6% of each run, Pallas kernels for 11% -> 10%
where the time goes in v6:
time: 207 us; the launch traced here: 206 us
  starting transfers between devices  70.5 us (34%)
  waiting for transfers between devices  62.2 us (30%)
  Pallas kernels  25.8 us (12%)
  local copies, waits for them, and re-layouts  13.7 us (7%)
  other arithmetic  12.7 us (6%)
  blocking collectives  10.8 us (5%)
  matrix products  8.11 us (4%)
    ppermute x29, waiting for transfers between devices, phase(): got = [lax.ppermute(value, *send[1:]) for value, send in zip(values, sends)]  58.8 us
    ppermute x29, starting transfers between devices, phase(): got = [lax.ppermute(value, *send[1:]) for value, send in zip(values, sends)]  54.4 us
    pallas_call x3, Pallas kernels, call(): pl.pallas_call(kernel, grid_spec=pltpu.PrefetchScalarGridSpec(num_scalar_...  16.6 us
    all_to_all x1, blocking collectives, all_sum(): lax.all_to_all(jnp.full((n, 128), value, f32), axis, 0, 0, tiled=True)  10.8 us
    pallas_call x3, Pallas kernels, slots(): pl.pallas_call(kernel, grid_spec=pltpu.PrefetchScalarGridSpec(num_scalar_...  9.2 us
    unnamed x52, local copies, waits for them, and re-layouts  8.44 us
    dot_general x3, matrix products, mdot(): return jnp.dot(a, b, preferred_element_type=f32)  8.11 us
    all_to_all x1, starting transfers between devices, all_sum(): lax.all_to_all(jnp.full((n, 128), value, f32), axis, 0, 0, tiled=True)  5.74 us
  transfers between devices with their start and end apart: 36, of which 19 were waited for; matrix products, arithmetic and copies ran while one was open for 6% of the time, Pallas kernels for 10%

profile of v6, /device:TPU:16, one launch (start us, length us, event | category | flops | bytes accessed | tf_op | source)
XLA Modules:
  0.0 205.8 jit_solution(2630777895292618594)
XLA Ops:
  6.1 3.9 %shard_map.38 = (bf16[8,256,384]{2,1,0:T(8,128)(2,1)S(1)}, bf16[1,256,384]{2,1,0:T(8,128)(2,1)S(1)}) custom-call(s32[29]{0:T(128)S(1)} %stack.142.at_ref, bf16[128,4608]{1,0:T(8,128)(2,1)S(1)} %shard_map.37.pick_ref, bf16[128,4608]{1,0:T(8,128)(2,1)S(1)} %collective-permute-done.recv_ref, bf16[128,1024]{1,0:T(8,128)(2,1)S(1)} %multiply_convert_fusion.own_ref, ...), custom_call_target="tpu_custom_call" | custom-call | tf_op jit(solution)/shard_map/pallas_call | solution.py:291
  11.3 5.9 %collective-permute-start.2 = (bf16[256,384]{1,0:T(8,128)(2,1)S(1)}, bf16[256,384]{1,0:T(8,128)(2,1)S(1)}, u32[]{:S(2)}, u32[]{:S(2)}) collective-permute-start(bf16[256,384]{1,0:T(8,128)(2,1)S(1)} %bitcast.68), channel_id=1, source_target_pairs={{0,224},{8,40},{32,0},{40,72},{64,32},{72,104},{96,64},{104,136},{... | collective-permute-start | bytes 589832 | tf_op jit(solution)/shard_map/ppermute | solution.py:231
  17.1 2.2 %shard_map.39 = (bf16[3,128,1024]{2,1,0:T(8,128)(2,1)S(1)}, bf16[1,128,1024]{2,1,0:T(8,128)(2,1)S(1)}, bf16[1,128,1024]{2,1,0:T(8,128)(2,1)S(1)}, bf16[1,128,1024]{2,1,0:T(8,128)(2,1)S(1)}) custom-call(s32[29]{0:T(128)S(1)} %stack.142.at_ref, bf16[128,4608]{1,0:T(8,128)(2,1)S(1)} %shard_map.37.pick_ref, bf16[128,4608]{1,0:T(8,128)(2,1)S(1)} %collective-permute-done.recv_ref, ...), custom_call_target="tpu_custom_call" | custom-call | tf_op jit(solution)/shard_map/pallas_call | solution.py:291
  20.5 3.8 %collective-permute-start.3 = (bf16[2,256,384]{2,1,0:T(8,128)(2,1)S(1)}, bf16[2,256,384]{2,1,0:T(8,128)(2,1)S(1)}, u32[]{:S(2)}, u32[]{:S(2)}) collective-permute-start(bf16[2,256,384]{2,1,0:T(8,128)(2,1)S(1)} %add_convert_fusion.5), channel_id=1, source_target_pairs={{0,224},{8,40},{32,0},{40,72},{64,32},{72,104},{96,64},{104,136},{... | collective-permute-start | bytes 1179656 | tf_op jit(solution)/shard_map/ppermute | solution.py:231
  24.6 7.5 %collective-permute-done.4 = bf16[1,128,1024]{2,1,0:T(8,128)(2,1)S(1)} collective-permute-done((bf16[1,128,1024]{2,1,0:T(8,128)(2,1)S(1)}, bf16[1,128,1024]{2,1,0:T(8,128)(2,1)S(1)}, u32[]{:S(2)}, u32[]{:S(2)}) %collective-permute-start.4) | collective-permute-done | bytes 262176 | tf_op jit(solution)/shard_map/ppermute | solution.py:231
  33.8 7.5 %collective-permute-done.6 = bf16[1,128,1024]{2,1,0:T(8,128)(2,1)S(1)} collective-permute-done((bf16[1,128,1024]{2,1,0:T(8,128)(2,1)S(1)}, bf16[1,128,1024]{2,1,0:T(8,128)(2,1)S(1)}, u32[]{:S(2)}, u32[]{:S(2)}) %collective-permute-start.6) | collective-permute-done | bytes 262176 | tf_op jit(solution)/shard_map/ppermute | solution.py:231
  43.3 3.0 %shard_map.40 = (bf16[5,128,1024]{2,1,0:T(8,128)(2,1)S(1)}, bf16[1,128,1024]{2,1,0:T(8,128)(2,1)S(1)}, bf16[1,128,1024]{2,1,0:T(8,128)(2,1)S(1)}, bf16[1,128,102...) custom-call(s32[29]{0:T(128)S(1)} %stack.142.at_ref, ...), custom_call_target="tpu_custom_call" | custom-call | tf_op jit(solution)/shard_map/pallas_call | solution.py:291
  46.4 4.4 %collective-permute-done.8 = bf16[1,128,1024]{2,1,0:T(8,128)(2,1)S(1)} collective-permute-done((bf16[1,128,1024]{2,1,0:T(8,128)(2,1)S(1)}, bf16[1,128,1024]{2,1,0:T(8,128)(2,1)S(1)}, u32[]{:S(2)}, u32[]{:S(2)}) %collective-permute-start.8) | collective-permute-done | bytes 262176 | tf_op jit(solution)/shard_map/ppermute | solution.py:231
  53.2 3.0 %collective-permute-start.11 = (bf16[128,1024]{1,0:T(8,128)(2,1)S(1)}, bf16[128,1024]{1,0:T(8,128)(2,1)S(1)}, u32[]{:S(2)}, u32[]{:S(2)}) collective-permute-start(bf16[128,1024]{1,0:T(8,128)(2,1)S(1)} %fusion.11), channel_id=1, source_target_pairs={{0,224},{8,40},{32,0},{40,72},{96,64},{104,136},{128,96},{136,168}... | collective-permute-start | bytes 786440 | tf_op jit(solution)/shard_map/ppermute | solution.py:231
  56.2 6.5 %collective-permute-done.10 = bf16[256,512]{1,0:T(8,128)(2,1)S(1)} collective-permute-done((bf16[256,512]{1,0:T(8,128)(2,1)S(1)}, bf16[256,512]{1,0:T(8,128)(2,1)S(1)}, u32[]{:S(2)}, u32[]{:S(2)}) %collective-permute-start.10) | collective-permute-done | bytes 262176 | tf_op jit(solution)/shard_map/ppermute | solution.py:231
  67.9 3.0 %collective-permute-start.14 = (bf16[2,128,1024]{2,1,0:T(8,128)(2,1)S(1)}, bf16[2,128,1024]{2,1,0:T(8,128)(2,1)S(1)}, u32[]{:S(2)}, u32[]{:S(2)}) collective-permute-start(bf16[2,128,1024]{2,1,0:T(8,128)(2,1)S(1)} %add_convert_fusion.2), channel_id=1, source_target_pairs={{0,224},{8,40},{40,72},{64,32},{72,104},{96,64},{128,96},{136,168}... | collective-permute-start | bytes 1572872 | tf_op jit(solution)/shard_map/ppermute | solution.py:231
  72.2 2.2 %collective-permute-start.15 = (bf16[1,128,1024]{2,1,0:T(8,128)(2,1)S(1)}, bf16[1,128,1024]{2,1,0:T(8,128)(2,1)S(1)}, u32[]{:S(2)}, u32[]{:S(2)}) collective-permute-start(bf16[1,128,1024]{2,1,0:T(8,128)(2,1)S(1)} %copy-done.18), channel_id=1, source_target_pairs={{0,16},{16,0},{1,17},{17,1},{2,18},{18,2},{3,19},{19,3},{4,20},{20... | collective-permute-start | bytes 786440 | tf_op jit(solution)/shard_map/ppermute | solution.py:231
  74.5 5.9 %collective-permute-done.13 = bf16[2,256,256]{2,1,0:T(8,128)(2,1)S(1)} collective-permute-done((bf16[2,256,256]{2,1,0:T(8,128)(2,1)S(1)}, bf16[2,256,256]{2,1,0:T(8,128)(2,1)S(1)}, u32[]{:S(2)}, u32[]{:S(2)}) %collective-permute-start.13) | collective-permute-done | bytes 262176 | tf_op jit(solution)/shard_map/ppermute | solution.py:231
  81.4 2.7 %collective-permute-start.16 = (bf16[2,256,256]{2,1,0:T(8,128)(2,1)S(1)}, bf16[2,256,256]{2,1,0:T(8,128)(2,1)S(1)}, u32[]{:S(2)}, u32[]{:S(2)}) collective-permute-start(bf16[2,256,256]{2,1,0:T(8,128)(2,1)S(1)} %collective-permute-done.13), channel_id=1, source_target_pairs={{0,224},{8,40},{32,0},{40,72},{64,32},{72,104},{96,64},{104,136},{... | collective-permute-start | bytes 786440 | tf_op jit(solution)/shard_map/ppermute | solution.py:231
  84.1 3.1 %collective-permute-start.17 = (bf16[1,128,1024]{2,1,0:T(8,128)(2,1)S(1)}, bf16[1,128,1024]{2,1,0:T(8,128)(2,1)S(1)}, u32[]{:S(2)}, u32[]{:S(2)}) collective-permute-start(bf16[1,128,1024]{2,1,0:T(8,128)(2,1)S(1)} %copy-done.16), channel_id=1, source_target_pairs={{0,16},{16,0},{1,17},{17,1},{2,18},{18,2},{3,19},{19,3},{4,20},{20... | collective-permute-start | bytes 786440 | tf_op jit(solution)/shard_map/ppermute | solution.py:231
  88.8 3.2 %collective-permute-done.17 = bf16[1,128,1024]{2,1,0:T(8,128)(2,1)S(1)} collective-permute-done((bf16[1,128,1024]{2,1,0:T(8,128)(2,1)S(1)}, bf16[1,128,1024]{2,1,0:T(8,128)(2,1)S(1)}, u32[]{:S(2)}, u32[]{:S(2)}) %collective-permute-start.17) | collective-permute-done | bytes 262176 | tf_op jit(solution)/shard_map/ppermute | solution.py:231
  92.7 2.5 %collective-permute-start.19 = (bf16[1,128,1024]{2,1,0:T(8,128)(2,1)S(1)}, bf16[1,128,1024]{2,1,0:T(8,128)(2,1)S(1)}, u32[]{:S(2)}, u32[]{:S(2)}) collective-permute-start(bf16[1,128,1024]{2,1,0:T(8,128)(2,1)S(1)} %copy-done.14), channel_id=1, source_target_pairs={{0,16},{16,0},{1,17},{17,1},{2,18},{18,2},{3,19},{19,3},{4,20},{20... | collective-permute-start | bytes 786440 | tf_op jit(solution)/shard_map/ppermute | solution.py:231
  95.2 3.1 %collective-permute-done.18 = bf16[2,256,256]{2,1,0:T(8,128)(2,1)S(1)} collective-permute-done((bf16[2,256,256]{2,1,0:T(8,128)(2,1)S(1)}, bf16[2,256,256]{2,1,0:T(8,128)(2,1)S(1)}, u32[]{:S(2)}, u32[]{:S(2)}) %collective-permute-start.18) | collective-permute-done | bytes 262176 | tf_op jit(solution)/shard_map/ppermute | solution.py:231
  98.4 2.2 %collective-permute-done.19 = bf16[1,128,1024]{2,1,0:T(8,128)(2,1)S(1)} collective-permute-done((bf16[1,128,1024]{2,1,0:T(8,128)(2,1)S(1)}, bf16[1,128,1024]{2,1,0:T(8,128)(2,1)S(1)}, u32[]{:S(2)}, u32[]{:S(2)}) %collective-permute-start.19) | collective-permute-done | bytes 262176 | tf_op jit(solution)/shard_map/ppermute | solution.py:231
  102.2 2.5 %collective-permute-start.21 = (bf16[1,128,1024]{2,1,0:T(8,128)(2,1)S(1)}, bf16[1,128,1024]{2,1,0:T(8,128)(2,1)S(1)}, u32[]{:S(2)}, u32[]{:S(2)}) collective-permute-start(bf16[1,128,1024]{2,1,0:T(8,128)(2,1)S(1)} %copy-done.12), channel_id=1, source_target_pairs={{0,16},{16,0},{1,17},{17,1},{2,18},{18,2},{3,19},{19,3},{4,20},{20... | collective-permute-start | bytes 786440 | tf_op jit(solution)/shard_map/ppermute | solution.py:231
  106.9 3.2 %collective-permute-done.21 = bf16[1,128,1024]{2,1,0:T(8,128)(2,1)S(1)} collective-permute-done((bf16[1,128,1024]{2,1,0:T(8,128)(2,1)S(1)}, bf16[1,128,1024]{2,1,0:T(8,128)(2,1)S(1)}, u32[]{:S(2)}, u32[]{:S(2)}) %collective-permute-start.21) | collective-permute-done | bytes 262176 | tf_op jit(solution)/shard_map/ppermute | solution.py:231
  113.1 5.1 %all-to-all-start = ((bf16[8,256,256]{2,1,0:T(8,128)(2,1)}), bf16[8,256,256]{2,1,0:T(8,128)(2,1)S(1)}, u32[]{:S(2)}, u32[]{:S(2)}) async-start(bf16[8,256,256]{2,1,0:T(8,128)(2,1)} %broadcast_in_dim.22), calls=%async_computation | async-start | bytes 2097152 | tf_op jit(solution)/shard_map/all_to_all | solution.py:356
  118.3 5.0 %collective-permute-done.22 = bf16[2,128,1024]{2,1,0:T(8,128)(2,1)} collective-permute-done((bf16[2,128,1024]{2,1,0:T(8,128)(2,1)}, bf16[2,128,1024]{2,1,0:T(8,128)(2,1)}, u32[]{:S(2)}, u32[]{:S(2)}) %collective-permute-start.22) | collective-permute-done | bytes 524320 | tf_op jit(solution)/shard_map/ppermute | solution.py:231
  124.9 7.9 %collective-permute-start.24 = (bf16[2,128,1024]{2,1,0:T(8,128)(2,1)S(1)}, bf16[2,128,1024]{2,1,0:T(8,128)(2,1)}, u32[]{:S(2)}, u32[]{:S(2)}) collective-permute-start(bf16[2,128,1024]{2,1,0:T(8,128)(2,1)S(1)} %add_convert_fusion), channel_id=1, source_target_pairs={{0,224},{8,40},{32,0},{64,32},{72,104},{104,136},{128,96},{136,168... | collective-permute-start | bytes 1572872 | tf_op jit(solution)/shard_map/ppermute | solution.py:231
  134.9 8.5 %shard_map.41 = bf16[1024,1024]{1,0:T(8,128)(2,1)S(1)} custom-call(s32[2]{0:T(128)S(1)} %pad_add_fusion.1.at_ref, bf16[2,256,256]{2,1,0:T(8,128)(2,1)S(1)} %pad_maximum_fusion.6.shard_ref, bf16[7,256,256]{2,1,0:T(8,128)(2,1)S(1)} %pad_maximum_fusion.own_ref, bf16[7,256,256]{2,1,0:T(8,128)(2,1)S(1)} %collective-permute-done.23.other_ref), custom_call_target="tpu_custom_call" | custom-call | tf_op jit(solution)/shard_map/pallas_call | solution.py:206
  146.0 3.1 %collective-permute-done.26 = bf16[2,128,1024]{2,1,0:T(8,128)(2,1)S(1)} collective-permute-done((bf16[2,128,1024]{2,1,0:T(8,128)(2,1)}, bf16[2,128,1024]{2,1,0:T(8,128)(2,1)S(1)}, u32[]{:S(2)}, u32[]{:S(2)}) %collective-permute-start.26) | collective-permute-done | bytes 524320 | tf_op jit(solution)/shard_map/ppermute | solution.py:231
  149.1 2.9 %convolution_convert_fusion = bf16[128,1024]{1,0:T(8,128)(2,1)S(1)} fusion(bf16[1024,1024]{1,0:T(8,128)(2,1)} %copy-done.2, bf16[1,128,1024]{2,1,0:T(8,128)(2,1)} %copy-done.25, bf16[5,128,1024]{2,1,0:T(8,128)(2,1)} %copy-done.8, bf16[2,128,1024]{2,1,0:T(8,128)(2,1)S(1)} %collective-permute-done.26, bf16[2,128,1024]{2,1,0:T(8,128)(2,1)} %collective-permute-done.24, ...), kind=kOutput, calls=%fused_computation.4 | convolution fusion | flops 269877248 | bytes 3932161 | tf_op jit(solution)/shard_map/dot_general | solution.py:32
  159.6 7.4 %shard_map.42 = bf16[1536,1024]{1,0:T(8,128)(2,1)S(1)} custom-call(s32[1]{0:T(128)} %bitcast.4.at_ref, bf16[8,256,256]{2,1,0:T(8,128)(2,1)S(1)} %copy-done.1, bf16[8,256,256]{2,1,0:T(8,128)(2,1)S(1)} %copy-done.7), custom_call_target="tpu_custom_call" | custom-call | tf_op jit(solution)/shard_map/pallas_call | solution.py:206
  173.7 3.3 %multiply_reduce_fusion = f32[]{:T(128)} fusion(bf16[1024,512]{1,0:T(8,128)(2,1)} %bitcast.39, bf16[1536,1024]{1,0:T(8,128)(2,1)S(1)} %shard_map.42), kind=kOutput, calls=%fused_computation | convolution fusion | flops 1074790400 | bytes 3145732 | tf_op jit(solution)/shard_map/dot_general | solution.py:32
  178.3 5.7 %all-to-all-start.1 = ((f32[8,1,128]{2,1,0:T(1,128)}), f32[8,1,128]{2,1,0:T(1,128)S(1)}, u32[]{:S(2)}, u32[]{:S(2)}) async-start(f32[8,1,128]{2,1,0:T(1,128)} %broadcast_in_dim.23), calls=%async_computation.1 | async-start | bytes 8192 | tf_op jit(solution)/shard_map/all_to_all | solution.py:247
  186.0 3.9 %collective-permute-start.32 = (bf16[192,512]{1,0:T(8,128)(2,1)S(1)}, bf16[192,512]{1,0:T(8,128)(2,1)S(1)}, u32[]{:S(2)}, u32[]{:S(2)}) collective-permute-start(bf16[192,512]{1,0:T(8,128)(2,1)S(1)} %slice.175), channel_id=1, source_target_pairs={{0,32},{32,64},{128,160},{160,192},{1,33},{33,65},{129,161},{161,1... | collective-permute-start | bytes 589832 | tf_op jit(solution)/shard_map/ppermute | solution.py:415
  192.9 10.8 %all_to_all.23 = f32[8,1,128]{2,1,0:T(1,128)S(1)} all-to-all(f32[8,1,128]{2,1,0:T(1,128)S(1)} %broadcast_in_dim.24), channel_id=1, replica_groups=mesh['dp_0'=8,'dp_1'=2,'dp_2'=2,'owner_0'=2,'owner_1'=4] {'owner_0','own..., dimensions={0} | all-to-all | bytes 8192 | tf_op jit(solution)/shard_map/all_to_all | solution.py:247
  (145 shorter events, 58.4 us)
Async XLA Ops:
  2.2 3.9 %collective-permute-start = (bf16[128,4608]{1,0:T(8,128)(2,1)S(1)}, bf16[128,4608]{1,0:T(8,128)(2,1)S(1)}, u32[]{:S(2)}, u32[]{:S(2)}) collective-permute-start(bf16[128,4608]{1,0:T(8,128)(2,1)S(1)} %shard_map.37.pick_ref), channel_id=1, source_target_pairs={{0,8},{8,0},{1,9},{9,1},{2,10},{10,2},{3,11},{11,3},{4,12},{12,4},... | collective-permute-start | bytes 3538952 | tf_op jit(solution)/shard_map/ppermute | solution.py:271
  11.3 9.1 %collective-permute-start.2 = (bf16[256,384]{1,0:T(8,128)(2,1)S(1)}, bf16[256,384]{1,0:T(8,128)(2,1)S(1)}, u32[]{:S(2)}, u32[]{:S(2)}) collective-permute-start(bf16[256,384]{1,0:T(8,128)(2,1)S(1)} %bitcast.68), channel_id=1, source_target_pairs={{0,224},{8,40},{32,0},{40,72},{64,32},{72,104},{96,64},{104,136},{... | collective-permute-start | bytes 589832 | tf_op jit(solution)/shard_map/ppermute | solution.py:231
  20.5 11.6 %collective-permute-start.3 = (bf16[2,256,384]{2,1,0:T(8,128)(2,1)S(1)}, bf16[2,256,384]{2,1,0:T(8,128)(2,1)S(1)}, u32[]{:S(2)}, u32[]{:S(2)}) collective-permute-start(bf16[2,256,384]{2,1,0:T(8,128)(2,1)S(1)} %add_convert_fusion.5), channel_id=1, source_target_pairs={{0,224},{8,40},{32,0},{40,72},{64,32},{72,104},{96,64},{104,136},{... | collective-permute-start | bytes 1179656 | tf_op jit(solution)/shard_map/ppermute | solution.py:231
  24.3 7.9 %collective-permute-start.4 = (bf16[1,128,1024]{2,1,0:T(8,128)(2,1)S(1)}, bf16[1,128,1024]{2,1,0:T(8,128)(2,1)S(1)}, u32[]{:S(2)}, u32[]{:S(2)}) collective-permute-start(bf16[1,128,1024]{2,1,0:T(8,128)(2,1)S(1)} %get-tuple-element.81), channel_id=1, source_target_pairs={{0,16},{16,0},{1,17},{17,1},{2,18},{18,2},{3,19},{19,3},{4,20},{20... | collective-permute-start | bytes 786440 | tf_op jit(solution)/shard_map/ppermute | solution.py:231
  32.2 9.8 %collective-permute-start.5 = (bf16[2,256,384]{2,1,0:T(8,128)(2,1)S(1)}, bf16[2,256,384]{2,1,0:T(8,128)(2,1)S(1)}, u32[]{:S(2)}, u32[]{:S(2)}) collective-permute-start(bf16[2,256,384]{2,1,0:T(8,128)(2,1)S(1)} %add_convert_fusion.4), channel_id=1, source_target_pairs={{0,224},{8,40},{32,0},{40,72},{64,32},{72,104},{96,64},{104,136},{... | collective-permute-start | bytes 1179656 | tf_op jit(solution)/shard_map/ppermute | solution.py:231
  33.4 7.9 %collective-permute-start.6 = (bf16[1,128,1024]{2,1,0:T(8,128)(2,1)S(1)}, bf16[1,128,1024]{2,1,0:T(8,128)(2,1)S(1)}, u32[]{:S(2)}, u32[]{:S(2)}) collective-permute-start(bf16[1,128,1024]{2,1,0:T(8,128)(2,1)S(1)} %get-tuple-element.85), channel_id=1, source_target_pairs={{0,16},{16,0},{1,17},{17,1},{2,18},{18,2},{3,19},{19,3},{4,20},{20... | collective-permute-start | bytes 786440 | tf_op jit(solution)/shard_map/ppermute | solution.py:231
  42.1 8.8 %collective-permute-start.7 = (bf16[2,256,384]{2,1,0:T(8,128)(2,1)S(1)}, bf16[2,256,384]{2,1,0:T(8,128)(2,1)S(1)}, u32[]{:S(2)}, u32[]{:S(2)}) collective-permute-start(bf16[2,256,384]{2,1,0:T(8,128)(2,1)S(1)} %add_convert_fusion.3), channel_id=1, source_target_pairs={{0,224},{8,40},{32,0},{40,72},{64,32},{72,104},{96,64},{104,136},{... | collective-permute-start | bytes 1179656 | tf_op jit(solution)/shard_map/ppermute | solution.py:231
  43.0 7.9 %collective-permute-start.8 = (bf16[1,128,1024]{2,1,0:T(8,128)(2,1)S(1)}, bf16[1,128,1024]{2,1,0:T(8,128)(2,1)S(1)}, u32[]{:S(2)}, u32[]{:S(2)}) collective-permute-start(bf16[1,128,1024]{2,1,0:T(8,128)(2,1)S(1)} %get-tuple-element.89), channel_id=1, source_target_pairs={{0,16},{16,0},{1,17},{17,1},{2,18},{18,2},{3,19},{19,3},{4,20},{20... | collective-permute-start | bytes 786440 | tf_op jit(solution)/shard_map/ppermute | solution.py:231
  52.7 9.9 %collective-permute-start.10 = (bf16[256,512]{1,0:T(8,128)(2,1)S(1)}, bf16[256,512]{1,0:T(8,128)(2,1)S(1)}, u32[]{:S(2)}, u32[]{:S(2)}) collective-permute-start(bf16[256,512]{1,0:T(8,128)(2,1)S(1)} %add_convert_fusion.9), channel_id=1, source_target_pairs={{0,16},{16,0},{1,17},{17,1},{2,18},{18,2},{3,19},{19,3},{4,20},{20... | collective-permute-start | bytes 786440 | tf_op jit(solution)/shard_map/ppermute | solution.py:231
  53.2 9.5 %collective-permute-start.11 = (bf16[128,1024]{1,0:T(8,128)(2,1)S(1)}, bf16[128,1024]{1,0:T(8,128)(2,1)S(1)}, u32[]{:S(2)}, u32[]{:S(2)}) collective-permute-start(bf16[128,1024]{1,0:T(8,128)(2,1)S(1)} %fusion.11), channel_id=1, source_target_pairs={{0,224},{8,40},{32,0},{40,72},{96,64},{104,136},{128,96},{136,168}... | collective-permute-start | bytes 786440 | tf_op jit(solution)/shard_map/ppermute | solution.py:231
  62.8 5.1 %collective-permute-start.12 = (bf16[256,256]{1,0:T(8,128)(2,1)S(1)}, bf16[256,256]{1,0:T(8,128)(2,1)S(1)}, u32[]{:S(2)}, u32[]{:S(2)}) collective-permute-start(bf16[256,256]{1,0:T(8,128)(2,1)S(1)} %slice.115), channel_id=1, source_target_pairs={{0,1},{1,0},{2,3},{3,2},{4,5},{5,4},{6,7},{7,6},{8,9},{9,8},{10,11... | collective-permute-start | bytes 393224 | tf_op jit(solution)/shard_map/ppermute | solution.py:231
  67.9 13.5 %collective-permute-start.14 = (bf16[2,128,1024]{2,1,0:T(8,128)(2,1)S(1)}, bf16[2,128,1024]{2,1,0:T(8,128)(2,1)S(1)}, u32[]{:S(2)}, u32[]{:S(2)}) collective-permute-start(bf16[2,128,1024]{2,1,0:T(8,128)(2,1)S(1)} %add_convert_fusion.2), channel_id=1, source_target_pairs={{0,224},{8,40},{40,72},{64,32},{72,104},{96,64},{128,96},{136,168}... | collective-permute-start | bytes 1572872 | tf_op jit(solution)/shard_map/ppermute | solution.py:231
  70.9 9.5 %collective-permute-start.13 = (bf16[2,256,256]{2,1,0:T(8,128)(2,1)S(1)}, bf16[2,256,256]{2,1,0:T(8,128)(2,1)S(1)}, u32[]{:S(2)}, u32[]{:S(2)}) collective-permute-start(bf16[2,256,256]{2,1,0:T(8,128)(2,1)S(1)} %pad_maximum_fusion.6.shard_ref), channel_id=1, source_target_pairs={{0,224},{8,40},{32,0},{40,72},{64,32},{72,104},{96,64},{104,136},{... | collective-permute-start | bytes 786440 | tf_op jit(solution)/shard_map/ppermute | solution.py:231
  72.2 9.2 %collective-permute-start.15 = (bf16[1,128,1024]{2,1,0:T(8,128)(2,1)S(1)}, bf16[1,128,1024]{2,1,0:T(8,128)(2,1)S(1)}, u32[]{:S(2)}, u32[]{:S(2)}) collective-permute-start(bf16[1,128,1024]{2,1,0:T(8,128)(2,1)S(1)} %copy-done.18), channel_id=1, source_target_pairs={{0,16},{16,0},{1,17},{17,1},{2,18},{18,2},{3,19},{19,3},{4,20},{20... | collective-permute-start | bytes 786440 | tf_op jit(solution)/shard_map/ppermute | solution.py:231
  81.4 7.3 %collective-permute-start.16 = (bf16[2,256,256]{2,1,0:T(8,128)(2,1)S(1)}, bf16[2,256,256]{2,1,0:T(8,128)(2,1)S(1)}, u32[]{:S(2)}, u32[]{:S(2)}) collective-permute-start(bf16[2,256,256]{2,1,0:T(8,128)(2,1)S(1)} %collective-permute-done.13), channel_id=1, source_target_pairs={{0,224},{8,40},{32,0},{40,72},{64,32},{72,104},{96,64},{104,136},{... | collective-permute-start | bytes 786440 | tf_op jit(solution)/shard_map/ppermute | solution.py:231
  84.1 7.9 %collective-permute-start.17 = (bf16[1,128,1024]{2,1,0:T(8,128)(2,1)S(1)}, bf16[1,128,1024]{2,1,0:T(8,128)(2,1)S(1)}, u32[]{:S(2)}, u32[]{:S(2)}) collective-permute-start(bf16[1,128,1024]{2,1,0:T(8,128)(2,1)S(1)} %copy-done.16), channel_id=1, source_target_pairs={{0,16},{16,0},{1,17},{17,1},{2,18},{18,2},{3,19},{19,3},{4,20},{20... | collective-permute-start | bytes 786440 | tf_op jit(solution)/shard_map/ppermute | solution.py:231
  92.0 6.4 %collective-permute-start.18 = (bf16[2,256,256]{2,1,0:T(8,128)(2,1)S(1)}, bf16[2,256,256]{2,1,0:T(8,128)(2,1)S(1)}, u32[]{:S(2)}, u32[]{:S(2)}) collective-permute-start(bf16[2,256,256]{2,1,0:T(8,128)(2,1)S(1)} %collective-permute-done.16), channel_id=1, source_target_pairs={{0,224},{8,40},{32,0},{40,72},{64,32},{72,104},{96,64},{104,136},{... | collective-permute-start | bytes 786440 | tf_op jit(solution)/shard_map/ppermute | solution.py:231
  92.7 7.9 %collective-permute-start.19 = (bf16[1,128,1024]{2,1,0:T(8,128)(2,1)S(1)}, bf16[1,128,1024]{2,1,0:T(8,128)(2,1)S(1)}, u32[]{:S(2)}, u32[]{:S(2)}) collective-permute-start(bf16[1,128,1024]{2,1,0:T(8,128)(2,1)S(1)} %copy-done.14), channel_id=1, source_target_pairs={{0,16},{16,0},{1,17},{17,1},{2,18},{18,2},{3,19},{19,3},{4,20},{20... | collective-permute-start | bytes 786440 | tf_op jit(solution)/shard_map/ppermute | solution.py:231
  100.6 6.3 %collective-permute-start.20 = (bf16[1,256,256]{2,1,0:T(8,128)(2,1)S(1)}, bf16[1,256,256]{2,1,0:T(8,128)(2,1)S(1)}, u32[]{:S(2)}, u32[]{:S(2)}) collective-permute-start(bf16[1,256,256]{2,1,0:T(8,128)(2,1)S(1)} %slice_select_fusion), channel_id=1, source_target_pairs={{0,224},{8,40},{32,0},{40,72},{64,32},{72,104},{96,64},{104,136},{... | collective-permute-start | bytes 393224 | tf_op jit(solution)/shard_map/ppermute | solution.py:231
  102.2 7.9 %collective-permute-start.21 = (bf16[1,128,1024]{2,1,0:T(8,128)(2,1)S(1)}, bf16[1,128,1024]{2,1,0:T(8,128)(2,1)S(1)}, u32[]{:S(2)}, u32[]{:S(2)}) collective-permute-start(bf16[1,128,1024]{2,1,0:T(8,128)(2,1)S(1)} %copy-done.12), channel_id=1, source_target_pairs={{0,16},{16,0},{1,17},{17,1},{2,18},{18,2},{3,19},{19,3},{4,20},{20... | collective-permute-start | bytes 786440 | tf_op jit(solution)/shard_map/ppermute | solution.py:231
  111.9 11.4 %collective-permute-start.23 = (bf16[7,256,256]{2,1,0:T(8,128)(2,1)S(1)}, bf16[7,256,256]{2,1,0:T(8,128)(2,1)S(1)}, u32[]{:S(2)}, u32[]{:S(2)}) collective-permute-start(bf16[7,256,256]{2,1,0:T(8,128)(2,1)S(1)} %pad_maximum_fusion.own_ref), channel_id=1, source_target_pairs={{0,8},{8,0},{1,9},{9,1},{2,10},{10,2},{3,11},{11,3},{4,12},{12,4},... | collective-permute-start | bytes 2752520 | tf_op jit(solution)/shard_map/ppermute | solution.py:231
  111.9 11.4 %collective-permute-start.22 = (bf16[2,128,1024]{2,1,0:T(8,128)(2,1)}, bf16[2,128,1024]{2,1,0:T(8,128)(2,1)}, u32[]{:S(2)}, u32[]{:S(2)}) collective-permute-start(bf16[2,128,1024]{2,1,0:T(8,128)(2,1)} %add_convert_fusion.1), channel_id=1, source_target_pairs={{32,0},{40,72},{64,32},{72,104},{96,64},{104,136},{160,128},{168,2... | collective-permute-start | bytes 1572872 | tf_op jit(solution)/shard_map/ppermute | solution.py:231
  113.1 32.3 %all-to-all-start = ((bf16[8,256,256]{2,1,0:T(8,128)(2,1)}), bf16[8,256,256]{2,1,0:T(8,128)(2,1)S(1)}, u32[]{:S(2)}, u32[]{:S(2)}) async-start(bf16[8,256,256]{2,1,0:T(8,128)(2,1)} %broadcast_in_dim.22), calls=%async_computation | async-start | bytes 2097152 | tf_op jit(solution)/shard_map/all_to_all | solution.py:356
  124.9 20.5 %collective-permute-start.24 = (bf16[2,128,1024]{2,1,0:T(8,128)(2,1)S(1)}, bf16[2,128,1024]{2,1,0:T(8,128)(2,1)}, u32[]{:S(2)}, u32[]{:S(2)}) collective-permute-start(bf16[2,128,1024]{2,1,0:T(8,128)(2,1)S(1)} %add_convert_fusion), channel_id=1, source_target_pairs={{0,224},{8,40},{32,0},{64,32},{72,104},{104,136},{128,96},{136,168... | collective-permute-start | bytes 1572872 | tf_op jit(solution)/shard_map/ppermute | solution.py:231
  132.8 11.9 %collective-permute-start.25 = (bf16[1,128,1024]{2,1,0:T(8,128)(2,1)S(1)}, bf16[1,128,1024]{2,1,0:T(8,128)(2,1)S(1)}, u32[]{:S(2)}, u32[]{:S(2)}) collective-permute-start(bf16[1,128,1024]{2,1,0:T(8,128)(2,1)S(1)} %get-tuple-element.130), channel_id=1, source_target_pairs={{0,16},{16,0},{1,17},{17,1},{2,18},{18,2},{3,19},{19,3},{4,20},{20... | collective-permute-start | bytes 786440 | tf_op jit(solution)/shard_map/ppermute | solution.py:231
  145.4 3.7 %collective-permute-start.27 = (bf16[8,256,256]{2,1,0:T(8,128)(2,1)S(1)}, bf16[8,256,256]{2,1,0:T(8,128)(2,1)S(1)}, u32[]{:S(2)}, u32[]{:S(2)}) collective-permute-start(bf16[8,256,256]{2,1,0:T(8,128)(2,1)S(1)} %all-to-all-done.own_ref), channel_id=1, source_target_pairs={{0,8},{8,0},{1,9},{9,1},{2,10},{10,2},{3,11},{11,3},{4,12},{12,4},... | collective-permute-start | bytes 3145736 | tf_op jit(solution)/shard_map/ppermute | solution.py:231
  152.0 15.0 %collective-permute-start.28 = (bf16[128,512]{1,0:T(8,128)(2,1)S(1)}, bf16[128,512]{1,0:T(8,128)(2,1)S(1)}, u32[]{:S(2)}, u32[]{:S(2)}) collective-permute-start(bf16[128,512]{1,0:T(8,128)(2,1)S(1)} %get-tuple-element.142), channel_id=1, source_target_pairs={{0,1},{1,0},{2,3},{3,2},{4,5},{5,4},{6,7},{7,6},{8,9},{9,8},{10,11... | collective-permute-start | bytes 393224 | tf_op jit(solution)/shard_map/ppermute | solution.py:231
  153.6 13.4 %collective-permute-start.29 = (bf16[128,512]{1,0:T(8,128)(2,1)S(1)}, bf16[128,512]{1,0:T(8,128)(2,1)}, u32[]{:S(2)}, u32[]{:S(2)}) collective-permute-start(bf16[128,512]{1,0:T(8,128)(2,1)S(1)} %get-tuple-element.141), channel_id=1, source_target_pairs={{0,16},{16,0},{1,17},{17,1},{2,18},{18,2},{3,19},{19,3},{4,20},{20... | collective-permute-start | bytes 393224 | tf_op jit(solution)/shard_map/ppermute | solution.py:231
  155.2 11.9 %collective-permute-start.30 = (bf16[128,512]{1,0:T(8,128)(2,1)S(1)}, bf16[128,512]{1,0:T(8,128)(2,1)}, u32[]{:S(2)}, u32[]{:S(2)}) collective-permute-start(bf16[128,512]{1,0:T(8,128)(2,1)S(1)} %get-tuple-element.142), channel_id=1, source_target_pairs={{0,17},{1,16},{2,19},{3,18},{16,1},{17,0},{18,3},{19,2},{4,21},{5,... | collective-permute-start | bytes 393224 | tf_op jit(solution)/shard_map/ppermute | solution.py:231
  178.3 13.3 %all-to-all-start.1 = ((f32[8,1,128]{2,1,0:T(1,128)}), f32[8,1,128]{2,1,0:T(1,128)S(1)}, u32[]{:S(2)}, u32[]{:S(2)}) async-start(f32[8,1,128]{2,1,0:T(1,128)} %broadcast_in_dim.23), calls=%async_computation.1 | async-start | bytes 8192 | tf_op jit(solution)/shard_map/all_to_all | solution.py:247
  186.0 19.0 %collective-permute-start.32 = (bf16[192,512]{1,0:T(8,128)(2,1)S(1)}, bf16[192,512]{1,0:T(8,128)(2,1)S(1)}, u32[]{:S(2)}, u32[]{:S(2)}) collective-permute-start(bf16[192,512]{1,0:T(8,128)(2,1)S(1)} %slice.175), channel_id=1, source_target_pairs={{0,32},{32,64},{128,160},{160,192},{1,33},{33,65},{129,161},{161,1... | collective-permute-start | bytes 589832 | tf_op jit(solution)/shard_map/ppermute | solution.py:415
  189.9 15.1 %collective-permute-start.33 = (bf16[192,512]{1,0:T(8,128)(2,1)S(1)}, bf16[192,512]{1,0:T(8,128)(2,1)S(1)}, u32[]{:S(2)}, u32[]{:S(2)}) collective-permute-start(bf16[192,512]{1,0:T(8,128)(2,1)S(1)} %slice.175), channel_id=1, source_target_pairs={{96,64},{224,192},{97,65},{225,193},{98,66},{226,194},{99,67},{227... | collective-permute-start | bytes 589832 | tf_op jit(solution)/shard_map/ppermute | solution.py:416
  (30 other events, 216.8 us)

commit v7 on v6

--- a/solution.py
+++ b/solution.py
@@ -16,7 +16,7 @@
 OWNER = (YL, X)
 DAMPING = 0.1
 bf16, f32 = jnp.bfloat16, jnp.float32
-PARAMS = pltpu.CompilerParams(vmem_limit_bytes=48 * 1024 * 1024)
+MIB = 1024 * 1024
 
 AWAY = (4, 3, 3, 2, 2, 1, 1, 0, 0)
 SWAP2 = [(0, 1), (1, 0)]
@@ -114,32 +114,23 @@
                 ref[n] = give
 
 
-def scale_of(tokens, sums_ref):
-    largest = jnp.zeros((), f32)
-    for r in range(4):
-        rows = matrix_rows(tokens, sums_ref, r * PIECE)
-        largest = jnp.maximum(largest, jnp.max(jnp.sum(jnp.abs(rows), axis=1)))
-    return 1.0 / largest
-
-
-def eye_rows(start, count):
-    row = lax.broadcasted_iota(jnp.int32, (count, TILE), 0) + start
-    return (row == lax.broadcasted_iota(jnp.int32, (count, TILE), 1)).astype(f32)
-
-
-def matrix_rows(tokens, sums_ref, start):
-    return sums_ref[start : start + PIECE, :].astype(f32) / tokens + DAMPING * eye_rows(start, PIECE)
-
-
-def split_factor(tokens, sums_ref, first_ref, low_ref, offset):
-    scale = scale_of(tokens, sums_ref)
+def split_factor(tokens, sums_ref, first_ref, low_ref):
+    row = lax.broadcasted_iota(jnp.int32, (PIECE, PIECE), 0)
+    eye = (row == lax.broadcasted_iota(jnp.int32, (PIECE, PIECE), 1)).astype(f32)
+    largest = jnp.zeros((1, TILE), f32)
     for r in range(4):
         here = slice(r * PIECE, (r + 1) * PIECE)
-        rows = matrix_rows(tokens, sums_ref, r * PIECE)
-        first = 2.0 * scale * eye_rows(r * PIECE, PIECE) - (scale * scale) * rows
-        first_ref[offset + r * PIECE : offset + (r + 1) * PIECE, :] = first
-        low_ref[here, :] = first.astype(bf16)
-        sums_ref[here, :] = rows.astype(bf16)
+        first_ref[here, :] = sums_ref[here, :].astype(f32) / tokens
+        first_ref[here, here] += DAMPING * eye
+        largest += jnp.sum(jnp.abs(first_ref[here, :]), axis=0, keepdims=True)
+    scale = 1.0 / jnp.max(largest)
+    for r in range(4):
+        here = slice(r * PIECE, (r + 1) * PIECE)
+        matrix = first_ref[here, :]
+        sums_ref[here, :] = matrix.astype(bf16)
+        first_ref[here, :] = -(scale * scale) * matrix
+        first_ref[here, here] += (2.0 * scale) * eye
+        low_ref[here, :] = first_ref[here, :].astype(bf16)
 
 
 def inverse_rows(rows, sums_ref, low_ref):
@@ -171,7 +162,7 @@
                 put(h, -back * d, other_ref[2 * (d - 1) + h])
         put(core, 4, own_ref[6])
         put(1 - core, 4, other_ref[6])
-        split_factor(tokens, sums_ref, first_ref, low_ref, 0)
+        split_factor(tokens, sums_ref, first_ref, low_ref)
 
     out_ref[...] = inverse_rows(first_ref[aligned(i * PIECE, PIECE), :], sums_ref, low_ref)
 
@@ -186,7 +177,7 @@
             here = slice(owner // 2 * PIECE, (owner // 2 + 1) * PIECE)
             for piece, ref in ((core, own_ref), (1 - core, other_ref)):
                 sums_ref[aligned((2 * (owner % 2) + piece) * PIECE, PIECE), here] = ref[owner]
-        split_factor(tokens, sums_ref, first_ref, low_ref, 0)
+        split_factor(tokens, sums_ref, first_ref, low_ref)
 
     outside = jnp.logical_or(i == 0, i == 5)
 
@@ -199,7 +190,7 @@
         out_ref[...] = inverse_rows(first_ref[aligned((i - 1) * PIECE, PIECE), :], sums_ref, low_ref)
 
 
-def call(kernel, steps, block, out_shape, at, *args, scratch=()):
+def call(kernel, steps, block, out_shape, at, *args, limit, scratch=()):
     def whole(a):
         return pl.BlockSpec(a.shape, lambda i, at: (0,) * len(a.shape))
 
@@ -213,7 +204,7 @@
             scratch_shapes=[pltpu.VMEM(shape, dtype) for shape, dtype in scratch],
         ),
         out_shape=jax.ShapeDtypeStruct(out_shape, bf16),
-        compiler_params=PARAMS,
+        compiler_params=pltpu.CompilerParams(vmem_limit_bytes=limit * MIB),
     )(at, *args)
 
 
@@ -267,6 +258,7 @@
         (here, out_blocks * (HALF + PIECE)),
         numbers(h, k),
         cotangent,
+        limit=8,
     )
     recv = lax.ppermute(pick, CORE, SWAP2)
 
@@ -303,7 +295,7 @@
                 ],
             ),
             out_shape=[jax.ShapeDtypeStruct(m, bf16) for m in [(count - skip, *block)] + more],
-            compiler_params=PARAMS,
+            compiler_params=pltpu.CompilerParams(vmem_limit_bytes=12 * MIB),
         )(table, *tokens_in)
 
     def cross_part(base, count, gives):
@@ -368,6 +360,7 @@
         shard,
         in_own,
         in_other,
+        limit=26,
         scratch=[(square, bf16), (square, f32), (square, bf16)],
     )
     both_y = jnp.concatenate([y5, y6])
@@ -394,6 +387,7 @@
         numbers(core),
         out_tiles,
         out_other,
+        limit=26,
         scratch=[(square, bf16), (square, f32), (square, bf16)],
     )
     middle = mdot(cross, in_inverse).astype(bf16)

time: 207 us -> 207 us (level)
  no operation moved by 1% of the time
where the time goes in v7:
time: 207 us; the launch traced here: 206 us
  starting transfers between devices  70.8 us (34%)
  waiting for transfers between devices  62.2 us (30%)
  Pallas kernels  25.6 us (12%)
  local copies, waits for them, and re-layouts  13.7 us (7%)
  other arithmetic  12.7 us (6%)
  blocking collectives  10.8 us (5%)
  matrix products  8.11 us (4%)
    ppermute x29, waiting for transfers between devices, phase(): got = [lax.ppermute(value, *send[1:]) for value, send in zip(values, sends)]  58.8 us
    ppermute x29, starting transfers between devices, phase(): got = [lax.ppermute(value, *send[1:]) for value, send in zip(values, sends)]  54.4 us
    pallas_call x3, Pallas kernels, call(): pl.pallas_call(kernel, grid_spec=pltpu.PrefetchScalarGridSpec(num_scalar_...  16.4 us
    all_to_all x1, blocking collectives, all_sum(): lax.all_to_all(jnp.full((n, 128), value, f32), axis, 0, 0, tiled=True)  10.8 us
    pallas_call x3, Pallas kernels, slots(): pl.pallas_call(kernel, grid_spec=pltpu.PrefetchScalarGridSpec(num_scalar_...  9.2 us
    unnamed x52, local copies, waits for them, and re-layouts  8.44 us
    dot_general x3, matrix products, mdot(): return jnp.dot(a, b, preferred_element_type=f32)  8.11 us
    all_to_all x1, starting transfers between devices, all_sum(): lax.all_to_all(jnp.full((n, 128), value, f32), axis, 0, 0, tiled=True)  6.02 us
  transfers between devices with their start and end apart: 36, of which 19 were waited for; matrix products, arithmetic and copies ran while one was open for 6% of the time, Pallas kernels for 10%

profile of v7, /device:TPU:16, one launch (start us, length us, event | category | flops | bytes accessed | tf_op | source)
XLA Modules:
  0.0 205.9 jit_solution(970161332601052287)
XLA Ops:
  6.1 3.9 %shard_map.38 = (bf16[8,256,384]{2,1,0:T(8,128)(2,1)S(1)}, bf16[1,256,384]{2,1,0:T(8,128)(2,1)S(1)}) custom-call(s32[29]{0:T(128)S(1)} %stack.142.at_ref, bf16[128,4608]{1,0:T(8,128)(2,1)S(1)} %shard_map.37.pick_ref, bf16[128,4608]{1,0:T(8,128)(2,1)S(1)} %collective-permute-done.recv_ref, bf16[128,1024]{1,0:T(8,128)(2,1)S(1)} %multiply_convert_fusion.own_ref, ...), custom_call_target="tpu_custom_call" | custom-call | tf_op jit(solution)/shard_map/pallas_call | solution.py:283
  11.3 5.9 %collective-permute-start.2 = (bf16[256,384]{1,0:T(8,128)(2,1)S(1)}, bf16[256,384]{1,0:T(8,128)(2,1)S(1)}, u32[]{:S(2)}, u32[]{:S(2)}) collective-permute-start(bf16[256,384]{1,0:T(8,128)(2,1)S(1)} %bitcast.68), channel_id=1, source_target_pairs={{0,224},{8,40},{32,0},{40,72},{64,32},{72,104},{96,64},{104,136},{... | collective-permute-start | bytes 589832 | tf_op jit(solution)/shard_map/ppermute | solution.py:222
  17.1 2.2 %shard_map.39 = (bf16[3,128,1024]{2,1,0:T(8,128)(2,1)S(1)}, bf16[1,128,1024]{2,1,0:T(8,128)(2,1)S(1)}, bf16[1,128,1024]{2,1,0:T(8,128)(2,1)S(1)}, bf16[1,128,1024]{2,1,0:T(8,128)(2,1)S(1)}) custom-call(s32[29]{0:T(128)S(1)} %stack.142.at_ref, bf16[128,4608]{1,0:T(8,128)(2,1)S(1)} %shard_map.37.pick_ref, bf16[128,4608]{1,0:T(8,128)(2,1)S(1)} %collective-permute-done.recv_ref, ...), custom_call_target="tpu_custom_call" | custom-call | tf_op jit(solution)/shard_map/pallas_call | solution.py:283
  20.5 3.8 %collective-permute-start.3 = (bf16[2,256,384]{2,1,0:T(8,128)(2,1)S(1)}, bf16[2,256,384]{2,1,0:T(8,128)(2,1)S(1)}, u32[]{:S(2)}, u32[]{:S(2)}) collective-permute-start(bf16[2,256,384]{2,1,0:T(8,128)(2,1)S(1)} %add_convert_fusion.5), channel_id=1, source_target_pairs={{0,224},{8,40},{32,0},{40,72},{64,32},{72,104},{96,64},{104,136},{... | collective-permute-start | bytes 1179656 | tf_op jit(solution)/shard_map/ppermute | solution.py:222
  24.6 7.5 %collective-permute-done.4 = bf16[1,128,1024]{2,1,0:T(8,128)(2,1)S(1)} collective-permute-done((bf16[1,128,1024]{2,1,0:T(8,128)(2,1)S(1)}, bf16[1,128,1024]{2,1,0:T(8,128)(2,1)S(1)}, u32[]{:S(2)}, u32[]{:S(2)}) %collective-permute-start.4) | collective-permute-done | bytes 262176 | tf_op jit(solution)/shard_map/ppermute | solution.py:222
  33.8 7.5 %collective-permute-done.6 = bf16[1,128,1024]{2,1,0:T(8,128)(2,1)S(1)} collective-permute-done((bf16[1,128,1024]{2,1,0:T(8,128)(2,1)S(1)}, bf16[1,128,1024]{2,1,0:T(8,128)(2,1)S(1)}, u32[]{:S(2)}, u32[]{:S(2)}) %collective-permute-start.6) | collective-permute-done | bytes 262176 | tf_op jit(solution)/shard_map/ppermute | solution.py:222
  43.3 3.0 %shard_map.40 = (bf16[5,128,1024]{2,1,0:T(8,128)(2,1)S(1)}, bf16[1,128,1024]{2,1,0:T(8,128)(2,1)S(1)}, bf16[1,128,1024]{2,1,0:T(8,128)(2,1)S(1)}, bf16[1,128,102...) custom-call(s32[29]{0:T(128)S(1)} %stack.142.at_ref, ...), custom_call_target="tpu_custom_call" | custom-call | tf_op jit(solution)/shard_map/pallas_call | solution.py:283
  46.4 4.4 %collective-permute-done.8 = bf16[1,128,1024]{2,1,0:T(8,128)(2,1)S(1)} collective-permute-done((bf16[1,128,1024]{2,1,0:T(8,128)(2,1)S(1)}, bf16[1,128,1024]{2,1,0:T(8,128)(2,1)S(1)}, u32[]{:S(2)}, u32[]{:S(2)}) %collective-permute-start.8) | collective-permute-done | bytes 262176 | tf_op jit(solution)/shard_map/ppermute | solution.py:222
  53.2 3.0 %collective-permute-start.11 = (bf16[128,1024]{1,0:T(8,128)(2,1)S(1)}, bf16[128,1024]{1,0:T(8,128)(2,1)S(1)}, u32[]{:S(2)}, u32[]{:S(2)}) collective-permute-start(bf16[128,1024]{1,0:T(8,128)(2,1)S(1)} %fusion.11), channel_id=1, source_target_pairs={{0,224},{8,40},{32,0},{40,72},{96,64},{104,136},{128,96},{136,168}... | collective-permute-start | bytes 786440 | tf_op jit(solution)/shard_map/ppermute | solution.py:222
  56.2 6.5 %collective-permute-done.10 = bf16[256,512]{1,0:T(8,128)(2,1)S(1)} collective-permute-done((bf16[256,512]{1,0:T(8,128)(2,1)S(1)}, bf16[256,512]{1,0:T(8,128)(2,1)S(1)}, u32[]{:S(2)}, u32[]{:S(2)}) %collective-permute-start.10) | collective-permute-done | bytes 262176 | tf_op jit(solution)/shard_map/ppermute | solution.py:222
  67.9 3.0 %collective-permute-start.14 = (bf16[2,128,1024]{2,1,0:T(8,128)(2,1)S(1)}, bf16[2,128,1024]{2,1,0:T(8,128)(2,1)S(1)}, u32[]{:S(2)}, u32[]{:S(2)}) collective-permute-start(bf16[2,128,1024]{2,1,0:T(8,128)(2,1)S(1)} %add_convert_fusion.2), channel_id=1, source_target_pairs={{0,224},{8,40},{40,72},{64,32},{72,104},{96,64},{128,96},{136,168}... | collective-permute-start | bytes 1572872 | tf_op jit(solution)/shard_map/ppermute | solution.py:222
  72.2 2.2 %collective-permute-start.15 = (bf16[1,128,1024]{2,1,0:T(8,128)(2,1)S(1)}, bf16[1,128,1024]{2,1,0:T(8,128)(2,1)S(1)}, u32[]{:S(2)}, u32[]{:S(2)}) collective-permute-start(bf16[1,128,1024]{2,1,0:T(8,128)(2,1)S(1)} %copy-done.18), channel_id=1, source_target_pairs={{0,16},{16,0},{1,17},{17,1},{2,18},{18,2},{3,19},{19,3},{4,20},{20... | collective-permute-start | bytes 786440 | tf_op jit(solution)/shard_map/ppermute | solution.py:222
  74.5 5.9 %collective-permute-done.13 = bf16[2,256,256]{2,1,0:T(8,128)(2,1)S(1)} collective-permute-done((bf16[2,256,256]{2,1,0:T(8,128)(2,1)S(1)}, bf16[2,256,256]{2,1,0:T(8,128)(2,1)S(1)}, u32[]{:S(2)}, u32[]{:S(2)}) %collective-permute-start.13) | collective-permute-done | bytes 262176 | tf_op jit(solution)/shard_map/ppermute | solution.py:222
  81.4 2.7 %collective-permute-start.16 = (bf16[2,256,256]{2,1,0:T(8,128)(2,1)S(1)}, bf16[2,256,256]{2,1,0:T(8,128)(2,1)S(1)}, u32[]{:S(2)}, u32[]{:S(2)}) collective-permute-start(bf16[2,256,256]{2,1,0:T(8,128)(2,1)S(1)} %collective-permute-done.13), channel_id=1, source_target_pairs={{0,224},{8,40},{32,0},{40,72},{64,32},{72,104},{96,64},{104,136},{... | collective-permute-start | bytes 786440 | tf_op jit(solution)/shard_map/ppermute | solution.py:222
  84.1 3.1 %collective-permute-start.17 = (bf16[1,128,1024]{2,1,0:T(8,128)(2,1)S(1)}, bf16[1,128,1024]{2,1,0:T(8,128)(2,1)S(1)}, u32[]{:S(2)}, u32[]{:S(2)}) collective-permute-start(bf16[1,128,1024]{2,1,0:T(8,128)(2,1)S(1)} %copy-done.16), channel_id=1, source_target_pairs={{0,16},{16,0},{1,17},{17,1},{2,18},{18,2},{3,19},{19,3},{4,20},{20... | collective-permute-start | bytes 786440 | tf_op jit(solution)/shard_map/ppermute | solution.py:222
  88.8 3.2 %collective-permute-done.17 = bf16[1,128,1024]{2,1,0:T(8,128)(2,1)S(1)} collective-permute-done((bf16[1,128,1024]{2,1,0:T(8,128)(2,1)S(1)}, bf16[1,128,1024]{2,1,0:T(8,128)(2,1)S(1)}, u32[]{:S(2)}, u32[]{:S(2)}) %collective-permute-start.17) | collective-permute-done | bytes 262176 | tf_op jit(solution)/shard_map/ppermute | solution.py:222
  92.7 2.5 %collective-permute-start.19 = (bf16[1,128,1024]{2,1,0:T(8,128)(2,1)S(1)}, bf16[1,128,1024]{2,1,0:T(8,128)(2,1)S(1)}, u32[]{:S(2)}, u32[]{:S(2)}) collective-permute-start(bf16[1,128,1024]{2,1,0:T(8,128)(2,1)S(1)} %copy-done.14), channel_id=1, source_target_pairs={{0,16},{16,0},{1,17},{17,1},{2,18},{18,2},{3,19},{19,3},{4,20},{20... | collective-permute-start | bytes 786440 | tf_op jit(solution)/shard_map/ppermute | solution.py:222
  95.2 3.1 %collective-permute-done.18 = bf16[2,256,256]{2,1,0:T(8,128)(2,1)S(1)} collective-permute-done((bf16[2,256,256]{2,1,0:T(8,128)(2,1)S(1)}, bf16[2,256,256]{2,1,0:T(8,128)(2,1)S(1)}, u32[]{:S(2)}, u32[]{:S(2)}) %collective-permute-start.18) | collective-permute-done | bytes 262176 | tf_op jit(solution)/shard_map/ppermute | solution.py:222
  98.4 2.2 %collective-permute-done.19 = bf16[1,128,1024]{2,1,0:T(8,128)(2,1)S(1)} collective-permute-done((bf16[1,128,1024]{2,1,0:T(8,128)(2,1)S(1)}, bf16[1,128,1024]{2,1,0:T(8,128)(2,1)S(1)}, u32[]{:S(2)}, u32[]{:S(2)}) %collective-permute-start.19) | collective-permute-done | bytes 262176 | tf_op jit(solution)/shard_map/ppermute | solution.py:222
  102.2 2.5 %collective-permute-start.21 = (bf16[1,128,1024]{2,1,0:T(8,128)(2,1)S(1)}, bf16[1,128,1024]{2,1,0:T(8,128)(2,1)S(1)}, u32[]{:S(2)}, u32[]{:S(2)}) collective-permute-start(bf16[1,128,1024]{2,1,0:T(8,128)(2,1)S(1)} %copy-done.12), channel_id=1, source_target_pairs={{0,16},{16,0},{1,17},{17,1},{2,18},{18,2},{3,19},{19,3},{4,20},{20... | collective-permute-start | bytes 786440 | tf_op jit(solution)/shard_map/ppermute | solution.py:222
  106.9 3.2 %collective-permute-done.21 = bf16[1,128,1024]{2,1,0:T(8,128)(2,1)S(1)} collective-permute-done((bf16[1,128,1024]{2,1,0:T(8,128)(2,1)S(1)}, bf16[1,128,1024]{2,1,0:T(8,128)(2,1)S(1)}, u32[]{:S(2)}, u32[]{:S(2)}) %collective-permute-start.21) | collective-permute-done | bytes 262176 | tf_op jit(solution)/shard_map/ppermute | solution.py:222
  113.1 5.1 %all-to-all-start = ((bf16[8,256,256]{2,1,0:T(8,128)(2,1)}), bf16[8,256,256]{2,1,0:T(8,128)(2,1)S(1)}, u32[]{:S(2)}, u32[]{:S(2)}) async-start(bf16[8,256,256]{2,1,0:T(8,128)(2,1)} %broadcast_in_dim.22), calls=%async_computation | async-start | bytes 2097152 | tf_op jit(solution)/shard_map/all_to_all | solution.py:348
  118.2 5.0 %collective-permute-done.22 = bf16[2,128,1024]{2,1,0:T(8,128)(2,1)} collective-permute-done((bf16[2,128,1024]{2,1,0:T(8,128)(2,1)}, bf16[2,128,1024]{2,1,0:T(8,128)(2,1)}, u32[]{:S(2)}, u32[]{:S(2)}) %collective-permute-start.22) | collective-permute-done | bytes 524320 | tf_op jit(solution)/shard_map/ppermute | solution.py:222
  124.9 7.9 %collective-permute-start.24 = (bf16[2,128,1024]{2,1,0:T(8,128)(2,1)S(1)}, bf16[2,128,1024]{2,1,0:T(8,128)(2,1)}, u32[]{:S(2)}, u32[]{:S(2)}) collective-permute-start(bf16[2,128,1024]{2,1,0:T(8,128)(2,1)S(1)} %add_convert_fusion), channel_id=1, source_target_pairs={{0,224},{8,40},{32,0},{64,32},{72,104},{104,136},{128,96},{136,168... | collective-permute-start | bytes 1572872 | tf_op jit(solution)/shard_map/ppermute | solution.py:222
  134.9 8.2 %shard_map.41 = bf16[1024,1024]{1,0:T(8,128)(2,1)S(1)} custom-call(s32[2]{0:T(128)S(1)} %pad_add_fusion.1.at_ref, bf16[2,256,256]{2,1,0:T(8,128)(2,1)S(1)} %pad_maximum_fusion.6.shard_ref, bf16[7,256,256]{2,1,0:T(8,128)(2,1)S(1)} %pad_maximum_fusion.own_ref, bf16[7,256,256]{2,1,0:T(8,128)(2,1)S(1)} %collective-permute-done.23.other_ref), custom_call_target="tpu_custom_call" | custom-call | tf_op jit(solution)/shard_map/pallas_call | solution.py:197
  145.7 3.1 %collective-permute-done.26 = bf16[2,128,1024]{2,1,0:T(8,128)(2,1)S(1)} collective-permute-done((bf16[2,128,1024]{2,1,0:T(8,128)(2,1)}, bf16[2,128,1024]{2,1,0:T(8,128)(2,1)S(1)}, u32[]{:S(2)}, u32[]{:S(2)}) %collective-permute-start.26) | collective-permute-done | bytes 524320 | tf_op jit(solution)/shard_map/ppermute | solution.py:222
  148.8 2.9 %convolution_convert_fusion = bf16[128,1024]{1,0:T(8,128)(2,1)S(1)} fusion(bf16[1024,1024]{1,0:T(8,128)(2,1)} %copy-done.2, bf16[1,128,1024]{2,1,0:T(8,128)(2,1)} %copy-done.25, bf16[5,128,1024]{2,1,0:T(8,128)(2,1)} %copy-done.8, bf16[2,128,1024]{2,1,0:T(8,128)(2,1)S(1)} %collective-permute-done.26, bf16[2,128,1024]{2,1,0:T(8,128)(2,1)} %collective-permute-done.24, ...), kind=kOutput, calls=%fused_computation.4 | convolution fusion | flops 269877248 | bytes 3932161 | tf_op jit(solution)/shard_map/dot_general | solution.py:32
  159.3 7.5 %shard_map.42 = bf16[1536,1024]{1,0:T(8,128)(2,1)S(1)} custom-call(s32[1]{0:T(128)} %bitcast.4.at_ref, bf16[8,256,256]{2,1,0:T(8,128)(2,1)S(1)} %copy-done.1, bf16[8,256,256]{2,1,0:T(8,128)(2,1)S(1)} %copy-done.7), custom_call_target="tpu_custom_call" | custom-call | tf_op jit(solution)/shard_map/pallas_call | solution.py:197
  173.5 3.3 %multiply_reduce_fusion = f32[]{:T(128)} fusion(bf16[1024,512]{1,0:T(8,128)(2,1)} %bitcast.39, bf16[1536,1024]{1,0:T(8,128)(2,1)S(1)} %shard_map.42), kind=kOutput, calls=%fused_computation | convolution fusion | flops 1074790400 | bytes 3145732 | tf_op jit(solution)/shard_map/dot_general | solution.py:32
  178.1 6.0 %all-to-all-start.1 = ((f32[8,1,128]{2,1,0:T(1,128)}), f32[8,1,128]{2,1,0:T(1,128)S(1)}, u32[]{:S(2)}, u32[]{:S(2)}) async-start(f32[8,1,128]{2,1,0:T(1,128)} %broadcast_in_dim.23), calls=%async_computation.1 | async-start | bytes 8192 | tf_op jit(solution)/shard_map/all_to_all | solution.py:238
  186.1 3.9 %collective-permute-start.32 = (bf16[192,512]{1,0:T(8,128)(2,1)S(1)}, bf16[192,512]{1,0:T(8,128)(2,1)S(1)}, u32[]{:S(2)}, u32[]{:S(2)}) collective-permute-start(bf16[192,512]{1,0:T(8,128)(2,1)S(1)} %slice.175), channel_id=1, source_target_pairs={{0,32},{32,64},{128,160},{160,192},{1,33},{33,65},{129,161},{161,1... | collective-permute-start | bytes 589832 | tf_op jit(solution)/shard_map/ppermute | solution.py:409
  193.0 10.8 %all_to_all.23 = f32[8,1,128]{2,1,0:T(1,128)S(1)} all-to-all(f32[8,1,128]{2,1,0:T(1,128)S(1)} %broadcast_in_dim.24), channel_id=1, replica_groups=mesh['dp_0'=8,'dp_1'=2,'dp_2'=2,'owner_0'=2,'owner_1'=4] {'owner_0','own..., dimensions={0} | all-to-all | bytes 8192 | tf_op jit(solution)/shard_map/all_to_all | solution.py:238
  (145 shorter events, 58.4 us)
Async XLA Ops:
  2.2 3.9 %collective-permute-start = (bf16[128,4608]{1,0:T(8,128)(2,1)S(1)}, bf16[128,4608]{1,0:T(8,128)(2,1)S(1)}, u32[]{:S(2)}, u32[]{:S(2)}) collective-permute-start(bf16[128,4608]{1,0:T(8,128)(2,1)S(1)} %shard_map.37.pick_ref), channel_id=1, source_target_pairs={{0,8},{8,0},{1,9},{9,1},{2,10},{10,2},{3,11},{11,3},{4,12},{12,4},... | collective-permute-start | bytes 3538952 | tf_op jit(solution)/shard_map/ppermute | solution.py:263
  11.3 9.1 %collective-permute-start.2 = (bf16[256,384]{1,0:T(8,128)(2,1)S(1)}, bf16[256,384]{1,0:T(8,128)(2,1)S(1)}, u32[]{:S(2)}, u32[]{:S(2)}) collective-permute-start(bf16[256,384]{1,0:T(8,128)(2,1)S(1)} %bitcast.68), channel_id=1, source_target_pairs={{0,224},{8,40},{32,0},{40,72},{64,32},{72,104},{96,64},{104,136},{... | collective-permute-start | bytes 589832 | tf_op jit(solution)/shard_map/ppermute | solution.py:222
  20.5 11.6 %collective-permute-start.3 = (bf16[2,256,384]{2,1,0:T(8,128)(2,1)S(1)}, bf16[2,256,384]{2,1,0:T(8,128)(2,1)S(1)}, u32[]{:S(2)}, u32[]{:S(2)}) collective-permute-start(bf16[2,256,384]{2,1,0:T(8,128)(2,1)S(1)} %add_convert_fusion.5), channel_id=1, source_target_pairs={{0,224},{8,40},{32,0},{40,72},{64,32},{72,104},{96,64},{104,136},{... | collective-permute-start | bytes 1179656 | tf_op jit(solution)/shard_map/ppermute | solution.py:222
  24.3 7.9 %collective-permute-start.4 = (bf16[1,128,1024]{2,1,0:T(8,128)(2,1)S(1)}, bf16[1,128,1024]{2,1,0:T(8,128)(2,1)S(1)}, u32[]{:S(2)}, u32[]{:S(2)}) collective-permute-start(bf16[1,128,1024]{2,1,0:T(8,128)(2,1)S(1)} %get-tuple-element.81), channel_id=1, source_target_pairs={{0,16},{16,0},{1,17},{17,1},{2,18},{18,2},{3,19},{19,3},{4,20},{20... | collective-permute-start | bytes 786440 | tf_op jit(solution)/shard_map/ppermute | solution.py:222
  32.2 9.8 %collective-permute-start.5 = (bf16[2,256,384]{2,1,0:T(8,128)(2,1)S(1)}, bf16[2,256,384]{2,1,0:T(8,128)(2,1)S(1)}, u32[]{:S(2)}, u32[]{:S(2)}) collective-permute-start(bf16[2,256,384]{2,1,0:T(8,128)(2,1)S(1)} %add_convert_fusion.4), channel_id=1, source_target_pairs={{0,224},{8,40},{32,0},{40,72},{64,32},{72,104},{96,64},{104,136},{... | collective-permute-start | bytes 1179656 | tf_op jit(solution)/shard_map/ppermute | solution.py:222
  33.4 7.9 %collective-permute-start.6 = (bf16[1,128,1024]{2,1,0:T(8,128)(2,1)S(1)}, bf16[1,128,1024]{2,1,0:T(8,128)(2,1)S(1)}, u32[]{:S(2)}, u32[]{:S(2)}) collective-permute-start(bf16[1,128,1024]{2,1,0:T(8,128)(2,1)S(1)} %get-tuple-element.85), channel_id=1, source_target_pairs={{0,16},{16,0},{1,17},{17,1},{2,18},{18,2},{3,19},{19,3},{4,20},{20... | collective-permute-start | bytes 786440 | tf_op jit(solution)/shard_map/ppermute | solution.py:222
  42.1 8.8 %collective-permute-start.7 = (bf16[2,256,384]{2,1,0:T(8,128)(2,1)S(1)}, bf16[2,256,384]{2,1,0:T(8,128)(2,1)S(1)}, u32[]{:S(2)}, u32[]{:S(2)}) collective-permute-start(bf16[2,256,384]{2,1,0:T(8,128)(2,1)S(1)} %add_convert_fusion.3), channel_id=1, source_target_pairs={{0,224},{8,40},{32,0},{40,72},{64,32},{72,104},{96,64},{104,136},{... | collective-permute-start | bytes 1179656 | tf_op jit(solution)/shard_map/ppermute | solution.py:222
  43.0 7.9 %collective-permute-start.8 = (bf16[1,128,1024]{2,1,0:T(8,128)(2,1)S(1)}, bf16[1,128,1024]{2,1,0:T(8,128)(2,1)S(1)}, u32[]{:S(2)}, u32[]{:S(2)}) collective-permute-start(bf16[1,128,1024]{2,1,0:T(8,128)(2,1)S(1)} %get-tuple-element.89), channel_id=1, source_target_pairs={{0,16},{16,0},{1,17},{17,1},{2,18},{18,2},{3,19},{19,3},{4,20},{20... | collective-permute-start | bytes 786440 | tf_op jit(solution)/shard_map/ppermute | solution.py:222
  52.7 9.9 %collective-permute-start.10 = (bf16[256,512]{1,0:T(8,128)(2,1)S(1)}, bf16[256,512]{1,0:T(8,128)(2,1)S(1)}, u32[]{:S(2)}, u32[]{:S(2)}) collective-permute-start(bf16[256,512]{1,0:T(8,128)(2,1)S(1)} %add_convert_fusion.9), channel_id=1, source_target_pairs={{0,16},{16,0},{1,17},{17,1},{2,18},{18,2},{3,19},{19,3},{4,20},{20... | collective-permute-start | bytes 786440 | tf_op jit(solution)/shard_map/ppermute | solution.py:222
  53.2 9.5 %collective-permute-start.11 = (bf16[128,1024]{1,0:T(8,128)(2,1)S(1)}, bf16[128,1024]{1,0:T(8,128)(2,1)S(1)}, u32[]{:S(2)}, u32[]{:S(2)}) collective-permute-start(bf16[128,1024]{1,0:T(8,128)(2,1)S(1)} %fusion.11), channel_id=1, source_target_pairs={{0,224},{8,40},{32,0},{40,72},{96,64},{104,136},{128,96},{136,168}... | collective-permute-start | bytes 786440 | tf_op jit(solution)/shard_map/ppermute | solution.py:222
  62.8 5.1 %collective-permute-start.12 = (bf16[256,256]{1,0:T(8,128)(2,1)S(1)}, bf16[256,256]{1,0:T(8,128)(2,1)S(1)}, u32[]{:S(2)}, u32[]{:S(2)}) collective-permute-start(bf16[256,256]{1,0:T(8,128)(2,1)S(1)} %slice.115), channel_id=1, source_target_pairs={{0,1},{1,0},{2,3},{3,2},{4,5},{5,4},{6,7},{7,6},{8,9},{9,8},{10,11... | collective-permute-start | bytes 393224 | tf_op jit(solution)/shard_map/ppermute | solution.py:222
  67.9 13.5 %collective-permute-start.14 = (bf16[2,128,1024]{2,1,0:T(8,128)(2,1)S(1)}, bf16[2,128,1024]{2,1,0:T(8,128)(2,1)S(1)}, u32[]{:S(2)}, u32[]{:S(2)}) collective-permute-start(bf16[2,128,1024]{2,1,0:T(8,128)(2,1)S(1)} %add_convert_fusion.2), channel_id=1, source_target_pairs={{0,224},{8,40},{40,72},{64,32},{72,104},{96,64},{128,96},{136,168}... | collective-permute-start | bytes 1572872 | tf_op jit(solution)/shard_map/ppermute | solution.py:222
  70.9 9.5 %collective-permute-start.13 = (bf16[2,256,256]{2,1,0:T(8,128)(2,1)S(1)}, bf16[2,256,256]{2,1,0:T(8,128)(2,1)S(1)}, u32[]{:S(2)}, u32[]{:S(2)}) collective-permute-start(bf16[2,256,256]{2,1,0:T(8,128)(2,1)S(1)} %pad_maximum_fusion.6.shard_ref), channel_id=1, source_target_pairs={{0,224},{8,40},{32,0},{40,72},{64,32},{72,104},{96,64},{104,136},{... | collective-permute-start | bytes 786440 | tf_op jit(solution)/shard_map/ppermute | solution.py:222
  72.2 9.2 %collective-permute-start.15 = (bf16[1,128,1024]{2,1,0:T(8,128)(2,1)S(1)}, bf16[1,128,1024]{2,1,0:T(8,128)(2,1)S(1)}, u32[]{:S(2)}, u32[]{:S(2)}) collective-permute-start(bf16[1,128,1024]{2,1,0:T(8,128)(2,1)S(1)} %copy-done.18), channel_id=1, source_target_pairs={{0,16},{16,0},{1,17},{17,1},{2,18},{18,2},{3,19},{19,3},{4,20},{20... | collective-permute-start | bytes 786440 | tf_op jit(solution)/shard_map/ppermute | solution.py:222
  81.4 7.3 %collective-permute-start.16 = (bf16[2,256,256]{2,1,0:T(8,128)(2,1)S(1)}, bf16[2,256,256]{2,1,0:T(8,128)(2,1)S(1)}, u32[]{:S(2)}, u32[]{:S(2)}) collective-permute-start(bf16[2,256,256]{2,1,0:T(8,128)(2,1)S(1)} %collective-permute-done.13), channel_id=1, source_target_pairs={{0,224},{8,40},{32,0},{40,72},{64,32},{72,104},{96,64},{104,136},{... | collective-permute-start | bytes 786440 | tf_op jit(solution)/shard_map/ppermute | solution.py:222
  84.1 7.9 %collective-permute-start.17 = (bf16[1,128,1024]{2,1,0:T(8,128)(2,1)S(1)}, bf16[1,128,1024]{2,1,0:T(8,128)(2,1)S(1)}, u32[]{:S(2)}, u32[]{:S(2)}) collective-permute-start(bf16[1,128,1024]{2,1,0:T(8,128)(2,1)S(1)} %copy-done.16), channel_id=1, source_target_pairs={{0,16},{16,0},{1,17},{17,1},{2,18},{18,2},{3,19},{19,3},{4,20},{20... | collective-permute-start | bytes 786440 | tf_op jit(solution)/shard_map/ppermute | solution.py:222
  92.0 6.4 %collective-permute-start.18 = (bf16[2,256,256]{2,1,0:T(8,128)(2,1)S(1)}, bf16[2,256,256]{2,1,0:T(8,128)(2,1)S(1)}, u32[]{:S(2)}, u32[]{:S(2)}) collective-permute-start(bf16[2,256,256]{2,1,0:T(8,128)(2,1)S(1)} %collective-permute-done.16), channel_id=1, source_target_pairs={{0,224},{8,40},{32,0},{40,72},{64,32},{72,104},{96,64},{104,136},{... | collective-permute-start | bytes 786440 | tf_op jit(solution)/shard_map/ppermute | solution.py:222
  92.7 7.9 %collective-permute-start.19 = (bf16[1,128,1024]{2,1,0:T(8,128)(2,1)S(1)}, bf16[1,128,1024]{2,1,0:T(8,128)(2,1)S(1)}, u32[]{:S(2)}, u32[]{:S(2)}) collective-permute-start(bf16[1,128,1024]{2,1,0:T(8,128)(2,1)S(1)} %copy-done.14), channel_id=1, source_target_pairs={{0,16},{16,0},{1,17},{17,1},{2,18},{18,2},{3,19},{19,3},{4,20},{20... | collective-permute-start | bytes 786440 | tf_op jit(solution)/shard_map/ppermute | solution.py:222
  100.6 6.3 %collective-permute-start.20 = (bf16[1,256,256]{2,1,0:T(8,128)(2,1)S(1)}, bf16[1,256,256]{2,1,0:T(8,128)(2,1)S(1)}, u32[]{:S(2)}, u32[]{:S(2)}) collective-permute-start(bf16[1,256,256]{2,1,0:T(8,128)(2,1)S(1)} %slice_select_fusion), channel_id=1, source_target_pairs={{0,224},{8,40},{32,0},{40,72},{64,32},{72,104},{96,64},{104,136},{... | collective-permute-start | bytes 393224 | tf_op jit(solution)/shard_map/ppermute | solution.py:222
  102.2 7.9 %collective-permute-start.21 = (bf16[1,128,1024]{2,1,0:T(8,128)(2,1)S(1)}, bf16[1,128,1024]{2,1,0:T(8,128)(2,1)S(1)}, u32[]{:S(2)}, u32[]{:S(2)}) collective-permute-start(bf16[1,128,1024]{2,1,0:T(8,128)(2,1)S(1)} %copy-done.12), channel_id=1, source_target_pairs={{0,16},{16,0},{1,17},{17,1},{2,18},{18,2},{3,19},{19,3},{4,20},{20... | collective-permute-start | bytes 786440 | tf_op jit(solution)/shard_map/ppermute | solution.py:222
  111.9 11.4 %collective-permute-start.23 = (bf16[7,256,256]{2,1,0:T(8,128)(2,1)S(1)}, bf16[7,256,256]{2,1,0:T(8,128)(2,1)S(1)}, u32[]{:S(2)}, u32[]{:S(2)}) collective-permute-start(bf16[7,256,256]{2,1,0:T(8,128)(2,1)S(1)} %pad_maximum_fusion.own_ref), channel_id=1, source_target_pairs={{0,8},{8,0},{1,9},{9,1},{2,10},{10,2},{3,11},{11,3},{4,12},{12,4},... | collective-permute-start | bytes 2752520 | tf_op jit(solution)/shard_map/ppermute | solution.py:222
  111.9 11.4 %collective-permute-start.22 = (bf16[2,128,1024]{2,1,0:T(8,128)(2,1)}, bf16[2,128,1024]{2,1,0:T(8,128)(2,1)}, u32[]{:S(2)}, u32[]{:S(2)}) collective-permute-start(bf16[2,128,1024]{2,1,0:T(8,128)(2,1)} %add_convert_fusion.1), channel_id=1, source_target_pairs={{32,0},{40,72},{64,32},{72,104},{96,64},{104,136},{160,128},{168,2... | collective-permute-start | bytes 1572872 | tf_op jit(solution)/shard_map/ppermute | solution.py:222
  113.1 32.0 %all-to-all-start = ((bf16[8,256,256]{2,1,0:T(8,128)(2,1)}), bf16[8,256,256]{2,1,0:T(8,128)(2,1)S(1)}, u32[]{:S(2)}, u32[]{:S(2)}) async-start(bf16[8,256,256]{2,1,0:T(8,128)(2,1)} %broadcast_in_dim.22), calls=%async_computation | async-start | bytes 2097152 | tf_op jit(solution)/shard_map/all_to_all | solution.py:348
  124.9 20.2 %collective-permute-start.24 = (bf16[2,128,1024]{2,1,0:T(8,128)(2,1)S(1)}, bf16[2,128,1024]{2,1,0:T(8,128)(2,1)}, u32[]{:S(2)}, u32[]{:S(2)}) collective-permute-start(bf16[2,128,1024]{2,1,0:T(8,128)(2,1)S(1)} %add_convert_fusion), channel_id=1, source_target_pairs={{0,224},{8,40},{32,0},{64,32},{72,104},{104,136},{128,96},{136,168... | collective-permute-start | bytes 1572872 | tf_op jit(solution)/shard_map/ppermute | solution.py:222
  132.8 11.6 %collective-permute-start.25 = (bf16[1,128,1024]{2,1,0:T(8,128)(2,1)S(1)}, bf16[1,128,1024]{2,1,0:T(8,128)(2,1)S(1)}, u32[]{:S(2)}, u32[]{:S(2)}) collective-permute-start(bf16[1,128,1024]{2,1,0:T(8,128)(2,1)S(1)} %get-tuple-element.130), channel_id=1, source_target_pairs={{0,16},{16,0},{1,17},{17,1},{2,18},{18,2},{3,19},{19,3},{4,20},{20... | collective-permute-start | bytes 786440 | tf_op jit(solution)/shard_map/ppermute | solution.py:222
  145.1 3.7 %collective-permute-start.27 = (bf16[8,256,256]{2,1,0:T(8,128)(2,1)S(1)}, bf16[8,256,256]{2,1,0:T(8,128)(2,1)S(1)}, u32[]{:S(2)}, u32[]{:S(2)}) collective-permute-start(bf16[8,256,256]{2,1,0:T(8,128)(2,1)S(1)} %all-to-all-done.own_ref), channel_id=1, source_target_pairs={{0,8},{8,0},{1,9},{9,1},{2,10},{10,2},{3,11},{11,3},{4,12},{12,4},... | collective-permute-start | bytes 3145736 | tf_op jit(solution)/shard_map/ppermute | solution.py:222
  151.8 15.1 %collective-permute-start.28 = (bf16[128,512]{1,0:T(8,128)(2,1)S(1)}, bf16[128,512]{1,0:T(8,128)(2,1)S(1)}, u32[]{:S(2)}, u32[]{:S(2)}) collective-permute-start(bf16[128,512]{1,0:T(8,128)(2,1)S(1)} %get-tuple-element.142), channel_id=1, source_target_pairs={{0,1},{1,0},{2,3},{3,2},{4,5},{5,4},{6,7},{7,6},{8,9},{9,8},{10,11... | collective-permute-start | bytes 393224 | tf_op jit(solution)/shard_map/ppermute | solution.py:222
  153.4 13.5 %collective-permute-start.29 = (bf16[128,512]{1,0:T(8,128)(2,1)S(1)}, bf16[128,512]{1,0:T(8,128)(2,1)}, u32[]{:S(2)}, u32[]{:S(2)}) collective-permute-start(bf16[128,512]{1,0:T(8,128)(2,1)S(1)} %get-tuple-element.141), channel_id=1, source_target_pairs={{0,16},{16,0},{1,17},{17,1},{2,18},{18,2},{3,19},{19,3},{4,20},{20... | collective-permute-start | bytes 393224 | tf_op jit(solution)/shard_map/ppermute | solution.py:222
  154.9 12.0 %collective-permute-start.30 = (bf16[128,512]{1,0:T(8,128)(2,1)S(1)}, bf16[128,512]{1,0:T(8,128)(2,1)}, u32[]{:S(2)}, u32[]{:S(2)}) collective-permute-start(bf16[128,512]{1,0:T(8,128)(2,1)S(1)} %get-tuple-element.142), channel_id=1, source_target_pairs={{0,17},{1,16},{2,19},{3,18},{16,1},{17,0},{18,3},{19,2},{4,21},{5,... | collective-permute-start | bytes 393224 | tf_op jit(solution)/shard_map/ppermute | solution.py:222
  178.1 13.6 %all-to-all-start.1 = ((f32[8,1,128]{2,1,0:T(1,128)}), f32[8,1,128]{2,1,0:T(1,128)S(1)}, u32[]{:S(2)}, u32[]{:S(2)}) async-start(f32[8,1,128]{2,1,0:T(1,128)} %broadcast_in_dim.23), calls=%async_computation.1 | async-start | bytes 8192 | tf_op jit(solution)/shard_map/all_to_all | solution.py:238
  186.1 19.0 %collective-permute-start.32 = (bf16[192,512]{1,0:T(8,128)(2,1)S(1)}, bf16[192,512]{1,0:T(8,128)(2,1)S(1)}, u32[]{:S(2)}, u32[]{:S(2)}) collective-permute-start(bf16[192,512]{1,0:T(8,128)(2,1)S(1)} %slice.175), channel_id=1, source_target_pairs={{0,32},{32,64},{128,160},{160,192},{1,33},{33,65},{129,161},{161,1... | collective-permute-start | bytes 589832 | tf_op jit(solution)/shard_map/ppermute | solution.py:409
  190.0 15.1 %collective-permute-start.33 = (bf16[192,512]{1,0:T(8,128)(2,1)S(1)}, bf16[192,512]{1,0:T(8,128)(2,1)S(1)}, u32[]{:S(2)}, u32[]{:S(2)}) collective-permute-start(bf16[192,512]{1,0:T(8,128)(2,1)S(1)} %slice.175), channel_id=1, source_target_pairs={{96,64},{224,192},{97,65},{225,193},{98,66},{226,194},{99,67},{227... | collective-permute-start | bytes 589832 | tf_op jit(solution)/shard_map/ppermute | solution.py:410
  (30 other events, 216.7 us)

commit v8 on v7

--- a/solution.py
+++ b/solution.py
@@ -164,7 +164,7 @@
         put(1 - core, 4, other_ref[6])
         split_factor(tokens, sums_ref, first_ref, low_ref)
 
-    out_ref[...] = inverse_rows(first_ref[aligned(i * PIECE, PIECE), :], sums_ref, low_ref)
+    out_ref[...] = inverse_rows(first_ref[aligned(i * HALF, HALF), :], sums_ref, low_ref)
 
 
 def out_inverse_kernel(tokens, at_ref, own_ref, other_ref, out_ref, sums_ref, first_ref, low_ref):
@@ -179,7 +179,7 @@
                 sums_ref[aligned((2 * (owner % 2) + piece) * PIECE, PIECE), here] = ref[owner]
         split_factor(tokens, sums_ref, first_ref, low_ref)
 
-    outside = jnp.logical_or(i == 0, i == 5)
+    outside = jnp.logical_or(i == 0, i == 3)
 
     @pl.when(outside)
     def _():
@@ -187,7 +187,7 @@
 
     @pl.when(jnp.logical_not(outside))
     def _():
-        out_ref[...] = inverse_rows(first_ref[aligned((i - 1) * PIECE, PIECE), :], sums_ref, low_ref)
+        out_ref[...] = inverse_rows(first_ref[aligned((i - 1) * HALF, HALF), :], sums_ref, low_ref)
 
 
 def call(kernel, steps, block, out_shape, at, *args, limit, scratch=()):
@@ -353,14 +353,14 @@
     square = (TILE, TILE)
     in_inverse = call(
         functools.partial(in_inverse_kernel, tokens),
-        4,
-        (PIECE, TILE),
+        2,
+        (HALF, TILE),
         square,
         numbers(z, core),
         shard,
         in_own,
         in_other,
-        limit=26,
+        limit=32,
         scratch=[(square, bf16), (square, f32), (square, bf16)],
     )
     both_y = jnp.concatenate([y5, y6])
@@ -378,16 +378,16 @@
     near = jnp.where(m == 3, 2, m + 1)
     own_at = jnp.where(m == 2, TILE, slice_rows * (4 * m + row) - base)
     near_at = jnp.where(m == 2, TILE, slice_rows * (4 * near + row) - base)
-    own_at, near_at = [jnp.clip(a, -slice_rows, TILE) + PIECE for a in (own_at, near_at)]
+    own_at, near_at = [jnp.clip(a, -slice_rows, TILE) + HALF for a in (own_at, near_at)]
     padded = call(
         functools.partial(out_inverse_kernel, tokens),
-        6,
-        (PIECE, TILE),
-        (6 * PIECE, TILE),
+        4,
+        (HALF, TILE),
+        (4 * HALF, TILE),
         numbers(core),
         out_tiles,
         out_other,
-        limit=26,
+        limit=32,
         scratch=[(square, bf16), (square, f32), (square, bf16)],
     )
     middle = mdot(cross, in_inverse).astype(bf16)
@@ -408,7 +408,7 @@
     near_part = result[slice_rows:].astype(bf16)
     up = lax.ppermute(near_part, Z, [(0, 1), (1, 2), (4, 5), (5, 6)])
     down = lax.ppermute(near_part, Z, [(3, 2), (7, 6)])
-    whole = mdot(padded[PIECE : PIECE + TILE], middle)
+    whole = mdot(padded[HALF : HALF + TILE], middle)
     squares = jnp.where(m == 2, 0.0, jnp.sum(whole * whole))
     squares = all_sum(all_sum(squares, Z), OWNER)
     summed = result[:slice_rows] + up.astype(f32) + down.astype(f32)

time: 207 us -> 202 us (0.976)
  other arithmetic: 12.7 us -> 8.98 us
  matrix products: 8.11 us -> 4.6 us
    dot_general x3, matrix products: 8.11 us -> 4.6 us  [mdot(): return jnp.dot(a, b, preferred_element_type=f32)]
    another operation x7, other arithmetic: 3.26 us -> 0.31 us  [in_order(): return jnp.stack([first, second])]
    unnamed x52 -> x56, local copies, waits for them, and re-layouts: 8.44 us -> 9.05 us
  transfers between devices with their start and end apart: 36 -> 36, of which waited for: 19 -> 19; matrix products, arithmetic and copies ran while one was open for 6% -> 5% of each run, Pallas kernels for 10% -> 11%
where the time goes in v8:
time: 202 us
  starting transfers between devices  71.2 us (35%)
  waiting for transfers between devices  64.1 us (32%)
  Pallas kernels  26.2 us (13%)
  local copies, waits for them, and re-layouts  13.7 us (7%)
  blocking collectives  10.8 us (5%)
  other arithmetic  8.98 us (4%)
  matrix products  4.6 us (2%)
  between operations  2.09 us (1%)
    ppermute x29, waiting for transfers between devices, phase(): got = [lax.ppermute(value, *send[1:]) for value, send in zip(values, sends)]  60.2 us
    ppermute x29, starting transfers between devices, phase(): got = [lax.ppermute(value, *send[1:]) for value, send in zip(values, sends)]  54.5 us
    pallas_call x3, Pallas kernels, call(): pl.pallas_call(kernel, grid_spec=pltpu.PrefetchScalarGridSpec(num_scalar_...  17 us
    all_to_all x1, blocking collectives, all_sum(): lax.all_to_all(jnp.full((n, 128), value, f32), axis, 0, 0, tiled=True)  10.8 us
    pallas_call x3, Pallas kernels, slots(): pl.pallas_call(kernel, grid_spec=pltpu.PrefetchScalarGridSpec(num_scalar_...  9.2 us
    unnamed x56, local copies, waits for them, and re-layouts  9.05 us
    all_to_all x1, starting transfers between devices, all_sum(): lax.all_to_all(jnp.full((n, 128), value, f32), axis, 0, 0, tiled=True)  6.29 us
    all_to_all x1, starting transfers between devices, shards(): out_tiles = lax.all_to_all(copies, OWNER, 0, 0, tiled=True)  5.01 us
  transfers between devices with their start and end apart: 36, of which 19 were waited for; matrix products, arithmetic and copies ran while one was open for 5% of the time, Pallas kernels for 11%

profile of v8, /device:TPU:16, one launch (start us, length us, event | category | flops | bytes accessed | tf_op | source)
XLA Modules:
  0.0 201.6 jit_solution(13877176199617026999)
XLA Ops:
  6.1 3.9 %shard_map.38 = (bf16[8,256,384]{2,1,0:T(8,128)(2,1)S(1)}, bf16[1,256,384]{2,1,0:T(8,128)(2,1)S(1)}) custom-call(s32[29]{0:T(128)S(1)} %stack.142.at_ref, bf16[128,4608]{1,0:T(8,128)(2,1)S(1)} %shard_map.37.pick_ref, bf16[128,4608]{1,0:T(8,128)(2,1)S(1)} %collective-permute-done.recv_ref, bf16[128,1024]{1,0:T(8,128)(2,1)S(1)} %multiply_convert_fusion.own_ref, ...), custom_call_target="tpu_custom_call" | custom-call | tf_op jit(solution)/shard_map/pallas_call | solution.py:283
  11.3 5.9 %collective-permute-start.2 = (bf16[256,384]{1,0:T(8,128)(2,1)S(1)}, bf16[256,384]{1,0:T(8,128)(2,1)S(1)}, u32[]{:S(2)}, u32[]{:S(2)}) collective-permute-start(bf16[256,384]{1,0:T(8,128)(2,1)S(1)} %bitcast.68), channel_id=1, source_target_pairs={{0,224},{8,40},{32,0},{40,72},{64,32},{72,104},{96,64},{104,136},{... | collective-permute-start | bytes 589832 | tf_op jit(solution)/shard_map/ppermute | solution.py:222
  17.1 2.2 %shard_map.39 = (bf16[3,128,1024]{2,1,0:T(8,128)(2,1)S(1)}, bf16[1,128,1024]{2,1,0:T(8,128)(2,1)S(1)}, bf16[1,128,1024]{2,1,0:T(8,128)(2,1)S(1)}, bf16[1,128,1024]{2,1,0:T(8,128)(2,1)S(1)}) custom-call(s32[29]{0:T(128)S(1)} %stack.142.at_ref, bf16[128,4608]{1,0:T(8,128)(2,1)S(1)} %shard_map.37.pick_ref, bf16[128,4608]{1,0:T(8,128)(2,1)S(1)} %collective-permute-done.recv_ref, ...), custom_call_target="tpu_custom_call" | custom-call | tf_op jit(solution)/shard_map/pallas_call | solution.py:283
  20.5 3.8 %collective-permute-start.3 = (bf16[2,256,384]{2,1,0:T(8,128)(2,1)S(1)}, bf16[2,256,384]{2,1,0:T(8,128)(2,1)S(1)}, u32[]{:S(2)}, u32[]{:S(2)}) collective-permute-start(bf16[2,256,384]{2,1,0:T(8,128)(2,1)S(1)} %add_convert_fusion.5), channel_id=1, source_target_pairs={{0,224},{8,40},{32,0},{40,72},{64,32},{72,104},{96,64},{104,136},{... | collective-permute-start | bytes 1179656 | tf_op jit(solution)/shard_map/ppermute | solution.py:222
  24.6 7.5 %collective-permute-done.4 = bf16[1,128,1024]{2,1,0:T(8,128)(2,1)S(1)} collective-permute-done((bf16[1,128,1024]{2,1,0:T(8,128)(2,1)S(1)}, bf16[1,128,1024]{2,1,0:T(8,128)(2,1)S(1)}, u32[]{:S(2)}, u32[]{:S(2)}) %collective-permute-start.4) | collective-permute-done | bytes 262176 | tf_op jit(solution)/shard_map/ppermute | solution.py:222
  33.8 7.5 %collective-permute-done.6 = bf16[1,128,1024]{2,1,0:T(8,128)(2,1)S(1)} collective-permute-done((bf16[1,128,1024]{2,1,0:T(8,128)(2,1)S(1)}, bf16[1,128,1024]{2,1,0:T(8,128)(2,1)S(1)}, u32[]{:S(2)}, u32[]{:S(2)}) %collective-permute-start.6) | collective-permute-done | bytes 262176 | tf_op jit(solution)/shard_map/ppermute | solution.py:222
  43.1 3.0 %shard_map.40 = (bf16[5,128,1024]{2,1,0:T(8,128)(2,1)S(1)}, bf16[1,128,1024]{2,1,0:T(8,128)(2,1)S(1)}, bf16[1,128,1024]{2,1,0:T(8,128)(2,1)S(1)}, bf16[1,128,102...) custom-call(s32[29]{0:T(128)S(1)} %stack.142.at_ref, ...), custom_call_target="tpu_custom_call" | custom-call | tf_op jit(solution)/shard_map/pallas_call | solution.py:283
  46.2 4.4 %collective-permute-done.8 = bf16[1,128,1024]{2,1,0:T(8,128)(2,1)S(1)} collective-permute-done((bf16[1,128,1024]{2,1,0:T(8,128)(2,1)S(1)}, bf16[1,128,1024]{2,1,0:T(8,128)(2,1)S(1)}, u32[]{:S(2)}, u32[]{:S(2)}) %collective-permute-start.8) | collective-permute-done | bytes 262176 | tf_op jit(solution)/shard_map/ppermute | solution.py:222
  53.0 3.0 %collective-permute-start.11 = (bf16[128,1024]{1,0:T(8,128)(2,1)S(1)}, bf16[128,1024]{1,0:T(8,128)(2,1)S(1)}, u32[]{:S(2)}, u32[]{:S(2)}) collective-permute-start(bf16[128,1024]{1,0:T(8,128)(2,1)S(1)} %fusion.11), channel_id=1, source_target_pairs={{0,224},{8,40},{32,0},{40,72},{96,64},{104,136},{128,96},{136,168}... | collective-permute-start | bytes 786440 | tf_op jit(solution)/shard_map/ppermute | solution.py:222
  56.0 6.5 %collective-permute-done.10 = bf16[256,512]{1,0:T(8,128)(2,1)S(1)} collective-permute-done((bf16[256,512]{1,0:T(8,128)(2,1)S(1)}, bf16[256,512]{1,0:T(8,128)(2,1)S(1)}, u32[]{:S(2)}, u32[]{:S(2)}) %collective-permute-start.10) | collective-permute-done | bytes 262176 | tf_op jit(solution)/shard_map/ppermute | solution.py:222
  64.5 3.1 %collective-permute-done.12 = bf16[256,256]{1,0:T(8,128)(2,1)S(1)} collective-permute-done((bf16[256,256]{1,0:T(8,128)(2,1)S(1)}, bf16[256,256]{1,0:T(8,128)(2,1)S(1)}, u32[]{:S(2)}, u32[]{:S(2)}) %collective-permute-start.12) | collective-permute-done | bytes 131104 | tf_op jit(solution)/shard_map/ppermute | solution.py:222
  67.7 3.0 %collective-permute-start.14 = (bf16[2,128,1024]{2,1,0:T(8,128)(2,1)S(1)}, bf16[2,128,1024]{2,1,0:T(8,128)(2,1)S(1)}, u32[]{:S(2)}, u32[]{:S(2)}) collective-permute-start(bf16[2,128,1024]{2,1,0:T(8,128)(2,1)S(1)} %add_convert_fusion.2), channel_id=1, source_target_pairs={{0,224},{8,40},{40,72},{64,32},{72,104},{96,64},{128,96},{136,168}... | collective-permute-start | bytes 1572872 | tf_op jit(solution)/shard_map/ppermute | solution.py:222
  72.0 2.2 %collective-permute-start.15 = (bf16[1,128,1024]{2,1,0:T(8,128)(2,1)S(1)}, bf16[1,128,1024]{2,1,0:T(8,128)(2,1)S(1)}, u32[]{:S(2)}, u32[]{:S(2)}) collective-permute-start(bf16[1,128,1024]{2,1,0:T(8,128)(2,1)S(1)} %copy-done.19), channel_id=1, source_target_pairs={{0,16},{16,0},{1,17},{17,1},{2,18},{18,2},{3,19},{19,3},{4,20},{20... | collective-permute-start | bytes 786440 | tf_op jit(solution)/shard_map/ppermute | solution.py:222
  74.3 5.9 %collective-permute-done.13 = bf16[2,256,256]{2,1,0:T(8,128)(2,1)S(1)} collective-permute-done((bf16[2,256,256]{2,1,0:T(8,128)(2,1)S(1)}, bf16[2,256,256]{2,1,0:T(8,128)(2,1)S(1)}, u32[]{:S(2)}, u32[]{:S(2)}) %collective-permute-start.13) | collective-permute-done | bytes 262176 | tf_op jit(solution)/shard_map/ppermute | solution.py:222
  81.2 2.7 %collective-permute-start.16 = (bf16[2,256,256]{2,1,0:T(8,128)(2,1)S(1)}, bf16[2,256,256]{2,1,0:T(8,128)(2,1)S(1)}, u32[]{:S(2)}, u32[]{:S(2)}) collective-permute-start(bf16[2,256,256]{2,1,0:T(8,128)(2,1)S(1)} %collective-permute-done.13), channel_id=1, source_target_pairs={{0,224},{8,40},{32,0},{40,72},{64,32},{72,104},{96,64},{104,136},{... | collective-permute-start | bytes 786440 | tf_op jit(solution)/shard_map/ppermute | solution.py:222
  83.9 3.1 %collective-permute-start.17 = (bf16[1,128,1024]{2,1,0:T(8,128)(2,1)S(1)}, bf16[1,128,1024]{2,1,0:T(8,128)(2,1)S(1)}, u32[]{:S(2)}, u32[]{:S(2)}) collective-permute-start(bf16[1,128,1024]{2,1,0:T(8,128)(2,1)S(1)} %copy-done.17), channel_id=1, source_target_pairs={{0,16},{16,0},{1,17},{17,1},{2,18},{18,2},{3,19},{19,3},{4,20},{20... | collective-permute-start | bytes 786440 | tf_op jit(solution)/shard_map/ppermute | solution.py:222
  88.6 3.2 %collective-permute-done.17 = bf16[1,128,1024]{2,1,0:T(8,128)(2,1)S(1)} collective-permute-done((bf16[1,128,1024]{2,1,0:T(8,128)(2,1)S(1)}, bf16[1,128,1024]{2,1,0:T(8,128)(2,1)S(1)}, u32[]{:S(2)}, u32[]{:S(2)}) %collective-permute-start.17) | collective-permute-done | bytes 262176 | tf_op jit(solution)/shard_map/ppermute | solution.py:222
  92.5 2.5 %collective-permute-start.19 = (bf16[1,128,1024]{2,1,0:T(8,128)(2,1)S(1)}, bf16[1,128,1024]{2,1,0:T(8,128)(2,1)S(1)}, u32[]{:S(2)}, u32[]{:S(2)}) collective-permute-start(bf16[1,128,1024]{2,1,0:T(8,128)(2,1)S(1)} %get-tuple-element.113), channel_id=1, source_target_pairs={{0,16},{16,0},{1,17},{17,1},{2,18},{18,2},{3,19},{19,3},{4,20},{20... | collective-permute-start | bytes 786440 | tf_op jit(solution)/shard_map/ppermute | solution.py:222
  95.0 3.1 %collective-permute-done.18 = bf16[2,256,256]{2,1,0:T(8,128)(2,1)S(1)} collective-permute-done((bf16[2,256,256]{2,1,0:T(8,128)(2,1)S(1)}, bf16[2,256,256]{2,1,0:T(8,128)(2,1)S(1)}, u32[]{:S(2)}, u32[]{:S(2)}) %collective-permute-start.18) | collective-permute-done | bytes 262176 | tf_op jit(solution)/shard_map/ppermute | solution.py:222
  98.2 2.2 %collective-permute-done.19 = bf16[1,128,1024]{2,1,0:T(8,128)(2,1)S(1)} collective-permute-done((bf16[1,128,1024]{2,1,0:T(8,128)(2,1)S(1)}, bf16[1,128,1024]{2,1,0:T(8,128)(2,1)S(1)}, u32[]{:S(2)}, u32[]{:S(2)}) %collective-permute-start.19) | collective-permute-done | bytes 262176 | tf_op jit(solution)/shard_map/ppermute | solution.py:222
  102.0 2.5 %collective-permute-start.21 = (bf16[1,128,1024]{2,1,0:T(8,128)(2,1)S(1)}, bf16[1,128,1024]{2,1,0:T(8,128)(2,1)}, u32[]{:S(2)}, u32[]{:S(2)}) collective-permute-start(bf16[1,128,1024]{2,1,0:T(8,128)(2,1)S(1)} %get-tuple-element.118), channel_id=1, source_target_pairs={{0,16},{16,0},{1,17},{17,1},{2,18},{18,2},{3,19},{19,3},{4,20},{20... | collective-permute-start | bytes 786440 | tf_op jit(solution)/shard_map/ppermute | solution.py:222
  106.7 3.3 %collective-permute-done.21 = bf16[1,128,1024]{2,1,0:T(8,128)(2,1)} collective-permute-done((bf16[1,128,1024]{2,1,0:T(8,128)(2,1)S(1)}, bf16[1,128,1024]{2,1,0:T(8,128)(2,1)}, u32[]{:S(2)}, u32[]{:S(2)}) %collective-permute-start.21) | collective-permute-done | bytes 262176 | tf_op jit(solution)/shard_map/ppermute | solution.py:222
  112.5 5.0 %all-to-all-start = ((bf16[8,256,256]{2,1,0:T(8,128)(2,1)}), bf16[8,256,256]{2,1,0:T(8,128)(2,1)S(1)}, u32[]{:S(2)}, u32[]{:S(2)}) async-start(bf16[8,256,256]{2,1,0:T(8,128)(2,1)} %broadcast_in_dim.22), calls=%async_computation | async-start | bytes 2097152 | tf_op jit(solution)/shard_map/all_to_all | solution.py:348
  117.6 5.0 %collective-permute-done.22 = bf16[2,128,1024]{2,1,0:T(8,128)(2,1)} collective-permute-done((bf16[2,128,1024]{2,1,0:T(8,128)(2,1)}, bf16[2,128,1024]{2,1,0:T(8,128)(2,1)}, u32[]{:S(2)}, u32[]{:S(2)}) %collective-permute-start.22) | collective-permute-done | bytes 524320 | tf_op jit(solution)/shard_map/ppermute | solution.py:222
  124.5 8.0 %collective-permute-start.24 = (bf16[2,128,1024]{2,1,0:T(8,128)(2,1)S(1)}, bf16[2,128,1024]{2,1,0:T(8,128)(2,1)}, u32[]{:S(2)}, u32[]{:S(2)}) collective-permute-start(bf16[2,128,1024]{2,1,0:T(8,128)(2,1)S(1)} %add_convert_fusion), channel_id=1, source_target_pairs={{0,224},{8,40},{32,0},{64,32},{72,104},{104,136},{128,96},{136,168... | collective-permute-start | bytes 1572872 | tf_op jit(solution)/shard_map/ppermute | solution.py:222
  135.8 7.8 %shard_map.41 = bf16[1024,1024]{1,0:T(8,128)(2,1)S(1)} custom-call(s32[2]{0:T(128)S(1)} %pad_add_fusion.1.at_ref, bf16[2,256,256]{2,1,0:T(8,128)(2,1)S(1)} %copy-done.8, bf16[7,256,256]{2,1,0:T(8,128)(2,1)S(1)} %copy-done.3, bf16[7,256,256]{2,1,0:T(8,128)(2,1)S(1)} %copy-done.10), custom_call_target="tpu_custom_call" | custom-call | tf_op jit(solution)/shard_map/pallas_call | solution.py:197
  144.8 3.2 %collective-permute-done.26 = bf16[2,128,1024]{2,1,0:T(8,128)(2,1)} collective-permute-done((bf16[2,128,1024]{2,1,0:T(8,128)(2,1)}, bf16[2,128,1024]{2,1,0:T(8,128)(2,1)}, u32[]{:S(2)}, u32[]{:S(2)}) %collective-permute-start.26) | collective-permute-done | bytes 524320 | tf_op jit(solution)/shard_map/ppermute | solution.py:222
  155.3 8.4 %shard_map.42 = bf16[2048,1024]{1,0:T(8,128)(2,1)S(1)} custom-call(s32[1]{0:T(128)} %bitcast.4.at_ref, bf16[8,256,256]{2,1,0:T(8,128)(2,1)S(1)} %all-to-all-done.own_ref, bf16[8,256,256]{2,1,0:T(8,128)(2,1)} %collective-permute-done.27.other_ref), custom_call_target="tpu_custom_call" | custom-call | tf_op jit(solution)/shard_map/pallas_call | solution.py:197
  173.6 6.3 %all-to-all-start.1 = ((f32[8,1,128]{2,1,0:T(1,128)}), f32[8,1,128]{2,1,0:T(1,128)S(1)}, u32[]{:S(2)}, u32[]{:S(2)}) async-start(f32[8,1,128]{2,1,0:T(1,128)} %broadcast_in_dim.23), calls=%async_computation.1 | async-start | bytes 8192 | tf_op jit(solution)/shard_map/all_to_all | solution.py:238
  180.5 3.9 %collective-permute-start.32 = (bf16[192,512]{1,0:T(8,128)(2,1)S(1)}, bf16[192,512]{1,0:T(8,128)(2,1)S(1)}, u32[]{:S(2)}, u32[]{:S(2)}) collective-permute-start(bf16[192,512]{1,0:T(8,128)(2,1)S(1)} %slice.175), channel_id=1, source_target_pairs={{0,32},{32,64},{128,160},{160,192},{1,33},{33,65},{129,161},{161,1... | collective-permute-start | bytes 589832 | tf_op jit(solution)/shard_map/ppermute | solution.py:409
  185.1 2.4 %all-to-all-done.1 = f32[8,1,128]{2,1,0:T(1,128)S(1)} async-done(((f32[8,1,128]{2,1,0:T(1,128)}), f32[8,1,128]{2,1,0:T(1,128)S(1)}, u32[]{:S(2)}, u32[]{:S(2)}) %all-to-all-start.1) | async-done | bytes 4128 | tf_op jit(solution)/shard_map/all_to_all | solution.py:238
  188.7 10.8 %all_to_all.23 = f32[8,1,128]{2,1,0:T(1,128)S(1)} all-to-all(f32[8,1,128]{2,1,0:T(1,128)S(1)} %broadcast_in_dim.24), channel_id=1, replica_groups=mesh['dp_0'=8,'dp_1'=2,'dp_2'=2,'owner_0'=2,'owner_1'=4] {'owner_0','own..., dimensions={0} | all-to-all | bytes 8192 | tf_op jit(solution)/shard_map/all_to_all | solution.py:238
  (149 shorter events, 53.6 us)
Async XLA Ops:
  2.2 3.9 %collective-permute-start = (bf16[128,4608]{1,0:T(8,128)(2,1)S(1)}, bf16[128,4608]{1,0:T(8,128)(2,1)S(1)}, u32[]{:S(2)}, u32[]{:S(2)}) collective-permute-start(bf16[128,4608]{1,0:T(8,128)(2,1)S(1)} %shard_map.37.pick_ref), channel_id=1, source_target_pairs={{0,8},{8,0},{1,9},{9,1},{2,10},{10,2},{3,11},{11,3},{4,12},{12,4},... | collective-permute-start | bytes 3538952 | tf_op jit(solution)/shard_map/ppermute | solution.py:263
  11.3 9.1 %collective-permute-start.2 = (bf16[256,384]{1,0:T(8,128)(2,1)S(1)}, bf16[256,384]{1,0:T(8,128)(2,1)S(1)}, u32[]{:S(2)}, u32[]{:S(2)}) collective-permute-start(bf16[256,384]{1,0:T(8,128)(2,1)S(1)} %bitcast.68), channel_id=1, source_target_pairs={{0,224},{8,40},{32,0},{40,72},{64,32},{72,104},{96,64},{104,136},{... | collective-permute-start | bytes 589832 | tf_op jit(solution)/shard_map/ppermute | solution.py:222
  20.5 11.6 %collective-permute-start.3 = (bf16[2,256,384]{2,1,0:T(8,128)(2,1)S(1)}, bf16[2,256,384]{2,1,0:T(8,128)(2,1)S(1)}, u32[]{:S(2)}, u32[]{:S(2)}) collective-permute-start(bf16[2,256,384]{2,1,0:T(8,128)(2,1)S(1)} %add_convert_fusion.5), channel_id=1, source_target_pairs={{0,224},{8,40},{32,0},{40,72},{64,32},{72,104},{96,64},{104,136},{... | collective-permute-start | bytes 1179656 | tf_op jit(solution)/shard_map/ppermute | solution.py:222
  24.2 7.9 %collective-permute-start.4 = (bf16[1,128,1024]{2,1,0:T(8,128)(2,1)S(1)}, bf16[1,128,1024]{2,1,0:T(8,128)(2,1)S(1)}, u32[]{:S(2)}, u32[]{:S(2)}) collective-permute-start(bf16[1,128,1024]{2,1,0:T(8,128)(2,1)S(1)} %get-tuple-element.81), channel_id=1, source_target_pairs={{0,16},{16,0},{1,17},{17,1},{2,18},{18,2},{3,19},{19,3},{4,20},{20... | collective-permute-start | bytes 786440 | tf_op jit(solution)/shard_map/ppermute | solution.py:222
  32.2 9.1 %collective-permute-start.5 = (bf16[2,256,384]{2,1,0:T(8,128)(2,1)S(1)}, bf16[2,256,384]{2,1,0:T(8,128)(2,1)S(1)}, u32[]{:S(2)}, u32[]{:S(2)}) collective-permute-start(bf16[2,256,384]{2,1,0:T(8,128)(2,1)S(1)} %add_convert_fusion.4), channel_id=1, source_target_pairs={{0,224},{8,40},{32,0},{40,72},{64,32},{72,104},{96,64},{104,136},{... | collective-permute-start | bytes 1179656 | tf_op jit(solution)/shard_map/ppermute | solution.py:222
  33.4 7.9 %collective-permute-start.6 = (bf16[1,128,1024]{2,1,0:T(8,128)(2,1)S(1)}, bf16[1,128,1024]{2,1,0:T(8,128)(2,1)S(1)}, u32[]{:S(2)}, u32[]{:S(2)}) collective-permute-start(bf16[1,128,1024]{2,1,0:T(8,128)(2,1)S(1)} %get-tuple-element.85), channel_id=1, source_target_pairs={{0,16},{16,0},{1,17},{17,1},{2,18},{18,2},{3,19},{19,3},{4,20},{20... | collective-permute-start | bytes 786440 | tf_op jit(solution)/shard_map/ppermute | solution.py:222
  42.0 8.7 %collective-permute-start.7 = (bf16[2,256,384]{2,1,0:T(8,128)(2,1)S(1)}, bf16[2,256,384]{2,1,0:T(8,128)(2,1)S(1)}, u32[]{:S(2)}, u32[]{:S(2)}) collective-permute-start(bf16[2,256,384]{2,1,0:T(8,128)(2,1)S(1)} %add_convert_fusion.3), channel_id=1, source_target_pairs={{0,224},{8,40},{32,0},{40,72},{64,32},{72,104},{96,64},{104,136},{... | collective-permute-start | bytes 1179656 | tf_op jit(solution)/shard_map/ppermute | solution.py:222
  42.8 7.9 %collective-permute-start.8 = (bf16[1,128,1024]{2,1,0:T(8,128)(2,1)S(1)}, bf16[1,128,1024]{2,1,0:T(8,128)(2,1)S(1)}, u32[]{:S(2)}, u32[]{:S(2)}) collective-permute-start(bf16[1,128,1024]{2,1,0:T(8,128)(2,1)S(1)} %get-tuple-element.89), channel_id=1, source_target_pairs={{0,16},{16,0},{1,17},{17,1},{2,18},{18,2},{3,19},{19,3},{4,20},{20... | collective-permute-start | bytes 786440 | tf_op jit(solution)/shard_map/ppermute | solution.py:222
  52.5 9.9 %collective-permute-start.10 = (bf16[256,512]{1,0:T(8,128)(2,1)S(1)}, bf16[256,512]{1,0:T(8,128)(2,1)S(1)}, u32[]{:S(2)}, u32[]{:S(2)}) collective-permute-start(bf16[256,512]{1,0:T(8,128)(2,1)S(1)} %add_convert_fusion.9), channel_id=1, source_target_pairs={{0,16},{16,0},{1,17},{17,1},{2,18},{18,2},{3,19},{19,3},{4,20},{20... | collective-permute-start | bytes 786440 | tf_op jit(solution)/shard_map/ppermute | solution.py:222
  53.0 9.5 %collective-permute-start.11 = (bf16[128,1024]{1,0:T(8,128)(2,1)S(1)}, bf16[128,1024]{1,0:T(8,128)(2,1)S(1)}, u32[]{:S(2)}, u32[]{:S(2)}) collective-permute-start(bf16[128,1024]{1,0:T(8,128)(2,1)S(1)} %fusion.11), channel_id=1, source_target_pairs={{0,224},{8,40},{32,0},{40,72},{96,64},{104,136},{128,96},{136,168}... | collective-permute-start | bytes 786440 | tf_op jit(solution)/shard_map/ppermute | solution.py:222
  62.6 5.1 %collective-permute-start.12 = (bf16[256,256]{1,0:T(8,128)(2,1)S(1)}, bf16[256,256]{1,0:T(8,128)(2,1)S(1)}, u32[]{:S(2)}, u32[]{:S(2)}) collective-permute-start(bf16[256,256]{1,0:T(8,128)(2,1)S(1)} %slice.115), channel_id=1, source_target_pairs={{0,1},{1,0},{2,3},{3,2},{4,5},{5,4},{6,7},{7,6},{8,9},{9,8},{10,11... | collective-permute-start | bytes 393224 | tf_op jit(solution)/shard_map/ppermute | solution.py:222
  67.7 13.5 %collective-permute-start.14 = (bf16[2,128,1024]{2,1,0:T(8,128)(2,1)S(1)}, bf16[2,128,1024]{2,1,0:T(8,128)(2,1)S(1)}, u32[]{:S(2)}, u32[]{:S(2)}) collective-permute-start(bf16[2,128,1024]{2,1,0:T(8,128)(2,1)S(1)} %add_convert_fusion.2), channel_id=1, source_target_pairs={{0,224},{8,40},{40,72},{64,32},{72,104},{96,64},{128,96},{136,168}... | collective-permute-start | bytes 1572872 | tf_op jit(solution)/shard_map/ppermute | solution.py:222
  70.8 9.5 %collective-permute-start.13 = (bf16[2,256,256]{2,1,0:T(8,128)(2,1)S(1)}, bf16[2,256,256]{2,1,0:T(8,128)(2,1)S(1)}, u32[]{:S(2)}, u32[]{:S(2)}) collective-permute-start(bf16[2,256,256]{2,1,0:T(8,128)(2,1)S(1)} %pad_maximum_fusion.6.shard_ref), channel_id=1, source_target_pairs={{0,224},{8,40},{32,0},{40,72},{64,32},{72,104},{96,64},{104,136},{... | collective-permute-start | bytes 786440 | tf_op jit(solution)/shard_map/ppermute | solution.py:222
  72.0 9.2 %collective-permute-start.15 = (bf16[1,128,1024]{2,1,0:T(8,128)(2,1)S(1)}, bf16[1,128,1024]{2,1,0:T(8,128)(2,1)S(1)}, u32[]{:S(2)}, u32[]{:S(2)}) collective-permute-start(bf16[1,128,1024]{2,1,0:T(8,128)(2,1)S(1)} %copy-done.19), channel_id=1, source_target_pairs={{0,16},{16,0},{1,17},{17,1},{2,18},{18,2},{3,19},{19,3},{4,20},{20... | collective-permute-start | bytes 786440 | tf_op jit(solution)/shard_map/ppermute | solution.py:222
  81.2 7.3 %collective-permute-start.16 = (bf16[2,256,256]{2,1,0:T(8,128)(2,1)S(1)}, bf16[2,256,256]{2,1,0:T(8,128)(2,1)S(1)}, u32[]{:S(2)}, u32[]{:S(2)}) collective-permute-start(bf16[2,256,256]{2,1,0:T(8,128)(2,1)S(1)} %collective-permute-done.13), channel_id=1, source_target_pairs={{0,224},{8,40},{32,0},{40,72},{64,32},{72,104},{96,64},{104,136},{... | collective-permute-start | bytes 786440 | tf_op jit(solution)/shard_map/ppermute | solution.py:222
  83.9 7.9 %collective-permute-start.17 = (bf16[1,128,1024]{2,1,0:T(8,128)(2,1)S(1)}, bf16[1,128,1024]{2,1,0:T(8,128)(2,1)S(1)}, u32[]{:S(2)}, u32[]{:S(2)}) collective-permute-start(bf16[1,128,1024]{2,1,0:T(8,128)(2,1)S(1)} %copy-done.17), channel_id=1, source_target_pairs={{0,16},{16,0},{1,17},{17,1},{2,18},{18,2},{3,19},{19,3},{4,20},{20... | collective-permute-start | bytes 786440 | tf_op jit(solution)/shard_map/ppermute | solution.py:222
  91.8 6.4 %collective-permute-start.18 = (bf16[2,256,256]{2,1,0:T(8,128)(2,1)S(1)}, bf16[2,256,256]{2,1,0:T(8,128)(2,1)S(1)}, u32[]{:S(2)}, u32[]{:S(2)}) collective-permute-start(bf16[2,256,256]{2,1,0:T(8,128)(2,1)S(1)} %collective-permute-done.16), channel_id=1, source_target_pairs={{0,224},{8,40},{32,0},{40,72},{64,32},{72,104},{96,64},{104,136},{... | collective-permute-start | bytes 786440 | tf_op jit(solution)/shard_map/ppermute | solution.py:222
  92.5 7.9 %collective-permute-start.19 = (bf16[1,128,1024]{2,1,0:T(8,128)(2,1)S(1)}, bf16[1,128,1024]{2,1,0:T(8,128)(2,1)S(1)}, u32[]{:S(2)}, u32[]{:S(2)}) collective-permute-start(bf16[1,128,1024]{2,1,0:T(8,128)(2,1)S(1)} %get-tuple-element.113), channel_id=1, source_target_pairs={{0,16},{16,0},{1,17},{17,1},{2,18},{18,2},{3,19},{19,3},{4,20},{20... | collective-permute-start | bytes 786440 | tf_op jit(solution)/shard_map/ppermute | solution.py:222
  100.4 6.3 %collective-permute-start.20 = (bf16[1,256,256]{2,1,0:T(8,128)(2,1)S(1)}, bf16[1,256,256]{2,1,0:T(8,128)(2,1)S(1)}, u32[]{:S(2)}, u32[]{:S(2)}) collective-permute-start(bf16[1,256,256]{2,1,0:T(8,128)(2,1)S(1)} %slice_select_fusion), channel_id=1, source_target_pairs={{0,224},{8,40},{32,0},{40,72},{64,32},{72,104},{96,64},{104,136},{... | collective-permute-start | bytes 393224 | tf_op jit(solution)/shard_map/ppermute | solution.py:222
  102.0 8.0 %collective-permute-start.21 = (bf16[1,128,1024]{2,1,0:T(8,128)(2,1)S(1)}, bf16[1,128,1024]{2,1,0:T(8,128)(2,1)}, u32[]{:S(2)}, u32[]{:S(2)}) collective-permute-start(bf16[1,128,1024]{2,1,0:T(8,128)(2,1)S(1)} %get-tuple-element.118), channel_id=1, source_target_pairs={{0,16},{16,0},{1,17},{17,1},{2,18},{18,2},{3,19},{19,3},{4,20},{20... | collective-permute-start | bytes 786440 | tf_op jit(solution)/shard_map/ppermute | solution.py:222
  111.2 11.4 %collective-permute-start.23 = (bf16[7,256,256]{2,1,0:T(8,128)(2,1)S(1)}, bf16[7,256,256]{2,1,0:T(8,128)(2,1)S(1)}, u32[]{:S(2)}, u32[]{:S(2)}) collective-permute-start(bf16[7,256,256]{2,1,0:T(8,128)(2,1)S(1)} %pad_maximum_fusion.own_ref), channel_id=1, source_target_pairs={{0,8},{8,0},{1,9},{9,1},{2,10},{10,2},{3,11},{11,3},{4,12},{12,4},... | collective-permute-start | bytes 2752520 | tf_op jit(solution)/shard_map/ppermute | solution.py:222
  111.2 11.4 %collective-permute-start.22 = (bf16[2,128,1024]{2,1,0:T(8,128)(2,1)}, bf16[2,128,1024]{2,1,0:T(8,128)(2,1)}, u32[]{:S(2)}, u32[]{:S(2)}) collective-permute-start(bf16[2,128,1024]{2,1,0:T(8,128)(2,1)} %add_convert_fusion.1), channel_id=1, source_target_pairs={{32,0},{40,72},{64,32},{72,104},{96,64},{104,136},{160,128},{168,2... | collective-permute-start | bytes 1572872 | tf_op jit(solution)/shard_map/ppermute | solution.py:222
  112.5 31.8 %all-to-all-start = ((bf16[8,256,256]{2,1,0:T(8,128)(2,1)}), bf16[8,256,256]{2,1,0:T(8,128)(2,1)S(1)}, u32[]{:S(2)}, u32[]{:S(2)}) async-start(bf16[8,256,256]{2,1,0:T(8,128)(2,1)} %broadcast_in_dim.22), calls=%async_computation | async-start | bytes 2097152 | tf_op jit(solution)/shard_map/all_to_all | solution.py:348
  124.5 19.8 %collective-permute-start.24 = (bf16[2,128,1024]{2,1,0:T(8,128)(2,1)S(1)}, bf16[2,128,1024]{2,1,0:T(8,128)(2,1)}, u32[]{:S(2)}, u32[]{:S(2)}) collective-permute-start(bf16[2,128,1024]{2,1,0:T(8,128)(2,1)S(1)} %add_convert_fusion), channel_id=1, source_target_pairs={{0,224},{8,40},{32,0},{64,32},{72,104},{104,136},{128,96},{136,168... | collective-permute-start | bytes 1572872 | tf_op jit(solution)/shard_map/ppermute | solution.py:222
  132.5 11.1 %collective-permute-start.25 = (bf16[1,128,1024]{2,1,0:T(8,128)(2,1)S(1)}, bf16[1,128,1024]{2,1,0:T(8,128)(2,1)S(1)}, u32[]{:S(2)}, u32[]{:S(2)}) collective-permute-start(bf16[1,128,1024]{2,1,0:T(8,128)(2,1)S(1)} %copy-done.15), channel_id=1, source_target_pairs={{0,16},{16,0},{1,17},{17,1},{2,18},{18,2},{3,19},{19,3},{4,20},{20... | collective-permute-start | bytes 786440 | tf_op jit(solution)/shard_map/ppermute | solution.py:222
  144.3 3.8 %collective-permute-start.27 = (bf16[8,256,256]{2,1,0:T(8,128)(2,1)S(1)}, bf16[8,256,256]{2,1,0:T(8,128)(2,1)}, u32[]{:S(2)}, u32[]{:S(2)}) collective-permute-start(bf16[8,256,256]{2,1,0:T(8,128)(2,1)S(1)} %all-to-all-done.own_ref), channel_id=1, source_target_pairs={{0,8},{8,0},{1,9},{9,1},{2,10},{10,2},{3,11},{11,3},{4,12},{12,4},... | collective-permute-start | bytes 3145736 | tf_op jit(solution)/shard_map/ppermute | solution.py:222
  150.0 15.7 %collective-permute-start.28 = (bf16[128,512]{1,0:T(8,128)(2,1)S(1)}, bf16[128,512]{1,0:T(8,128)(2,1)S(1)}, u32[]{:S(2)}, u32[]{:S(2)}) collective-permute-start(bf16[128,512]{1,0:T(8,128)(2,1)S(1)} %get-tuple-element.142), channel_id=1, source_target_pairs={{0,1},{1,0},{2,3},{3,2},{4,5},{5,4},{6,7},{7,6},{8,9},{9,8},{10,11... | collective-permute-start | bytes 393224 | tf_op jit(solution)/shard_map/ppermute | solution.py:222
  151.8 13.9 %collective-permute-start.29 = (bf16[128,512]{1,0:T(8,128)(2,1)S(1)}, bf16[128,512]{1,0:T(8,128)(2,1)S(1)}, u32[]{:S(2)}, u32[]{:S(2)}) collective-permute-start(bf16[128,512]{1,0:T(8,128)(2,1)S(1)} %get-tuple-element.141), channel_id=1, source_target_pairs={{0,16},{16,0},{1,17},{17,1},{2,18},{18,2},{3,19},{19,3},{4,20},{20... | collective-permute-start | bytes 393224 | tf_op jit(solution)/shard_map/ppermute | solution.py:222
  153.3 12.5 %collective-permute-start.30 = (bf16[128,512]{1,0:T(8,128)(2,1)S(1)}, bf16[128,512]{1,0:T(8,128)(2,1)S(1)}, u32[]{:S(2)}, u32[]{:S(2)}) collective-permute-start(bf16[128,512]{1,0:T(8,128)(2,1)S(1)} %get-tuple-element.142), channel_id=1, source_target_pairs={{0,17},{1,16},{2,19},{3,18},{16,1},{17,0},{18,3},{19,2},{4,21},{5,... | collective-permute-start | bytes 393224 | tf_op jit(solution)/shard_map/ppermute | solution.py:222
  173.6 13.9 %all-to-all-start.1 = ((f32[8,1,128]{2,1,0:T(1,128)}), f32[8,1,128]{2,1,0:T(1,128)S(1)}, u32[]{:S(2)}, u32[]{:S(2)}) async-start(f32[8,1,128]{2,1,0:T(1,128)} %broadcast_in_dim.23), calls=%async_computation.1 | async-start | bytes 8192 | tf_op jit(solution)/shard_map/all_to_all | solution.py:238
  180.5 20.3 %collective-permute-start.32 = (bf16[192,512]{1,0:T(8,128)(2,1)S(1)}, bf16[192,512]{1,0:T(8,128)(2,1)S(1)}, u32[]{:S(2)}, u32[]{:S(2)}) collective-permute-start(bf16[192,512]{1,0:T(8,128)(2,1)S(1)} %slice.175), channel_id=1, source_target_pairs={{0,32},{32,64},{128,160},{160,192},{1,33},{33,65},{129,161},{161,1... | collective-permute-start | bytes 589832 | tf_op jit(solution)/shard_map/ppermute | solution.py:409
  184.4 16.4 %collective-permute-start.33 = (bf16[192,512]{1,0:T(8,128)(2,1)S(1)}, bf16[192,512]{1,0:T(8,128)(2,1)S(1)}, u32[]{:S(2)}, u32[]{:S(2)}) collective-permute-start(bf16[192,512]{1,0:T(8,128)(2,1)S(1)} %slice.175), channel_id=1, source_target_pairs={{96,64},{224,192},{97,65},{225,193},{98,66},{226,194},{99,67},{227... | collective-permute-start | bytes 589832 | tf_op jit(solution)/shard_map/ppermute | solution.py:410
  (32 other events, 265.5 us)

commit v9 on v8

--- a/solution.py
+++ b/solution.py
@@ -167,7 +167,10 @@
     out_ref[...] = inverse_rows(first_ref[aligned(i * HALF, HALF), :], sums_ref, low_ref)
 
 
-def out_inverse_kernel(tokens, at_ref, own_ref, other_ref, out_ref, sums_ref, first_ref, low_ref):
+def out_inverse_kernel(
+    tokens, count, at_ref, own_ref, other_ref,
+    out_ref, rows_ref, sums_ref, first_ref, low_ref, padded_ref,
+):
     i = pl.program_id(0)
 
     @pl.when(i == 0)
@@ -178,34 +181,39 @@
             for piece, ref in ((core, own_ref), (1 - core, other_ref)):
                 sums_ref[aligned((2 * (owner % 2) + piece) * PIECE, PIECE), here] = ref[owner]
         split_factor(tokens, sums_ref, first_ref, low_ref)
-
-    outside = jnp.logical_or(i == 0, i == 3)
-
-    @pl.when(outside)
+        nothing = jnp.zeros((count, TILE), bf16)
+        padded_ref[:count, :] = nothing
+        padded_ref[count + TILE :, :] = nothing
+
+    inverse = inverse_rows(first_ref[aligned(i * HALF, HALF), :], sums_ref, low_ref)
+    out_ref[...] = inverse
+    padded_ref[pl.ds(pl.multiple_of(count + i * HALF, 64), HALF), :] = inverse
+
+    @pl.when(i == 1)
     def _():
-        out_ref[...] = jnp.zeros_like(out_ref)
-
-    @pl.when(jnp.logical_not(outside))
-    def _():
-        out_ref[...] = inverse_rows(first_ref[aligned((i - 1) * HALF, HALF), :], sums_ref, low_ref)
-
-
-def call(kernel, steps, block, out_shape, at, *args, limit, scratch=()):
+        for n in range(2):
+            at = pl.ds(pl.multiple_of(at_ref[1 + n], 64), count)
+            rows_ref[n * count : (n + 1) * count, :] = padded_ref[at, :]
+
+
+def call(kernel, steps, block, out_shape, at, *args, limit, scratch=(), more=()):
     def whole(a):
         return pl.BlockSpec(a.shape, lambda i, at: (0,) * len(a.shape))
 
-    return pl.pallas_call(
+    outs = pl.pallas_call(
         kernel,
         grid_spec=pltpu.PrefetchScalarGridSpec(
             num_scalar_prefetch=1,
             grid=(steps,),
             in_specs=[whole(a) for a in args],
-            out_specs=pl.BlockSpec(block, lambda i, at: (i, 0)),
+            out_specs=[pl.BlockSpec(block, lambda i, at: (i, 0))]
+            + [pl.BlockSpec(m, lambda i, at: (0, 0)) for m in more],
             scratch_shapes=[pltpu.VMEM(shape, dtype) for shape, dtype in scratch],
         ),
-        out_shape=jax.ShapeDtypeStruct(out_shape, bf16),
+        out_shape=[jax.ShapeDtypeStruct(m, bf16) for m in [out_shape, *more]],
         compiler_params=pltpu.CompilerParams(vmem_limit_bytes=limit * MIB),
     )(at, *args)
+    return outs if more else outs[0]
 
 
 def ring_pairs(away=0, skip=False):
@@ -378,17 +386,19 @@
     near = jnp.where(m == 3, 2, m + 1)
     own_at = jnp.where(m == 2, TILE, slice_rows * (4 * m + row) - base)
     near_at = jnp.where(m == 2, TILE, slice_rows * (4 * near + row) - base)
-    own_at, near_at = [jnp.clip(a, -slice_rows, TILE) + HALF for a in (own_at, near_at)]
-    padded = call(
-        functools.partial(out_inverse_kernel, tokens),
-        4,
+    own_at, near_at = [jnp.clip(a, -slice_rows, TILE) + slice_rows for a in (own_at, near_at)]
+    rows_of_two = (2 * slice_rows, TILE)
+    inverse, out_inverse = call(
+        functools.partial(out_inverse_kernel, tokens, slice_rows),
+        2,
         (HALF, TILE),
-        (4 * HALF, TILE),
-        numbers(core),
+        square,
+        numbers(core, own_at, near_at),
         out_tiles,
         out_other,
         limit=32,
-        scratch=[(square, bf16), (square, f32), (square, bf16)],
+        scratch=[(square, bf16), (square, f32), (square, bf16), ((TILE + 2 * slice_rows, TILE), bf16)],
+        more=(rows_of_two,),
     )
     middle = mdot(cross, in_inverse).astype(bf16)
     mine = lax.dynamic_slice_in_dim(middle, h * HALF, HALF, 1)
@@ -397,18 +407,15 @@
         (theirs, X, SWAP_X), (mine, YH, SWAP2), (theirs, (YH, X), SWAP_BOTH)
     )
     middle = in_order(h, in_order(yh, mine, near_y), in_order(yh, near_x, near_xy))
-    middle, padded = lax.optimization_barrier((middle, padded))
+    middle, inverse, out_inverse = lax.optimization_barrier((middle, inverse, out_inverse))
     other = lax.ppermute(middle, CORE, SWAP2)
     middle = jnp.moveaxis(in_order(core, middle, other), 0, 1).reshape(TILE, HALF)
-    out_inverse = jnp.concatenate(
-        [lax.dynamic_slice_in_dim(padded, at, slice_rows, 0) for at in (own_at, near_at)], 0
-    )
     result = mdot(out_inverse, middle)
 
     near_part = result[slice_rows:].astype(bf16)
     up = lax.ppermute(near_part, Z, [(0, 1), (1, 2), (4, 5), (5, 6)])
     down = lax.ppermute(near_part, Z, [(3, 2), (7, 6)])
-    whole = mdot(padded[HALF : HALF + TILE], middle)
+    whole = mdot(inverse, middle)
     squares = jnp.where(m == 2, 0.0, jnp.sum(whole * whole))
     squares = all_sum(all_sum(squares, Z), OWNER)
     summed = result[:slice_rows] + up.astype(f32) + down.astype(f32)

time: 202 us -> 198 us (0.980)
  local copies, waits for them, and re-layouts: 13.7 us -> 8.51 us
    unnamed x56 -> x42, local copies, waits for them, and re-layouts: 9.05 us -> 5.28 us
where the time goes in v9:
time: 198 us; the launch traced here: 197 us
  starting transfers between devices  71.8 us (36%)
  waiting for transfers between devices  63.8 us (32%)
  Pallas kernels  25.4 us (13%)
  blocking collectives  10.8 us (5%)
  other arithmetic  9.82 us (5%)
  local copies, waits for them, and re-layouts  8.51 us (4%)
  matrix products  5.18 us (3%)
    ppermute x29, waiting for transfers between devices, phase(): got = [lax.ppermute(value, *send[1:]) for value, send in zip(values, sends)]  58.5 us
    ppermute x29, starting transfers between devices, phase(): got = [lax.ppermute(value, *send[1:]) for value, send in zip(values, sends)]  54.9 us
    pallas_call x3, Pallas kernels, call(): pl.pallas_call(kernel, grid_spec=pltpu.PrefetchScalarGridSpec(num_scalar_...  16.2 us
    all_to_all x1, blocking collectives, all_sum(): lax.all_to_all(jnp.full((n, 128), value, f32), axis, 0, 0, tiled=True)  10.8 us
    pallas_call x3, Pallas kernels, slots(): pl.pallas_call(kernel, grid_spec=pltpu.PrefetchScalarGridSpec(num_scalar_...  9.2 us
    all_to_all x1, starting transfers between devices, all_sum(): lax.all_to_all(jnp.full((n, 128), value, f32), axis, 0, 0, tiled=True)  6.36 us
    unnamed x42, local copies, waits for them, and re-layouts  5.28 us
    dot_general x3, matrix products, mdot(): return jnp.dot(a, b, preferred_element_type=f32)  5.18 us
  transfers between devices with their start and end apart: 36, of which 19 were waited for; matrix products, arithmetic and copies ran while one was open for 5% of the time, Pallas kernels for 11%

profile of v9, /device:TPU:16, one launch (start us, length us, event | category | flops | bytes accessed | tf_op | source)
XLA Modules:
  0.0 197.3 jit_solution(7959465847663196530)
XLA Ops:
  6.1 3.9 %shard_map.38 = (bf16[8,256,384]{2,1,0:T(8,128)(2,1)S(1)}, bf16[1,256,384]{2,1,0:T(8,128)(2,1)S(1)}) custom-call(s32[29]{0:T(128)S(1)} %stack.151.at_ref, bf16[128,4608]{1,0:T(8,128)(2,1)S(1)} %shard_map.37.pick_ref, bf16[128,4608]{1,0:T(8,128)(2,1)S(1)} %collective-permute-done.recv_ref, bf16[128,1024]{1,0:T(8,128)(2,1)S(1)} %multiply_convert_fusion.own_ref, ...), custom_call_target="tpu_custom_call" | custom-call | tf_op jit(solution)/shard_map/pallas_call | solution.py:291
  11.3 5.9 %collective-permute-start.2 = (bf16[256,384]{1,0:T(8,128)(2,1)S(1)}, bf16[256,384]{1,0:T(8,128)(2,1)S(1)}, u32[]{:S(2)}, u32[]{:S(2)}) collective-permute-start(bf16[256,384]{1,0:T(8,128)(2,1)S(1)} %bitcast.72), channel_id=1, source_target_pairs={{0,224},{8,40},{32,0},{40,72},{64,32},{72,104},{96,64},{104,136},{... | collective-permute-start | bytes 589832 | tf_op jit(solution)/shard_map/ppermute | solution.py:230
  17.1 2.2 %shard_map.39 = (bf16[3,128,1024]{2,1,0:T(8,128)(2,1)S(1)}, bf16[1,128,1024]{2,1,0:T(8,128)(2,1)S(1)}, bf16[1,128,1024]{2,1,0:T(8,128)(2,1)S(1)}, bf16[1,128,1024]{2,1,0:T(8,128)(2,1)S(1)}) custom-call(s32[29]{0:T(128)S(1)} %stack.151.at_ref, bf16[128,4608]{1,0:T(8,128)(2,1)S(1)} %shard_map.37.pick_ref, bf16[128,4608]{1,0:T(8,128)(2,1)S(1)} %collective-permute-done.recv_ref, ...), custom_call_target="tpu_custom_call" | custom-call | tf_op jit(solution)/shard_map/pallas_call | solution.py:291
  20.5 3.8 %collective-permute-start.3 = (bf16[2,256,384]{2,1,0:T(8,128)(2,1)S(1)}, bf16[2,256,384]{2,1,0:T(8,128)(2,1)S(1)}, u32[]{:S(2)}, u32[]{:S(2)}) collective-permute-start(bf16[2,256,384]{2,1,0:T(8,128)(2,1)S(1)} %add_convert_fusion.5), channel_id=1, source_target_pairs={{0,224},{8,40},{32,0},{40,72},{64,32},{72,104},{96,64},{104,136},{... | collective-permute-start | bytes 1179656 | tf_op jit(solution)/shard_map/ppermute | solution.py:230
  24.6 7.5 %collective-permute-done.4 = bf16[1,128,1024]{2,1,0:T(8,128)(2,1)S(1)} collective-permute-done((bf16[1,128,1024]{2,1,0:T(8,128)(2,1)S(1)}, bf16[1,128,1024]{2,1,0:T(8,128)(2,1)S(1)}, u32[]{:S(2)}, u32[]{:S(2)}) %collective-permute-start.4) | collective-permute-done | bytes 262176 | tf_op jit(solution)/shard_map/ppermute | solution.py:230
  33.8 7.6 %collective-permute-done.6 = bf16[1,128,1024]{2,1,0:T(8,128)(2,1)} collective-permute-done((bf16[1,128,1024]{2,1,0:T(8,128)(2,1)S(1)}, bf16[1,128,1024]{2,1,0:T(8,128)(2,1)}, u32[]{:S(2)}, u32[]{:S(2)}) %collective-permute-start.6) | collective-permute-done | bytes 262176 | tf_op jit(solution)/shard_map/ppermute | solution.py:230
  42.9 3.0 %shard_map.40 = (bf16[5,128,1024]{2,1,0:T(8,128)(2,1)S(1)}, bf16[1,128,1024]{2,1,0:T(8,128)(2,1)S(1)}, bf16[1,128,1024]{2,1,0:T(8,128)(2,1)S(1)}, bf16[1,128,102...) custom-call(s32[29]{0:T(128)S(1)} %stack.151.at_ref, ...), custom_call_target="tpu_custom_call" | custom-call | tf_op jit(solution)/shard_map/pallas_call | solution.py:291
  46.0 4.4 %collective-permute-done.8 = bf16[1,128,1024]{2,1,0:T(8,128)(2,1)S(1)} collective-permute-done((bf16[1,128,1024]{2,1,0:T(8,128)(2,1)S(1)}, bf16[1,128,1024]{2,1,0:T(8,128)(2,1)S(1)}, u32[]{:S(2)}, u32[]{:S(2)}) %collective-permute-start.8) | collective-permute-done | bytes 262176 | tf_op jit(solution)/shard_map/ppermute | solution.py:230
  52.8 3.0 %collective-permute-start.11 = (bf16[128,1024]{1,0:T(8,128)(2,1)S(1)}, bf16[128,1024]{1,0:T(8,128)(2,1)S(1)}, u32[]{:S(2)}, u32[]{:S(2)}) collective-permute-start(bf16[128,1024]{1,0:T(8,128)(2,1)S(1)} %fusion.3), channel_id=1, source_target_pairs={{0,224},{8,40},{32,0},{40,72},{96,64},{104,136},{128,96},{136,168}... | collective-permute-start | bytes 786440 | tf_op jit(solution)/shard_map/ppermute | solution.py:230
  55.8 6.5 %collective-permute-done.10 = bf16[256,512]{1,0:T(8,128)(2,1)S(1)} collective-permute-done((bf16[256,512]{1,0:T(8,128)(2,1)S(1)}, bf16[256,512]{1,0:T(8,128)(2,1)S(1)}, u32[]{:S(2)}, u32[]{:S(2)}) %collective-permute-start.10) | collective-permute-done | bytes 262176 | tf_op jit(solution)/shard_map/ppermute | solution.py:230
  67.5 3.0 %collective-permute-start.14 = (bf16[2,128,1024]{2,1,0:T(8,128)(2,1)S(1)}, bf16[2,128,1024]{2,1,0:T(8,128)(2,1)S(1)}, u32[]{:S(2)}, u32[]{:S(2)}) collective-permute-start(bf16[2,128,1024]{2,1,0:T(8,128)(2,1)S(1)} %add_convert_fusion.2), channel_id=1, source_target_pairs={{0,224},{8,40},{40,72},{64,32},{72,104},{96,64},{128,96},{136,168}... | collective-permute-start | bytes 1572872 | tf_op jit(solution)/shard_map/ppermute | solution.py:230
  71.6 2.4 %collective-permute-start.15 = (bf16[1,128,1024]{2,1,0:T(8,128)(2,1)S(1)}, bf16[1,128,1024]{2,1,0:T(8,128)(2,1)S(1)}, u32[]{:S(2)}, u32[]{:S(2)}) collective-permute-start(bf16[1,128,1024]{2,1,0:T(8,128)(2,1)S(1)} %copy-done.14), channel_id=1, source_target_pairs={{0,16},{16,0},{1,17},{17,1},{2,18},{18,2},{3,19},{19,3},{4,20},{20... | collective-permute-start | bytes 786440 | tf_op jit(solution)/shard_map/ppermute | solution.py:230
  74.0 5.9 %collective-permute-done.13 = bf16[2,256,256]{2,1,0:T(8,128)(2,1)S(1)} collective-permute-done((bf16[2,256,256]{2,1,0:T(8,128)(2,1)S(1)}, bf16[2,256,256]{2,1,0:T(8,128)(2,1)S(1)}, u32[]{:S(2)}, u32[]{:S(2)}) %collective-permute-start.13) | collective-permute-done | bytes 262176 | tf_op jit(solution)/shard_map/ppermute | solution.py:230
  80.8 2.9 %collective-permute-start.16 = (bf16[2,256,256]{2,1,0:T(8,128)(2,1)S(1)}, bf16[2,256,256]{2,1,0:T(8,128)(2,1)S(1)}, u32[]{:S(2)}, u32[]{:S(2)}) collective-permute-start(bf16[2,256,256]{2,1,0:T(8,128)(2,1)S(1)} %collective-permute-done.13), channel_id=1, source_target_pairs={{0,224},{8,40},{32,0},{40,72},{64,32},{72,104},{96,64},{104,136},{... | collective-permute-start | bytes 786440 | tf_op jit(solution)/shard_map/ppermute | solution.py:230
  83.7 3.1 %collective-permute-start.17 = (bf16[1,128,1024]{2,1,0:T(8,128)(2,1)S(1)}, bf16[1,128,1024]{2,1,0:T(8,128)(2,1)S(1)}, u32[]{:S(2)}, u32[]{:S(2)}) collective-permute-start(bf16[1,128,1024]{2,1,0:T(8,128)(2,1)S(1)} %copy-done.12), channel_id=1, source_target_pairs={{0,16},{16,0},{1,17},{17,1},{2,18},{18,2},{3,19},{19,3},{4,20},{20... | collective-permute-start | bytes 786440 | tf_op jit(solution)/shard_map/ppermute | solution.py:230
  88.2 3.4 %collective-permute-done.17 = bf16[1,128,1024]{2,1,0:T(8,128)(2,1)S(1)} collective-permute-done((bf16[1,128,1024]{2,1,0:T(8,128)(2,1)S(1)}, bf16[1,128,1024]{2,1,0:T(8,128)(2,1)S(1)}, u32[]{:S(2)}, u32[]{:S(2)}) %collective-permute-start.17) | collective-permute-done | bytes 262176 | tf_op jit(solution)/shard_map/ppermute | solution.py:230
  92.1 2.7 %collective-permute-start.19 = (bf16[1,128,1024]{2,1,0:T(8,128)(2,1)S(1)}, bf16[1,128,1024]{2,1,0:T(8,128)(2,1)S(1)}, u32[]{:S(2)}, u32[]{:S(2)}) collective-permute-start(bf16[1,128,1024]{2,1,0:T(8,128)(2,1)S(1)} %copy-done.10), channel_id=1, source_target_pairs={{0,16},{16,0},{1,17},{17,1},{2,18},{18,2},{3,19},{19,3},{4,20},{20... | collective-permute-start | bytes 786440 | tf_op jit(solution)/shard_map/ppermute | solution.py:230
  94.8 3.1 %collective-permute-done.18 = bf16[2,256,256]{2,1,0:T(8,128)(2,1)S(1)} collective-permute-done((bf16[2,256,256]{2,1,0:T(8,128)(2,1)S(1)}, bf16[2,256,256]{2,1,0:T(8,128)(2,1)S(1)}, u32[]{:S(2)}, u32[]{:S(2)}) %collective-permute-start.18) | collective-permute-done | bytes 262176 | tf_op jit(solution)/shard_map/ppermute | solution.py:230
  101.6 2.5 %collective-permute-start.21 = (bf16[1,128,1024]{2,1,0:T(8,128)(2,1)S(1)}, bf16[1,128,1024]{2,1,0:T(8,128)(2,1)S(1)}, u32[]{:S(2)}, u32[]{:S(2)}) collective-permute-start(bf16[1,128,1024]{2,1,0:T(8,128)(2,1)S(1)} %copy-done.8), channel_id=1, source_target_pairs={{0,16},{16,0},{1,17},{17,1},{2,18},{18,2},{3,19},{19,3},{4,20},{20... | collective-permute-start | bytes 786440 | tf_op jit(solution)/shard_map/ppermute | solution.py:230
  104.1 2.1 %add_convert_fusion.1 = bf16[2,128,1024]{2,1,0:T(8,128)(2,1)} fusion(bf16[2,128,1024]{2,1,0:T(8,128)(2,1)S(1)} %collective-permute-done.14, bf16[1,128,1024]{2,1,0:T(8,128)(2,1)S(1)} %collective-permute-done.17, bf16[1,128,1024]{2,1,0:T(8,128)(2,1)S(1)} %collective-permute-done.15, bf16[5,128,1024]{2,1,0:T(8,128)(2,1)} %copy-done.4), kind=kLoop, calls=%fused_computation.5 | loop fusion | flops 1835008 | bytes 2097152 | tf_op jit(solution)/shard_map/convert_element_type | solution.py:359
  106.3 3.2 %collective-permute-done.21 = bf16[1,128,1024]{2,1,0:T(8,128)(2,1)S(1)} collective-permute-done((bf16[1,128,1024]{2,1,0:T(8,128)(2,1)S(1)}, bf16[1,128,1024]{2,1,0:T(8,128)(2,1)S(1)}, u32[]{:S(2)}, u32[]{:S(2)}) %collective-permute-start.21) | collective-permute-done | bytes 262176 | tf_op jit(solution)/shard_map/ppermute | solution.py:230
  112.5 5.1 %all-to-all-start = ((bf16[8,256,256]{2,1,0:T(8,128)(2,1)}), bf16[8,256,256]{2,1,0:T(8,128)(2,1)S(1)}, u32[]{:S(2)}, u32[]{:S(2)}) async-start(bf16[8,256,256]{2,1,0:T(8,128)(2,1)} %broadcast_in_dim.22), calls=%async_computation | async-start | bytes 2097152 | tf_op jit(solution)/shard_map/all_to_all | solution.py:356
  117.6 5.0 %collective-permute-done.22 = bf16[2,128,1024]{2,1,0:T(8,128)(2,1)} collective-permute-done((bf16[2,128,1024]{2,1,0:T(8,128)(2,1)}, bf16[2,128,1024]{2,1,0:T(8,128)(2,1)}, u32[]{:S(2)}, u32[]{:S(2)}) %collective-permute-start.22) | collective-permute-done | bytes 524320 | tf_op jit(solution)/shard_map/ppermute | solution.py:230
  124.2 7.9 %collective-permute-start.24 = (bf16[2,128,1024]{2,1,0:T(8,128)(2,1)S(1)}, bf16[2,128,1024]{2,1,0:T(8,128)(2,1)}, u32[]{:S(2)}, u32[]{:S(2)}) collective-permute-start(bf16[2,128,1024]{2,1,0:T(8,128)(2,1)S(1)} %add_convert_fusion), channel_id=1, source_target_pairs={{0,224},{8,40},{32,0},{64,32},{72,104},{104,136},{128,96},{136,168... | collective-permute-start | bytes 1572872 | tf_op jit(solution)/shard_map/ppermute | solution.py:230
  134.2 7.8 %shard_map.41 = bf16[1024,1024]{1,0:T(8,128)(2,1)S(1)} custom-call(s32[2]{0:T(128)S(1)} %pad_add_fusion.1.at_ref, bf16[2,256,256]{2,1,0:T(8,128)(2,1)S(1)} %pad_maximum_fusion.6.shard_ref, bf16[7,256,256]{2,1,0:T(8,128)(2,1)S(1)} %pad_maximum_fusion.own_ref, bf16[7,256,256]{2,1,0:T(8,128)(2,1)S(1)} %collective-permute-done.23.other_ref), custom_call_target="tpu_custom_call" | custom-call | tf_op jit(solution)/shard_map/pallas_call | solution.py:203
  144.7 3.1 %collective-permute-done.26 = bf16[2,128,1024]{2,1,0:T(8,128)(2,1)S(1)} collective-permute-done((bf16[2,128,1024]{2,1,0:T(8,128)(2,1)}, bf16[2,128,1024]{2,1,0:T(8,128)(2,1)S(1)}, u32[]{:S(2)}, u32[]{:S(2)}) %collective-permute-start.26) | collective-permute-done | bytes 524320 | tf_op jit(solution)/shard_map/ppermute | solution.py:230
  147.8 2.5 %convolution_convert_fusion = bf16[128,1024]{1,0:T(8,128)(2,1)S(1)} fusion(bf16[1024,1024]{1,0:T(8,128)(2,1)} %copy-done, bf16[1,128,1024]{2,1,0:T(8,128)(2,1)} %copy-done.20, bf16[5,128,1024]{2,1,0:T(8,128)(2,1)} %copy-done.4, bf16[2,128,1024]{2,1,0:T(8,128)(2,1)S(1)} %collective-permute-done.26, bf16[2,128,1024]{2,1,0:T(8,128)(2,1)} %collective-permute-done.24, ...), kind=kOutput, calls=%fused_computation.2 | convolution fusion | flops 269877248 | bytes 3932161 | tf_op jit(solution)/shard_map/dot_general | solution.py:32
  155.7 7.7 %shard_map.42 = (bf16[1024,1024]{1,0:T(8,128)(2,1)S(1)}, bf16[384,1024]{1,0:T(8,128)(2,1)S(1)}) custom-call(s32[3]{0:T(128)S(1)} %pad_add_fusion.2.at_ref, bf16[8,256,256]{2,1,0:T(8,128)(2,1)S(1)} %all-to-all-done.own_ref, bf16[8,256,256]{2,1,0:T(8,128)(2,1)S(1)} %collective-permute-done.27.other_ref), custom_call_target="tpu_custom_call" | custom-call | tf_op jit(solution)/shard_map/pallas_call | solution.py:203
  169.2 6.4 %all-to-all-start.1 = ((f32[8,1,128]{2,1,0:T(1,128)}), f32[8,1,128]{2,1,0:T(1,128)S(1)}, u32[]{:S(2)}, u32[]{:S(2)}) async-start(f32[8,1,128]{2,1,0:T(1,128)} %broadcast_in_dim.23), calls=%async_computation.1 | async-start | bytes 8192 | tf_op jit(solution)/shard_map/all_to_all | solution.py:246
  176.2 3.9 %collective-permute-start.32 = (bf16[192,512]{1,0:T(8,128)(2,1)S(1)}, bf16[192,512]{1,0:T(8,128)(2,1)S(1)}, u32[]{:S(2)}, u32[]{:S(2)}) collective-permute-start(bf16[192,512]{1,0:T(8,128)(2,1)S(1)} %slice.167), channel_id=1, source_target_pairs={{0,32},{32,64},{128,160},{160,192},{1,33},{33,65},{129,161},{161,1... | collective-permute-start | bytes 589832 | tf_op jit(solution)/shard_map/ppermute | solution.py:416
  180.8 2.4 %all-to-all-done.1 = f32[8,1,128]{2,1,0:T(1,128)S(1)} async-done(((f32[8,1,128]{2,1,0:T(1,128)}), f32[8,1,128]{2,1,0:T(1,128)S(1)}, u32[]{:S(2)}, u32[]{:S(2)}) %all-to-all-start.1) | async-done | bytes 4128 | tf_op jit(solution)/shard_map/all_to_all | solution.py:246
  184.4 10.8 %all_to_all.23 = f32[8,1,128]{2,1,0:T(1,128)S(1)} all-to-all(f32[8,1,128]{2,1,0:T(1,128)S(1)} %broadcast_in_dim.24), channel_id=1, replica_groups=mesh['dp_0'=8,'dp_1'=2,'dp_2'=2,'owner_0'=2,'owner_1'=4] {'owner_0','own..., dimensions={0} | all-to-all | bytes 8192 | tf_op jit(solution)/shard_map/all_to_all | solution.py:246
  (135 shorter events, 50.3 us)
Async XLA Ops:
  2.2 3.9 %collective-permute-start = (bf16[128,4608]{1,0:T(8,128)(2,1)S(1)}, bf16[128,4608]{1,0:T(8,128)(2,1)S(1)}, u32[]{:S(2)}, u32[]{:S(2)}) collective-permute-start(bf16[128,4608]{1,0:T(8,128)(2,1)S(1)} %shard_map.37.pick_ref), channel_id=1, source_target_pairs={{0,8},{8,0},{1,9},{9,1},{2,10},{10,2},{3,11},{11,3},{4,12},{12,4},... | collective-permute-start | bytes 3538952 | tf_op jit(solution)/shard_map/ppermute | solution.py:271
  11.3 9.1 %collective-permute-start.2 = (bf16[256,384]{1,0:T(8,128)(2,1)S(1)}, bf16[256,384]{1,0:T(8,128)(2,1)S(1)}, u32[]{:S(2)}, u32[]{:S(2)}) collective-permute-start(bf16[256,384]{1,0:T(8,128)(2,1)S(1)} %bitcast.72), channel_id=1, source_target_pairs={{0,224},{8,40},{32,0},{40,72},{64,32},{72,104},{96,64},{104,136},{... | collective-permute-start | bytes 589832 | tf_op jit(solution)/shard_map/ppermute | solution.py:230
  20.5 11.6 %collective-permute-start.3 = (bf16[2,256,384]{2,1,0:T(8,128)(2,1)S(1)}, bf16[2,256,384]{2,1,0:T(8,128)(2,1)S(1)}, u32[]{:S(2)}, u32[]{:S(2)}) collective-permute-start(bf16[2,256,384]{2,1,0:T(8,128)(2,1)S(1)} %add_convert_fusion.5), channel_id=1, source_target_pairs={{0,224},{8,40},{32,0},{40,72},{64,32},{72,104},{96,64},{104,136},{... | collective-permute-start | bytes 1179656 | tf_op jit(solution)/shard_map/ppermute | solution.py:230
  24.2 7.9 %collective-permute-start.4 = (bf16[1,128,1024]{2,1,0:T(8,128)(2,1)S(1)}, bf16[1,128,1024]{2,1,0:T(8,128)(2,1)S(1)}, u32[]{:S(2)}, u32[]{:S(2)}) collective-permute-start(bf16[1,128,1024]{2,1,0:T(8,128)(2,1)S(1)} %get-tuple-element.84), channel_id=1, source_target_pairs={{0,16},{16,0},{1,17},{17,1},{2,18},{18,2},{3,19},{19,3},{4,20},{20... | collective-permute-start | bytes 786440 | tf_op jit(solution)/shard_map/ppermute | solution.py:230
  32.2 9.2 %collective-permute-start.5 = (bf16[2,256,384]{2,1,0:T(8,128)(2,1)S(1)}, bf16[2,256,384]{2,1,0:T(8,128)(2,1)S(1)}, u32[]{:S(2)}, u32[]{:S(2)}) collective-permute-start(bf16[2,256,384]{2,1,0:T(8,128)(2,1)S(1)} %add_convert_fusion.4), channel_id=1, source_target_pairs={{0,224},{8,40},{32,0},{40,72},{64,32},{72,104},{96,64},{104,136},{... | collective-permute-start | bytes 1179656 | tf_op jit(solution)/shard_map/ppermute | solution.py:230
  33.4 8.0 %collective-permute-start.6 = (bf16[1,128,1024]{2,1,0:T(8,128)(2,1)S(1)}, bf16[1,128,1024]{2,1,0:T(8,128)(2,1)}, u32[]{:S(2)}, u32[]{:S(2)}) collective-permute-start(bf16[1,128,1024]{2,1,0:T(8,128)(2,1)S(1)} %get-tuple-element.88), channel_id=1, source_target_pairs={{0,16},{16,0},{1,17},{17,1},{2,18},{18,2},{3,19},{19,3},{4,20},{20... | collective-permute-start | bytes 786440 | tf_op jit(solution)/shard_map/ppermute | solution.py:230
  41.5 9.0 %collective-permute-start.7 = (bf16[2,256,384]{2,1,0:T(8,128)(2,1)S(1)}, bf16[2,256,384]{2,1,0:T(8,128)(2,1)S(1)}, u32[]{:S(2)}, u32[]{:S(2)}) collective-permute-start(bf16[2,256,384]{2,1,0:T(8,128)(2,1)S(1)} %add_convert_fusion.3), channel_id=1, source_target_pairs={{0,224},{8,40},{32,0},{40,72},{64,32},{72,104},{96,64},{104,136},{... | collective-permute-start | bytes 1179656 | tf_op jit(solution)/shard_map/ppermute | solution.py:230
  42.6 7.9 %collective-permute-start.8 = (bf16[1,128,1024]{2,1,0:T(8,128)(2,1)S(1)}, bf16[1,128,1024]{2,1,0:T(8,128)(2,1)S(1)}, u32[]{:S(2)}, u32[]{:S(2)}) collective-permute-start(bf16[1,128,1024]{2,1,0:T(8,128)(2,1)S(1)} %get-tuple-element.92), channel_id=1, source_target_pairs={{0,16},{16,0},{1,17},{17,1},{2,18},{18,2},{3,19},{19,3},{4,20},{20... | collective-permute-start | bytes 786440 | tf_op jit(solution)/shard_map/ppermute | solution.py:230
  52.3 9.9 %collective-permute-start.10 = (bf16[256,512]{1,0:T(8,128)(2,1)S(1)}, bf16[256,512]{1,0:T(8,128)(2,1)S(1)}, u32[]{:S(2)}, u32[]{:S(2)}) collective-permute-start(bf16[256,512]{1,0:T(8,128)(2,1)S(1)} %add_convert_fusion.9), channel_id=1, source_target_pairs={{0,16},{16,0},{1,17},{17,1},{2,18},{18,2},{3,19},{19,3},{4,20},{20... | collective-permute-start | bytes 786440 | tf_op jit(solution)/shard_map/ppermute | solution.py:230
  52.8 9.5 %collective-permute-start.11 = (bf16[128,1024]{1,0:T(8,128)(2,1)S(1)}, bf16[128,1024]{1,0:T(8,128)(2,1)S(1)}, u32[]{:S(2)}, u32[]{:S(2)}) collective-permute-start(bf16[128,1024]{1,0:T(8,128)(2,1)S(1)} %fusion.3), channel_id=1, source_target_pairs={{0,224},{8,40},{32,0},{40,72},{96,64},{104,136},{128,96},{136,168}... | collective-permute-start | bytes 786440 | tf_op jit(solution)/shard_map/ppermute | solution.py:230
  62.4 5.1 %collective-permute-start.12 = (bf16[256,256]{1,0:T(8,128)(2,1)S(1)}, bf16[256,256]{1,0:T(8,128)(2,1)S(1)}, u32[]{:S(2)}, u32[]{:S(2)}) collective-permute-start(bf16[256,256]{1,0:T(8,128)(2,1)S(1)} %slice.111), channel_id=1, source_target_pairs={{0,1},{1,0},{2,3},{3,2},{4,5},{5,4},{6,7},{7,6},{8,9},{9,8},{10,11... | collective-permute-start | bytes 393224 | tf_op jit(solution)/shard_map/ppermute | solution.py:230
  67.5 13.3 %collective-permute-start.14 = (bf16[2,128,1024]{2,1,0:T(8,128)(2,1)S(1)}, bf16[2,128,1024]{2,1,0:T(8,128)(2,1)S(1)}, u32[]{:S(2)}, u32[]{:S(2)}) collective-permute-start(bf16[2,128,1024]{2,1,0:T(8,128)(2,1)S(1)} %add_convert_fusion.2), channel_id=1, source_target_pairs={{0,224},{8,40},{40,72},{64,32},{72,104},{96,64},{128,96},{136,168}... | collective-permute-start | bytes 1572872 | tf_op jit(solution)/shard_map/ppermute | solution.py:230
  70.5 9.5 %collective-permute-start.13 = (bf16[2,256,256]{2,1,0:T(8,128)(2,1)S(1)}, bf16[2,256,256]{2,1,0:T(8,128)(2,1)S(1)}, u32[]{:S(2)}, u32[]{:S(2)}) collective-permute-start(bf16[2,256,256]{2,1,0:T(8,128)(2,1)S(1)} %pad_maximum_fusion.6.shard_ref), channel_id=1, source_target_pairs={{0,224},{8,40},{32,0},{40,72},{64,32},{72,104},{96,64},{104,136},{... | collective-permute-start | bytes 786440 | tf_op jit(solution)/shard_map/ppermute | solution.py:230
  71.6 9.2 %collective-permute-start.15 = (bf16[1,128,1024]{2,1,0:T(8,128)(2,1)S(1)}, bf16[1,128,1024]{2,1,0:T(8,128)(2,1)S(1)}, u32[]{:S(2)}, u32[]{:S(2)}) collective-permute-start(bf16[1,128,1024]{2,1,0:T(8,128)(2,1)S(1)} %copy-done.14), channel_id=1, source_target_pairs={{0,16},{16,0},{1,17},{17,1},{2,18},{18,2},{3,19},{19,3},{4,20},{20... | collective-permute-start | bytes 786440 | tf_op jit(solution)/shard_map/ppermute | solution.py:230
  80.8 7.3 %collective-permute-start.16 = (bf16[2,256,256]{2,1,0:T(8,128)(2,1)S(1)}, bf16[2,256,256]{2,1,0:T(8,128)(2,1)S(1)}, u32[]{:S(2)}, u32[]{:S(2)}) collective-permute-start(bf16[2,256,256]{2,1,0:T(8,128)(2,1)S(1)} %collective-permute-done.13), channel_id=1, source_target_pairs={{0,224},{8,40},{32,0},{40,72},{64,32},{72,104},{96,64},{104,136},{... | collective-permute-start | bytes 786440 | tf_op jit(solution)/shard_map/ppermute | solution.py:230
  83.7 7.9 %collective-permute-start.17 = (bf16[1,128,1024]{2,1,0:T(8,128)(2,1)S(1)}, bf16[1,128,1024]{2,1,0:T(8,128)(2,1)S(1)}, u32[]{:S(2)}, u32[]{:S(2)}) collective-permute-start(bf16[1,128,1024]{2,1,0:T(8,128)(2,1)S(1)} %copy-done.12), channel_id=1, source_target_pairs={{0,16},{16,0},{1,17},{17,1},{2,18},{18,2},{3,19},{19,3},{4,20},{20... | collective-permute-start | bytes 786440 | tf_op jit(solution)/shard_map/ppermute | solution.py:230
  91.6 6.4 %collective-permute-start.18 = (bf16[2,256,256]{2,1,0:T(8,128)(2,1)S(1)}, bf16[2,256,256]{2,1,0:T(8,128)(2,1)S(1)}, u32[]{:S(2)}, u32[]{:S(2)}) collective-permute-start(bf16[2,256,256]{2,1,0:T(8,128)(2,1)S(1)} %collective-permute-done.16), channel_id=1, source_target_pairs={{0,224},{8,40},{32,0},{40,72},{64,32},{72,104},{96,64},{104,136},{... | collective-permute-start | bytes 786440 | tf_op jit(solution)/shard_map/ppermute | solution.py:230
  92.1 7.9 %collective-permute-start.19 = (bf16[1,128,1024]{2,1,0:T(8,128)(2,1)S(1)}, bf16[1,128,1024]{2,1,0:T(8,128)(2,1)S(1)}, u32[]{:S(2)}, u32[]{:S(2)}) collective-permute-start(bf16[1,128,1024]{2,1,0:T(8,128)(2,1)S(1)} %copy-done.10), channel_id=1, source_target_pairs={{0,16},{16,0},{1,17},{17,1},{2,18},{18,2},{3,19},{19,3},{4,20},{20... | collective-permute-start | bytes 786440 | tf_op jit(solution)/shard_map/ppermute | solution.py:230
  100.0 6.3 %collective-permute-start.20 = (bf16[1,256,256]{2,1,0:T(8,128)(2,1)S(1)}, bf16[1,256,256]{2,1,0:T(8,128)(2,1)S(1)}, u32[]{:S(2)}, u32[]{:S(2)}) collective-permute-start(bf16[1,256,256]{2,1,0:T(8,128)(2,1)S(1)} %slice_select_fusion), channel_id=1, source_target_pairs={{0,224},{8,40},{32,0},{40,72},{64,32},{72,104},{96,64},{104,136},{... | collective-permute-start | bytes 393224 | tf_op jit(solution)/shard_map/ppermute | solution.py:230
  101.6 7.9 %collective-permute-start.21 = (bf16[1,128,1024]{2,1,0:T(8,128)(2,1)S(1)}, bf16[1,128,1024]{2,1,0:T(8,128)(2,1)S(1)}, u32[]{:S(2)}, u32[]{:S(2)}) collective-permute-start(bf16[1,128,1024]{2,1,0:T(8,128)(2,1)S(1)} %copy-done.8), channel_id=1, source_target_pairs={{0,16},{16,0},{1,17},{17,1},{2,18},{18,2},{3,19},{19,3},{4,20},{20... | collective-permute-start | bytes 786440 | tf_op jit(solution)/shard_map/ppermute | solution.py:230
  111.2 11.4 %collective-permute-start.23 = (bf16[7,256,256]{2,1,0:T(8,128)(2,1)S(1)}, bf16[7,256,256]{2,1,0:T(8,128)(2,1)S(1)}, u32[]{:S(2)}, u32[]{:S(2)}) collective-permute-start(bf16[7,256,256]{2,1,0:T(8,128)(2,1)S(1)} %pad_maximum_fusion.own_ref), channel_id=1, source_target_pairs={{0,8},{8,0},{1,9},{9,1},{2,10},{10,2},{3,11},{11,3},{4,12},{12,4},... | collective-permute-start | bytes 2752520 | tf_op jit(solution)/shard_map/ppermute | solution.py:230
  111.2 11.4 %collective-permute-start.22 = (bf16[2,128,1024]{2,1,0:T(8,128)(2,1)}, bf16[2,128,1024]{2,1,0:T(8,128)(2,1)}, u32[]{:S(2)}, u32[]{:S(2)}) collective-permute-start(bf16[2,128,1024]{2,1,0:T(8,128)(2,1)} %add_convert_fusion.1), channel_id=1, source_target_pairs={{32,0},{40,72},{64,32},{72,104},{96,64},{104,136},{160,128},{168,2... | collective-permute-start | bytes 1572872 | tf_op jit(solution)/shard_map/ppermute | solution.py:230
  112.5 31.6 %all-to-all-start = ((bf16[8,256,256]{2,1,0:T(8,128)(2,1)}), bf16[8,256,256]{2,1,0:T(8,128)(2,1)S(1)}, u32[]{:S(2)}, u32[]{:S(2)}) async-start(bf16[8,256,256]{2,1,0:T(8,128)(2,1)} %broadcast_in_dim.22), calls=%async_computation | async-start | bytes 2097152 | tf_op jit(solution)/shard_map/all_to_all | solution.py:356
  124.2 19.9 %collective-permute-start.24 = (bf16[2,128,1024]{2,1,0:T(8,128)(2,1)S(1)}, bf16[2,128,1024]{2,1,0:T(8,128)(2,1)}, u32[]{:S(2)}, u32[]{:S(2)}) collective-permute-start(bf16[2,128,1024]{2,1,0:T(8,128)(2,1)S(1)} %add_convert_fusion), channel_id=1, source_target_pairs={{0,224},{8,40},{32,0},{64,32},{72,104},{104,136},{128,96},{136,168... | collective-permute-start | bytes 1572872 | tf_op jit(solution)/shard_map/ppermute | solution.py:230
  132.2 11.3 %collective-permute-start.25 = (bf16[1,128,1024]{2,1,0:T(8,128)(2,1)S(1)}, bf16[1,128,1024]{2,1,0:T(8,128)(2,1)S(1)}, u32[]{:S(2)}, u32[]{:S(2)}) collective-permute-start(bf16[1,128,1024]{2,1,0:T(8,128)(2,1)S(1)} %get-tuple-element.133), channel_id=1, source_target_pairs={{0,16},{16,0},{1,17},{17,1},{2,18},{18,2},{3,19},{19,3},{4,20},{20... | collective-permute-start | bytes 786440 | tf_op jit(solution)/shard_map/ppermute | solution.py:230
  144.1 3.6 %collective-permute-start.27 = (bf16[8,256,256]{2,1,0:T(8,128)(2,1)S(1)}, bf16[8,256,256]{2,1,0:T(8,128)(2,1)S(1)}, u32[]{:S(2)}, u32[]{:S(2)}) collective-permute-start(bf16[8,256,256]{2,1,0:T(8,128)(2,1)S(1)} %all-to-all-done.own_ref), channel_id=1, source_target_pairs={{0,8},{8,0},{1,9},{9,1},{2,10},{10,2},{3,11},{11,3},{4,12},{12,4},... | collective-permute-start | bytes 3145736 | tf_op jit(solution)/shard_map/ppermute | solution.py:230
  150.3 13.1 %collective-permute-start.28 = (bf16[128,512]{1,0:T(8,128)(2,1)S(1)}, bf16[128,512]{1,0:T(8,128)(2,1)S(1)}, u32[]{:S(2)}, u32[]{:S(2)}) collective-permute-start(bf16[128,512]{1,0:T(8,128)(2,1)S(1)} %get-tuple-element.145), channel_id=1, source_target_pairs={{0,1},{1,0},{2,3},{3,2},{4,5},{5,4},{6,7},{7,6},{8,9},{9,8},{10,11... | collective-permute-start | bytes 393224 | tf_op jit(solution)/shard_map/ppermute | solution.py:230
  152.1 11.3 %collective-permute-start.29 = (bf16[128,512]{1,0:T(8,128)(2,1)S(1)}, bf16[128,512]{1,0:T(8,128)(2,1)S(1)}, u32[]{:S(2)}, u32[]{:S(2)}) collective-permute-start(bf16[128,512]{1,0:T(8,128)(2,1)S(1)} %get-tuple-element.144), channel_id=1, source_target_pairs={{0,16},{16,0},{1,17},{17,1},{2,18},{18,2},{3,19},{19,3},{4,20},{20... | collective-permute-start | bytes 393224 | tf_op jit(solution)/shard_map/ppermute | solution.py:230
  153.6 9.9 %collective-permute-start.30 = (bf16[128,512]{1,0:T(8,128)(2,1)S(1)}, bf16[128,512]{1,0:T(8,128)(2,1)S(1)}, u32[]{:S(2)}, u32[]{:S(2)}) collective-permute-start(bf16[128,512]{1,0:T(8,128)(2,1)S(1)} %get-tuple-element.145), channel_id=1, source_target_pairs={{0,17},{1,16},{2,19},{3,18},{16,1},{17,0},{18,3},{19,2},{4,21},{5,... | collective-permute-start | bytes 393224 | tf_op jit(solution)/shard_map/ppermute | solution.py:230
  169.2 14.0 %all-to-all-start.1 = ((f32[8,1,128]{2,1,0:T(1,128)}), f32[8,1,128]{2,1,0:T(1,128)S(1)}, u32[]{:S(2)}, u32[]{:S(2)}) async-start(f32[8,1,128]{2,1,0:T(1,128)} %broadcast_in_dim.23), calls=%async_computation.1 | async-start | bytes 8192 | tf_op jit(solution)/shard_map/all_to_all | solution.py:246
  176.2 20.3 %collective-permute-start.32 = (bf16[192,512]{1,0:T(8,128)(2,1)S(1)}, bf16[192,512]{1,0:T(8,128)(2,1)S(1)}, u32[]{:S(2)}, u32[]{:S(2)}) collective-permute-start(bf16[192,512]{1,0:T(8,128)(2,1)S(1)} %slice.167), channel_id=1, source_target_pairs={{0,32},{32,64},{128,160},{160,192},{1,33},{33,65},{129,161},{161,1... | collective-permute-start | bytes 589832 | tf_op jit(solution)/shard_map/ppermute | solution.py:416
  180.1 16.4 %collective-permute-start.33 = (bf16[192,512]{1,0:T(8,128)(2,1)S(1)}, bf16[192,512]{1,0:T(8,128)(2,1)S(1)}, u32[]{:S(2)}, u32[]{:S(2)}) collective-permute-start(bf16[192,512]{1,0:T(8,128)(2,1)S(1)} %slice.167), channel_id=1, source_target_pairs={{96,64},{224,192},{97,65},{225,193},{98,66},{226,194},{99,67},{227... | collective-permute-start | bytes 589832 | tf_op jit(solution)/shard_map/ppermute | solution.py:417
  (25 other events, 202.8 us)

commit v10 on v9

--- a/solution.py
+++ b/solution.py
@@ -412,12 +412,12 @@
     middle = jnp.moveaxis(in_order(core, middle, other), 0, 1).reshape(TILE, HALF)
     result = mdot(out_inverse, middle)
 
-    near_part = result[slice_rows:].astype(bf16)
+    whole = mdot(inverse, middle)
+    squares = all_sum(jnp.where(m == 2, 0.0, jnp.sum(whole * whole)), Z)
+    near_part, squares = lax.optimization_barrier((result[slice_rows:].astype(bf16), squares))
     up = lax.ppermute(near_part, Z, [(0, 1), (1, 2), (4, 5), (5, 6)])
     down = lax.ppermute(near_part, Z, [(3, 2), (7, 6)])
-    whole = mdot(inverse, middle)
-    squares = jnp.where(m == 2, 0.0, jnp.sum(whole * whole))
-    squares = all_sum(all_sum(squares, Z), OWNER)
+    squares = all_sum(squares, OWNER)
     summed = result[:slice_rows] + up.astype(f32) + down.astype(f32)
     return (summed * lax.rsqrt(squares / (width * out_width) + 1e-06)).astype(bf16)
 

time: 198 us -> 201 us (1.015)
  waiting for transfers between devices: 63.8 us -> 68.5 us
    all_to_all x1, waiting for transfers between devices: 2.37 us -> 7 us  [all_sum(): lax.all_to_all(jnp.full((n, 128), value, f32), axis, 0, 0, tiled=True)]
  transfers between devices with their start and end apart: 36 -> 36, of which waited for: 19 -> 19; matrix products, arithmetic and copies ran while one was open for 5% -> 5% of each run, Pallas kernels for 11% -> 10%
where the time goes in v10:
time: 201 us; the launch traced here: 200 us
  starting transfers between devices  70.3 us (35%)
  waiting for transfers between devices  68.5 us (34%)
  Pallas kernels  25.4 us (13%)
  blocking collectives  10.8 us (5%)
  other arithmetic  9.82 us (5%)
  local copies, waits for them, and re-layouts  8.51 us (4%)
  matrix products  5.18 us (3%)
    ppermute x29, waiting for transfers between devices, phase(): got = [lax.ppermute(value, *send[1:]) for value, send in zip(values, sends)]  58.5 us
    ppermute x29, starting transfers between devices, phase(): got = [lax.ppermute(value, *send[1:]) for value, send in zip(values, sends)]  54.9 us
    pallas_call x3, Pallas kernels, call(): pl.pallas_call(kernel, grid_spec=pltpu.PrefetchScalarGridSpec(num_scalar_...  16.2 us
    all_to_all x1, blocking collectives, all_sum(): lax.all_to_all(jnp.full((n, 128), value, f32), axis, 0, 0, tiled=True)  10.8 us
    pallas_call x3, Pallas kernels, slots(): pl.pallas_call(kernel, grid_spec=pltpu.PrefetchScalarGridSpec(num_scalar_...  9.2 us
    all_to_all x1, waiting for transfers between devices, all_sum(): lax.all_to_all(jnp.full((n, 128), value, f32), axis, 0, 0, tiled=True)  7 us
    all_to_all x1, starting transfers between devices, all_sum(): lax.all_to_all(jnp.full((n, 128), value, f32), axis, 0, 0, tiled=True)  6.36 us
    unnamed x42, local copies, waits for them, and re-layouts  5.28 us
  transfers between devices with their start and end apart: 36, of which 19 were waited for; matrix products, arithmetic and copies ran while one was open for 5% of the time, Pallas kernels for 10%

profile of v10, /device:TPU:16, one launch (start us, length us, event | category | flops | bytes accessed | tf_op | source)
XLA Modules:
  0.0 200.5 jit_solution(8863117259931354993)
XLA Ops:
  6.1 3.9 %shard_map.38 = (bf16[8,256,384]{2,1,0:T(8,128)(2,1)S(1)}, bf16[1,256,384]{2,1,0:T(8,128)(2,1)S(1)}) custom-call(s32[29]{0:T(128)S(1)} %stack.151.at_ref, bf16[128,4608]{1,0:T(8,128)(2,1)S(1)} %shard_map.37.pick_ref, bf16[128,4608]{1,0:T(8,128)(2,1)S(1)} %collective-permute-done.recv_ref, bf16[128,1024]{1,0:T(8,128)(2,1)S(1)} %multiply_convert_fusion.own_ref, ...), custom_call_target="tpu_custom_call" | custom-call | tf_op jit(solution)/shard_map/pallas_call | solution.py:291
  11.3 5.9 %collective-permute-start.2 = (bf16[256,384]{1,0:T(8,128)(2,1)S(1)}, bf16[256,384]{1,0:T(8,128)(2,1)S(1)}, u32[]{:S(2)}, u32[]{:S(2)}) collective-permute-start(bf16[256,384]{1,0:T(8,128)(2,1)S(1)} %bitcast.72), channel_id=1, source_target_pairs={{0,224},{8,40},{32,0},{40,72},{64,32},{72,104},{96,64},{104,136},{... | collective-permute-start | bytes 589832 | tf_op jit(solution)/shard_map/ppermute | solution.py:230
  17.1 2.2 %shard_map.39 = (bf16[3,128,1024]{2,1,0:T(8,128)(2,1)S(1)}, bf16[1,128,1024]{2,1,0:T(8,128)(2,1)S(1)}, bf16[1,128,1024]{2,1,0:T(8,128)(2,1)S(1)}, bf16[1,128,1024]{2,1,0:T(8,128)(2,1)S(1)}) custom-call(s32[29]{0:T(128)S(1)} %stack.151.at_ref, bf16[128,4608]{1,0:T(8,128)(2,1)S(1)} %shard_map.37.pick_ref, bf16[128,4608]{1,0:T(8,128)(2,1)S(1)} %collective-permute-done.recv_ref, ...), custom_call_target="tpu_custom_call" | custom-call | tf_op jit(solution)/shard_map/pallas_call | solution.py:291
  20.5 3.8 %collective-permute-start.3 = (bf16[2,256,384]{2,1,0:T(8,128)(2,1)S(1)}, bf16[2,256,384]{2,1,0:T(8,128)(2,1)S(1)}, u32[]{:S(2)}, u32[]{:S(2)}) collective-permute-start(bf16[2,256,384]{2,1,0:T(8,128)(2,1)S(1)} %add_convert_fusion.5), channel_id=1, source_target_pairs={{0,224},{8,40},{32,0},{40,72},{64,32},{72,104},{96,64},{104,136},{... | collective-permute-start | bytes 1179656 | tf_op jit(solution)/shard_map/ppermute | solution.py:230
  24.6 7.5 %collective-permute-done.4 = bf16[1,128,1024]{2,1,0:T(8,128)(2,1)S(1)} collective-permute-done((bf16[1,128,1024]{2,1,0:T(8,128)(2,1)S(1)}, bf16[1,128,1024]{2,1,0:T(8,128)(2,1)S(1)}, u32[]{:S(2)}, u32[]{:S(2)}) %collective-permute-start.4) | collective-permute-done | bytes 262176 | tf_op jit(solution)/shard_map/ppermute | solution.py:230
  33.8 7.6 %collective-permute-done.6 = bf16[1,128,1024]{2,1,0:T(8,128)(2,1)} collective-permute-done((bf16[1,128,1024]{2,1,0:T(8,128)(2,1)S(1)}, bf16[1,128,1024]{2,1,0:T(8,128)(2,1)}, u32[]{:S(2)}, u32[]{:S(2)}) %collective-permute-start.6) | collective-permute-done | bytes 262176 | tf_op jit(solution)/shard_map/ppermute | solution.py:230
  42.9 3.0 %shard_map.40 = (bf16[5,128,1024]{2,1,0:T(8,128)(2,1)S(1)}, bf16[1,128,1024]{2,1,0:T(8,128)(2,1)S(1)}, bf16[1,128,1024]{2,1,0:T(8,128)(2,1)S(1)}, bf16[1,128,102...) custom-call(s32[29]{0:T(128)S(1)} %stack.151.at_ref, ...), custom_call_target="tpu_custom_call" | custom-call | tf_op jit(solution)/shard_map/pallas_call | solution.py:291
  46.0 4.4 %collective-permute-done.8 = bf16[1,128,1024]{2,1,0:T(8,128)(2,1)S(1)} collective-permute-done((bf16[1,128,1024]{2,1,0:T(8,128)(2,1)S(1)}, bf16[1,128,1024]{2,1,0:T(8,128)(2,1)S(1)}, u32[]{:S(2)}, u32[]{:S(2)}) %collective-permute-start.8) | collective-permute-done | bytes 262176 | tf_op jit(solution)/shard_map/ppermute | solution.py:230
  52.8 3.0 %collective-permute-start.11 = (bf16[128,1024]{1,0:T(8,128)(2,1)S(1)}, bf16[128,1024]{1,0:T(8,128)(2,1)S(1)}, u32[]{:S(2)}, u32[]{:S(2)}) collective-permute-start(bf16[128,1024]{1,0:T(8,128)(2,1)S(1)} %fusion.3), channel_id=1, source_target_pairs={{0,224},{8,40},{32,0},{40,72},{96,64},{104,136},{128,96},{136,168}... | collective-permute-start | bytes 786440 | tf_op jit(solution)/shard_map/ppermute | solution.py:230
  55.8 6.5 %collective-permute-done.10 = bf16[256,512]{1,0:T(8,128)(2,1)S(1)} collective-permute-done((bf16[256,512]{1,0:T(8,128)(2,1)S(1)}, bf16[256,512]{1,0:T(8,128)(2,1)S(1)}, u32[]{:S(2)}, u32[]{:S(2)}) %collective-permute-start.10) | collective-permute-done | bytes 262176 | tf_op jit(solution)/shard_map/ppermute | solution.py:230
  67.5 3.0 %collective-permute-start.14 = (bf16[2,128,1024]{2,1,0:T(8,128)(2,1)S(1)}, bf16[2,128,1024]{2,1,0:T(8,128)(2,1)S(1)}, u32[]{:S(2)}, u32[]{:S(2)}) collective-permute-start(bf16[2,128,1024]{2,1,0:T(8,128)(2,1)S(1)} %add_convert_fusion.2), channel_id=1, source_target_pairs={{0,224},{8,40},{40,72},{64,32},{72,104},{96,64},{128,96},{136,168}... | collective-permute-start | bytes 1572872 | tf_op jit(solution)/shard_map/ppermute | solution.py:230
  71.6 2.4 %collective-permute-start.15 = (bf16[1,128,1024]{2,1,0:T(8,128)(2,1)S(1)}, bf16[1,128,1024]{2,1,0:T(8,128)(2,1)S(1)}, u32[]{:S(2)}, u32[]{:S(2)}) collective-permute-start(bf16[1,128,1024]{2,1,0:T(8,128)(2,1)S(1)} %copy-done.14), channel_id=1, source_target_pairs={{0,16},{16,0},{1,17},{17,1},{2,18},{18,2},{3,19},{19,3},{4,20},{20... | collective-permute-start | bytes 786440 | tf_op jit(solution)/shard_map/ppermute | solution.py:230
  74.0 5.9 %collective-permute-done.13 = bf16[2,256,256]{2,1,0:T(8,128)(2,1)S(1)} collective-permute-done((bf16[2,256,256]{2,1,0:T(8,128)(2,1)S(1)}, bf16[2,256,256]{2,1,0:T(8,128)(2,1)S(1)}, u32[]{:S(2)}, u32[]{:S(2)}) %collective-permute-start.13) | collective-permute-done | bytes 262176 | tf_op jit(solution)/shard_map/ppermute | solution.py:230
  80.8 2.9 %collective-permute-start.16 = (bf16[2,256,256]{2,1,0:T(8,128)(2,1)S(1)}, bf16[2,256,256]{2,1,0:T(8,128)(2,1)S(1)}, u32[]{:S(2)}, u32[]{:S(2)}) collective-permute-start(bf16[2,256,256]{2,1,0:T(8,128)(2,1)S(1)} %collective-permute-done.13), channel_id=1, source_target_pairs={{0,224},{8,40},{32,0},{40,72},{64,32},{72,104},{96,64},{104,136},{... | collective-permute-start | bytes 786440 | tf_op jit(solution)/shard_map/ppermute | solution.py:230
  83.7 3.1 %collective-permute-start.17 = (bf16[1,128,1024]{2,1,0:T(8,128)(2,1)S(1)}, bf16[1,128,1024]{2,1,0:T(8,128)(2,1)S(1)}, u32[]{:S(2)}, u32[]{:S(2)}) collective-permute-start(bf16[1,128,1024]{2,1,0:T(8,128)(2,1)S(1)} %copy-done.12), channel_id=1, source_target_pairs={{0,16},{16,0},{1,17},{17,1},{2,18},{18,2},{3,19},{19,3},{4,20},{20... | collective-permute-start | bytes 786440 | tf_op jit(solution)/shard_map/ppermute | solution.py:230
  88.2 3.4 %collective-permute-done.17 = bf16[1,128,1024]{2,1,0:T(8,128)(2,1)S(1)} collective-permute-done((bf16[1,128,1024]{2,1,0:T(8,128)(2,1)S(1)}, bf16[1,128,1024]{2,1,0:T(8,128)(2,1)S(1)}, u32[]{:S(2)}, u32[]{:S(2)}) %collective-permute-start.17) | collective-permute-done | bytes 262176 | tf_op jit(solution)/shard_map/ppermute | solution.py:230
  92.1 2.7 %collective-permute-start.19 = (bf16[1,128,1024]{2,1,0:T(8,128)(2,1)S(1)}, bf16[1,128,1024]{2,1,0:T(8,128)(2,1)S(1)}, u32[]{:S(2)}, u32[]{:S(2)}) collective-permute-start(bf16[1,128,1024]{2,1,0:T(8,128)(2,1)S(1)} %copy-done.10), channel_id=1, source_target_pairs={{0,16},{16,0},{1,17},{17,1},{2,18},{18,2},{3,19},{19,3},{4,20},{20... | collective-permute-start | bytes 786440 | tf_op jit(solution)/shard_map/ppermute | solution.py:230
  94.8 3.1 %collective-permute-done.18 = bf16[2,256,256]{2,1,0:T(8,128)(2,1)S(1)} collective-permute-done((bf16[2,256,256]{2,1,0:T(8,128)(2,1)S(1)}, bf16[2,256,256]{2,1,0:T(8,128)(2,1)S(1)}, u32[]{:S(2)}, u32[]{:S(2)}) %collective-permute-start.18) | collective-permute-done | bytes 262176 | tf_op jit(solution)/shard_map/ppermute | solution.py:230
  101.6 2.5 %collective-permute-start.21 = (bf16[1,128,1024]{2,1,0:T(8,128)(2,1)S(1)}, bf16[1,128,1024]{2,1,0:T(8,128)(2,1)S(1)}, u32[]{:S(2)}, u32[]{:S(2)}) collective-permute-start(bf16[1,128,1024]{2,1,0:T(8,128)(2,1)S(1)} %copy-done.8), channel_id=1, source_target_pairs={{0,16},{16,0},{1,17},{17,1},{2,18},{18,2},{3,19},{19,3},{4,20},{20... | collective-permute-start | bytes 786440 | tf_op jit(solution)/shard_map/ppermute | solution.py:230
  104.1 2.1 %add_convert_fusion.1 = bf16[2,128,1024]{2,1,0:T(8,128)(2,1)} fusion(bf16[2,128,1024]{2,1,0:T(8,128)(2,1)S(1)} %collective-permute-done.14, bf16[1,128,1024]{2,1,0:T(8,128)(2,1)S(1)} %collective-permute-done.17, bf16[1,128,1024]{2,1,0:T(8,128)(2,1)S(1)} %collective-permute-done.15, bf16[5,128,1024]{2,1,0:T(8,128)(2,1)} %copy-done.4), kind=kLoop, calls=%fused_computation.5 | loop fusion | flops 1835008 | bytes 2097152 | tf_op jit(solution)/shard_map/convert_element_type | solution.py:359
  106.3 3.2 %collective-permute-done.21 = bf16[1,128,1024]{2,1,0:T(8,128)(2,1)S(1)} collective-permute-done((bf16[1,128,1024]{2,1,0:T(8,128)(2,1)S(1)}, bf16[1,128,1024]{2,1,0:T(8,128)(2,1)S(1)}, u32[]{:S(2)}, u32[]{:S(2)}) %collective-permute-start.21) | collective-permute-done | bytes 262176 | tf_op jit(solution)/shard_map/ppermute | solution.py:230
  112.5 5.1 %all-to-all-start = ((bf16[8,256,256]{2,1,0:T(8,128)(2,1)}), bf16[8,256,256]{2,1,0:T(8,128)(2,1)S(1)}, u32[]{:S(2)}, u32[]{:S(2)}) async-start(bf16[8,256,256]{2,1,0:T(8,128)(2,1)} %broadcast_in_dim.22), calls=%async_computation | async-start | bytes 2097152 | tf_op jit(solution)/shard_map/all_to_all | solution.py:356
  117.6 5.0 %collective-permute-done.22 = bf16[2,128,1024]{2,1,0:T(8,128)(2,1)} collective-permute-done((bf16[2,128,1024]{2,1,0:T(8,128)(2,1)}, bf16[2,128,1024]{2,1,0:T(8,128)(2,1)}, u32[]{:S(2)}, u32[]{:S(2)}) %collective-permute-start.22) | collective-permute-done | bytes 524320 | tf_op jit(solution)/shard_map/ppermute | solution.py:230
  124.2 7.9 %collective-permute-start.24 = (bf16[2,128,1024]{2,1,0:T(8,128)(2,1)S(1)}, bf16[2,128,1024]{2,1,0:T(8,128)(2,1)}, u32[]{:S(2)}, u32[]{:S(2)}) collective-permute-start(bf16[2,128,1024]{2,1,0:T(8,128)(2,1)S(1)} %add_convert_fusion), channel_id=1, source_target_pairs={{0,224},{8,40},{32,0},{64,32},{72,104},{104,136},{128,96},{136,168... | collective-permute-start | bytes 1572872 | tf_op jit(solution)/shard_map/ppermute | solution.py:230
  134.2 7.8 %shard_map.41 = bf16[1024,1024]{1,0:T(8,128)(2,1)S(1)} custom-call(s32[2]{0:T(128)S(1)} %pad_add_fusion.1.at_ref, bf16[2,256,256]{2,1,0:T(8,128)(2,1)S(1)} %pad_maximum_fusion.6.shard_ref, bf16[7,256,256]{2,1,0:T(8,128)(2,1)S(1)} %pad_maximum_fusion.own_ref, bf16[7,256,256]{2,1,0:T(8,128)(2,1)S(1)} %collective-permute-done.23.other_ref), custom_call_target="tpu_custom_call" | custom-call | tf_op jit(solution)/shard_map/pallas_call | solution.py:203
  144.7 3.1 %collective-permute-done.26 = bf16[2,128,1024]{2,1,0:T(8,128)(2,1)S(1)} collective-permute-done((bf16[2,128,1024]{2,1,0:T(8,128)(2,1)}, bf16[2,128,1024]{2,1,0:T(8,128)(2,1)S(1)}, u32[]{:S(2)}, u32[]{:S(2)}) %collective-permute-start.26) | collective-permute-done | bytes 524320 | tf_op jit(solution)/shard_map/ppermute | solution.py:230
  147.8 2.5 %convolution_convert_fusion = bf16[128,1024]{1,0:T(8,128)(2,1)S(1)} fusion(bf16[1024,1024]{1,0:T(8,128)(2,1)} %copy-done, bf16[1,128,1024]{2,1,0:T(8,128)(2,1)} %copy-done.20, bf16[5,128,1024]{2,1,0:T(8,128)(2,1)} %copy-done.4, bf16[2,128,1024]{2,1,0:T(8,128)(2,1)S(1)} %collective-permute-done.26, bf16[2,128,1024]{2,1,0:T(8,128)(2,1)} %collective-permute-done.24, ...), kind=kOutput, calls=%fused_computation.2 | convolution fusion | flops 269877248 | bytes 3932161 | tf_op jit(solution)/shard_map/dot_general | solution.py:32
  155.7 7.7 %shard_map.42 = (bf16[1024,1024]{1,0:T(8,128)(2,1)S(1)}, bf16[384,1024]{1,0:T(8,128)(2,1)S(1)}) custom-call(s32[3]{0:T(128)S(1)} %pad_add_fusion.2.at_ref, bf16[8,256,256]{2,1,0:T(8,128)(2,1)S(1)} %all-to-all-done.own_ref, bf16[8,256,256]{2,1,0:T(8,128)(2,1)S(1)} %collective-permute-done.27.other_ref), custom_call_target="tpu_custom_call" | custom-call | tf_op jit(solution)/shard_map/pallas_call | solution.py:203
  169.2 6.4 %all-to-all-start.1 = ((f32[8,1,128]{2,1,0:T(1,128)}), f32[8,1,128]{2,1,0:T(1,128)S(1)}, u32[]{:S(2)}, u32[]{:S(2)}) async-start(f32[8,1,128]{2,1,0:T(1,128)} %broadcast_in_dim.23), calls=%async_computation.1 | async-start | bytes 8192 | tf_op jit(solution)/shard_map/all_to_all | solution.py:246
  176.2 7.0 %all-to-all-done.1 = f32[8,1,128]{2,1,0:T(1,128)S(1)} async-done(((f32[8,1,128]{2,1,0:T(1,128)}), f32[8,1,128]{2,1,0:T(1,128)S(1)}, u32[]{:S(2)}, u32[]{:S(2)}) %all-to-all-start.1) | async-done | bytes 4128 | tf_op jit(solution)/shard_map/all_to_all | solution.py:246
  184.4 2.5 %collective-permute-start.32 = (bf16[192,512]{1,0:T(8,128)(2,1)S(1)}, bf16[192,512]{1,0:T(8,128)(2,1)S(1)}, u32[]{:S(2)}, u32[]{:S(2)}) collective-permute-start(bf16[192,512]{1,0:T(8,128)(2,1)S(1)} %slice.167), channel_id=1, source_target_pairs={{0,32},{32,64},{128,160},{160,192},{1,33},{33,65},{129,161},{161,1... | collective-permute-start | bytes 589832 | tf_op jit(solution)/shard_map/ppermute | solution.py:418
  187.6 10.8 %all_to_all.23 = f32[8,1,128]{2,1,0:T(1,128)S(1)} all-to-all(f32[8,1,128]{2,1,0:T(1,128)S(1)} %broadcast_in_dim.24), channel_id=1, replica_groups=mesh['dp_0'=8,'dp_1'=2,'dp_2'=2,'owner_0'=2,'owner_1'=4] {'owner_0','own..., dimensions={0} | all-to-all | bytes 8192 | tf_op jit(solution)/shard_map/all_to_all | solution.py:246
  (135 shorter events, 50.2 us)
Async XLA Ops:
  2.2 3.9 %collective-permute-start = (bf16[128,4608]{1,0:T(8,128)(2,1)S(1)}, bf16[128,4608]{1,0:T(8,128)(2,1)S(1)}, u32[]{:S(2)}, u32[]{:S(2)}) collective-permute-start(bf16[128,4608]{1,0:T(8,128)(2,1)S(1)} %shard_map.37.pick_ref), channel_id=1, source_target_pairs={{0,8},{8,0},{1,9},{9,1},{2,10},{10,2},{3,11},{11,3},{4,12},{12,4},... | collective-permute-start | bytes 3538952 | tf_op jit(solution)/shard_map/ppermute | solution.py:271
  11.3 9.1 %collective-permute-start.2 = (bf16[256,384]{1,0:T(8,128)(2,1)S(1)}, bf16[256,384]{1,0:T(8,128)(2,1)S(1)}, u32[]{:S(2)}, u32[]{:S(2)}) collective-permute-start(bf16[256,384]{1,0:T(8,128)(2,1)S(1)} %bitcast.72), channel_id=1, source_target_pairs={{0,224},{8,40},{32,0},{40,72},{64,32},{72,104},{96,64},{104,136},{... | collective-permute-start | bytes 589832 | tf_op jit(solution)/shard_map/ppermute | solution.py:230
  20.5 11.6 %collective-permute-start.3 = (bf16[2,256,384]{2,1,0:T(8,128)(2,1)S(1)}, bf16[2,256,384]{2,1,0:T(8,128)(2,1)S(1)}, u32[]{:S(2)}, u32[]{:S(2)}) collective-permute-start(bf16[2,256,384]{2,1,0:T(8,128)(2,1)S(1)} %add_convert_fusion.5), channel_id=1, source_target_pairs={{0,224},{8,40},{32,0},{40,72},{64,32},{72,104},{96,64},{104,136},{... | collective-permute-start | bytes 1179656 | tf_op jit(solution)/shard_map/ppermute | solution.py:230
  24.2 7.9 %collective-permute-start.4 = (bf16[1,128,1024]{2,1,0:T(8,128)(2,1)S(1)}, bf16[1,128,1024]{2,1,0:T(8,128)(2,1)S(1)}, u32[]{:S(2)}, u32[]{:S(2)}) collective-permute-start(bf16[1,128,1024]{2,1,0:T(8,128)(2,1)S(1)} %get-tuple-element.86), channel_id=1, source_target_pairs={{0,16},{16,0},{1,17},{17,1},{2,18},{18,2},{3,19},{19,3},{4,20},{20... | collective-permute-start | bytes 786440 | tf_op jit(solution)/shard_map/ppermute | solution.py:230
  32.2 9.2 %collective-permute-start.5 = (bf16[2,256,384]{2,1,0:T(8,128)(2,1)S(1)}, bf16[2,256,384]{2,1,0:T(8,128)(2,1)S(1)}, u32[]{:S(2)}, u32[]{:S(2)}) collective-permute-start(bf16[2,256,384]{2,1,0:T(8,128)(2,1)S(1)} %add_convert_fusion.4), channel_id=1, source_target_pairs={{0,224},{8,40},{32,0},{40,72},{64,32},{72,104},{96,64},{104,136},{... | collective-permute-start | bytes 1179656 | tf_op jit(solution)/shard_map/ppermute | solution.py:230
  33.4 8.0 %collective-permute-start.6 = (bf16[1,128,1024]{2,1,0:T(8,128)(2,1)S(1)}, bf16[1,128,1024]{2,1,0:T(8,128)(2,1)}, u32[]{:S(2)}, u32[]{:S(2)}) collective-permute-start(bf16[1,128,1024]{2,1,0:T(8,128)(2,1)S(1)} %get-tuple-element.90), channel_id=1, source_target_pairs={{0,16},{16,0},{1,17},{17,1},{2,18},{18,2},{3,19},{19,3},{4,20},{20... | collective-permute-start | bytes 786440 | tf_op jit(solution)/shard_map/ppermute | solution.py:230
  41.5 9.0 %collective-permute-start.7 = (bf16[2,256,384]{2,1,0:T(8,128)(2,1)S(1)}, bf16[2,256,384]{2,1,0:T(8,128)(2,1)S(1)}, u32[]{:S(2)}, u32[]{:S(2)}) collective-permute-start(bf16[2,256,384]{2,1,0:T(8,128)(2,1)S(1)} %add_convert_fusion.3), channel_id=1, source_target_pairs={{0,224},{8,40},{32,0},{40,72},{64,32},{72,104},{96,64},{104,136},{... | collective-permute-start | bytes 1179656 | tf_op jit(solution)/shard_map/ppermute | solution.py:230
  42.6 7.9 %collective-permute-start.8 = (bf16[1,128,1024]{2,1,0:T(8,128)(2,1)S(1)}, bf16[1,128,1024]{2,1,0:T(8,128)(2,1)S(1)}, u32[]{:S(2)}, u32[]{:S(2)}) collective-permute-start(bf16[1,128,1024]{2,1,0:T(8,128)(2,1)S(1)} %get-tuple-element.94), channel_id=1, source_target_pairs={{0,16},{16,0},{1,17},{17,1},{2,18},{18,2},{3,19},{19,3},{4,20},{20... | collective-permute-start | bytes 786440 | tf_op jit(solution)/shard_map/ppermute | solution.py:230
  52.3 9.9 %collective-permute-start.10 = (bf16[256,512]{1,0:T(8,128)(2,1)S(1)}, bf16[256,512]{1,0:T(8,128)(2,1)S(1)}, u32[]{:S(2)}, u32[]{:S(2)}) collective-permute-start(bf16[256,512]{1,0:T(8,128)(2,1)S(1)} %add_convert_fusion.9), channel_id=1, source_target_pairs={{0,16},{16,0},{1,17},{17,1},{2,18},{18,2},{3,19},{19,3},{4,20},{20... | collective-permute-start | bytes 786440 | tf_op jit(solution)/shard_map/ppermute | solution.py:230
  52.8 9.5 %collective-permute-start.11 = (bf16[128,1024]{1,0:T(8,128)(2,1)S(1)}, bf16[128,1024]{1,0:T(8,128)(2,1)S(1)}, u32[]{:S(2)}, u32[]{:S(2)}) collective-permute-start(bf16[128,1024]{1,0:T(8,128)(2,1)S(1)} %fusion.3), channel_id=1, source_target_pairs={{0,224},{8,40},{32,0},{40,72},{96,64},{104,136},{128,96},{136,168}... | collective-permute-start | bytes 786440 | tf_op jit(solution)/shard_map/ppermute | solution.py:230
  62.4 5.1 %collective-permute-start.12 = (bf16[256,256]{1,0:T(8,128)(2,1)S(1)}, bf16[256,256]{1,0:T(8,128)(2,1)S(1)}, u32[]{:S(2)}, u32[]{:S(2)}) collective-permute-start(bf16[256,256]{1,0:T(8,128)(2,1)S(1)} %slice.111), channel_id=1, source_target_pairs={{0,1},{1,0},{2,3},{3,2},{4,5},{5,4},{6,7},{7,6},{8,9},{9,8},{10,11... | collective-permute-start | bytes 393224 | tf_op jit(solution)/shard_map/ppermute | solution.py:230
  67.5 13.3 %collective-permute-start.14 = (bf16[2,128,1024]{2,1,0:T(8,128)(2,1)S(1)}, bf16[2,128,1024]{2,1,0:T(8,128)(2,1)S(1)}, u32[]{:S(2)}, u32[]{:S(2)}) collective-permute-start(bf16[2,128,1024]{2,1,0:T(8,128)(2,1)S(1)} %add_convert_fusion.2), channel_id=1, source_target_pairs={{0,224},{8,40},{40,72},{64,32},{72,104},{96,64},{128,96},{136,168}... | collective-permute-start | bytes 1572872 | tf_op jit(solution)/shard_map/ppermute | solution.py:230
  70.5 9.5 %collective-permute-start.13 = (bf16[2,256,256]{2,1,0:T(8,128)(2,1)S(1)}, bf16[2,256,256]{2,1,0:T(8,128)(2,1)S(1)}, u32[]{:S(2)}, u32[]{:S(2)}) collective-permute-start(bf16[2,256,256]{2,1,0:T(8,128)(2,1)S(1)} %pad_maximum_fusion.6.shard_ref), channel_id=1, source_target_pairs={{0,224},{8,40},{32,0},{40,72},{64,32},{72,104},{96,64},{104,136},{... | collective-permute-start | bytes 786440 | tf_op jit(solution)/shard_map/ppermute | solution.py:230
  71.6 9.2 %collective-permute-start.15 = (bf16[1,128,1024]{2,1,0:T(8,128)(2,1)S(1)}, bf16[1,128,1024]{2,1,0:T(8,128)(2,1)S(1)}, u32[]{:S(2)}, u32[]{:S(2)}) collective-permute-start(bf16[1,128,1024]{2,1,0:T(8,128)(2,1)S(1)} %copy-done.14), channel_id=1, source_target_pairs={{0,16},{16,0},{1,17},{17,1},{2,18},{18,2},{3,19},{19,3},{4,20},{20... | collective-permute-start | bytes 786440 | tf_op jit(solution)/shard_map/ppermute | solution.py:230
  80.8 7.3 %collective-permute-start.16 = (bf16[2,256,256]{2,1,0:T(8,128)(2,1)S(1)}, bf16[2,256,256]{2,1,0:T(8,128)(2,1)S(1)}, u32[]{:S(2)}, u32[]{:S(2)}) collective-permute-start(bf16[2,256,256]{2,1,0:T(8,128)(2,1)S(1)} %collective-permute-done.13), channel_id=1, source_target_pairs={{0,224},{8,40},{32,0},{40,72},{64,32},{72,104},{96,64},{104,136},{... | collective-permute-start | bytes 786440 | tf_op jit(solution)/shard_map/ppermute | solution.py:230
  83.7 7.9 %collective-permute-start.17 = (bf16[1,128,1024]{2,1,0:T(8,128)(2,1)S(1)}, bf16[1,128,1024]{2,1,0:T(8,128)(2,1)S(1)}, u32[]{:S(2)}, u32[]{:S(2)}) collective-permute-start(bf16[1,128,1024]{2,1,0:T(8,128)(2,1)S(1)} %copy-done.12), channel_id=1, source_target_pairs={{0,16},{16,0},{1,17},{17,1},{2,18},{18,2},{3,19},{19,3},{4,20},{20... | collective-permute-start | bytes 786440 | tf_op jit(solution)/shard_map/ppermute | solution.py:230
  91.6 6.4 %collective-permute-start.18 = (bf16[2,256,256]{2,1,0:T(8,128)(2,1)S(1)}, bf16[2,256,256]{2,1,0:T(8,128)(2,1)S(1)}, u32[]{:S(2)}, u32[]{:S(2)}) collective-permute-start(bf16[2,256,256]{2,1,0:T(8,128)(2,1)S(1)} %collective-permute-done.16), channel_id=1, source_target_pairs={{0,224},{8,40},{32,0},{40,72},{64,32},{72,104},{96,64},{104,136},{... | collective-permute-start | bytes 786440 | tf_op jit(solution)/shard_map/ppermute | solution.py:230
  92.1 7.9 %collective-permute-start.19 = (bf16[1,128,1024]{2,1,0:T(8,128)(2,1)S(1)}, bf16[1,128,1024]{2,1,0:T(8,128)(2,1)S(1)}, u32[]{:S(2)}, u32[]{:S(2)}) collective-permute-start(bf16[1,128,1024]{2,1,0:T(8,128)(2,1)S(1)} %copy-done.10), channel_id=1, source_target_pairs={{0,16},{16,0},{1,17},{17,1},{2,18},{18,2},{3,19},{19,3},{4,20},{20... | collective-permute-start | bytes 786440 | tf_op jit(solution)/shard_map/ppermute | solution.py:230
  100.0 6.3 %collective-permute-start.20 = (bf16[1,256,256]{2,1,0:T(8,128)(2,1)S(1)}, bf16[1,256,256]{2,1,0:T(8,128)(2,1)S(1)}, u32[]{:S(2)}, u32[]{:S(2)}) collective-permute-start(bf16[1,256,256]{2,1,0:T(8,128)(2,1)S(1)} %slice_select_fusion), channel_id=1, source_target_pairs={{0,224},{8,40},{32,0},{40,72},{64,32},{72,104},{96,64},{104,136},{... | collective-permute-start | bytes 393224 | tf_op jit(solution)/shard_map/ppermute | solution.py:230
  101.6 7.9 %collective-permute-start.21 = (bf16[1,128,1024]{2,1,0:T(8,128)(2,1)S(1)}, bf16[1,128,1024]{2,1,0:T(8,128)(2,1)S(1)}, u32[]{:S(2)}, u32[]{:S(2)}) collective-permute-start(bf16[1,128,1024]{2,1,0:T(8,128)(2,1)S(1)} %copy-done.8), channel_id=1, source_target_pairs={{0,16},{16,0},{1,17},{17,1},{2,18},{18,2},{3,19},{19,3},{4,20},{20... | collective-permute-start | bytes 786440 | tf_op jit(solution)/shard_map/ppermute | solution.py:230
  111.2 11.4 %collective-permute-start.23 = (bf16[7,256,256]{2,1,0:T(8,128)(2,1)S(1)}, bf16[7,256,256]{2,1,0:T(8,128)(2,1)S(1)}, u32[]{:S(2)}, u32[]{:S(2)}) collective-permute-start(bf16[7,256,256]{2,1,0:T(8,128)(2,1)S(1)} %pad_maximum_fusion.own_ref), channel_id=1, source_target_pairs={{0,8},{8,0},{1,9},{9,1},{2,10},{10,2},{3,11},{11,3},{4,12},{12,4},... | collective-permute-start | bytes 2752520 | tf_op jit(solution)/shard_map/ppermute | solution.py:230
  111.2 11.4 %collective-permute-start.22 = (bf16[2,128,1024]{2,1,0:T(8,128)(2,1)}, bf16[2,128,1024]{2,1,0:T(8,128)(2,1)}, u32[]{:S(2)}, u32[]{:S(2)}) collective-permute-start(bf16[2,128,1024]{2,1,0:T(8,128)(2,1)} %add_convert_fusion.1), channel_id=1, source_target_pairs={{32,0},{40,72},{64,32},{72,104},{96,64},{104,136},{160,128},{168,2... | collective-permute-start | bytes 1572872 | tf_op jit(solution)/shard_map/ppermute | solution.py:230
  112.5 31.6 %all-to-all-start = ((bf16[8,256,256]{2,1,0:T(8,128)(2,1)}), bf16[8,256,256]{2,1,0:T(8,128)(2,1)S(1)}, u32[]{:S(2)}, u32[]{:S(2)}) async-start(bf16[8,256,256]{2,1,0:T(8,128)(2,1)} %broadcast_in_dim.22), calls=%async_computation | async-start | bytes 2097152 | tf_op jit(solution)/shard_map/all_to_all | solution.py:356
  124.2 19.9 %collective-permute-start.24 = (bf16[2,128,1024]{2,1,0:T(8,128)(2,1)S(1)}, bf16[2,128,1024]{2,1,0:T(8,128)(2,1)}, u32[]{:S(2)}, u32[]{:S(2)}) collective-permute-start(bf16[2,128,1024]{2,1,0:T(8,128)(2,1)S(1)} %add_convert_fusion), channel_id=1, source_target_pairs={{0,224},{8,40},{32,0},{64,32},{72,104},{104,136},{128,96},{136,168... | collective-permute-start | bytes 1572872 | tf_op jit(solution)/shard_map/ppermute | solution.py:230
  132.2 11.3 %collective-permute-start.25 = (bf16[1,128,1024]{2,1,0:T(8,128)(2,1)S(1)}, bf16[1,128,1024]{2,1,0:T(8,128)(2,1)S(1)}, u32[]{:S(2)}, u32[]{:S(2)}) collective-permute-start(bf16[1,128,1024]{2,1,0:T(8,128)(2,1)S(1)} %get-tuple-element.135), channel_id=1, source_target_pairs={{0,16},{16,0},{1,17},{17,1},{2,18},{18,2},{3,19},{19,3},{4,20},{20... | collective-permute-start | bytes 786440 | tf_op jit(solution)/shard_map/ppermute | solution.py:230
  144.1 3.6 %collective-permute-start.27 = (bf16[8,256,256]{2,1,0:T(8,128)(2,1)S(1)}, bf16[8,256,256]{2,1,0:T(8,128)(2,1)S(1)}, u32[]{:S(2)}, u32[]{:S(2)}) collective-permute-start(bf16[8,256,256]{2,1,0:T(8,128)(2,1)S(1)} %all-to-all-done.own_ref), channel_id=1, source_target_pairs={{0,8},{8,0},{1,9},{9,1},{2,10},{10,2},{3,11},{11,3},{4,12},{12,4},... | collective-permute-start | bytes 3145736 | tf_op jit(solution)/shard_map/ppermute | solution.py:230
  150.3 13.1 %collective-permute-start.28 = (bf16[128,512]{1,0:T(8,128)(2,1)S(1)}, bf16[128,512]{1,0:T(8,128)(2,1)S(1)}, u32[]{:S(2)}, u32[]{:S(2)}) collective-permute-start(bf16[128,512]{1,0:T(8,128)(2,1)S(1)} %get-tuple-element.147), channel_id=1, source_target_pairs={{0,1},{1,0},{2,3},{3,2},{4,5},{5,4},{6,7},{7,6},{8,9},{9,8},{10,11... | collective-permute-start | bytes 393224 | tf_op jit(solution)/shard_map/ppermute | solution.py:230
  152.1 11.3 %collective-permute-start.29 = (bf16[128,512]{1,0:T(8,128)(2,1)S(1)}, bf16[128,512]{1,0:T(8,128)(2,1)S(1)}, u32[]{:S(2)}, u32[]{:S(2)}) collective-permute-start(bf16[128,512]{1,0:T(8,128)(2,1)S(1)} %get-tuple-element.146), channel_id=1, source_target_pairs={{0,16},{16,0},{1,17},{17,1},{2,18},{18,2},{3,19},{19,3},{4,20},{20... | collective-permute-start | bytes 393224 | tf_op jit(solution)/shard_map/ppermute | solution.py:230
  153.6 9.9 %collective-permute-start.30 = (bf16[128,512]{1,0:T(8,128)(2,1)S(1)}, bf16[128,512]{1,0:T(8,128)(2,1)S(1)}, u32[]{:S(2)}, u32[]{:S(2)}) collective-permute-start(bf16[128,512]{1,0:T(8,128)(2,1)S(1)} %get-tuple-element.147), channel_id=1, source_target_pairs={{0,17},{1,16},{2,19},{3,18},{16,1},{17,0},{18,3},{19,2},{4,21},{5,... | collective-permute-start | bytes 393224 | tf_op jit(solution)/shard_map/ppermute | solution.py:230
  169.2 14.0 %all-to-all-start.1 = ((f32[8,1,128]{2,1,0:T(1,128)}), f32[8,1,128]{2,1,0:T(1,128)S(1)}, u32[]{:S(2)}, u32[]{:S(2)}) async-start(f32[8,1,128]{2,1,0:T(1,128)} %broadcast_in_dim.23), calls=%async_computation.1 | async-start | bytes 8192 | tf_op jit(solution)/shard_map/all_to_all | solution.py:246
  183.8 15.9 %collective-permute-start.33 = (bf16[192,512]{1,0:T(8,128)(2,1)S(1)}, bf16[192,512]{1,0:T(8,128)(2,1)S(1)}, u32[]{:S(2)}, u32[]{:S(2)}) collective-permute-start(bf16[192,512]{1,0:T(8,128)(2,1)S(1)} %slice.167), channel_id=1, source_target_pairs={{96,64},{224,192},{97,65},{225,193},{98,66},{226,194},{99,67},{227... | collective-permute-start | bytes 589832 | tf_op jit(solution)/shard_map/ppermute | solution.py:419
  184.4 15.3 %collective-permute-start.32 = (bf16[192,512]{1,0:T(8,128)(2,1)S(1)}, bf16[192,512]{1,0:T(8,128)(2,1)S(1)}, u32[]{:S(2)}, u32[]{:S(2)}) collective-permute-start(bf16[192,512]{1,0:T(8,128)(2,1)S(1)} %slice.167), channel_id=1, source_target_pairs={{0,32},{32,64},{128,160},{160,192},{1,33},{33,65},{129,161},{161,1... | collective-permute-start | bytes 589832 | tf_op jit(solution)/shard_map/ppermute | solution.py:418
  (25 other events, 202.8 us)
